TPU v7x, 32 devices: a whole 2x2x4 slice. The times are simulated.
32 devices in a mesh: dom: 8 (over z, y), box: 4 (over x, core).
Axes of the slice: x: 2, y: 2, z: 4, core: 2. Of those that a mesh axis runs over, the one named last changes fastest.
Arguments:
- old_history: bfloat16 [256, 128, 128], P(('dom', 'box')), may hold values from -24 to 24
- box_route: int32 [256], P(('dom', 'box')), may hold values from 0 to 3, as said below
- entry_slot: int32 [256, 4], P(('dom', 'box')), may hold values from 0 to 15
- entry_count: int32 [256], P(('dom', 'box')), may hold values from 1 to 4, as said below
- weights: bfloat16 [256, 4, 128, 128], P(('dom', 'box')), may hold values from 0.049804688 to 1
- owner_route: int32 [32768], P(('dom', 'box')), may hold values from 0 to 7, as said below
- owner_slot: int32 [32768], P(('dom', 'box')), may hold values from 0 to 1023, as said below
- connectivity: int32 [8, 32768], P(None, ('dom', 'box')), may hold values from 0 to 1023
- shared_nodes: int32 [4, 4096], P(None, ('dom', 'box')), may hold values from 0 to 1023, as said below
- node_motion: float32 [3, 32768], P(None, ('dom', 'box')), may hold values from -6 to 6
- elem_size: float32 [32768], P(('dom', 'box')), may hold values from 0.7 to 1.4
- decay: float32 [128], replicated, may hold values from 0.2 to 0.95
- couple: float32 [128, 6], replicated, may hold values from -2.5 to 2.5
- readout: float32 [128, 6], replicated, may hold values from -0.5 to 0.5
Outputs:
- new_history: bfloat16 [32768, 128], P(('dom', 'box'))
- node_force: float32 [3, 32768], P(None, ('dom', 'box'))
Inputs may be any that keep to these rules, and one draw needn't show every extreme that they name: `box_route`: among the 8 blocks of one device at most 4 name the same box. For every dom index one box receives exactly 4 blocks from each of the 4 devices of that dom index; every box receives at least one block. `entry_count`: entries at or beyond a target's count are padding. Every device has a target with 4 entries. Within one box index, the pairs (owner_route, owner_slot) of all rows are distinct, so each new owner receives exactly 1024 rows. A device sends 128 rows to every new owner of its box index except 256 to one and none to another. `owner_slot`: see owner_route. `shared_nodes`: the 512 entries of one device are distinct local nodes. Entry m of row 0 on a device is the same node as entry m of row 1 on the device one lower along dom; rows 2 and 3 likewise along box.
All inputs are finite; a program needn't handle non-finite values.
Results may differ from a plain program's by a relative error of at most 0.0029.
Values may be sent and summed in bfloat16 or wider, within the bound.
No kernel may reach another device: no remote copies, remote signals or barrier semaphores. Data moves between devices by JAX's collectives and lax.ppermute only.
A program may use at most 64 MiB of HBM per device.

v0:
```python
import jax
import jax.numpy as jnp
from jax import lax
from jax.sharding import PartitionSpec as P


def extended(cells, sides, width):
    for axis, dim in sides:
        count = lax.axis_size(axis)
        ends = count - 1
        head = lax.slice_in_dim(cells, 0, width, axis=dim)
        tail = lax.slice_in_dim(cells, cells.shape[dim] - width, cells.shape[dim], axis=dim)
        cells = jnp.concatenate(
            [
                lax.ppermute(tail, axis, [(i, (i + 1) % count) for i in range(ends)]),
                cells,
                lax.ppermute(head, axis, [((i + 1) % count, i) for i in range(ends)]),
            ],
            axis=dim,
        )
    return cells


def exclusive_order(targets, choice_total):
    one_hot = (targets[:, None] == jnp.arange(choice_total, dtype=jnp.int32)[None, :]).astype(
        jnp.int32
    )
    return jnp.sum((jnp.cumsum(one_hot, axis=0) - one_hot) * one_hot, axis=1)


def corner_signs():
    corners = jnp.arange(8, dtype=jnp.int32)
    directions = jnp.arange(3, dtype=jnp.int32)
    return (2 * (corners[None, :] >> directions[:, None] & 1) - 1).astype(jnp.float32)


def element_forces(arrived, connectivity, node_motion, elem_size, decay, couple, readout):
    highest = lax.Precision.HIGHEST
    signs = corner_signs()
    corner_motion = node_motion[:, connectivity]
    gradient = (
        jnp.einsum("ca,iae->ice", signs, corner_motion, precision=highest)
        / (4.0 * elem_size)[None, None, :]
    )
    strain = jnp.stack(
        [
            gradient[0, 0],
            gradient[1, 1],
            gradient[2, 2],
            gradient[0, 1] + gradient[1, 0],
            gradient[1, 2] + gradient[2, 1],
            gradient[2, 0] + gradient[0, 2],
        ]
    )
    history = arrived.astype(jnp.float32) * decay[None, :] + jnp.einsum(
        "ce,hc->eh", strain, couple, precision=highest
    )
    volume_part = 1.2 * (strain[0] + strain[1] + strain[2])
    elastic = jnp.stack(
        [
            volume_part + 1.6 * strain[0],
            volume_part + 1.6 * strain[1],
            volume_part + 1.6 * strain[2],
            0.8 * strain[3],
            0.8 * strain[4],
            0.8 * strain[5],
        ]
    )
    stress = elastic + jnp.einsum("eh,hc->ce", history, readout, precision=highest)
    tensor = jnp.stack(
        [
            jnp.stack([stress[0], stress[3], stress[5]]),
            jnp.stack([stress[3], stress[1], stress[4]]),
            jnp.stack([stress[5], stress[4], stress[2]]),
        ]
    )
    corner_force = (elem_size * elem_size / 4.0)[None, None, :] * jnp.einsum(
        "ca,ice->iae", signs, tensor, precision=highest
    )
    local = jax.ops.segment_sum(
        corner_force.reshape(3, -1).T, connectivity.reshape(-1), num_segments=node_motion.shape[1]
    ).T
    return (history.astype(jnp.bfloat16), local)


def body(
    old_history,
    box_route,
    entry_slot,
    entry_count,
    weights,
    owner_route,
    owner_slot,
    connectivity,
    shared_nodes,
    node_motion,
    elem_size,
    decay,
    couple,
    readout,
):
    block_count, width, block_size = old_history.shape
    targets, entries = entry_slot.shape
    box_total = lax.axis_size("box")
    capacity = block_count // 2
    live = jnp.arange(entries, dtype=jnp.int32)[None, :] < entry_count[:, None]
    live_weight = live.astype(jnp.bfloat16)
    mass = jnp.einsum("tl,tlij->tj", live_weight, weights, preferred_element_type=jnp.float32)
    order_in = exclusive_order(box_route, box_total)
    send_slot = box_route * capacity + order_in
    outgoing = (
        jnp.zeros((box_total * capacity, width, block_size), jnp.bfloat16)
        .at[send_slot]
        .set(old_history)
    )
    incoming = lax.all_to_all(
        outgoing.reshape(box_total, capacity, width, block_size),
        "box",
        split_axis=0,
        concat_axis=0,
        tiled=True,
    )
    incoming = incoming.reshape(box_total * capacity, width, block_size)
    picked = incoming[entry_slot] * live_weight[:, :, None, None]
    numerator = jnp.einsum("tlhi,tlij->tjh", picked, weights, preferred_element_type=jnp.float32)
    projected = (
        (numerator / mass[:, :, None]).astype(jnp.bfloat16).reshape(targets * block_size, width)
    )
    element_total = projected.shape[0]
    dom_total = lax.axis_size("dom")
    usual = element_total // dom_total
    owner_order = exclusive_order(owner_route, dom_total)
    owner_capacity = 2 * usual
    owner_place = owner_route * owner_capacity + owner_order
    send_rows = (
        jnp.zeros((dom_total * owner_capacity, width), jnp.bfloat16).at[owner_place].set(projected)
    )
    send_positions = (
        jnp.full((dom_total * owner_capacity,), element_total, jnp.int32)
        .at[owner_place]
        .set(owner_slot)
    )
    got_rows, got_positions = (
        lax.all_to_all(
            send_rows.reshape(dom_total, owner_capacity, width),
            "dom",
            split_axis=0,
            concat_axis=0,
            tiled=True,
        ),
        lax.all_to_all(
            send_positions.reshape(dom_total, owner_capacity),
            "dom",
            split_axis=0,
            concat_axis=0,
            tiled=True,
        ),
    )
    arrived = (
        jnp.zeros((element_total, width), jnp.bfloat16)
        .at[got_positions.reshape(-1)]
        .set(got_rows.reshape(-1, width), mode="drop")
    )
    new_history, local = element_forces(
        arrived, connectivity, node_motion, elem_size, decay, couple, readout
    )
    dom_exports = jnp.stack([local[:, shared_nodes[0]], local[:, shared_nodes[1]]])
    padded = extended(dom_exports, (("dom", 0),), 1)
    below = padded[0]
    above = padded[3]
    depth_exports = jnp.stack([local[:, shared_nodes[2]], local[:, shared_nodes[3]]])
    depth_padded = extended(depth_exports, (("box", 0),), 1)
    force = local.at[:, shared_nodes[0]].add(below)
    force = force.at[:, shared_nodes[1]].add(above)
    force = force.at[:, shared_nodes[2]].add(depth_padded[0])
    force = force.at[:, shared_nodes[3]].add(depth_padded[3])
    return (new_history, force)


def solution(mesh):
    return jax.shard_map(
        body,
        mesh=mesh,
        in_specs=(
            P(("dom", "box"), None, None),
            P(("dom", "box")),
            P(("dom", "box"), None),
            P(("dom", "box")),
            P(("dom", "box"), None, None, None),
            P(("dom", "box")),
            P(("dom", "box")),
            P(None, ("dom", "box")),
            P(None, ("dom", "box")),
            P(None, ("dom", "box")),
            P(("dom", "box")),
            P(),
            P(),
            P(),
        ),
        out_specs=(P(("dom", "box"), None), P(None, ("dom", "box"))),
        check_vma=False,
    )
```

profile of v0, /device:TPU:5, one launch (start us, length us, event | category | flops | bytes accessed | tf_op | source)
XLA Modules:
  0.0 159.2 jit_solution(7608276111490252436)
XLA Ops:
  0.7 0.7 fusion.49
  1.5 0.7 select_reduce_fusion
  2.2 0.7 compare_select_fusion.8
  2.8 0.9 broadcast_in_dim.19
  3.7 2.4 %scatter_fusion = bf16[16,128,128]{2,1,0:T(8,128)(2,1)} fusion(bf16[16,128,128]{2,1,0:T(8,128)(2,1)} %broadcast_in_dim.19, s32[8]{0:T(128)S(1)} %compare_select_fusion.8, bf16[8,128,128]{2,1,0:T(8,128)(2,1)} %param.14), kind=kCustom, calls=%fused_computation.7 | custom fusion | bytes 786464 | tf_op jit(solution)/shard_map/scatter | solution.py:114
  6.2 4.2 %all-to-all-start.1 = ((bf16[4,4,128,128]{3,2,1,0:T(8,128)(2,1)}), bf16[4,4,128,128]{3,2,1,0:T(8,128)(2,1)S(1)}, u32[]{:S(2)}, u32[]{:S(2)}) async-start(bf16[4,4,128,128]{3,2,1,0:T(8,128)(2,1)} %bitcast.5), calls=%async_computation.1 | async-start | bytes 1048576 | tf_op jit(solution)/shard_map/all_to_all | solution.py:116
  10.4 0.9 copy.24
  11.4 0.8 fusion.31
  12.1 27.7 %gather_fusion.1 = f32[8192,3]{1,0:T(8,128)} fusion(f32[3,1024]{0,1:T(8,128)S(1)} %copy.24, s32[8192]{0:T(1024)S(1)} %bitcast_clamp_fusion), kind=kCustom, calls=%fused_computation.1 | custom fusion | bytes 229376 | tf_op jit(solution)/shard_map/gather | solution.py:40
  39.8 2.9 %copy.25 = f32[8,1024,3]{1,0,2:T(8,128)S(1)} copy(f32[8,1024,3]{2,1,0:T(8,128)} %bitcast.162) | data formatting | bytes 196608 | tf_op jit(solution)/shard_map/gather | solution.py:40
  43.0 2.3 %reduce-window.6 = s32[8,8,128]{2,1,0:T(8,128)S(1)} reduce-window(s32[8,8,128]{2,1,0:T(8,128)S(1)} %fusion.35, s32[]{:T(128)} %constant.19.clone.1), window={size=1x1x128 pad=0_0x0_0x127_0}, to_apply=%region_0.0 | reduce-window | flops 1040384 | bytes 65540 | tf_op jit(solution)/shard_map/reduce-window
  46.5 5.0 %scatter_custom_fusion = s32[2048]{0:T(1024)} fusion(s32[1024]{0:T(1024)S(1)} %compare_select_fusion.2, s32[1024]{0:T(1024)} %param.20, s32[]{:T(128)} %constant.17.clone.1), kind=kCustom, calls=%fused_computation.91 | custom fusion | bytes 8704 | tf_op jit(solution)/shard_map/scatter | solution.py:141
  51.5 5.8 %all-to-all-start = ((s32[8,1,256]{2,1,0:T(1,128)}), s32[8,1,256]{2,1,0:T(1,128)S(1)}, u32[]{:S(2)}, u32[]{:S(2)}) async-start(s32[8,1,256]{2,1,0:T(1,128)} %bitcast.2), calls=%async_computation | async-start | bytes 16384 | tf_op jit(solution)/shard_map/all_to_all | solution.py:151
  57.4 0.7 gather_fusion
  58.7 4.0 %scatter_custom_fusion.2 = bf16[2048,128]{1,0:T(8,128)(2,1)} fusion(s32[1024]{0:T(1024)S(1)} %compare_select_fusion.2, bf16[1024,128]{1,0:T(8,128)(2,1)S(1)} %bitcast.181, bf16[]{:T(256)} %constant.16.clone.1), kind=kCustom, calls=%fused_computation.30 | custom fusion | bytes 524290 | tf_op jit(solution)/shard_map/scatter | solution.py:136
  62.7 5.4 %all-to-all-start.2 = ((bf16[8,256,128]{2,1,0:T(8,128)(2,1)}), bf16[8,256,128]{2,1,0:T(8,128)(2,1)S(1)}, u32[]{:S(2)}, u32[]{:S(2)}) async-start(bf16[8,256,128]{2,1,0:T(8,128)(2,1)} %bitcast.15), calls=%async_computation.2 | async-start | bytes 1048576 | tf_op jit(solution)/shard_map/all_to_all | solution.py:144
  68.3 13.5 %all-to-all-done.2 = bf16[8,256,128]{2,1,0:T(8,128)(2,1)S(1)} async-done(((bf16[8,256,128]{2,1,0:T(8,128)(2,1)}), bf16[8,256,128]{2,1,0:T(8,128)(2,1)S(1)}, u32[]{:S(2)}, u32[]{:S(2)}) %all-to-all-start.2) | async-done | bytes 524320 | tf_op jit(solution)/shard_map/all_to_all | solution.py:144
  81.9 5.8 %scatter_custom_fusion.3 = bf16[1024,128]{1,0:T(8,128)(2,1)S(1)} fusion(s32[2048]{0:T(1024)S(1)} %bitcast.176, bf16[2048,128]{1,0:T(8,128)(2,1)S(1)} %bitcast.170, bf16[]{:T(256)} %constant.16.clone.1), kind=kCustom, calls=%fused_computation.32 | custom fusion | bytes 262146 | tf_op jit(solution)/shard_map/scatter | solution.py:162
  87.7 1.7 %fusion.71 = (bf16[1024,128]{1,0:T(8,128)(2,1)}, f32[1024,128]{1,0:T(8,128)S(1)}) fusion(f32[6,1024]{1,0:T(8,128)S(1)} %stack.48, f32[128,6]{0,1:T(8,128)S(1)} %copy-done, f32[128]{0:T(128)S(1)} %copy-done.8, bf16[1024,128]{1,0:T(8,128)(2,1)S(1)} %scatter_custom_fusion.3), kind=kOutput, calls=%fused_computation.128 | convolution fusion | flops 9961472 | bytes 1076736 | tf_op jit(solution)/shard_map/ce,hc->eh/dot_general | solution.py:55
  90.3 2.6 %copy.32 = f32[3,8,1024]{0,2,1:T(8,128)} copy(f32[3,8,1024]{2,1,0:T(8,128)S(1)} %fusion) | data formatting | bytes 196608 | tf_op jit(solution)/shard_map/reshape | solution.py:81
  93.0 44.4 %scatter_custom_fusion.4 = f32[1024,3]{1,0:T(8,128)S(1)} fusion(s32[8192]{0:T(1024)S(1)} %bitcast.173, f32[8192,3]{1,0:T(8,128)} %bitcast.163, f32[]{:T(128)} %constant.23.clone.1), kind=kCustom, calls=%fused_computation.28 | custom fusion | flops 24576 | bytes 12800 | tf_op jit(solution)/shard_map/scatter-add | solution.py:80
  137.4 0.6 gather_fusion.5
  138.0 0.6 gather_fusion.4
  140.0 1.9 %collective-permute-start = (f32[1,3,128]{1,2,0:T(8,128)S(1)}, f32[1,3,128]{1,2,0:T(8,128)S(1)}, u32[]{:S(2)}, u32[]{:S(2)}) collective-permute-start(f32[1,3,128]{1,2,0:T(8,128)S(1)} %bitcast.180), channel_id=1, source_target_pairs={{0,4},{4,8},{8,12},{12,16},{16,20},{20,24},{24,28},{1,5},{5,9},{9,... | collective-permute-start | bytes 4616 | tf_op jit(solution)/shard_map/ppermute | solution.py:15
  141.9 3.4 %collective-permute-start.1 = (f32[1,3,128]{1,2,0:T(8,128)S(1)}, f32[1,3,128]{1,2,0:T(8,128)S(1)}, u32[]{:S(2)}, u32[]{:S(2)}) collective-permute-start(f32[1,3,128]{1,2,0:T(8,128)S(1)} %bitcast.179), channel_id=1, source_target_pairs={{4,0},{8,4},{12,8},{16,12},{20,16},{24,20},{28,24},{5,1},{9,5},{13... | collective-permute-start | bytes 4616 | tf_op jit(solution)/shard_map/ppermute | solution.py:17
  145.3 5.1 %collective-permute-start.2 = (f32[1,3,128]{1,2,0:T(8,128)S(1)}, f32[1,3,128]{1,2,0:T(8,128)S(1)}, u32[]{:S(2)}, u32[]{:S(2)}) collective-permute-start(f32[1,3,128]{1,2,0:T(8,128)S(1)} %bitcast.178), channel_id=1, source_target_pairs={{0,1},{1,2},{2,3},{4,5},{5,6},{6,7},{8,9},{9,10},{10,11},{12,13},{... | collective-permute-start | bytes 4616 | tf_op jit(solution)/shard_map/ppermute | solution.py:15
  150.4 1.9 %collective-permute-start.3 = (f32[1,3,128]{1,2,0:T(8,128)S(1)}, f32[1,3,128]{1,2,0:T(8,128)S(1)}, u32[]{:S(2)}, u32[]{:S(2)}) collective-permute-start(f32[1,3,128]{1,2,0:T(8,128)S(1)} %bitcast.177), channel_id=1, source_target_pairs={{1,0},{2,1},{3,2},{5,4},{6,5},{7,6},{9,8},{10,9},{11,10},{13,12},{... | collective-permute-start | bytes 4616 | tf_op jit(solution)/shard_map/ppermute | solution.py:17
  152.3 1.6 %scatter_custom_fusion.5 = f32[3,1024]{0,1:T(8,128)S(1)} fusion(f32[3,1024]{0,1:T(8,128)S(1)} %bitcast.168, s32[128]{0:T(128)S(1)} %get-tuple-element.38, f32[1,3,128]{1,2,0:T(8,128)S(1)} %collective-permute-done), kind=kCustom, calls=%fused_computation.42 | custom fusion | flops 384 | bytes 77824 | tf_op jit(solution)/shard_map/scatter-add | solution.py:173
  154.0 1.5 scatter_custom_fusion.6
  155.5 1.5 scatter_custom_fusion.7
  156.9 1.5 scatter_custom_fusion.8
  158.4 0.8 copy.27
  (60 shorter events, 4.6 us)
Async XLA Ops:
  0.6 87.0 %copy-start = (f32[128,6]{0,1:T(8,128)S(1)}, f32[128,6]{0,1:T(8,128)}, u32[]{:S(2)}) copy-start(f32[128,6]{0,1:T(8,128)} %param.26) | copy-start | bytes 9220
  0.6 42.1 %copy-start.5 = (f32[1024]{0:T(1024)S(1)}, f32[1024]{0:T(1024)}, u32[]{:S(2)}) copy-start(f32[1024]{0:T(1024)} %param.24) | copy-start | bytes 12292
  2.8 40.1 %copy-start.3 = (s32[1024]{0:T(1024)S(1)}, s32[1024]{0:T(1024)}, u32[]{:S(2)}) copy-start(s32[1024]{0:T(1024)} %param.19) | copy-start | bytes 12292
  3.7 42.1 %copy-start.9 = (s32[8]{0:T(128)S(1)}, s32[8]{0:T(128)}, u32[]{:S(2)}) copy-start(s32[8]{0:T(128)} %param.17) | copy-start | bytes 100
  3.7 42.2 %copy-start.1 = (bf16[8,4,128,128]{3,2,1,0:T(8,128)(2,1)S(1)}, bf16[8,4,128,128]{3,2,1,0:T(8,128)(2,1)}, u32[]{:S(2)}) copy-start(bf16[8,4,128,128]{3,2,1,0:T(8,128)(2,1)} %param.18) | copy-start | bytes 3145732
  6.2 40.1 %copy-start.6 = (s32[8,4]{0,1:T(4,128)S(1)}, s32[8,4]{0,1:T(4,128)}, u32[]{:S(2)}) copy-start(s32[8,4]{0,1:T(4,128)} %param.16) | copy-start | bytes 388
  6.2 45.4 %all-to-all-start.1 = ((bf16[4,4,128,128]{3,2,1,0:T(8,128)(2,1)}), bf16[4,4,128,128]{3,2,1,0:T(8,128)(2,1)S(1)}, u32[]{:S(2)}, u32[]{:S(2)}) async-start(bf16[4,4,128,128]{3,2,1,0:T(8,128)(2,1)} %bitcast.5), calls=%async_computation.1 | async-start | bytes 1048576 | tf_op jit(solution)/shard_map/all_to_all | solution.py:116
  46.1 22.0 %copy-start.2 = (s32[8,1024]{1,0:T(8,128)S(1)}, s32[8,1024]{1,0:T(8,128)}, u32[]{:S(2)}) copy-start(s32[8,1024]{1,0:T(8,128)} %param.21) | copy-start | bytes 98308
  46.1 22.1 %copy-start.7 = (s32[4,128]{1,0:T(4,128)S(1)}, s32[4,128]{1,0:T(4,128)}, u32[]{:S(2)}) copy-start(s32[4,128]{1,0:T(4,128)} %param.22) | copy-start | bytes 6148
  51.5 11.1 %all-to-all-start = ((s32[8,1,256]{2,1,0:T(1,128)}), s32[8,1,256]{2,1,0:T(1,128)S(1)}, u32[]{:S(2)}, u32[]{:S(2)}) async-start(s32[8,1,256]{2,1,0:T(1,128)} %bitcast.2), calls=%async_computation | async-start | bytes 16384 | tf_op jit(solution)/shard_map/all_to_all | solution.py:151
  57.3 30.3 %copy-start.8 = (f32[128]{0:T(128)S(1)}, f32[128]{0:T(128)}, u32[]{:S(2)}) copy-start(f32[128]{0:T(128)} %param.25) | copy-start | bytes 1540
  58.1 31.3 %copy-start.4 = (f32[128,6]{0,1:T(8,128)S(1)}, f32[128,6]{0,1:T(8,128)}, u32[]{:S(2)}) copy-start(f32[128,6]{0,1:T(8,128)} %param.27) | copy-start | bytes 9220
  62.7 19.2 %all-to-all-start.2 = ((bf16[8,256,128]{2,1,0:T(8,128)(2,1)}), bf16[8,256,128]{2,1,0:T(8,128)(2,1)S(1)}, u32[]{:S(2)}, u32[]{:S(2)}) async-start(bf16[8,256,128]{2,1,0:T(8,128)(2,1)} %bitcast.15), calls=%async_computation.2 | async-start | bytes 1048576 | tf_op jit(solution)/shard_map/all_to_all | solution.py:144
  140.0 12.3 %collective-permute-start = (f32[1,3,128]{1,2,0:T(8,128)S(1)}, f32[1,3,128]{1,2,0:T(8,128)S(1)}, u32[]{:S(2)}, u32[]{:S(2)}) collective-permute-start(f32[1,3,128]{1,2,0:T(8,128)S(1)} %bitcast.180), channel_id=1, source_target_pairs={{0,4},{4,8},{8,12},{12,16},{16,20},{20,24},{24,28},{1,5},{5,9},{9,... | collective-permute-start | bytes 4616 | tf_op jit(solution)/shard_map/ppermute | solution.py:15
  141.9 12.1 %collective-permute-start.1 = (f32[1,3,128]{1,2,0:T(8,128)S(1)}, f32[1,3,128]{1,2,0:T(8,128)S(1)}, u32[]{:S(2)}, u32[]{:S(2)}) collective-permute-start(f32[1,3,128]{1,2,0:T(8,128)S(1)} %bitcast.179), channel_id=1, source_target_pairs={{4,0},{8,4},{12,8},{16,12},{20,16},{24,20},{28,24},{5,1},{9,5},{13... | collective-permute-start | bytes 4616 | tf_op jit(solution)/shard_map/ppermute | solution.py:17
  145.3 10.2 %collective-permute-start.2 = (f32[1,3,128]{1,2,0:T(8,128)S(1)}, f32[1,3,128]{1,2,0:T(8,128)S(1)}, u32[]{:S(2)}, u32[]{:S(2)}) collective-permute-start(f32[1,3,128]{1,2,0:T(8,128)S(1)} %bitcast.178), channel_id=1, source_target_pairs={{0,1},{1,2},{2,3},{4,5},{5,6},{6,7},{8,9},{9,10},{10,11},{12,13},{... | collective-permute-start | bytes 4616 | tf_op jit(solution)/shard_map/ppermute | solution.py:15
  150.4 6.6 %collective-permute-start.3 = (f32[1,3,128]{1,2,0:T(8,128)S(1)}, f32[1,3,128]{1,2,0:T(8,128)S(1)}, u32[]{:S(2)}, u32[]{:S(2)}) collective-permute-start(f32[1,3,128]{1,2,0:T(8,128)S(1)} %bitcast.177), channel_id=1, source_target_pairs={{1,0},{2,1},{3,2},{5,4},{6,5},{7,6},{9,8},{10,9},{11,10},{13,12},{... | collective-permute-start | bytes 4616 | tf_op jit(solution)/shard_map/ppermute | solution.py:17
where the time goes:
time: 160 us; the launch traced here: 159 us
  local copies, waits for them, and re-layouts  57 us (36%)
  other arithmetic  56.4 us (35%)
  starting transfers between devices  27.8 us (17%)
  waiting for transfers between devices  13.6 us (8%)
  matrix products  3.46 us (2%)
    scatter-add x1, other arithmetic, element_forces(): jax.ops.segment_sum(corner_force.reshape(3, -1).T, connectivity.reshape(-...  44.4 us
    gather x2, local copies, waits for them, and re-layouts, element_forces(): corner_motion = node_motion[:, connectivity]  30.5 us
    all_to_all x1, waiting for transfers between devices, body(): lax.all_to_all(send_rows.reshape(dom_total, owner_capacity, width), 'dom'...  13.5 us
    ppermute x2, starting transfers between devices, extended(): lax.ppermute(tail, axis, [(i, (i + 1) % count) for i in range(ends)])  7.02 us
    all_to_all x1, starting transfers between devices, body(): lax.all_to_all(send_positions.reshape(dom_total, owner_capacity), 'dom',...  5.8 us
    scatter x1, local copies, waits for them, and re-layouts, body(): arrived = jnp.zeros((element_total, width), jnp.bfloat16).at[got_position...  5.76 us
    all_to_all x1, starting transfers between devices, body(): lax.all_to_all(send_rows.reshape(dom_total, owner_capacity, width), 'dom'...  5.44 us
    ppermute x2, starting transfers between devices, extended(): lax.ppermute(head, axis, [((i + 1) % count, i) for i in range(ends)])  5.28 us
  transfers between devices with their start and end apart: 7, of which 1 were waited for; matrix products, arithmetic and copies ran while one was open for 32% of the time, Pallas kernels for 0%

commit v1 on v0

v1 whole, which is shorter than its diff:
```python
import functools

import jax
import jax.numpy as jnp
from jax import lax
from jax.experimental import pallas as pl
from jax.experimental.pallas import tpu as pltpu
from jax.sharding import PartitionSpec as P

BF = jnp.bfloat16
F32 = jnp.float32
I32 = jnp.int32
LANES = 128
SUBS = 8
POS_ROWS = 16
NOWHERE = 16.0
TENSOR = ((0, 3, 5), (3, 1, 4), (5, 4, 2))
NT_DIMS = (((1,), (1,)), ((), ()))
TN_DIMS = (((0,), (0,)), ((), ()))
HIGHEST = lax.Precision.HIGHEST


def iota(shape, dim):
    return lax.broadcasted_iota(I32, shape, dim)


def pieces(x, count):
    out = []
    for _ in range(count - 1):
        high = x.astype(BF)
        out.append(high)
        x = x - high.astype(F32)
    out.append(x.astype(BF))
    return out


def as_onehot(mask):
    return jnp.where(mask, 1.0, 0.0).astype(BF)


def lookup(rows, index):
    low = index & (LANES - 1)
    high = index >> 7
    out = jnp.zeros(index.shape, F32)
    for r, row in enumerate(rows):
        got = jnp.take_along_axis(
            jnp.broadcast_to(row, index.shape), low, axis=1, mode="promise_in_bounds"
        )
        out = jnp.where(high == r, got, out)
    return out


def pack_blocks(route, old, *rest):
    outs, table = rest[:-1], rest[-1]
    me = lax.axis_index("box")
    capacity = outs[0].shape[0]
    for m in range(len(outs) * capacity):
        table[m] = 0
    routes = [route[i] for i in range(old.shape[0])]
    for i, target in enumerate(routes):
        order = jnp.int32(0)
        for earlier in routes[:i]:
            order = order + (earlier == target).astype(I32)
        table[(target ^ me) * capacity + order] = i
    for k, out in enumerate(outs):
        for s in range(capacity):
            out[s] = old[table[k * capacity + s]]


def sort_rows(count, owner_route, owner_slot, weights, sorter, positions, chunks, mass_inv,
              high_rows, low_rows, starts):
    dom_total = positions.shape[0]
    row_groups = owner_route.shape[0]
    rows = row_groups * LANES
    me = lax.axis_index("dom")
    route = owner_route[...]
    picks = jnp.concatenate([as_onehot(route == d) for d in range(dom_total)], axis=0)
    span = dom_total * row_groups
    ahead = as_onehot(iota((LANES, LANES), 0) < iota((LANES, LANES), 1))
    within = jnp.dot(picks, ahead, preferred_element_type=F32)
    totals = jnp.dot(picks, jnp.ones((LANES, LANES), BF), preferred_element_type=F32).astype(BF)
    before = as_onehot(iota((span, span), 1) < iota((span, span), 0))
    base = jnp.dot(before, totals, preferred_element_type=F32)
    ranked = within + base
    place = jnp.zeros((row_groups, LANES), F32)
    for d in range(dom_total):
        place = jnp.where(route == d, ranked[d * row_groups : (d + 1) * row_groups], place)
        starts[d] = jnp.max(base[d * row_groups : d * row_groups + 1]).astype(I32)
    starts[dom_total] = rows
    place = place.astype(I32)
    slots = iota((rows, LANES), 0)
    for g in range(row_groups):
        sorter[:, g * LANES : (g + 1) * LANES] = as_onehot(slots == place[g : g + 1])
    slot = owner_slot[...]
    which = iota((POS_ROWS, rows), 0)
    parts = jnp.where(which == 0, slot >> 7, jnp.where(which == 1, slot & (LANES - 1), 0))
    ordered = lax.dot_general(
        parts.astype(F32).astype(BF), sorter[...], NT_DIMS, preferred_element_type=F32
    )
    for g in range(row_groups):
        high_rows[g : g + 1] = ordered[0:1, g * LANES : (g + 1) * LANES]
        low_rows[g : g + 1] = ordered[1:2, g * LANES : (g + 1) * LANES]
    which = iota((POS_ROWS, LANES), 0)
    for k in range(dom_total):
        owner = lax.rem(me + k, dom_total)
        start = starts[owner]
        held = starts[owner + 1] - start
        block = jnp.zeros((POS_ROWS, LANES), F32)
        for j in range(2):
            chunk = jnp.minimum(start // LANES + j, row_groups - 1)
            chunks[2 * k + j] = chunk
            high = jnp.where(held > j * LANES, high_rows[pl.ds(chunk, 1)], NOWHERE)
            block = jnp.where(which == j, high, block)
            block = jnp.where(which == 2 + j, low_rows[pl.ds(chunk, 1)], block)
        positions[k] = block.astype(BF)
    entries = weights.shape[1] // LANES
    for t in range(weights.shape[0]):
        total = jnp.zeros((1, LANES), F32)
        for l in range(entries):
            part = jnp.sum(
                weights[t, l * LANES : (l + 1) * LANES, :].astype(F32), axis=0, keepdims=True
            )
            total = total + jnp.where(l < count[t], part, 0.0)
        mass_inv[t : t + 1] = 1.0 / total


def element_parts(connectivity, motion, size, couple, readout, shared, drive, base, onehot,
                  chosen, inverse, strain, elastic, wide):
    elements = connectivity.shape[1]
    corners = connectivity.shape[0]
    groups = motion.shape[1] // LANES
    corner = iota((corners, LANES), 0)
    signs = [(2 * ((corner >> c) & 1) - 1).astype(F32) for c in range(3)]
    low_iota = iota((LANES, LANES), 0)
    strain[...] = jnp.zeros_like(strain)
    elastic[...] = jnp.zeros_like(elastic)
    for j in range(elements // LANES):
        lanes = slice(j * LANES, (j + 1) * LANES)
        nodes = connectivity[:, lanes]
        scale = 1.0 / (4.0 * size[:, lanes])
        grad = []
        for i in range(3):
            moved = lookup(
                [motion[i : i + 1, r * LANES : (r + 1) * LANES] for r in range(groups)], nodes
            )
            grad.append(
                [jnp.sum(moved * signs[c], axis=0, keepdims=True) * scale for c in range(3)]
            )
        rows = [
            grad[0][0],
            grad[1][1],
            grad[2][2],
            grad[0][1] + grad[1][0],
            grad[1][2] + grad[2][1],
            grad[2][0] + grad[0][2],
        ]
        volume = 1.2 * (rows[0] + rows[1] + rows[2])
        for c in range(6):
            strain[c : c + 1, lanes] = rows[c]
            elastic[c : c + 1, lanes] = volume + 1.6 * rows[c] if c < 3 else 0.8 * rows[c]
        for a in range(corners):
            onehot[a, :, lanes] = as_onehot(low_iota == (nodes[a : a + 1] & (LANES - 1)))
    wide[...] = jnp.zeros_like(wide)
    wide[0, 0:6] = couple[...]
    wide[1, 0:6] = readout[...]
    drive[...] = lax.dot_general(
        strain[...], wide[0], TN_DIMS, preferred_element_type=F32, precision=HIGHEST
    )
    base[...] = elastic[...] + lax.dot_general(
        wide[1], drive[...], NT_DIMS, preferred_element_type=F32, precision=HIGHEST
    )
    odd_dom = lax.axis_index("dom") & 1
    odd_box = lax.axis_index("box") & 1
    chosen[...] = jnp.zeros_like(chosen)
    chosen[0:1] = shared[pl.ds(1 - odd_dom, 1)]
    chosen[1:2] = shared[pl.ds(odd_dom, 1)]
    chosen[2:3] = shared[pl.ds(3 - odd_box, 1)]
    chosen[3:4] = shared[pl.ds(2 + odd_box, 1)]
    group = iota((groups, LANES), 0)
    lane = iota((groups, LANES), 1)
    total = jnp.zeros((2 * groups, LANES), F32)
    for m in range(4):
        nodes = chosen[m : m + 1]
        here = group == (nodes >> 7)
        marks = jnp.concatenate(
            [jnp.where(here, m + 1, 0), jnp.where(here, lane, 0)], axis=0
        ).astype(F32)
        total = total + lax.dot_general(
            marks.astype(BF),
            as_onehot(low_iota == (nodes & (LANES - 1))),
            NT_DIMS,
            preferred_element_type=F32,
        )
    total = total.astype(I32)
    inverse[0] = total[:groups] - 1
    inverse[1] = total[groups:]


def project_rows(slot, count, chunks, weights, mass_inv, sorter, positions, *rest):
    dom_total = positions.shape[0]
    box_total = lax.axis_size("box")
    received = rest[:box_total]
    outs = rest[box_total : box_total + dom_total]
    held, turned, ordered = rest[box_total + dom_total :]
    me = lax.axis_index("box")
    capacity = received[0].shape[0]
    for k, block in enumerate(received):
        for s in range(capacity):
            held[k * capacity + s] = block[s]
    targets = weights.shape[0]
    entries = slot.shape[0]
    for t in range(targets):
        picked = []
        for l in range(entries):
            entry = slot[l, t]
            source = lax.div(entry, capacity) ^ me
            block = held[source * capacity + lax.rem(entry, capacity)]
            picked.append(jnp.where(l < count[t], block, jnp.zeros_like(block)))
        numerator = jnp.dot(
            jnp.concatenate(picked, axis=1), weights[t], preferred_element_type=F32
        )
        turned[:, t * LANES : (t + 1) * LANES] = (numerator * mass_inv[t : t + 1]).astype(BF)
    sort = lax.dot_general(sorter[...], turned[...], NT_DIMS, preferred_element_type=F32)
    for g in range(ordered.shape[0]):
        ordered[g] = sort[g * LANES : (g + 1) * LANES].astype(BF)
    for k, out in enumerate(outs):
        for j in range(2):
            out[j * LANES : (j + 1) * LANES] = ordered[chunks[2 * k + j]]
        out[2 * LANES :] = positions[k]


def finish(placed, sources, *refs):
    payloads = refs[:sources]
    drive, base, size, connectivity, onehot, decay, readout, chosen = refs[sources : sources + 8]
    history, local = refs[sources + 8 : sources + 10]
    exports = refs[sources + 10 : sources + 14]
    scratch = refs[sources + 14 :]
    elements = base.shape[1]
    groups = elements // LANES
    if placed:
        arrived = payloads[0][...]
        wide = arrived.astype(F32)
    else:
        placing, rows = scratch
        low_iota = iota((LANES, LANES), 0)
        for k, payload in enumerate(payloads):
            rows[k * 2 * LANES : (k + 1) * 2 * LANES] = payload[: 2 * LANES]
            where = payload[2 * LANES :].astype(F32).astype(I32)
            for j in range(2):
                match = low_iota == where[2 + j : 3 + j]
                lanes = slice((2 * k + j) * LANES, (2 * k + j + 1) * LANES)
                for g in range(groups):
                    placing[g * LANES : (g + 1) * LANES, lanes] = as_onehot(
                        match & (where[j : j + 1] == g)
                    )
        wide = jnp.dot(placing[...], rows[...], preferred_element_type=F32)
        arrived = wide.astype(BF)
    history[...] = (wide * decay[...] + drive[...]).astype(BF)
    taken = readout[...] * decay[...]
    taken = jnp.concatenate([taken, jnp.zeros((SUBS - 6, LANES), F32)], axis=0)
    share = lax.dot_general(
        jnp.concatenate(pieces(taken, 3), axis=0), arrived, NT_DIMS, preferred_element_type=F32
    )
    stress = base[...] + (share[0:SUBS] + share[SUBS : 2 * SUBS] + share[2 * SUBS : 3 * SUBS])
    row = iota((3 * SUBS, 2 * SUBS), 0)
    column = iota((3 * SUBS, 2 * SUBS), 1) & (SUBS - 1)
    spread = jnp.zeros(row.shape, I32)
    for i in range(3):
        for c in range(3):
            spread = jnp.where(
                ((row >> 3) == i) & (column == TENSOR[i][c]),
                2 * ((row >> c) & 1) - 1,
                spread,
            )
    forces = jnp.dot(
        spread.astype(F32).astype(BF),
        jnp.concatenate(pieces(stress, 2), axis=0),
        preferred_element_type=F32,
    )
    edge = size[...]
    forces = forces * (edge * edge * 0.25)
    group = iota((SUBS, elements), 0)
    total = jnp.zeros((6 * SUBS, LANES), F32)
    for a in range(SUBS):
        here = group == (connectivity[a : a + 1] >> 7)
        highs, lows = [], []
        for i in range(3):
            value = jnp.where(here, forces[i * SUBS + a : i * SUBS + a + 1], 0.0)
            high, low = pieces(value, 2)
            highs.append(high)
            lows.append(low)
        total = total + lax.dot_general(
            jnp.concatenate(highs + lows, axis=0), onehot[a], NT_DIMS, preferred_element_type=F32
        )
    nodes = chosen[...]
    for i in range(3):
        summed = (
            total[i * SUBS : (i + 1) * SUBS] + total[(3 + i) * SUBS : (4 + i) * SUBS]
        )
        local[i] = summed
        got = lookup([summed[r : r + 1] for r in range(SUBS)], nodes)
        for m, out in enumerate(exports):
            out[i : i + 1] = got[m : m + 1]


def add_shared(local, inverse, *rest):
    received, force = rest[:-1], rest[-1]
    row, column = inverse[0], inverse[1]
    for i in range(local.shape[0]):
        total = local[i]
        for m, got in enumerate(received):
            share = jnp.take_along_axis(
                jnp.broadcast_to(got[i : i + 1], column.shape),
                column,
                axis=1,
                mode="promise_in_bounds",
            )
            total = total + jnp.where(row == m, share, 0.0)
        for r in range(local.shape[1]):
            force[i : i + 1, r * LANES : (r + 1) * LANES] = total[r : r + 1]


VMEM = pl.BlockSpec(memory_space=pltpu.VMEM)
SMEM = pl.BlockSpec(memory_space=pltpu.SMEM)


def call(kernel, name, ins, outs, scratch, args, cost=100_000, out_specs=None):
    single = not isinstance(outs, (list, tuple))
    return pl.pallas_call(
        kernel,
        name=name,
        out_shape=outs,
        in_specs=ins,
        out_specs=out_specs or (VMEM if single else [VMEM] * len(outs)),
        scratch_shapes=scratch,
        cost_estimate=pl.CostEstimate(flops=1000, bytes_accessed=cost, transcendentals=0),
        compiler_params=pltpu.CompilerParams(vmem_limit_bytes=24 * 1024 * 1024),
    )(*args)


def swaps(axis, first):
    total = lax.axis_size(axis)
    pairs = []
    for i in range(first, total - 1, 2):
        pairs += [(i, i + 1), (i + 1, i)]
    return pairs


def arrays(shape, dtype):
    return jax.ShapeDtypeStruct(shape, dtype)


def exclusive_order(targets, choice_total):
    one_hot = (targets[:, None] == jnp.arange(choice_total, dtype=I32)[None, :]).astype(I32)
    return jnp.sum((jnp.cumsum(one_hot, axis=0) - one_hot) * one_hot, axis=1)


def spread_rows(received, entry_slot, entry_count, weights, owner_route, owner_slot):
    targets, entries = entry_slot.shape
    block_size = weights.shape[-1]
    capacity, width, _ = received[0].shape
    me = lax.axis_index("box")
    stacked = jnp.concatenate(received, axis=0)
    held = ((entry_slot // capacity) ^ me) * capacity + entry_slot % capacity
    live = (jnp.arange(entries, dtype=I32)[None, :] < entry_count[:, None]).astype(BF)
    mass = jnp.einsum("tl,tlij->tj", live, weights, preferred_element_type=F32)
    picked = stacked[held] * live[:, :, None, None]
    numerator = jnp.einsum("tlhi,tlij->tjh", picked, weights, preferred_element_type=F32)
    projected = (numerator / mass[:, :, None]).astype(BF).reshape(targets * block_size, width)
    total = projected.shape[0]
    dom_total = lax.axis_size("dom")
    owner_capacity = 2 * (total // dom_total)
    place = owner_route * owner_capacity + exclusive_order(owner_route, dom_total)
    rows = jnp.zeros((dom_total * owner_capacity, width), BF).at[place].set(projected)
    spots = jnp.full((dom_total * owner_capacity,), total, I32).at[place].set(owner_slot)
    rows = lax.all_to_all(
        rows.reshape(dom_total, owner_capacity, width), "dom", 0, 0, tiled=True
    )
    spots = lax.all_to_all(spots.reshape(dom_total, owner_capacity), "dom", 0, 0, tiled=True)
    return (
        jnp.zeros((total, width), BF)
        .at[spots.reshape(-1)]
        .set(rows.reshape(-1, width), mode="drop")
    )


def body(old_history, box_route, entry_slot, entry_count, weights, owner_route, owner_slot,
         connectivity, shared_nodes, node_motion, elem_size, decay, couple, readout):
    blocks, width, block_size = old_history.shape
    targets, entries = entry_slot.shape
    box_total = lax.axis_size("box")
    dom_total = lax.axis_size("dom")
    capacity = blocks // 2
    rows = targets * block_size
    row_groups = rows // LANES
    elements = connectivity.shape[1]
    nodes = node_motion.shape[1]

    packed = call(
        pack_blocks, "pack_blocks", [SMEM, VMEM],
        [arrays((capacity, width, block_size), BF)] * box_total,
        [pltpu.SMEM((box_total * capacity,), I32)],
        (box_route, old_history),
    )
    received = [packed[0]] + [
        lax.ppermute(packed[k], "box", [(i, i ^ k) for i in range(box_total)])
        for k in range(1, box_total)
    ]
    flat_weights = weights.reshape(targets, entries * block_size, block_size)
    edge = elem_size.reshape(1, elements)
    drive, base, onehot, chosen, inverse = call(
        element_parts, "element_parts", [VMEM] * 6,
        [
            arrays((elements, width), F32),
            arrays((SUBS, elements), F32),
            arrays((connectivity.shape[0], LANES, elements), BF),
            arrays((SUBS, shared_nodes.shape[1]), I32),
            arrays((2, nodes // LANES, LANES), I32),
        ],
        [
            pltpu.VMEM((SUBS, elements), F32),
            pltpu.VMEM((SUBS, elements), F32),
            pltpu.VMEM((2, SUBS, width), F32),
        ],
        (connectivity, node_motion, edge, couple.T, readout.T, shared_nodes),
    )
    usual = rows // dom_total
    if usual == LANES:
        sorter, positions, chunks, mass_inv = call(
            sort_rows, "sort_rows", [SMEM, VMEM, VMEM, VMEM],
            [
                arrays((rows, rows), BF),
                arrays((dom_total, POS_ROWS, LANES), BF),
                arrays((2 * dom_total,), I32),
                arrays((targets, block_size), F32),
            ],
            [
                pltpu.VMEM((row_groups, LANES), F32),
                pltpu.VMEM((row_groups, LANES), F32),
                pltpu.SMEM((dom_total + 1,), I32),
            ],
            (
                entry_count,
                owner_route.reshape(row_groups, LANES),
                owner_slot.reshape(1, rows),
                flat_weights,
            ),
            out_specs=[VMEM, VMEM, SMEM, VMEM],
        )
        payload = arrays((2 * usual + POS_ROWS, width), BF)
        outgoing = call(
            project_rows, "project_rows", [SMEM, SMEM, SMEM] + [VMEM] * (4 + box_total),
            [payload] * dom_total,
            [
                pltpu.VMEM((box_total * capacity, width, block_size), BF),
                pltpu.VMEM((width, rows), BF),
                pltpu.VMEM((row_groups, LANES, width), BF),
            ],
            (entry_slot.T, entry_count, chunks, flat_weights, mass_inv, sorter, positions, *received),
        )
        payloads = [outgoing[0]] + [
            lax.ppermute(outgoing[k], "dom", [(i, (i + k) % dom_total) for i in range(dom_total)])
            for k in range(1, dom_total)
        ]
        placed = False
        scratch = [
            pltpu.VMEM((elements, dom_total * 2 * usual), BF),
            pltpu.VMEM((dom_total * 2 * usual, width), BF),
        ]
    else:
        payloads = [
            spread_rows(received, entry_slot, entry_count, weights, owner_route, owner_slot)
        ]
        placed, scratch = True, []
    export = arrays((3, shared_nodes.shape[1]), F32)
    history, local, *exports = call(
        functools.partial(finish, placed, len(payloads)), "finish",
        [VMEM] * (len(payloads) + 8),
        [arrays((elements, width), BF), arrays((3, nodes // LANES, LANES), F32)] + [export] * 4,
        scratch,
        (
            *payloads, drive, base, edge, connectivity, onehot,
            decay.reshape(1, width), readout.T, chosen,
        ),
    )
    halo = [
        lax.ppermute(exports[0], "dom", swaps("dom", 0)),
        lax.ppermute(exports[1], "dom", swaps("dom", 1)),
        lax.ppermute(exports[2], "box", swaps("box", 0)),
        lax.ppermute(exports[3], "box", swaps("box", 1)),
    ]
    force = call(
        add_shared, "add_shared", [VMEM] * (2 + len(halo)), arrays((3, nodes), F32), [],
        (local, inverse, *halo),
    )
    return history, force


def solution(mesh):
    return jax.shard_map(
        body,
        mesh=mesh,
        in_specs=(
            P(("dom", "box"), None, None),
            P(("dom", "box")),
            P(("dom", "box"), None),
            P(("dom", "box")),
            P(("dom", "box"), None, None, None),
            P(("dom", "box")),
            P(("dom", "box")),
            P(None, ("dom", "box")),
            P(None, ("dom", "box")),
            P(None, ("dom", "box")),
            P(("dom", "box")),
            P(),
            P(),
            P(),
        ),
        out_specs=(P(("dom", "box"), None), P(None, ("dom", "box"))),
        check_vma=False,
    )
```

time: 160 us -> 48.2 us (0.30)
  other arithmetic: 56.4 us -> 0 us
  local copies, waits for them, and re-layouts: 57 us -> 6.79 us
  Pallas kernels: 0 us -> 12.4 us
  waiting for transfers between devices: 13.6 us -> 5.72 us
  starting transfers between devices: 27.8 us -> 22.2 us
  matrix products: 3.46 us -> 0 us
    scatter-add x5 -> x0, other arithmetic: 50.5 us -> none  [the longest x1 44.4 us: element_forces(): jax.ops.segment_sum(corner_force.reshape(3, -1).T, connectivity.reshape(-...]
    gather x7 -> x0, local copies, waits for them, and re-layouts: 33.9 us -> none  [the longest x2 30.5 us: element_forces(): corner_motion = node_motion[:, connectivity]]
    scatter x4 -> x0, local copies, waits for them, and re-layouts: 17.2 us -> none  [the longest x1 5.76 us: body(): arrived = jnp.zeros((element_total, width), jnp.bfloat16).at[got_position...]
    all_to_all x3 -> x0, starting transfers between devices: 15.5 us -> none  [the longest x1 5.8 us: body(): lax.all_to_all(send_positions.reshape(dom_total, owner_capacity), 'dom',...]
    all_to_all x3 -> x0, waiting for transfers between devices: 13.6 us -> none  [the longest x1 13.5 us: body(): lax.all_to_all(send_rows.reshape(dom_total, owner_capacity, width), 'dom'...]
    pallas_call x0 -> x6, Pallas kernels: none -> 12.4 us  [call(): pl.pallas_call(kernel, name=name, out_shape=outs, in_specs=ins, out_specs...]
    ppermute x4 -> x14, starting transfers between devices: 12.3 us -> 22.2 us  [the longest x7 9.46 us: body(): lax.ppermute(outgoing[k], 'dom', [(i, (i + k) % dom_total) for i in range...]
    ppermute x4 -> x14, waiting for transfers between devices: 0.01 us -> 5.72 us  [the longest x7 3.18 us: body(): lax.ppermute(outgoing[k], 'dom', [(i, (i + k) % dom_total) for i in range...]
  transfers between devices with their start and end apart: 7 -> 14, of which waited for: 1 -> 5; matrix products, arithmetic and copies ran while one was open for 32% -> 0% of each run, Pallas kernels for 0% -> 11%
where the time goes in v1:
time: 48.2 us; the launch traced here: 47.9 us
  starting transfers between devices  22.2 us (46%)
  Pallas kernels  12.4 us (26%)
  local copies, waits for them, and re-layouts  6.79 us (14%)
  waiting for transfers between devices  5.72 us (12%)
  between operations  0.79 us (2%)
    pallas_call x6, Pallas kernels, call(): pl.pallas_call(kernel, name=name, out_shape=outs, in_specs=ins, out_specs...  12.4 us
    ppermute x7, starting transfers between devices, body(): lax.ppermute(outgoing[k], 'dom', [(i, (i + k) % dom_total) for i in range...  9.46 us
    unnamed x30, local copies, waits for them, and re-layouts  6.79 us
    ppermute x1, starting transfers between devices, body(): lax.ppermute(exports[1], 'dom', swaps('dom', 1))  6.14 us
    ppermute x7, waiting for transfers between devices, body(): lax.ppermute(outgoing[k], 'dom', [(i, (i + k) % dom_total) for i in range...  3.18 us
    ppermute x1, starting transfers between devices, body(): lax.ppermute(exports[3], 'box', swaps('box', 1))  3.02 us
    ppermute x3, starting transfers between devices, body(): lax.ppermute(packed[k], 'box', [(i, i ^ k) for i in range(box_total)])  2.45 us
    ppermute x1, waiting for transfers between devices, body(): lax.ppermute(exports[3], 'box', swaps('box', 1))  1.83 us
  transfers between devices with their start and end apart: 14, of which 5 were waited for; matrix products, arithmetic and copies ran while one was open for 0% of the time, Pallas kernels for 11%

profile of v1, /device:TPU:5, one launch (start us, length us, event | category | flops | bytes accessed | tf_op | source)
XLA Modules:
  0.0 47.9 jit_solution(2708934182871732884)
XLA Ops:
  0.6 0.9 %copy-done.2 = bf16[8,128,128]{2,1,0:T(8,128)(2,1)S(1)} copy-done((bf16[8,128,128]{2,1,0:T(8,128)(2,1)S(1)}, bf16[8,128,128]{2,1,0:T(8,128)(2,1)}, u32[]{:S(2)}) %copy-start.2) | copy-done | bytes 262168
  1.6 0.7 %copy-done.13 = s32[8]{0:T(128)S(1)} copy-done((s32[8]{0:T(128)S(1)}, s32[8]{0:T(128)}, u32[]{:S(2)}) %copy-start.13) | copy-done | bytes 56
  2.2 0.6 %pack_blocks.1 = (bf16[4,128,128]{2,1,0:T(8,128)(2,1)S(1)}, bf16[4,128,128]{2,1,0:T(8,128)(2,1)S(1)}, bf16[4,128,128]{2,1,0:T(8,128)(2,1)S(1)}, bf16[4,128,128]{2,1,0:T(8,128)(2,1)S(1)}) custom-call(s32[8]{0:T(128)S(1)} %copy-done.13, bf16[8,128,128]{2,1,0:T(8,128)(2,1)S(1)} %copy-done.2), custom_call_target="tpu_custom_call" | custom-call | flops 1000 | bytes 100000 | tf_op jit(solution)/shard_map/pack_blocks/pallas_call | solution.py:329
  2.9 0.7 %collective-permute-start = (bf16[4,128,128]{2,1,0:T(8,128)(2,1)S(1)}, bf16[4,128,128]{2,1,0:T(8,128)(2,1)S(1)}, u32[]{:S(2)}, u32[]{:S(2)}) collective-permute-start(bf16[4,128,128]{2,1,0:T(8,128)(2,1)S(1)} %get-tuple-element.34), channel_id=1, source_target_pairs={{0,1},{1,0},{2,3},{3,2},{4,5},{5,4},{6,7},{7,6},{8,9},{9,8},{10,11... | collective-permute-start | bytes 393224 | tf_op jit(solution)/shard_map/ppermute | solution.py:406
  3.6 1.2 %collective-permute-start.1 = (bf16[4,128,128]{2,1,0:T(8,128)(2,1)S(1)}, bf16[4,128,128]{2,1,0:T(8,128)(2,1)S(1)}, u32[]{:S(2)}, u32[]{:S(2)}) collective-permute-start(bf16[4,128,128]{2,1,0:T(8,128)(2,1)S(1)} %get-tuple-element.35), channel_id=1, source_target_pairs={{0,2},{1,3},{2,0},{3,1},{4,6},{5,7},{6,4},{7,5},{8,10},{9,11},{10,... | collective-permute-start | bytes 393224 | tf_op jit(solution)/shard_map/ppermute | solution.py:406
  4.8 0.5 %collective-permute-start.2 = (bf16[4,128,128]{2,1,0:T(8,128)(2,1)S(1)}, bf16[4,128,128]{2,1,0:T(8,128)(2,1)S(1)}, u32[]{:S(2)}, u32[]{:S(2)}) collective-permute-start(bf16[4,128,128]{2,1,0:T(8,128)(2,1)S(1)} %get-tuple-element.36), channel_id=1, source_target_pairs={{0,3},{1,2},{2,1},{3,0},{4,7},{5,6},{6,5},{7,4},{8,11},{9,10},{10,... | collective-permute-start | bytes 393224 | tf_op jit(solution)/shard_map/ppermute | solution.py:406
  5.3 1.2 %copy-done = bf16[8,4,128,128]{3,2,1,0:T(8,128)(2,1)S(1)} copy-done((bf16[8,4,128,128]{3,2,1,0:T(8,128)(2,1)S(1)}, bf16[8,4,128,128]{3,2,1,0:T(8,128)(2,1)}, u32[]{:S(2)}) %copy-start) | copy-done | bytes 1048600
  6.6 0.7 %copy-done.7 = s32[1024]{0:T(1024)S(1)} copy-done((s32[1024]{0:T(1024)S(1)}, s32[1024]{0:T(1024)}, u32[]{:S(2)}) %copy-start.7) | copy-done | bytes 4120
  7.2 0.7 %copy-done.8 = s32[1024]{0:T(1024)S(1)} copy-done((s32[1024]{0:T(1024)S(1)}, s32[1024]{0:T(1024)}, u32[]{:S(2)}) %copy-start.8) | copy-done | bytes 4120
  7.9 0.7 %copy-done.11 = s32[8]{0:T(128)S(1)} copy-done((s32[8]{0:T(128)S(1)}, s32[8]{0:T(128)}, u32[]{:S(2)}) %copy-start.11) | copy-done | bytes 56
  8.6 2.3 %sort_rows.1 = (bf16[1024,1024]{1,0:T(8,128)(2,1)S(1)}, bf16[8,16,128]{2,1,0:T(8,128)(2,1)S(1)}, s32[16]{0:T(128)S(1)}, f32[8,128]{1,0:T(8,128)S(1)}) custom-call(s32[8]{0:T(128)S(1)} %copy-done.11, s32[8,128]{1,0:T(8,128)S(1)} %bitcast.14, s32[1,1024]{1,0:T(1,128)S(1)} %bitcast.15, bf16[8,512,128]{2,1,0:T(8,128)(2,1)S(1)} %bitcast.8), custom_call_target="tpu_custom_call" | custom-call | flops 1000 | bytes 100000 | tf_op jit(solution)/shard_map/sort_rows/pallas_call | solution.py:329
  10.9 0.7 %collective-permute-done.2.rest_3_ = bf16[4,128,128]{2,1,0:T(8,128)(2,1)S(1)} collective-permute-done((bf16[4,128,128]{2,1,0:T(8,128)(2,1)S(1)}, bf16[4,128,128]{2,1,0:T(8,128)(2,1)S(1)}, u32[]{:S(2)}, u32[]{:S(2)}) %collective-permute-start.2) | collective-permute-done | bytes 131104 | tf_op jit(solution)/shard_map/ppermute | solution.py:406
  11.6 1.2 %copy-done.1 = bf16[8,4,128,128]{3,2,1,0:T(8,128)(2,1)S(1)} copy-done((bf16[8,4,128,128]{3,2,1,0:T(8,128)(2,1)S(1)}, bf16[8,4,128,128]{3,2,1,0:T(8,128)(2,1)}, u32[]{:S(2)}) %copy-start.1) | copy-done | bytes 1048600
  12.9 0.7 %copy-done.10 = s32[8,4]{0,1:T(4,128)S(1)} copy-done((s32[8,4]{0,1:T(4,128)S(1)}, s32[8,4]{0,1:T(4,128)}, u32[]{:S(2)}) %copy-start.10) | copy-done | bytes 152
  13.6 1.7 %project_rows.1 = (bf16[272,128]{1,0:T(8,128)(2,1)S(1)}, bf16[272,128]{1,0:T(8,128)(2,1)S(1)}, bf16[272,128]{1,0:T(8,128)(2,1)S(1)}, bf16[272,128]{1,0:T(8,128)(...) custom-call(s32[4,8]{1,0:T(4,128)S(1)} %bitcast.17, ...), custom_call_target="tpu_custom_call" | custom-call | flops 1000 | bytes 100000 | tf_op jit(solution)/shard_map/project_rows/pallas_call | solution.py:329
  15.3 1.3 %collective-permute-start.3 = (bf16[272,128]{1,0:T(8,128)(2,1)S(1)}, bf16[272,128]{1,0:T(8,128)(2,1)S(1)}, u32[]{:S(2)}, u32[]{:S(2)}) collective-permute-start(bf16[272,128]{1,0:T(8,128)(2,1)S(1)} %get-tuple-element.38), channel_id=1, source_target_pairs={{0,4},{4,8},{8,12},{12,16},{16,20},{20,24},{24,28},{28,0},{1,5},{5... | collective-permute-start | bytes 208904 | tf_op jit(solution)/shard_map/ppermute | solution.py:462
  16.6 1.3 %collective-permute-start.4 = (bf16[272,128]{1,0:T(8,128)(2,1)S(1)}, bf16[272,128]{1,0:T(8,128)(2,1)S(1)}, u32[]{:S(2)}, u32[]{:S(2)}) collective-permute-start(bf16[272,128]{1,0:T(8,128)(2,1)S(1)} %get-tuple-element.39), channel_id=1, source_target_pairs={{0,8},{4,12},{8,16},{12,20},{16,24},{20,28},{24,0},{28,4},{1,9},{5... | collective-permute-start | bytes 208904 | tf_op jit(solution)/shard_map/ppermute | solution.py:462
  17.9 2.3 %collective-permute-start.5 = (bf16[272,128]{1,0:T(8,128)(2,1)S(1)}, bf16[272,128]{1,0:T(8,128)(2,1)S(1)}, u32[]{:S(2)}, u32[]{:S(2)}) collective-permute-start(bf16[272,128]{1,0:T(8,128)(2,1)S(1)} %get-tuple-element.40), channel_id=1, source_target_pairs={{0,12},{4,16},{8,20},{12,24},{16,28},{20,0},{24,4},{28,8},{1,13},{... | collective-permute-start | bytes 208904 | tf_op jit(solution)/shard_map/ppermute | solution.py:462
  20.1 0.1 collective-permute-start.6
  20.2 2.1 %collective-permute-start.7 = (bf16[272,128]{1,0:T(8,128)(2,1)S(1)}, bf16[272,128]{1,0:T(8,128)(2,1)S(1)}, u32[]{:S(2)}, u32[]{:S(2)}) collective-permute-start(bf16[272,128]{1,0:T(8,128)(2,1)S(1)} %get-tuple-element.42), channel_id=1, source_target_pairs={{0,20},{4,24},{8,28},{12,0},{16,4},{20,8},{24,12},{28,16},{1,21},{... | collective-permute-start | bytes 208904 | tf_op jit(solution)/shard_map/ppermute | solution.py:462
  22.3 1.3 %collective-permute-start.8 = (bf16[272,128]{1,0:T(8,128)(2,1)S(1)}, bf16[272,128]{1,0:T(8,128)(2,1)S(1)}, u32[]{:S(2)}, u32[]{:S(2)}) collective-permute-start(bf16[272,128]{1,0:T(8,128)(2,1)S(1)} %get-tuple-element.43), channel_id=1, source_target_pairs={{0,24},{4,28},{8,0},{12,4},{16,8},{20,12},{24,16},{28,20},{1,25},{... | collective-permute-start | bytes 208904 | tf_op jit(solution)/shard_map/ppermute | solution.py:462
  23.6 1.1 %collective-permute-start.9 = (bf16[272,128]{1,0:T(8,128)(2,1)S(1)}, bf16[272,128]{1,0:T(8,128)(2,1)S(1)}, u32[]{:S(2)}, u32[]{:S(2)}) collective-permute-start(bf16[272,128]{1,0:T(8,128)(2,1)S(1)} %get-tuple-element.44), channel_id=1, source_target_pairs={{0,28},{4,0},{8,4},{12,8},{16,12},{20,16},{24,20},{28,24},{1,29},{... | collective-permute-start | bytes 208904 | tf_op jit(solution)/shard_map/ppermute | solution.py:462
  24.8 2.9 %element_parts.1 = (f32[1024,128]{1,0:T(8,128)S(1)}, f32[8,1024]{1,0:T(8,128)S(1)}, bf16[8,128,1024]{2,1,0:T(8,128)(2,1)S(1)}, s32[8,128]{1,0:T(8,128)S(1)}, s32[2,8,128]{2,1,0:T(8,128)S(1)}) custom-call(s32[8,1024]{1,0:T(8,128)S(1)} %copy-done.3, f32[3,1024]{1,0:T(4,128)S(1)} %copy-done.6, f32[1,1024]{1,0:T(1,128)S(1)} %bitcast.10, f32[6,128]{1,0:T(8,128)S(1)} %bitcast.16, ...), custom_call_target="tpu_custom_call" | custom-call | flops 1000 | bytes 100000 | tf_op jit(solution)/shard_map/element_parts/pallas_call | solution.py:329
  27.7 1.1 %collective-permute-done.6.refs_4_ = bf16[272,128]{1,0:T(8,128)(2,1)S(1)} collective-permute-done((bf16[272,128]{1,0:T(8,128)(2,1)S(1)}, bf16[272,128]{1,0:T(8,128)(2,1)S(1)}, u32[]{:S(2)}, u32[]{:S(2)}) %collective-permute-start.6) | collective-permute-done | bytes 69664 | tf_op jit(solution)/shard_map/ppermute | solution.py:462
  28.8 1.8 %collective-permute-done.7.refs_5_ = bf16[272,128]{1,0:T(8,128)(2,1)S(1)} collective-permute-done((bf16[272,128]{1,0:T(8,128)(2,1)S(1)}, bf16[272,128]{1,0:T(8,128)(2,1)S(1)}, u32[]{:S(2)}, u32[]{:S(2)}) %collective-permute-start.7) | collective-permute-done | bytes 69664 | tf_op jit(solution)/shard_map/ppermute | solution.py:462
  30.7 0.2 collective-permute-done.9.refs_7_
  30.9 4.2 %finish.1 = (bf16[1024,128]{1,0:T(8,128)(2,1)}, f32[3,8,128]{2,1,0:T(8,128)S(1)}, f32[3,128]{1,0:T(4,128)S(1)}, f32[3,128]{1,0:T(4,128)S(1)}, f32[3,128]{1,0:T(4,128)S(1)}, /*index=5*/f32[3,128]{1,0:T(4,128)S(1)}) custom-call(bf16[272,128]{1,0:T(8,128)(2,1)S(1)} %get-tuple-element.37.refs_0_, bf16[272,128]{1,0:T(8,128)(2,1)S(1)} %collective-permute-done.3.refs_1_, ...), custom_call_target="tpu_custom_call" | custom-call | flops 1000 | bytes 100000 | tf_op jit(solution)/shard_map/finish/pallas_call | solution.py:329
  35.0 6.1 %collective-permute-start.11 = (f32[3,128]{1,0:T(4,128)S(1)}, f32[3,128]{1,0:T(4,128)S(1)}, u32[]{:S(2)}, u32[]{:S(2)}) collective-permute-start(f32[3,128]{1,0:T(4,128)S(1)} %get-tuple-element.53), channel_id=1, source_target_pairs={{4,8},{8,4},{12,16},{16,12},{20,24},{24,20},{5,9},{9,5},{13,17},{1... | collective-permute-start | bytes 4616 | tf_op jit(solution)/shard_map/ppermute | solution.py:488
  41.2 1.1 %collective-permute-start.12 = (f32[3,128]{1,0:T(4,128)S(1)}, f32[3,128]{1,0:T(4,128)S(1)}, u32[]{:S(2)}, u32[]{:S(2)}) collective-permute-start(f32[3,128]{1,0:T(4,128)S(1)} %get-tuple-element.54), channel_id=1, source_target_pairs={{0,1},{1,0},{2,3},{3,2},{4,5},{5,4},{6,7},{7,6},{8,9},{9,8},{10,11... | collective-permute-start | bytes 4616 | tf_op jit(solution)/shard_map/ppermute | solution.py:489
  42.3 3.0 %collective-permute-start.13 = (f32[3,128]{1,0:T(4,128)S(1)}, f32[3,128]{1,0:T(4,128)S(1)}, u32[]{:S(2)}, u32[]{:S(2)}) collective-permute-start(f32[3,128]{1,0:T(4,128)S(1)} %get-tuple-element.55), channel_id=1, source_target_pairs={{1,2},{2,1},{5,6},{6,5},{9,10},{10,9},{13,14},{14,13},{17,18},{18,... | collective-permute-start | bytes 4616 | tf_op jit(solution)/shard_map/ppermute | solution.py:490
  45.4 1.8 %collective-permute-done.13.rest_3_ = f32[3,128]{1,0:T(4,128)S(1)} collective-permute-done((f32[3,128]{1,0:T(4,128)S(1)}, f32[3,128]{1,0:T(4,128)S(1)}, u32[]{:S(2)}, u32[]{:S(2)}) %collective-permute-start.13) | collective-permute-done | bytes 1568 | tf_op jit(solution)/shard_map/ppermute | solution.py:490
  47.2 0.7 %add_shared.1 = f32[3,1024]{1,0:T(4,128)} custom-call(f32[3,8,128]{2,1,0:T(8,128)S(1)} %get-tuple-element.50.local, s32[2,8,128]{2,1,0:T(8,128)S(1)} %get-tuple-element.51.inverse, f32[3,128]{1,0:T(4,128)S(1)} %collective-permute-done.10.rest_0_, f32[3,128]{1,0:T(4,128)S(1)} %collective-permute-done.11.rest_1_, ...), custom_call_target="tpu_custom_call" | custom-call | flops 1000 | bytes 100000 | tf_op jit(solution)/shard_map/add_shared/pallas_call | solution.py:329
  (32 shorter events, 0.1 us)
Async XLA Ops:
  0.6 1.0 %copy-start.2 = (bf16[8,128,128]{2,1,0:T(8,128)(2,1)S(1)}, bf16[8,128,128]{2,1,0:T(8,128)(2,1)}, u32[]{:S(2)}) copy-start(bf16[8,128,128]{2,1,0:T(8,128)(2,1)} %old.1) | copy-start | bytes 786436
  1.6 0.7 %copy-start.13 = (s32[8]{0:T(128)S(1)}, s32[8]{0:T(128)}, u32[]{:S(2)}) copy-start(s32[8]{0:T(128)} %route.1) | copy-start | bytes 100
  2.9 8.1 %collective-permute-start = (bf16[4,128,128]{2,1,0:T(8,128)(2,1)S(1)}, bf16[4,128,128]{2,1,0:T(8,128)(2,1)S(1)}, u32[]{:S(2)}, u32[]{:S(2)}) collective-permute-start(bf16[4,128,128]{2,1,0:T(8,128)(2,1)S(1)} %get-tuple-element.34), channel_id=1, source_target_pairs={{0,1},{1,0},{2,3},{3,2},{4,5},{5,4},{6,7},{7,6},{8,9},{9,8},{10,11... | collective-permute-start | bytes 393224 | tf_op jit(solution)/shard_map/ppermute | solution.py:406
  3.6 7.3 %collective-permute-start.1 = (bf16[4,128,128]{2,1,0:T(8,128)(2,1)S(1)}, bf16[4,128,128]{2,1,0:T(8,128)(2,1)S(1)}, u32[]{:S(2)}, u32[]{:S(2)}) collective-permute-start(bf16[4,128,128]{2,1,0:T(8,128)(2,1)S(1)} %get-tuple-element.35), channel_id=1, source_target_pairs={{0,2},{1,3},{2,0},{3,1},{4,6},{5,7},{6,4},{7,5},{8,10},{9,11},{10,... | collective-permute-start | bytes 393224 | tf_op jit(solution)/shard_map/ppermute | solution.py:406
  4.8 6.8 %collective-permute-start.2 = (bf16[4,128,128]{2,1,0:T(8,128)(2,1)S(1)}, bf16[4,128,128]{2,1,0:T(8,128)(2,1)S(1)}, u32[]{:S(2)}, u32[]{:S(2)}) collective-permute-start(bf16[4,128,128]{2,1,0:T(8,128)(2,1)S(1)} %get-tuple-element.36), channel_id=1, source_target_pairs={{0,3},{1,2},{2,1},{3,0},{4,7},{5,6},{6,5},{7,4},{8,11},{9,10},{10,... | collective-permute-start | bytes 393224 | tf_op jit(solution)/shard_map/ppermute | solution.py:406
  5.3 1.2 %copy-start = (bf16[8,4,128,128]{3,2,1,0:T(8,128)(2,1)S(1)}, bf16[8,4,128,128]{3,2,1,0:T(8,128)(2,1)}, u32[]{:S(2)}) copy-start(bf16[8,4,128,128]{3,2,1,0:T(8,128)(2,1)} %param.18) | copy-start | bytes 3145732
  6.5 0.7 %copy-start.7 = (s32[1024]{0:T(1024)S(1)}, s32[1024]{0:T(1024)}, u32[]{:S(2)}) copy-start(s32[1024]{0:T(1024)} %param.19) | copy-start | bytes 12292
  7.2 0.7 %copy-start.8 = (s32[1024]{0:T(1024)S(1)}, s32[1024]{0:T(1024)}, u32[]{:S(2)}) copy-start(s32[1024]{0:T(1024)} %param.20) | copy-start | bytes 12292
  7.9 0.7 %copy-start.11 = (s32[8]{0:T(128)S(1)}, s32[8]{0:T(128)}, u32[]{:S(2)}) copy-start(s32[8]{0:T(128)} %count.3) | copy-start | bytes 100
  8.6 16.2 %copy-start.3 = (s32[8,1024]{1,0:T(8,128)S(1)}, s32[8,1024]{1,0:T(8,128)}, u32[]{:S(2)}) copy-start(s32[8,1024]{1,0:T(8,128)} %refs_11_.1) | copy-start | bytes 98308
  8.6 16.2 %copy-start.6 = (f32[3,1024]{1,0:T(4,128)S(1)}, f32[3,1024]{1,0:T(4,128)}, u32[]{:S(2)}) copy-start(f32[3,1024]{1,0:T(4,128)} %motion.1) | copy-start | bytes 36868
  8.6 16.2 %copy-start.9 = (f32[128,6]{0,1:T(8,128)S(1)}, f32[128,6]{0,1:T(8,128)}, u32[]{:S(2)}) copy-start(f32[128,6]{0,1:T(8,128)} %param.26) | copy-start | bytes 9220
  10.9 13.9 %copy-start.4 = (f32[1024]{0:T(1024)S(1)}, f32[1024]{0:T(1024)}, u32[]{:S(2)}) copy-start(f32[1024]{0:T(1024)} %param.24) | copy-start | bytes 12292
  10.9 13.9 %copy-start.5 = (f32[128,6]{0,1:T(8,128)S(1)}, f32[128,6]{0,1:T(8,128)}, u32[]{:S(2)}) copy-start(f32[128,6]{0,1:T(8,128)} %param.27) | copy-start | bytes 9220
  10.9 13.9 %copy-start.12 = (s32[4,128]{1,0:T(4,128)S(1)}, s32[4,128]{1,0:T(4,128)}, u32[]{:S(2)}) copy-start(s32[4,128]{1,0:T(4,128)} %shared.1) | copy-start | bytes 6148
  10.9 20.0 %copy-start.14 = (f32[128]{0:T(128)S(1)}, f32[128]{0:T(128)}, u32[]{:S(2)}) copy-start(f32[128]{0:T(128)} %param.25) | copy-start | bytes 1540
  11.6 1.2 %copy-start.1 = (bf16[8,4,128,128]{3,2,1,0:T(8,128)(2,1)S(1)}, bf16[8,4,128,128]{3,2,1,0:T(8,128)(2,1)}, u32[]{:S(2)}) copy-start(bf16[8,4,128,128]{3,2,1,0:T(8,128)(2,1)} %param.18) | copy-start | bytes 3145732
  12.9 0.7 %copy-start.10 = (s32[8,4]{0,1:T(4,128)S(1)}, s32[8,4]{0,1:T(4,128)}, u32[]{:S(2)}) copy-start(s32[8,4]{0,1:T(4,128)} %param.16) | copy-start | bytes 388
  15.3 7.0 %collective-permute-start.3 = (bf16[272,128]{1,0:T(8,128)(2,1)S(1)}, bf16[272,128]{1,0:T(8,128)(2,1)S(1)}, u32[]{:S(2)}, u32[]{:S(2)}) collective-permute-start(bf16[272,128]{1,0:T(8,128)(2,1)S(1)} %get-tuple-element.38), channel_id=1, source_target_pairs={{0,4},{4,8},{8,12},{12,16},{16,20},{20,24},{24,28},{28,0},{1,5},{5... | collective-permute-start | bytes 208904 | tf_op jit(solution)/shard_map/ppermute | solution.py:462
  16.6 7.0 %collective-permute-start.4 = (bf16[272,128]{1,0:T(8,128)(2,1)S(1)}, bf16[272,128]{1,0:T(8,128)(2,1)S(1)}, u32[]{:S(2)}, u32[]{:S(2)}) collective-permute-start(bf16[272,128]{1,0:T(8,128)(2,1)S(1)} %get-tuple-element.39), channel_id=1, source_target_pairs={{0,8},{4,12},{8,16},{12,20},{16,24},{20,28},{24,0},{28,4},{1,9},{5... | collective-permute-start | bytes 208904 | tf_op jit(solution)/shard_map/ppermute | solution.py:462
  17.9 9.8 %collective-permute-start.5 = (bf16[272,128]{1,0:T(8,128)(2,1)S(1)}, bf16[272,128]{1,0:T(8,128)(2,1)S(1)}, u32[]{:S(2)}, u32[]{:S(2)}) collective-permute-start(bf16[272,128]{1,0:T(8,128)(2,1)S(1)} %get-tuple-element.40), channel_id=1, source_target_pairs={{0,12},{4,16},{8,20},{12,24},{16,28},{20,0},{24,4},{28,8},{1,13},{... | collective-permute-start | bytes 208904 | tf_op jit(solution)/shard_map/ppermute | solution.py:462
  20.1 8.7 %collective-permute-start.6 = (bf16[272,128]{1,0:T(8,128)(2,1)S(1)}, bf16[272,128]{1,0:T(8,128)(2,1)S(1)}, u32[]{:S(2)}, u32[]{:S(2)}) collective-permute-start(bf16[272,128]{1,0:T(8,128)(2,1)S(1)} %get-tuple-element.41), channel_id=1, source_target_pairs={{0,16},{4,20},{8,24},{12,28},{16,0},{20,4},{24,8},{28,12},{1,17},{... | collective-permute-start | bytes 208904 | tf_op jit(solution)/shard_map/ppermute | solution.py:462
  20.2 10.5 %collective-permute-start.7 = (bf16[272,128]{1,0:T(8,128)(2,1)S(1)}, bf16[272,128]{1,0:T(8,128)(2,1)S(1)}, u32[]{:S(2)}, u32[]{:S(2)}) collective-permute-start(bf16[272,128]{1,0:T(8,128)(2,1)S(1)} %get-tuple-element.42), channel_id=1, source_target_pairs={{0,20},{4,24},{8,28},{12,0},{16,4},{20,8},{24,12},{28,16},{1,21},{... | collective-permute-start | bytes 208904 | tf_op jit(solution)/shard_map/ppermute | solution.py:462
  22.3 8.4 %collective-permute-start.8 = (bf16[272,128]{1,0:T(8,128)(2,1)S(1)}, bf16[272,128]{1,0:T(8,128)(2,1)S(1)}, u32[]{:S(2)}, u32[]{:S(2)}) collective-permute-start(bf16[272,128]{1,0:T(8,128)(2,1)S(1)} %get-tuple-element.43), channel_id=1, source_target_pairs={{0,24},{4,28},{8,0},{12,4},{16,8},{20,12},{24,16},{28,20},{1,25},{... | collective-permute-start | bytes 208904 | tf_op jit(solution)/shard_map/ppermute | solution.py:462
  23.6 7.2 %collective-permute-start.9 = (bf16[272,128]{1,0:T(8,128)(2,1)S(1)}, bf16[272,128]{1,0:T(8,128)(2,1)S(1)}, u32[]{:S(2)}, u32[]{:S(2)}) collective-permute-start(bf16[272,128]{1,0:T(8,128)(2,1)S(1)} %get-tuple-element.44), channel_id=1, source_target_pairs={{0,28},{4,0},{8,4},{12,8},{16,12},{20,16},{24,20},{28,24},{1,29},{... | collective-permute-start | bytes 208904 | tf_op jit(solution)/shard_map/ppermute | solution.py:462
  35.0 10.3 %collective-permute-start.10 = (f32[3,128]{1,0:T(4,128)S(1)}, f32[3,128]{1,0:T(4,128)S(1)}, u32[]{:S(2)}, u32[]{:S(2)}) collective-permute-start(f32[3,128]{1,0:T(4,128)S(1)} %get-tuple-element.52), channel_id=1, source_target_pairs={{0,4},{4,0},{8,12},{12,8},{16,20},{20,16},{24,28},{28,24},{1,5},{5... | collective-permute-start | bytes 4616 | tf_op jit(solution)/shard_map/ppermute | solution.py:487
  35.0 10.3 %collective-permute-start.11 = (f32[3,128]{1,0:T(4,128)S(1)}, f32[3,128]{1,0:T(4,128)S(1)}, u32[]{:S(2)}, u32[]{:S(2)}) collective-permute-start(f32[3,128]{1,0:T(4,128)S(1)} %get-tuple-element.53), channel_id=1, source_target_pairs={{4,8},{8,4},{12,16},{16,12},{20,24},{24,20},{5,9},{9,5},{13,17},{1... | collective-permute-start | bytes 4616 | tf_op jit(solution)/shard_map/ppermute | solution.py:488
  41.2 4.2 %collective-permute-start.12 = (f32[3,128]{1,0:T(4,128)S(1)}, f32[3,128]{1,0:T(4,128)S(1)}, u32[]{:S(2)}, u32[]{:S(2)}) collective-permute-start(f32[3,128]{1,0:T(4,128)S(1)} %get-tuple-element.54), channel_id=1, source_target_pairs={{0,1},{1,0},{2,3},{3,2},{4,5},{5,4},{6,7},{7,6},{8,9},{9,8},{10,11... | collective-permute-start | bytes 4616 | tf_op jit(solution)/shard_map/ppermute | solution.py:489
  42.3 4.9 %collective-permute-start.13 = (f32[3,128]{1,0:T(4,128)S(1)}, f32[3,128]{1,0:T(4,128)S(1)}, u32[]{:S(2)}, u32[]{:S(2)}) collective-permute-start(f32[3,128]{1,0:T(4,128)S(1)} %get-tuple-element.55), channel_id=1, source_target_pairs={{1,2},{2,1},{5,6},{6,5},{9,10},{10,9},{13,14},{14,13},{17,18},{18,... | collective-permute-start | bytes 4616 | tf_op jit(solution)/shard_map/ppermute | solution.py:490

commit v2 on v1

--- a/solution.py
+++ b/solution.py
@@ -50,8 +50,21 @@
     return out
 
 
-def pack_blocks(route, old, *rest):
-    outs, table = rest[:-1], rest[-1]
+def fetch(pairs, sems):
+    copies = [
+        pltpu.make_async_copy(source, target, sems.at[i])
+        for i, (source, target) in enumerate(pairs)
+    ]
+    for copy in copies:
+        copy.start()
+    for copy in copies:
+        copy.wait()
+
+
+def pack_blocks(route_hbm, old_hbm, *rest):
+    outs = rest[:-4]
+    table, route, old, sems = rest[-4:]
+    fetch([(route_hbm, route), (old_hbm, old)], sems)
     me = lax.axis_index("box")
     capacity = outs[0].shape[0]
     for m in range(len(outs) * capacity):
@@ -67,8 +80,19 @@
             out[s] = old[table[k * capacity + s]]
 
 
-def sort_rows(count, owner_route, owner_slot, weights, sorter, positions, chunks, mass_inv,
-              high_rows, low_rows, starts):
+def sort_rows(capacity, slot_hbm, count_hbm, route_hbm, place_hbm, weights_hbm, sorter, positions, table,
+              mass_inv, masked, high_rows, low_rows, starts, slot, count, owner_route, owner_slot,
+              sems):
+    fetch(
+        [
+            (slot_hbm, slot),
+            (count_hbm, count),
+            (route_hbm, owner_route),
+            (place_hbm, owner_slot),
+            (weights_hbm, masked),
+        ],
+        sems,
+    )
     dom_total = positions.shape[0]
     row_groups = owner_route.shape[0]
     rows = row_groups * LANES
@@ -91,9 +115,9 @@
     slots = iota((rows, LANES), 0)
     for g in range(row_groups):
         sorter[:, g * LANES : (g + 1) * LANES] = as_onehot(slots == place[g : g + 1])
-    slot = owner_slot[...]
+    spot = owner_slot[...]
     which = iota((POS_ROWS, rows), 0)
-    parts = jnp.where(which == 0, slot >> 7, jnp.where(which == 1, slot & (LANES - 1), 0))
+    parts = jnp.where(which == 0, spot >> 7, jnp.where(which == 1, spot & (LANES - 1), 0))
     ordered = lax.dot_general(
         parts.astype(F32).astype(BF), sorter[...], NT_DIMS, preferred_element_type=F32
     )
@@ -102,25 +126,32 @@
         low_rows[g : g + 1] = ordered[1:2, g * LANES : (g + 1) * LANES]
     which = iota((POS_ROWS, LANES), 0)
     for k in range(dom_total):
-        owner = lax.rem(me + k, dom_total)
+        owner = me ^ k
         start = starts[owner]
         held = starts[owner + 1] - start
         block = jnp.zeros((POS_ROWS, LANES), F32)
         for j in range(2):
             chunk = jnp.minimum(start // LANES + j, row_groups - 1)
-            chunks[2 * k + j] = chunk
+            table[2 * k + j] = chunk
             high = jnp.where(held > j * LANES, high_rows[pl.ds(chunk, 1)], NOWHERE)
             block = jnp.where(which == j, high, block)
             block = jnp.where(which == 2 + j, low_rows[pl.ds(chunk, 1)], block)
         positions[k] = block.astype(BF)
-    entries = weights.shape[1] // LANES
-    for t in range(weights.shape[0]):
+    targets = masked.shape[0]
+    entries = masked.shape[1] // LANES
+    box = lax.axis_index("box")
+    for t in range(targets):
         total = jnp.zeros((1, LANES), F32)
         for l in range(entries):
-            part = jnp.sum(
-                weights[t, l * LANES : (l + 1) * LANES, :].astype(F32), axis=0, keepdims=True
-            )
-            total = total + jnp.where(l < count[t], part, 0.0)
+            live = l < count[t]
+            span = slice(l * LANES, (l + 1) * LANES)
+            part = masked[t, span, :]
+            part = jnp.where(live, part, jnp.zeros_like(part))
+            masked[t, span, :] = part
+            total = total + jnp.sum(part.astype(F32), axis=0, keepdims=True)
+            entry = jnp.where(live, slot[l, t], slot[0, t])
+            source = lax.div(entry, capacity)
+            table[2 * dom_total + t * entries + l] = (source ^ box) * capacity + lax.rem(entry, capacity)
         mass_inv[t : t + 1] = 1.0 / total
 
 
@@ -132,6 +163,7 @@
     corner = iota((corners, LANES), 0)
     signs = [(2 * ((corner >> c) & 1) - 1).astype(F32) for c in range(3)]
     low_iota = iota((LANES, LANES), 0)
+    lane_iota = iota((LANES, LANES), 1).astype(F32)
     strain[...] = jnp.zeros_like(strain)
     elastic[...] = jnp.zeros_like(elastic)
     for j in range(elements // LANES):
@@ -158,8 +190,9 @@
         for c in range(6):
             strain[c : c + 1, lanes] = rows[c]
             elastic[c : c + 1, lanes] = volume + 1.6 * rows[c] if c < 3 else 0.8 * rows[c]
+        turned = (nodes & (LANES - 1)).astype(F32).T
         for a in range(corners):
-            onehot[a, :, lanes] = as_onehot(low_iota == (nodes[a : a + 1] & (LANES - 1)))
+            onehot[a, lanes, :] = as_onehot(lane_iota == turned[:, a : a + 1])
     wide[...] = jnp.zeros_like(wide)
     wide[0, 0:6] = couple[...]
     wide[1, 0:6] = readout[...]
@@ -196,28 +229,22 @@
     inverse[1] = total[groups:]
 
 
-def project_rows(slot, count, chunks, weights, mass_inv, sorter, positions, *rest):
+def project_rows(table, masked, mass_inv, sorter, positions, *rest):
     dom_total = positions.shape[0]
     box_total = lax.axis_size("box")
     received = rest[:box_total]
     outs = rest[box_total : box_total + dom_total]
     held, turned, ordered = rest[box_total + dom_total :]
-    me = lax.axis_index("box")
     capacity = received[0].shape[0]
     for k, block in enumerate(received):
         for s in range(capacity):
             held[k * capacity + s] = block[s]
-    targets = weights.shape[0]
-    entries = slot.shape[0]
+    targets = masked.shape[0]
+    entries = masked.shape[1] // LANES
     for t in range(targets):
-        picked = []
-        for l in range(entries):
-            entry = slot[l, t]
-            source = lax.div(entry, capacity) ^ me
-            block = held[source * capacity + lax.rem(entry, capacity)]
-            picked.append(jnp.where(l < count[t], block, jnp.zeros_like(block)))
+        picked = [held[table[2 * dom_total + t * entries + l]] for l in range(entries)]
         numerator = jnp.dot(
-            jnp.concatenate(picked, axis=1), weights[t], preferred_element_type=F32
+            jnp.concatenate(picked, axis=1), masked[t], preferred_element_type=F32
         )
         turned[:, t * LANES : (t + 1) * LANES] = (numerator * mass_inv[t : t + 1]).astype(BF)
     sort = lax.dot_general(sorter[...], turned[...], NT_DIMS, preferred_element_type=F32)
@@ -225,37 +252,45 @@
         ordered[g] = sort[g * LANES : (g + 1) * LANES].astype(BF)
     for k, out in enumerate(outs):
         for j in range(2):
-            out[j * LANES : (j + 1) * LANES] = ordered[chunks[2 * k + j]]
+            out[j * LANES : (j + 1) * LANES] = ordered[table[2 * k + j]]
         out[2 * LANES :] = positions[k]
 
 
-def finish(placed, sources, *refs):
-    payloads = refs[:sources]
-    drive, base, size, connectivity, onehot, decay, readout, chosen = refs[sources : sources + 8]
-    history, local = refs[sources + 8 : sources + 10]
-    exports = refs[sources + 10 : sources + 14]
-    scratch = refs[sources + 14 :]
+def place(payloads, placing, rows):
+    groups = placing.shape[0] // LANES
+    low_iota = iota((LANES, LANES), 0).astype(F32).astype(BF)
+    for k, payload in enumerate(payloads):
+        rows[k * 2 * LANES : (k + 1) * 2 * LANES] = payload[: 2 * LANES]
+        where = payload[2 * LANES :].astype(F32)
+        for j in range(2):
+            low = jnp.broadcast_to(where[2 + j : 3 + j], (LANES, LANES)).astype(BF)
+            match = jnp.where(low_iota == low, jnp.ones_like(low), jnp.zeros_like(low))
+            lanes = slice((2 * k + j) * LANES, (2 * k + j + 1) * LANES)
+            for g in range(groups):
+                here = jnp.where(where[j : j + 1] == g, 1.0, 0.0)
+                placing[g * LANES : (g + 1) * LANES, lanes] = match * jnp.broadcast_to(
+                    here, (LANES, LANES)
+                ).astype(BF)
+    return jnp.dot(placing[...], rows[...], preferred_element_type=F32)
+
+
+def place_early(count, *refs):
+    out, placing, rows = refs[count:]
+    out[...] = place(refs[:count], placing, rows)
+
+
+def finish(placed, count, *refs):
+    payloads = refs[:count]
+    early, base, size, connectivity, onehot, decay, readout, chosen = refs[count : count + 8]
+    settled, local = refs[count + 8 : count + 10]
+    exports = refs[count + 10 : count + 14]
+    scratch = refs[count + 14 :]
     elements = base.shape[1]
-    groups = elements // LANES
     if placed:
-        arrived = payloads[0][...]
-        wide = arrived.astype(F32)
+        arrived = early[...]
     else:
-        placing, rows = scratch
-        low_iota = iota((LANES, LANES), 0)
-        for k, payload in enumerate(payloads):
-            rows[k * 2 * LANES : (k + 1) * 2 * LANES] = payload[: 2 * LANES]
-            where = payload[2 * LANES :].astype(F32).astype(I32)
-            for j in range(2):
-                match = low_iota == where[2 + j : 3 + j]
-                lanes = slice((2 * k + j) * LANES, (2 * k + j + 1) * LANES)
-                for g in range(groups):
-                    placing[g * LANES : (g + 1) * LANES, lanes] = as_onehot(
-                        match & (where[j : j + 1] == g)
-                    )
-        wide = jnp.dot(placing[...], rows[...], preferred_element_type=F32)
-        arrived = wide.astype(BF)
-    history[...] = (wide * decay[...] + drive[...]).astype(BF)
+        arrived = (early[...] + place(payloads, *scratch)).astype(BF)
+    settled[...] = arrived
     taken = readout[...] * decay[...]
     taken = jnp.concatenate([taken, jnp.zeros((SUBS - 6, LANES), F32)], axis=0)
     share = lax.dot_general(
@@ -280,7 +315,7 @@
     edge = size[...]
     forces = forces * (edge * edge * 0.25)
     group = iota((SUBS, elements), 0)
-    total = jnp.zeros((6 * SUBS, LANES), F32)
+    halves = [jnp.zeros((6 * SUBS, LANES), F32) for _ in range(2)]
     for a in range(SUBS):
         here = group == (connectivity[a : a + 1] >> 7)
         highs, lows = [], []
@@ -289,9 +324,10 @@
             high, low = pieces(value, 2)
             highs.append(high)
             lows.append(low)
-        total = total + lax.dot_general(
-            jnp.concatenate(highs + lows, axis=0), onehot[a], NT_DIMS, preferred_element_type=F32
-        )
+        halves[a % 2] = halves[a % 2] + jnp.dot(
+            jnp.concatenate(highs + lows, axis=0), onehot[a], preferred_element_type=F32
+        )
+    total = halves[0] + halves[1]
     nodes = chosen[...]
     for i in range(3):
         summed = (
@@ -301,6 +337,10 @@
         got = lookup([summed[r : r + 1] for r in range(SUBS)], nodes)
         for m, out in enumerate(exports):
             out[i : i + 1] = got[m : m + 1]
+
+
+def relax(arrived, drive, decay, history):
+    history[...] = (arrived[...].astype(F32) * decay[...] + drive[...]).astype(BF)
 
 
 def add_shared(local, inverse, *rest):
@@ -322,6 +362,7 @@
 
 VMEM = pl.BlockSpec(memory_space=pltpu.VMEM)
 SMEM = pl.BlockSpec(memory_space=pltpu.SMEM)
+HBM = pl.BlockSpec(memory_space=pltpu.HBM)
 
 
 def call(kernel, name, ins, outs, scratch, args, cost=100_000, out_specs=None):
@@ -397,15 +438,20 @@
     nodes = node_motion.shape[1]
 
     packed = call(
-        pack_blocks, "pack_blocks", [SMEM, VMEM],
+        pack_blocks, "pack_blocks", [HBM, HBM],
         [arrays((capacity, width, block_size), BF)] * box_total,
-        [pltpu.SMEM((box_total * capacity,), I32)],
+        [
+            pltpu.SMEM((box_total * capacity,), I32),
+            pltpu.SMEM((blocks,), I32),
+            pltpu.VMEM(old_history.shape, BF),
+            pltpu.SemaphoreType.DMA((2,)),
+        ],
         (box_route, old_history),
     )
-    received = [packed[0]] + [
-        lax.ppermute(packed[k], "box", [(i, i ^ k) for i in range(box_total)])
-        for k in range(1, box_total)
-    ]
+    received = {0: packed[0]}
+    for k in [k for k in range(2, box_total)] + [1]:
+        received[k] = lax.ppermute(packed[k], "box", [(i, i ^ k) for i in range(box_total)])
+    received = [received[k] for k in range(box_total)]
     flat_weights = weights.reshape(targets, entries * block_size, block_size)
     edge = elem_size.reshape(1, elements)
     drive, base, onehot, chosen, inverse = call(
@@ -413,7 +459,7 @@
         [
             arrays((elements, width), F32),
             arrays((SUBS, elements), F32),
-            arrays((connectivity.shape[0], LANES, elements), BF),
+            arrays((connectivity.shape[0], elements, LANES), BF),
             arrays((SUBS, shared_nodes.shape[1]), I32),
             arrays((2, nodes // LANES, LANES), I32),
         ],
@@ -425,70 +471,86 @@
         (connectivity, node_motion, edge, couple.T, readout.T, shared_nodes),
     )
     usual = rows // dom_total
+    relaxing = decay.reshape(1, width)
     if usual == LANES:
-        sorter, positions, chunks, mass_inv = call(
-            sort_rows, "sort_rows", [SMEM, VMEM, VMEM, VMEM],
+        sorter, positions, table, mass_inv, masked = call(
+            functools.partial(sort_rows, capacity), "sort_rows", [HBM] * 5,
             [
                 arrays((rows, rows), BF),
                 arrays((dom_total, POS_ROWS, LANES), BF),
-                arrays((2 * dom_total,), I32),
+                arrays((2 * dom_total + targets * entries,), I32),
                 arrays((targets, block_size), F32),
+                arrays(flat_weights.shape, BF),
             ],
             [
                 pltpu.VMEM((row_groups, LANES), F32),
                 pltpu.VMEM((row_groups, LANES), F32),
                 pltpu.SMEM((dom_total + 1,), I32),
+                pltpu.SMEM((entries, targets), I32),
+                pltpu.SMEM((targets,), I32),
+                pltpu.VMEM((row_groups, LANES), I32),
+                pltpu.VMEM((1, rows), I32),
+                pltpu.SemaphoreType.DMA((5,)),
             ],
             (
+                entry_slot.T,
                 entry_count,
                 owner_route.reshape(row_groups, LANES),
                 owner_slot.reshape(1, rows),
                 flat_weights,
             ),
-            out_specs=[VMEM, VMEM, SMEM, VMEM],
+            out_specs=[VMEM, VMEM, SMEM, VMEM, VMEM],
         )
         payload = arrays((2 * usual + POS_ROWS, width), BF)
         outgoing = call(
-            project_rows, "project_rows", [SMEM, SMEM, SMEM] + [VMEM] * (4 + box_total),
+            project_rows, "project_rows", [SMEM] + [VMEM] * (4 + box_total),
             [payload] * dom_total,
             [
                 pltpu.VMEM((box_total * capacity, width, block_size), BF),
                 pltpu.VMEM((width, rows), BF),
                 pltpu.VMEM((row_groups, LANES, width), BF),
             ],
-            (entry_slot.T, entry_count, chunks, flat_weights, mass_inv, sorter, positions, *received),
-        )
-        payloads = [outgoing[0]] + [
-            lax.ppermute(outgoing[k], "dom", [(i, (i + k) % dom_total) for i in range(dom_total)])
-            for k in range(1, dom_total)
-        ]
-        placed = False
-        scratch = [
-            pltpu.VMEM((elements, dom_total * 2 * usual), BF),
-            pltpu.VMEM((dom_total * 2 * usual, width), BF),
-        ]
+            (table, masked, mass_inv, sorter, positions, *received),
+        )
+        far = dom_total // 2
+        order = [*range(far, dom_total), *range(2, far), 1]
+        payloads = {0: outgoing[0]}
+        for k in order:
+            payloads[k] = lax.ppermute(
+                outgoing[k], "dom", [(i, i ^ k) for i in range(dom_total)]
+            )
+        soon = [0, *range(1, far + 1)]
+        late = [payloads[k] for k in range(far + 1, dom_total)]
+
+        def placing(count):
+            return [
+                pltpu.VMEM((elements, count * 2 * usual), BF),
+                pltpu.VMEM((count * 2 * usual, width), BF),
+            ]
+
+        early = call(
+            functools.partial(place_early, len(soon)), "place_early", [VMEM] * len(soon),
+            arrays((elements, width), F32), placing(len(soon)), [payloads[k] for k in soon],
+        )
+        placed, scratch = False, placing(len(late))
     else:
-        payloads = [
-            spread_rows(received, entry_slot, entry_count, weights, owner_route, owner_slot)
-        ]
+        early = spread_rows(received, entry_slot, entry_count, weights, owner_route, owner_slot)
+        late = []
         placed, scratch = True, []
     export = arrays((3, shared_nodes.shape[1]), F32)
-    history, local, *exports = call(
-        functools.partial(finish, placed, len(payloads)), "finish",
-        [VMEM] * (len(payloads) + 8),
+    arrived, local, *exports = call(
+        functools.partial(finish, placed, len(late)), "finish",
+        [VMEM] * (len(late) + 8),
         [arrays((elements, width), BF), arrays((3, nodes // LANES, LANES), F32)] + [export] * 4,
         scratch,
-        (
-            *payloads, drive, base, edge, connectivity, onehot,
-            decay.reshape(1, width), readout.T, chosen,
-        ),
-    )
-    halo = [
-        lax.ppermute(exports[0], "dom", swaps("dom", 0)),
-        lax.ppermute(exports[1], "dom", swaps("dom", 1)),
-        lax.ppermute(exports[2], "box", swaps("box", 0)),
-        lax.ppermute(exports[3], "box", swaps("box", 1)),
-    ]
+        (*late, early, base, edge, connectivity, onehot, relaxing, readout.T, chosen),
+    )
+    history = call(
+        relax, "relax", [VMEM] * 3, arrays((elements, width), BF), [], (arrived, drive, relaxing)
+    )
+    halo = [None] * 4
+    for m, axis, first in ((3, "box", 1), (1, "dom", 1), (0, "dom", 0), (2, "box", 0)):
+        halo[m] = lax.ppermute(exports[m], axis, swaps(axis, first))
     force = call(
         add_shared, "add_shared", [VMEM] * (2 + len(halo)), arrays((3, nodes), F32), [],
         (local, inverse, *halo),

time: 48.2 us -> 44.9 us (0.932)
  waiting for transfers between devices: 5.72 us -> 3.37 us
  local copies, waits for them, and re-layouts: 6.79 us -> 5.57 us
  starting transfers between devices: 22.2 us -> 23.3 us
  Pallas kernels: 12.4 us -> 11.5 us
    ppermute x11, waiting for transfers between devices: 5.02 us -> 3.37 us  [the longest x7 2.29 us: body(): lax.ppermute(outgoing[k], 'dom', [(i, i ^ k) for i in range(dom_total)])]
    unnamed x30 -> x28, local copies, waits for them, and re-layouts: 6.79 us -> 5.57 us
    ppermute x11, starting transfers between devices: 19.7 us -> 20.8 us  [the longest x4 11.5 us: body(): halo[m] = lax.ppermute(exports[m], axis, swaps(axis, first))]
    pallas_call x6 -> x8, Pallas kernels: 12.4 us -> 11.5 us  [call(): pl.pallas_call(kernel, name=name, out_shape=outs, in_specs=ins, out_specs...]
    ppermute x3, waiting for transfers between devices: 0.7 us -> 0.01 us  [body(): lax.ppermute(packed[k], 'box', [(i, i ^ k) for i in range(box_total)])]
  transfers between devices with their start and end apart: 14 -> 14, of which waited for: 5 -> 2; matrix products, arithmetic and copies ran while one was open for 0% -> 0% of each run, Pallas kernels for 11% -> 16%
where the time goes in v2:
time: 44.9 us; the launch traced here: 44.6 us
  starting transfers between devices  23.3 us (52%)
  Pallas kernels  11.5 us (26%)
  local copies, waits for them, and re-layouts  5.57 us (12%)
  waiting for transfers between devices  3.37 us (8%)
  between operations  0.82 us (2%)
    pallas_call x8, Pallas kernels, call(): pl.pallas_call(kernel, name=name, out_shape=outs, in_specs=ins, out_specs...  11.5 us
    ppermute x4, starting transfers between devices, body(): halo[m] = lax.ppermute(exports[m], axis, swaps(axis, first))  11.5 us
    ppermute x7, starting transfers between devices, body(): lax.ppermute(outgoing[k], 'dom', [(i, i ^ k) for i in range(dom_total)])  9.37 us
    unnamed x28, local copies, waits for them, and re-layouts  5.57 us
    ppermute x3, starting transfers between devices, body(): lax.ppermute(packed[k], 'box', [(i, i ^ k) for i in range(box_total)])  2.45 us
    ppermute x7, waiting for transfers between devices, body(): lax.ppermute(outgoing[k], 'dom', [(i, i ^ k) for i in range(dom_total)])  2.29 us
    ppermute x4, waiting for transfers between devices, body(): halo[m] = lax.ppermute(exports[m], axis, swaps(axis, first))  1.07 us
  transfers between devices with their start and end apart: 14, of which 2 were waited for; matrix products, arithmetic and copies ran while one was open for 0% of the time, Pallas kernels for 16%

profile of v2, /device:TPU:5, one launch (start us, length us, event | category | flops | bytes accessed | tf_op | source)
XLA Modules:
  0.0 44.6 jit_solution(13443102217021910901)
XLA Ops:
  0.6 0.9 %copy-done.1 = bf16[8,128,128]{2,1,0:T(8,128)(2,1)S(1)} copy-done((bf16[8,128,128]{2,1,0:T(8,128)(2,1)S(1)}, bf16[8,128,128]{2,1,0:T(8,128)(2,1)}, u32[]{:S(2)}) %copy-start.1) | copy-done | bytes 262168
  1.6 0.7 %copy-done.12 = s32[8]{0:T(128)S(1)} copy-done((s32[8]{0:T(128)S(1)}, s32[8]{0:T(128)}, u32[]{:S(2)}) %copy-start.12) | copy-done | bytes 56
  2.2 0.6 %pack_blocks.1 = (bf16[4,128,128]{2,1,0:T(8,128)(2,1)S(1)}, bf16[4,128,128]{2,1,0:T(8,128)(2,1)S(1)}, bf16[4,128,128]{2,1,0:T(8,128)(2,1)S(1)}, bf16[4,128,128]{2,1,0:T(8,128)(2,1)S(1)}) custom-call(s32[8]{0:T(128)S(1)} %copy-done.12, bf16[8,128,128]{2,1,0:T(8,128)(2,1)S(1)} %copy-done.1), custom_call_target="tpu_custom_call" | custom-call | flops 1000 | bytes 100000 | tf_op jit(solution)/shard_map/pack_blocks/pallas_call | solution.py:370
  2.9 0.7 %collective-permute-start = (bf16[4,128,128]{2,1,0:T(8,128)(2,1)S(1)}, bf16[4,128,128]{2,1,0:T(8,128)(2,1)S(1)}, u32[]{:S(2)}, u32[]{:S(2)}) collective-permute-start(bf16[4,128,128]{2,1,0:T(8,128)(2,1)S(1)} %get-tuple-element.36), channel_id=1, source_target_pairs={{0,1},{1,0},{2,3},{3,2},{4,5},{5,4},{6,7},{7,6},{8,9},{9,8},{10,11... | collective-permute-start | bytes 393224 | tf_op jit(solution)/shard_map/ppermute | solution.py:453
  3.6 1.2 %collective-permute-start.1 = (bf16[4,128,128]{2,1,0:T(8,128)(2,1)S(1)}, bf16[4,128,128]{2,1,0:T(8,128)(2,1)S(1)}, u32[]{:S(2)}, u32[]{:S(2)}) collective-permute-start(bf16[4,128,128]{2,1,0:T(8,128)(2,1)S(1)} %get-tuple-element.37), channel_id=1, source_target_pairs={{0,2},{1,3},{2,0},{3,1},{4,6},{5,7},{6,4},{7,5},{8,10},{9,11},{10,... | collective-permute-start | bytes 393224 | tf_op jit(solution)/shard_map/ppermute | solution.py:453
  4.8 0.5 %collective-permute-start.2 = (bf16[4,128,128]{2,1,0:T(8,128)(2,1)S(1)}, bf16[4,128,128]{2,1,0:T(8,128)(2,1)S(1)}, u32[]{:S(2)}, u32[]{:S(2)}) collective-permute-start(bf16[4,128,128]{2,1,0:T(8,128)(2,1)S(1)} %get-tuple-element.38), channel_id=1, source_target_pairs={{0,3},{1,2},{2,1},{3,0},{4,7},{5,6},{6,5},{7,4},{8,11},{9,10},{10,... | collective-permute-start | bytes 393224 | tf_op jit(solution)/shard_map/ppermute | solution.py:453
  5.3 1.2 %copy-done = bf16[8,4,128,128]{3,2,1,0:T(8,128)(2,1)S(1)} copy-done((bf16[8,4,128,128]{3,2,1,0:T(8,128)(2,1)S(1)}, bf16[8,4,128,128]{3,2,1,0:T(8,128)(2,1)}, u32[]{:S(2)}) %copy-start) | copy-done | bytes 1048600
  6.6 0.7 %copy-done.6 = s32[1024]{0:T(1024)S(1)} copy-done((s32[1024]{0:T(1024)S(1)}, s32[1024]{0:T(1024)}, u32[]{:S(2)}) %copy-start.6) | copy-done | bytes 4120
  7.3 0.7 %copy-done.7 = s32[1024]{0:T(1024)S(1)} copy-done((s32[1024]{0:T(1024)S(1)}, s32[1024]{0:T(1024)}, u32[]{:S(2)}) %copy-start.7) | copy-done | bytes 4120
  7.9 0.7 %copy-done.9 = s32[8,4]{0,1:T(4,128)S(1)} copy-done((s32[8,4]{0,1:T(4,128)S(1)}, s32[8,4]{0,1:T(4,128)}, u32[]{:S(2)}) %copy-start.9) | copy-done | bytes 152
  8.6 0.7 %copy-done.13 = s32[8]{0:T(128)S(1)} copy-done((s32[8]{0:T(128)S(1)}, s32[8]{0:T(128)}, u32[]{:S(2)}) %copy-start.13) | copy-done | bytes 56
  9.3 2.5 %sort_rows.1 = (bf16[1024,1024]{1,0:T(8,128)(2,1)S(1)}, bf16[8,16,128]{2,1,0:T(8,128)(2,1)S(1)}, s32[48]{0:T(128)S(1)}, f32[8,128]{1,0:T(8,128)S(1)}, bf16[8,512,128]{2,1,0:T(8,128)(2,1)S(1)}) custom-call(s32[4,8]{1,0:T(4,128)S(1)} %bitcast.16, s32[8]{0:T(128)S(1)} %copy-done.13, s32[8,128]{1,0:T(8,128)S(1)} %bitcast.13, s32[1,1024]{1,0:T(1,128)S(1)} %bitcast.14, ...), custom_call_target="tpu_custom_call" | custom-call | flops 1000 | bytes 100000 | tf_op jit(solution)/shard_map/sort_rows/pallas_call | solution.py:370
  11.9 0.0 copy-start.4
  11.9 0.0 copy-start.5
  11.9 1.7 %project_rows.1 = (bf16[272,128]{1,0:T(8,128)(2,1)S(1)}, bf16[272,128]{1,0:T(8,128)(2,1)S(1)}, bf16[272,128]{1,0:T(8,128)(2,1)S(1)}, bf16[272,128]{1,0:T(8,128)(...) custom-call(s32[48]{0:T(128)S(1)} %get-tuple-element.30.table, ...), custom_call_target="tpu_custom_call" | custom-call | flops 1000 | bytes 100000 | tf_op jit(solution)/shard_map/project_rows/pallas_call | solution.py:370
  13.6 0.1 collective-permute-start.6
  13.7 1.5 %collective-permute-start.7 = (bf16[272,128]{1,0:T(8,128)(2,1)S(1)}, bf16[272,128]{1,0:T(8,128)(2,1)S(1)}, u32[]{:S(2)}, u32[]{:S(2)}) collective-permute-start(bf16[272,128]{1,0:T(8,128)(2,1)S(1)} %get-tuple-element.44), channel_id=1, source_target_pairs={{0,8},{4,12},{8,0},{12,4},{16,24},{20,28},{24,16},{28,20},{1,9},{5... | collective-permute-start | bytes 208904 | tf_op jit(solution)/shard_map/ppermute | solution.py:519
  15.2 1.1 %collective-permute-start.8 = (bf16[272,128]{1,0:T(8,128)(2,1)S(1)}, bf16[272,128]{1,0:T(8,128)(2,1)S(1)}, u32[]{:S(2)}, u32[]{:S(2)}) collective-permute-start(bf16[272,128]{1,0:T(8,128)(2,1)S(1)} %get-tuple-element.45), channel_id=1, source_target_pairs={{0,12},{4,8},{8,4},{12,0},{16,28},{20,24},{24,20},{28,16},{1,13},{... | collective-permute-start | bytes 208904 | tf_op jit(solution)/shard_map/ppermute | solution.py:519
  16.3 2.3 %collective-permute-start.9 = (bf16[272,128]{1,0:T(8,128)(2,1)S(1)}, bf16[272,128]{1,0:T(8,128)(2,1)S(1)}, u32[]{:S(2)}, u32[]{:S(2)}) collective-permute-start(bf16[272,128]{1,0:T(8,128)(2,1)S(1)} %get-tuple-element.46), channel_id=1, source_target_pairs={{0,16},{4,20},{8,24},{12,28},{16,0},{20,4},{24,8},{28,12},{1,17},{... | collective-permute-start | bytes 208904 | tf_op jit(solution)/shard_map/ppermute | solution.py:519
  18.7 3.3 %collective-permute-start.4 = (bf16[272,128]{1,0:T(8,128)(2,1)S(1)}, bf16[272,128]{1,0:T(8,128)(2,1)S(1)}, u32[]{:S(2)}, u32[]{:S(2)}) collective-permute-start(bf16[272,128]{1,0:T(8,128)(2,1)S(1)} %get-tuple-element.40), channel_id=1, source_target_pairs={{0,24},{4,28},{8,16},{12,20},{16,8},{20,12},{24,0},{28,4},{1,25},{... | collective-permute-start | bytes 208904 | tf_op jit(solution)/shard_map/ppermute | solution.py:519
  22.0 1.0 %collective-permute-start.5 = (bf16[272,128]{1,0:T(8,128)(2,1)S(1)}, bf16[272,128]{1,0:T(8,128)(2,1)S(1)}, u32[]{:S(2)}, u32[]{:S(2)}) collective-permute-start(bf16[272,128]{1,0:T(8,128)(2,1)S(1)} %get-tuple-element.41), channel_id=1, source_target_pairs={{0,28},{4,24},{8,20},{12,16},{16,12},{20,8},{24,4},{28,0},{1,29},{... | collective-permute-start | bytes 208904 | tf_op jit(solution)/shard_map/ppermute | solution.py:519
  23.0 2.8 %element_parts.1 = (f32[1024,128]{1,0:T(8,128)S(1)}, f32[8,1024]{1,0:T(8,128)S(1)}, bf16[8,1024,128]{2,1,0:T(8,128)(2,1)S(1)}, s32[8,128]{1,0:T(8,128)S(1)}, s32[2,8,128]{2,1,0:T(8,128)S(1)}) custom-call(s32[8,1024]{1,0:T(8,128)S(1)} %copy-done.2, f32[3,1024]{1,0:T(4,128)S(1)} %copy-done.5, f32[1,1024]{1,0:T(1,128)S(1)} %bitcast.9, f32[6,128]{1,0:T(8,128)S(1)} %bitcast.15, ...), custom_call_target="tpu_custom_call" | custom-call | flops 1000 | bytes 100000 | tf_op jit(solution)/shard_map/element_parts/pallas_call | solution.py:370
  25.8 0.9 %place_early.1.refs_3_ = f32[1024,128]{1,0:T(8,128)S(1)} custom-call(bf16[272,128]{1,0:T(8,128)(2,1)S(1)} %get-tuple-element.42.refs_0_, bf16[272,128]{1,0:T(8,128)(2,1)S(1)} %collective-permute-done.6.refs_1_, bf16[272,128]{1,0:T(8,128)(2,1)S(1)} %collective-permute-done.7.refs_2_, bf16[272,128]{1,0:T(8,128)(2,1)S(1)} %collective-permute-done.8.refs_3_, ...), custom_call_target="tpu_custom_call" | custom-call | flops 1000 | bytes 100000 | tf_op jit(solution)/shard_map/place_early/pallas_call | solution.py:370
  26.7 2.3 %collective-permute-done.3.refs_0_ = bf16[272,128]{1,0:T(8,128)(2,1)S(1)} collective-permute-done((bf16[272,128]{1,0:T(8,128)(2,1)S(1)}, bf16[272,128]{1,0:T(8,128)(2,1)S(1)}, u32[]{:S(2)}, u32[]{:S(2)}) %collective-permute-start.3) | collective-permute-done | bytes 69664 | tf_op jit(solution)/shard_map/ppermute | solution.py:519
  29.0 1.5 %finish.1 = (bf16[1024,128]{1,0:T(8,128)(2,1)S(1)}, f32[3,8,128]{2,1,0:T(8,128)S(1)}, f32[3,128]{1,0:T(4,128)S(1)}, f32[3,128]{1,0:T(4,128)S(1)}, f32[3,128]{1,0:T(4,128)S(1)}, /*index=5*/f32[3,128]{1,0:T(4,128)S(1)}) custom-call(bf16[272,128]{1,0:T(8,128)(2,1)S(1)} %collective-permute-done.3.refs_0_, bf16[272,128]{1,0:T(8,128)(2,1)S(1)} %collective-permute-done.4.refs_1_, ...), custom_call_target="tpu_custom_call" | custom-call | flops 1000 | bytes 100000 | tf_op jit(solution)/shard_map/finish/pallas_call | solution.py:370
  30.6 0.7 %collective-permute-start.10 = (f32[3,128]{1,0:T(4,128)S(1)}, f32[3,128]{1,0:T(4,128)S(1)}, u32[]{:S(2)}, u32[]{:S(2)}) collective-permute-start(f32[3,128]{1,0:T(4,128)S(1)} %get-tuple-element.54), channel_id=1, source_target_pairs={{0,4},{4,0},{8,12},{12,8},{16,20},{20,16},{24,28},{28,24},{1,5},{5... | collective-permute-start | bytes 4616 | tf_op jit(solution)/shard_map/ppermute | solution.py:553
  31.3 6.4 %collective-permute-start.11 = (f32[3,128]{1,0:T(4,128)S(1)}, f32[3,128]{1,0:T(4,128)S(1)}, u32[]{:S(2)}, u32[]{:S(2)}) collective-permute-start(f32[3,128]{1,0:T(4,128)S(1)} %get-tuple-element.55), channel_id=1, source_target_pairs={{4,8},{8,4},{12,16},{16,12},{20,24},{24,20},{5,9},{9,5},{13,17},{1... | collective-permute-start | bytes 4616 | tf_op jit(solution)/shard_map/ppermute | solution.py:553
  37.7 1.3 %collective-permute-start.12 = (f32[3,128]{1,0:T(4,128)S(1)}, f32[3,128]{1,0:T(4,128)S(1)}, u32[]{:S(2)}, u32[]{:S(2)}) collective-permute-start(f32[3,128]{1,0:T(4,128)S(1)} %get-tuple-element.56), channel_id=1, source_target_pairs={{0,1},{1,0},{2,3},{3,2},{4,5},{5,4},{6,7},{7,6},{8,9},{9,8},{10,11... | collective-permute-start | bytes 4616 | tf_op jit(solution)/shard_map/ppermute | solution.py:553
  39.0 3.0 %collective-permute-start.13 = (f32[3,128]{1,0:T(4,128)S(1)}, f32[3,128]{1,0:T(4,128)S(1)}, u32[]{:S(2)}, u32[]{:S(2)}) collective-permute-start(f32[3,128]{1,0:T(4,128)S(1)} %get-tuple-element.57), channel_id=1, source_target_pairs={{1,2},{2,1},{5,6},{6,5},{9,10},{10,9},{13,14},{14,13},{17,18},{18,... | collective-permute-start | bytes 4616 | tf_op jit(solution)/shard_map/ppermute | solution.py:553
  42.0 0.8 %relax.1 = bf16[1024,128]{1,0:T(8,128)(2,1)} custom-call(bf16[1024,128]{1,0:T(8,128)(2,1)S(1)} %get-tuple-element.50.arrived, f32[1024,128]{1,0:T(8,128)S(1)} %get-tuple-element.51.drive, f32[1,128]{1,0:T(1,128)S(1)} %bitcast.18), custom_call_target="tpu_custom_call" | custom-call | flops 1000 | bytes 100000 | tf_op jit(solution)/shard_map/relax/pallas_call | solution.py:370
  42.8 1.1 %collective-permute-done.13.rest_3_ = f32[3,128]{1,0:T(4,128)S(1)} collective-permute-done((f32[3,128]{1,0:T(4,128)S(1)}, f32[3,128]{1,0:T(4,128)S(1)}, u32[]{:S(2)}, u32[]{:S(2)}) %collective-permute-start.13) | collective-permute-done | bytes 1568 | tf_op jit(solution)/shard_map/ppermute | solution.py:553
  43.9 0.7 %add_shared.1 = f32[3,1024]{1,0:T(4,128)} custom-call(f32[3,8,128]{2,1,0:T(8,128)S(1)} %get-tuple-element.52.local, s32[2,8,128]{2,1,0:T(8,128)S(1)} %get-tuple-element.53.inverse, f32[3,128]{1,0:T(4,128)S(1)} %collective-permute-done.10.rest_0_, f32[3,128]{1,0:T(4,128)S(1)} %collective-permute-done.11.rest_1_, ...), custom_call_target="tpu_custom_call" | custom-call | flops 1000 | bytes 100000 | tf_op jit(solution)/shard_map/add_shared/pallas_call | solution.py:370
  (32 shorter events, 0.1 us)
Async XLA Ops:
  0.6 1.0 %copy-start.1 = (bf16[8,128,128]{2,1,0:T(8,128)(2,1)S(1)}, bf16[8,128,128]{2,1,0:T(8,128)(2,1)}, u32[]{:S(2)}) copy-start(bf16[8,128,128]{2,1,0:T(8,128)(2,1)} %old_hbm.1) | copy-start | bytes 786436
  1.6 0.7 %copy-start.12 = (s32[8]{0:T(128)S(1)}, s32[8]{0:T(128)}, u32[]{:S(2)}) copy-start(s32[8]{0:T(128)} %route_hbm.1) | copy-start | bytes 100
  2.9 9.0 %collective-permute-start = (bf16[4,128,128]{2,1,0:T(8,128)(2,1)S(1)}, bf16[4,128,128]{2,1,0:T(8,128)(2,1)S(1)}, u32[]{:S(2)}, u32[]{:S(2)}) collective-permute-start(bf16[4,128,128]{2,1,0:T(8,128)(2,1)S(1)} %get-tuple-element.36), channel_id=1, source_target_pairs={{0,1},{1,0},{2,3},{3,2},{4,5},{5,4},{6,7},{7,6},{8,9},{9,8},{10,11... | collective-permute-start | bytes 393224 | tf_op jit(solution)/shard_map/ppermute | solution.py:453
  3.6 8.3 %collective-permute-start.1 = (bf16[4,128,128]{2,1,0:T(8,128)(2,1)S(1)}, bf16[4,128,128]{2,1,0:T(8,128)(2,1)S(1)}, u32[]{:S(2)}, u32[]{:S(2)}) collective-permute-start(bf16[4,128,128]{2,1,0:T(8,128)(2,1)S(1)} %get-tuple-element.37), channel_id=1, source_target_pairs={{0,2},{1,3},{2,0},{3,1},{4,6},{5,7},{6,4},{7,5},{8,10},{9,11},{10,... | collective-permute-start | bytes 393224 | tf_op jit(solution)/shard_map/ppermute | solution.py:453
  4.8 7.1 %collective-permute-start.2 = (bf16[4,128,128]{2,1,0:T(8,128)(2,1)S(1)}, bf16[4,128,128]{2,1,0:T(8,128)(2,1)S(1)}, u32[]{:S(2)}, u32[]{:S(2)}) collective-permute-start(bf16[4,128,128]{2,1,0:T(8,128)(2,1)S(1)} %get-tuple-element.38), channel_id=1, source_target_pairs={{0,3},{1,2},{2,1},{3,0},{4,7},{5,6},{6,5},{7,4},{8,11},{9,10},{10,... | collective-permute-start | bytes 393224 | tf_op jit(solution)/shard_map/ppermute | solution.py:453
  5.3 1.2 %copy-start = (bf16[8,4,128,128]{3,2,1,0:T(8,128)(2,1)S(1)}, bf16[8,4,128,128]{3,2,1,0:T(8,128)(2,1)}, u32[]{:S(2)}) copy-start(bf16[8,4,128,128]{3,2,1,0:T(8,128)(2,1)} %param.18) | copy-start | bytes 3145732
  6.6 0.7 %copy-start.6 = (s32[1024]{0:T(1024)S(1)}, s32[1024]{0:T(1024)}, u32[]{:S(2)}) copy-start(s32[1024]{0:T(1024)} %param.19) | copy-start | bytes 12292
  7.3 0.7 %copy-start.7 = (s32[1024]{0:T(1024)S(1)}, s32[1024]{0:T(1024)}, u32[]{:S(2)}) copy-start(s32[1024]{0:T(1024)} %param.20) | copy-start | bytes 12292
  7.9 0.7 %copy-start.9 = (s32[8,4]{0,1:T(4,128)S(1)}, s32[8,4]{0,1:T(4,128)}, u32[]{:S(2)}) copy-start(s32[8,4]{0,1:T(4,128)} %param.16) | copy-start | bytes 388
  8.6 0.7 %copy-start.13 = (s32[8]{0:T(128)S(1)}, s32[8]{0:T(128)}, u32[]{:S(2)}) copy-start(s32[8]{0:T(128)} %count_hbm.1) | copy-start | bytes 100
  11.8 11.2 %copy-start.2 = (s32[8,1024]{1,0:T(8,128)S(1)}, s32[8,1024]{1,0:T(8,128)}, u32[]{:S(2)}) copy-start(s32[8,1024]{1,0:T(8,128)} %refs_6_.1) | copy-start | bytes 98308
  11.8 11.2 %copy-start.3 = (f32[1024]{0:T(1024)S(1)}, f32[1024]{0:T(1024)}, u32[]{:S(2)}) copy-start(f32[1024]{0:T(1024)} %param.24) | copy-start | bytes 12292
  11.9 11.2 %copy-start.4 = (f32[128,6]{0,1:T(8,128)S(1)}, f32[128,6]{0,1:T(8,128)}, u32[]{:S(2)}) copy-start(f32[128,6]{0,1:T(8,128)} %param.27) | copy-start | bytes 9220
  11.9 11.2 %copy-start.5 = (f32[3,1024]{1,0:T(4,128)S(1)}, f32[3,1024]{1,0:T(4,128)}, u32[]{:S(2)}) copy-start(f32[3,1024]{1,0:T(4,128)} %motion.1) | copy-start | bytes 36868
  11.9 11.2 %copy-start.8 = (f32[128,6]{0,1:T(8,128)S(1)}, f32[128,6]{0,1:T(8,128)}, u32[]{:S(2)}) copy-start(f32[128,6]{0,1:T(8,128)} %param.26) | copy-start | bytes 9220
  11.9 11.2 %copy-start.11 = (s32[4,128]{1,0:T(4,128)S(1)}, s32[4,128]{1,0:T(4,128)}, u32[]{:S(2)}) copy-start(s32[4,128]{1,0:T(4,128)} %shared.1) | copy-start | bytes 6148
  11.9 17.1 %copy-start.10 = (f32[128]{0:T(128)S(1)}, f32[128]{0:T(128)}, u32[]{:S(2)}) copy-start(f32[128]{0:T(128)} %param.25) | copy-start | bytes 1540
  13.6 5.0 %collective-permute-start.6 = (bf16[272,128]{1,0:T(8,128)(2,1)S(1)}, bf16[272,128]{1,0:T(8,128)(2,1)S(1)}, u32[]{:S(2)}, u32[]{:S(2)}) collective-permute-start(bf16[272,128]{1,0:T(8,128)(2,1)S(1)} %get-tuple-element.43), channel_id=1, source_target_pairs={{0,4},{4,0},{8,12},{12,8},{16,20},{20,16},{24,28},{28,24},{1,5},{5... | collective-permute-start | bytes 208904 | tf_op jit(solution)/shard_map/ppermute | solution.py:519
  13.7 8.3 %collective-permute-start.7 = (bf16[272,128]{1,0:T(8,128)(2,1)S(1)}, bf16[272,128]{1,0:T(8,128)(2,1)S(1)}, u32[]{:S(2)}, u32[]{:S(2)}) collective-permute-start(bf16[272,128]{1,0:T(8,128)(2,1)S(1)} %get-tuple-element.44), channel_id=1, source_target_pairs={{0,8},{4,12},{8,0},{12,4},{16,24},{20,28},{24,16},{28,20},{1,9},{5... | collective-permute-start | bytes 208904 | tf_op jit(solution)/shard_map/ppermute | solution.py:519
  15.2 10.6 %collective-permute-start.8 = (bf16[272,128]{1,0:T(8,128)(2,1)S(1)}, bf16[272,128]{1,0:T(8,128)(2,1)S(1)}, u32[]{:S(2)}, u32[]{:S(2)}) collective-permute-start(bf16[272,128]{1,0:T(8,128)(2,1)S(1)} %get-tuple-element.45), channel_id=1, source_target_pairs={{0,12},{4,8},{8,4},{12,0},{16,28},{20,24},{24,20},{28,16},{1,13},{... | collective-permute-start | bytes 208904 | tf_op jit(solution)/shard_map/ppermute | solution.py:519
  16.3 9.5 %collective-permute-start.9 = (bf16[272,128]{1,0:T(8,128)(2,1)S(1)}, bf16[272,128]{1,0:T(8,128)(2,1)S(1)}, u32[]{:S(2)}, u32[]{:S(2)}) collective-permute-start(bf16[272,128]{1,0:T(8,128)(2,1)S(1)} %get-tuple-element.46), channel_id=1, source_target_pairs={{0,16},{4,20},{8,24},{12,28},{16,0},{20,4},{24,8},{28,12},{1,17},{... | collective-permute-start | bytes 208904 | tf_op jit(solution)/shard_map/ppermute | solution.py:519
  18.7 10.4 %collective-permute-start.3 = (bf16[272,128]{1,0:T(8,128)(2,1)S(1)}, bf16[272,128]{1,0:T(8,128)(2,1)S(1)}, u32[]{:S(2)}, u32[]{:S(2)}) collective-permute-start(bf16[272,128]{1,0:T(8,128)(2,1)S(1)} %get-tuple-element.39), channel_id=1, source_target_pairs={{0,20},{4,16},{8,28},{12,24},{16,4},{20,0},{24,12},{28,8},{1,21},{... | collective-permute-start | bytes 208904 | tf_op jit(solution)/shard_map/ppermute | solution.py:519
  18.7 10.3 %collective-permute-start.4 = (bf16[272,128]{1,0:T(8,128)(2,1)S(1)}, bf16[272,128]{1,0:T(8,128)(2,1)S(1)}, u32[]{:S(2)}, u32[]{:S(2)}) collective-permute-start(bf16[272,128]{1,0:T(8,128)(2,1)S(1)} %get-tuple-element.40), channel_id=1, source_target_pairs={{0,24},{4,28},{8,16},{12,20},{16,8},{20,12},{24,0},{28,4},{1,25},{... | collective-permute-start | bytes 208904 | tf_op jit(solution)/shard_map/ppermute | solution.py:519
  22.0 7.0 %collective-permute-start.5 = (bf16[272,128]{1,0:T(8,128)(2,1)S(1)}, bf16[272,128]{1,0:T(8,128)(2,1)S(1)}, u32[]{:S(2)}, u32[]{:S(2)}) collective-permute-start(bf16[272,128]{1,0:T(8,128)(2,1)S(1)} %get-tuple-element.41), channel_id=1, source_target_pairs={{0,28},{4,24},{8,20},{12,16},{16,12},{20,8},{24,4},{28,0},{1,29},{... | collective-permute-start | bytes 208904 | tf_op jit(solution)/shard_map/ppermute | solution.py:519
  30.6 12.3 %collective-permute-start.10 = (f32[3,128]{1,0:T(4,128)S(1)}, f32[3,128]{1,0:T(4,128)S(1)}, u32[]{:S(2)}, u32[]{:S(2)}) collective-permute-start(f32[3,128]{1,0:T(4,128)S(1)} %get-tuple-element.54), channel_id=1, source_target_pairs={{0,4},{4,0},{8,12},{12,8},{16,20},{20,16},{24,28},{28,24},{1,5},{5... | collective-permute-start | bytes 4616 | tf_op jit(solution)/shard_map/ppermute | solution.py:553
  31.3 11.6 %collective-permute-start.11 = (f32[3,128]{1,0:T(4,128)S(1)}, f32[3,128]{1,0:T(4,128)S(1)}, u32[]{:S(2)}, u32[]{:S(2)}) collective-permute-start(f32[3,128]{1,0:T(4,128)S(1)} %get-tuple-element.55), channel_id=1, source_target_pairs={{4,8},{8,4},{12,16},{16,12},{20,24},{24,20},{5,9},{9,5},{13,17},{1... | collective-permute-start | bytes 4616 | tf_op jit(solution)/shard_map/ppermute | solution.py:553
  37.7 5.1 %collective-permute-start.12 = (f32[3,128]{1,0:T(4,128)S(1)}, f32[3,128]{1,0:T(4,128)S(1)}, u32[]{:S(2)}, u32[]{:S(2)}) collective-permute-start(f32[3,128]{1,0:T(4,128)S(1)} %get-tuple-element.56), channel_id=1, source_target_pairs={{0,1},{1,0},{2,3},{3,2},{4,5},{5,4},{6,7},{7,6},{8,9},{9,8},{10,11... | collective-permute-start | bytes 4616 | tf_op jit(solution)/shard_map/ppermute | solution.py:553
  39.0 4.9 %collective-permute-start.13 = (f32[3,128]{1,0:T(4,128)S(1)}, f32[3,128]{1,0:T(4,128)S(1)}, u32[]{:S(2)}, u32[]{:S(2)}) collective-permute-start(f32[3,128]{1,0:T(4,128)S(1)} %get-tuple-element.57), channel_id=1, source_target_pairs={{1,2},{2,1},{5,6},{6,5},{9,10},{10,9},{13,14},{14,13},{17,18},{18,... | collective-permute-start | bytes 4616 | tf_op jit(solution)/shard_map/ppermute | solution.py:553

commit v3 on v2

--- a/solution.py
+++ b/solution.py
@@ -6,6 +6,7 @@
 from jax.experimental import pallas as pl
 from jax.experimental.pallas import tpu as pltpu
 from jax.sharding import PartitionSpec as P
+
 
 BF = jnp.bfloat16
 F32 = jnp.float32
@@ -50,21 +51,8 @@
     return out
 
 
-def fetch(pairs, sems):
-    copies = [
-        pltpu.make_async_copy(source, target, sems.at[i])
-        for i, (source, target) in enumerate(pairs)
-    ]
-    for copy in copies:
-        copy.start()
-    for copy in copies:
-        copy.wait()
-
-
-def pack_blocks(route_hbm, old_hbm, *rest):
-    outs = rest[:-4]
-    table, route, old, sems = rest[-4:]
-    fetch([(route_hbm, route), (old_hbm, old)], sems)
+def pack_blocks(route, old, *rest):
+    outs, table = rest[:-1], rest[-1]
     me = lax.axis_index("box")
     capacity = outs[0].shape[0]
     for m in range(len(outs) * capacity):
@@ -80,19 +68,17 @@
             out[s] = old[table[k * capacity + s]]
 
 
-def sort_rows(capacity, slot_hbm, count_hbm, route_hbm, place_hbm, weights_hbm, sorter, positions, table,
-              mass_inv, masked, high_rows, low_rows, starts, slot, count, owner_route, owner_slot,
-              sems):
-    fetch(
-        [
-            (slot_hbm, slot),
-            (count_hbm, count),
-            (route_hbm, owner_route),
-            (place_hbm, owner_slot),
-            (weights_hbm, masked),
-        ],
-        sems,
-    )
+def mark_places(target, column, high, low):
+    low_iota = iota((LANES, LANES), 0).astype(F32).astype(BF)
+    low = jnp.broadcast_to(low, (LANES, LANES)).astype(BF)
+    match = jnp.where(low_iota == low, jnp.ones_like(low), jnp.zeros_like(low))
+    lanes = slice(column * LANES, (column + 1) * LANES)
+    for g in range(target.shape[0] // LANES):
+        here = jnp.broadcast_to(jnp.where(high == g, 1.0, 0.0), (LANES, LANES)).astype(BF)
+        target[g * LANES : (g + 1) * LANES, lanes] = match * here
+
+
+def sort_rows(owner_route, owner_slot, sorter, positions, table, high_rows, low_rows, starts):
     dom_total = positions.shape[0]
     row_groups = owner_route.shape[0]
     rows = row_groups * LANES
@@ -112,9 +98,10 @@
         starts[d] = jnp.max(base[d * row_groups : d * row_groups + 1]).astype(I32)
     starts[dom_total] = rows
     place = place.astype(I32)
-    slots = iota((rows, LANES), 0)
+    high = (place >> 7).astype(F32)
+    low = (place & (LANES - 1)).astype(F32)
     for g in range(row_groups):
-        sorter[:, g * LANES : (g + 1) * LANES] = as_onehot(slots == place[g : g + 1])
+        mark_places(sorter, g, high[g : g + 1], low[g : g + 1])
     spot = owner_slot[...]
     which = iota((POS_ROWS, rows), 0)
     parts = jnp.where(which == 0, spot >> 7, jnp.where(which == 1, spot & (LANES - 1), 0))
@@ -137,21 +124,24 @@
             block = jnp.where(which == j, high, block)
             block = jnp.where(which == 2 + j, low_rows[pl.ds(chunk, 1)], block)
         positions[k] = block.astype(BF)
-    targets = masked.shape[0]
-    entries = masked.shape[1] // LANES
+
+
+def mask_weights(capacity, slot, count, weights, masked, mass_inv, blocks):
+    targets = weights.shape[0]
+    entries = weights.shape[1] // LANES
     box = lax.axis_index("box")
     for t in range(targets):
         total = jnp.zeros((1, LANES), F32)
         for l in range(entries):
             live = l < count[t]
             span = slice(l * LANES, (l + 1) * LANES)
-            part = masked[t, span, :]
+            part = weights[t, span, :]
             part = jnp.where(live, part, jnp.zeros_like(part))
             masked[t, span, :] = part
             total = total + jnp.sum(part.astype(F32), axis=0, keepdims=True)
             entry = jnp.where(live, slot[l, t], slot[0, t])
-            source = lax.div(entry, capacity)
-            table[2 * dom_total + t * entries + l] = (source ^ box) * capacity + lax.rem(entry, capacity)
+            source = lax.div(entry, capacity) ^ box
+            blocks[t * entries + l] = source * capacity + lax.rem(entry, capacity)
         mass_inv[t : t + 1] = 1.0 / total
 
 
@@ -229,7 +219,7 @@
     inverse[1] = total[groups:]
 
 
-def project_rows(table, masked, mass_inv, sorter, positions, *rest):
+def project_rows(table, blocks, masked, mass_inv, sorter, positions, *rest):
     dom_total = positions.shape[0]
     box_total = lax.axis_size("box")
     received = rest[:box_total]
@@ -242,7 +232,7 @@
     targets = masked.shape[0]
     entries = masked.shape[1] // LANES
     for t in range(targets):
-        picked = [held[table[2 * dom_total + t * entries + l]] for l in range(entries)]
+        picked = [held[blocks[t * entries + l]] for l in range(entries)]
         numerator = jnp.dot(
             jnp.concatenate(picked, axis=1), masked[t], preferred_element_type=F32
         )
@@ -257,20 +247,11 @@
 
 
 def place(payloads, placing, rows):
-    groups = placing.shape[0] // LANES
-    low_iota = iota((LANES, LANES), 0).astype(F32).astype(BF)
     for k, payload in enumerate(payloads):
         rows[k * 2 * LANES : (k + 1) * 2 * LANES] = payload[: 2 * LANES]
         where = payload[2 * LANES :].astype(F32)
         for j in range(2):
-            low = jnp.broadcast_to(where[2 + j : 3 + j], (LANES, LANES)).astype(BF)
-            match = jnp.where(low_iota == low, jnp.ones_like(low), jnp.zeros_like(low))
-            lanes = slice((2 * k + j) * LANES, (2 * k + j + 1) * LANES)
-            for g in range(groups):
-                here = jnp.where(where[j : j + 1] == g, 1.0, 0.0)
-                placing[g * LANES : (g + 1) * LANES, lanes] = match * jnp.broadcast_to(
-                    here, (LANES, LANES)
-                ).astype(BF)
+            mark_places(placing, 2 * k + j, where[j : j + 1], where[2 + j : 3 + j])
     return jnp.dot(placing[...], rows[...], preferred_element_type=F32)
 
 
@@ -362,14 +343,12 @@
 
 VMEM = pl.BlockSpec(memory_space=pltpu.VMEM)
 SMEM = pl.BlockSpec(memory_space=pltpu.SMEM)
-HBM = pl.BlockSpec(memory_space=pltpu.HBM)
-
-
-def call(kernel, name, ins, outs, scratch, args, cost=100_000, out_specs=None):
+
+
+def call(kernel, ins, outs, scratch, args, cost=100_000, out_specs=None):
     single = not isinstance(outs, (list, tuple))
     return pl.pallas_call(
         kernel,
-        name=name,
         out_shape=outs,
         in_specs=ins,
         out_specs=out_specs or (VMEM if single else [VMEM] * len(outs)),
@@ -438,14 +417,9 @@
     nodes = node_motion.shape[1]
 
     packed = call(
-        pack_blocks, "pack_blocks", [HBM, HBM],
+        pack_blocks, [SMEM, VMEM],
         [arrays((capacity, width, block_size), BF)] * box_total,
-        [
-            pltpu.SMEM((box_total * capacity,), I32),
-            pltpu.SMEM((blocks,), I32),
-            pltpu.VMEM(old_history.shape, BF),
-            pltpu.SemaphoreType.DMA((2,)),
-        ],
+        [pltpu.SMEM((box_total * capacity,), I32)],
         (box_route, old_history),
     )
     received = {0: packed[0]}
@@ -455,7 +429,7 @@
     flat_weights = weights.reshape(targets, entries * block_size, block_size)
     edge = elem_size.reshape(1, elements)
     drive, base, onehot, chosen, inverse = call(
-        element_parts, "element_parts", [VMEM] * 6,
+        element_parts, [VMEM] * 6,
         [
             arrays((elements, width), F32),
             arrays((SUBS, elements), F32),
@@ -473,52 +447,47 @@
     usual = rows // dom_total
     relaxing = decay.reshape(1, width)
     if usual == LANES:
-        sorter, positions, table, mass_inv, masked = call(
-            functools.partial(sort_rows, capacity), "sort_rows", [HBM] * 5,
+        sorter, positions, table = call(
+            sort_rows, [VMEM, VMEM],
             [
                 arrays((rows, rows), BF),
                 arrays((dom_total, POS_ROWS, LANES), BF),
-                arrays((2 * dom_total + targets * entries,), I32),
-                arrays((targets, block_size), F32),
-                arrays(flat_weights.shape, BF),
+                arrays((2 * dom_total,), I32),
             ],
             [
                 pltpu.VMEM((row_groups, LANES), F32),
                 pltpu.VMEM((row_groups, LANES), F32),
                 pltpu.SMEM((dom_total + 1,), I32),
-                pltpu.SMEM((entries, targets), I32),
-                pltpu.SMEM((targets,), I32),
-                pltpu.VMEM((row_groups, LANES), I32),
-                pltpu.VMEM((1, rows), I32),
-                pltpu.SemaphoreType.DMA((5,)),
             ],
-            (
-                entry_slot.T,
-                entry_count,
-                owner_route.reshape(row_groups, LANES),
-                owner_slot.reshape(1, rows),
-                flat_weights,
-            ),
-            out_specs=[VMEM, VMEM, SMEM, VMEM, VMEM],
+            (owner_route.reshape(row_groups, LANES), owner_slot.reshape(1, rows)),
+            out_specs=[VMEM, VMEM, SMEM],
+        )
+        masked, mass_inv, block_of = call(
+            functools.partial(mask_weights, capacity), [SMEM, SMEM, VMEM],
+            [
+                arrays(flat_weights.shape, BF),
+                arrays((targets, block_size), F32),
+                arrays((targets * entries,), I32),
+            ],
+            [],
+            (entry_slot.T, entry_count, flat_weights),
+            out_specs=[VMEM, VMEM, SMEM],
         )
         payload = arrays((2 * usual + POS_ROWS, width), BF)
         outgoing = call(
-            project_rows, "project_rows", [SMEM] + [VMEM] * (4 + box_total),
+            project_rows, [SMEM, SMEM] + [VMEM] * (4 + box_total),
             [payload] * dom_total,
             [
                 pltpu.VMEM((box_total * capacity, width, block_size), BF),
                 pltpu.VMEM((width, rows), BF),
                 pltpu.VMEM((row_groups, LANES, width), BF),
             ],
-            (table, masked, mass_inv, sorter, positions, *received),
+            (table, block_of, masked, mass_inv, sorter, positions, *received),
         )
         far = dom_total // 2
-        order = [*range(far, dom_total), *range(2, far), 1]
         payloads = {0: outgoing[0]}
-        for k in order:
-            payloads[k] = lax.ppermute(
-                outgoing[k], "dom", [(i, i ^ k) for i in range(dom_total)]
-            )
+        for k in range(1, dom_total):
+            payloads[k] = lax.ppermute(outgoing[k], "dom", [(i, i ^ k) for i in range(dom_total)])
         soon = [0, *range(1, far + 1)]
         late = [payloads[k] for k in range(far + 1, dom_total)]
 
@@ -529,7 +498,7 @@
             ]
 
         early = call(
-            functools.partial(place_early, len(soon)), "place_early", [VMEM] * len(soon),
+            functools.partial(place_early, len(soon)), [VMEM] * len(soon),
             arrays((elements, width), F32), placing(len(soon)), [payloads[k] for k in soon],
         )
         placed, scratch = False, placing(len(late))
@@ -539,20 +508,18 @@
         placed, scratch = True, []
     export = arrays((3, shared_nodes.shape[1]), F32)
     arrived, local, *exports = call(
-        functools.partial(finish, placed, len(late)), "finish",
+        functools.partial(finish, placed, len(late)),
         [VMEM] * (len(late) + 8),
         [arrays((elements, width), BF), arrays((3, nodes // LANES, LANES), F32)] + [export] * 4,
         scratch,
         (*late, early, base, edge, connectivity, onehot, relaxing, readout.T, chosen),
     )
-    history = call(
-        relax, "relax", [VMEM] * 3, arrays((elements, width), BF), [], (arrived, drive, relaxing)
-    )
+    history = call(relax, [VMEM] * 3, arrays((elements, width), BF), [], (arrived, drive, relaxing))
     halo = [None] * 4
     for m, axis, first in ((3, "box", 1), (1, "dom", 1), (0, "dom", 0), (2, "box", 0)):
         halo[m] = lax.ppermute(exports[m], axis, swaps(axis, first))
     force = call(
-        add_shared, "add_shared", [VMEM] * (2 + len(halo)), arrays((3, nodes), F32), [],
+        add_shared, [VMEM] * (2 + len(halo)), arrays((3, nodes), F32), [],
         (local, inverse, *halo),
     )
     return history, force

time: 44.9 us -> 44.6 us (level)
  waiting for transfers between devices: 3.37 us -> 2.23 us
  Pallas kernels: 11.5 us -> 12 us
    ppermute x7, waiting for transfers between devices: 2.29 us -> 1.15 us  [body(): lax.ppermute(outgoing[k], 'dom', [(i, i ^ k) for i in range(dom_total)])]
    pallas_call x8 -> x9, Pallas kernels: 11.5 us -> 12 us  [call(): pl.pallas_call(kernel, out_shape=outs, in_specs=ins, out_specs=out_specs...]
  transfers between devices with their start and end apart: 14 -> 14, of which waited for: 2 -> 3; matrix products, arithmetic and copies ran while one was open for 0% -> 0% of each run, Pallas kernels for 16% -> 17%
where the time goes in v3:
time: 44.6 us; the launch traced here: 44.3 us
  starting transfers between devices  23.6 us (53%)
  Pallas kernels  12 us (27%)
  local copies, waits for them, and re-layouts  5.57 us (12%)
  waiting for transfers between devices  2.23 us (5%)
  between operations  0.85 us (2%)
    pallas_call x9, Pallas kernels, call(): pl.pallas_call(kernel, out_shape=outs, in_specs=ins, out_specs=out_specs...  12 us
    ppermute x4, starting transfers between devices, body(): halo[m] = lax.ppermute(exports[m], axis, swaps(axis, first))  11.8 us
    ppermute x7, starting transfers between devices, body(): lax.ppermute(outgoing[k], 'dom', [(i, i ^ k) for i in range(dom_total)])  9.37 us
    unnamed x28, local copies, waits for them, and re-layouts  5.57 us
    ppermute x3, starting transfers between devices, body(): lax.ppermute(packed[k], 'box', [(i, i ^ k) for i in range(box_total)])  2.45 us
    ppermute x7, waiting for transfers between devices, body(): lax.ppermute(outgoing[k], 'dom', [(i, i ^ k) for i in range(dom_total)])  1.15 us
    ppermute x4, waiting for transfers between devices, body(): halo[m] = lax.ppermute(exports[m], axis, swaps(axis, first))  1.08 us
  transfers between devices with their start and end apart: 14, of which 3 were waited for; matrix products, arithmetic and copies ran while one was open for 0% of the time, Pallas kernels for 17%

profile of v3, /device:TPU:5, one launch (start us, length us, event | category | flops | bytes accessed | tf_op | source)
XLA Modules:
  0.0 44.3 jit_solution(12778687574554845800)
XLA Ops:
  0.6 0.9 %copy-done.1 = bf16[8,128,128]{2,1,0:T(8,128)(2,1)S(1)} copy-done((bf16[8,128,128]{2,1,0:T(8,128)(2,1)S(1)}, bf16[8,128,128]{2,1,0:T(8,128)(2,1)}, u32[]{:S(2)}) %copy-start.1) | copy-done | bytes 262168
  1.6 0.7 %copy-done.12 = s32[8]{0:T(128)S(1)} copy-done((s32[8]{0:T(128)S(1)}, s32[8]{0:T(128)}, u32[]{:S(2)}) %copy-start.12) | copy-done | bytes 56
  2.2 0.6 %shard_map.151 = (bf16[4,128,128]{2,1,0:T(8,128)(2,1)S(1)}, bf16[4,128,128]{2,1,0:T(8,128)(2,1)S(1)}, bf16[4,128,128]{2,1,0:T(8,128)(2,1)S(1)}, bf16[4,128,128]{2,1,0:T(8,128)(2,1)S(1)}) custom-call(s32[8]{0:T(128)S(1)} %copy-done.12, bf16[8,128,128]{2,1,0:T(8,128)(2,1)S(1)} %copy-done.1), custom_call_target="tpu_custom_call" | custom-call | flops 1000 | bytes 100000 | tf_op jit(solution)/shard_map/pallas_call | solution.py:350
  2.9 0.7 %collective-permute-start = (bf16[4,128,128]{2,1,0:T(8,128)(2,1)S(1)}, bf16[4,128,128]{2,1,0:T(8,128)(2,1)S(1)}, u32[]{:S(2)}, u32[]{:S(2)}) collective-permute-start(bf16[4,128,128]{2,1,0:T(8,128)(2,1)S(1)} %get-tuple-element.38), channel_id=1, source_target_pairs={{0,1},{1,0},{2,3},{3,2},{4,5},{5,4},{6,7},{7,6},{8,9},{9,8},{10,11... | collective-permute-start | bytes 393224 | tf_op jit(solution)/shard_map/ppermute | solution.py:427
  3.6 1.2 %collective-permute-start.1 = (bf16[4,128,128]{2,1,0:T(8,128)(2,1)S(1)}, bf16[4,128,128]{2,1,0:T(8,128)(2,1)S(1)}, u32[]{:S(2)}, u32[]{:S(2)}) collective-permute-start(bf16[4,128,128]{2,1,0:T(8,128)(2,1)S(1)} %get-tuple-element.39), channel_id=1, source_target_pairs={{0,2},{1,3},{2,0},{3,1},{4,6},{5,7},{6,4},{7,5},{8,10},{9,11},{10,... | collective-permute-start | bytes 393224 | tf_op jit(solution)/shard_map/ppermute | solution.py:427
  4.8 0.5 %collective-permute-start.2 = (bf16[4,128,128]{2,1,0:T(8,128)(2,1)S(1)}, bf16[4,128,128]{2,1,0:T(8,128)(2,1)S(1)}, u32[]{:S(2)}, u32[]{:S(2)}) collective-permute-start(bf16[4,128,128]{2,1,0:T(8,128)(2,1)S(1)} %get-tuple-element.40), channel_id=1, source_target_pairs={{0,3},{1,2},{2,1},{3,0},{4,7},{5,6},{6,5},{7,4},{8,11},{9,10},{10,... | collective-permute-start | bytes 393224 | tf_op jit(solution)/shard_map/ppermute | solution.py:427
  5.3 0.7 %copy-done.7 = s32[1024]{0:T(1024)S(1)} copy-done((s32[1024]{0:T(1024)S(1)}, s32[1024]{0:T(1024)}, u32[]{:S(2)}) %copy-start.7) | copy-done | bytes 4120
  6.0 0.7 %copy-done.8 = s32[1024]{0:T(1024)S(1)} copy-done((s32[1024]{0:T(1024)S(1)}, s32[1024]{0:T(1024)}, u32[]{:S(2)}) %copy-start.8) | copy-done | bytes 4120
  6.7 1.6 %shard_map.149 = (bf16[1024,1024]{1,0:T(8,128)(2,1)S(1)}, bf16[8,16,128]{2,1,0:T(8,128)(2,1)S(1)}, s32[16]{0:T(128)S(1)}) custom-call(s32[8,128]{1,0:T(8,128)S(1)} %bitcast.14, s32[1,1024]{1,0:T(1,128)S(1)} %bitcast.15), custom_call_target="tpu_custom_call" | custom-call | flops 1000 | bytes 100000 | tf_op jit(solution)/shard_map/pallas_call | solution.py:350
  8.3 1.2 %copy-done = bf16[8,4,128,128]{3,2,1,0:T(8,128)(2,1)S(1)} copy-done((bf16[8,4,128,128]{3,2,1,0:T(8,128)(2,1)S(1)}, bf16[8,4,128,128]{3,2,1,0:T(8,128)(2,1)}, u32[]{:S(2)}) %copy-start) | copy-done | bytes 1048600
  9.6 0.7 %copy-done.9 = s32[8,4]{0,1:T(4,128)S(1)} copy-done((s32[8,4]{0,1:T(4,128)S(1)}, s32[8,4]{0,1:T(4,128)}, u32[]{:S(2)}) %copy-start.9) | copy-done | bytes 152
  10.2 0.7 %copy-done.13 = s32[8]{0:T(128)S(1)} copy-done((s32[8]{0:T(128)S(1)}, s32[8]{0:T(128)}, u32[]{:S(2)}) %copy-start.13) | copy-done | bytes 56
  10.9 1.4 %shard_map.150 = (bf16[8,512,128]{2,1,0:T(8,128)(2,1)S(1)}, f32[8,128]{1,0:T(8,128)S(1)}, s32[32]{0:T(128)S(1)}) custom-call(s32[4,8]{1,0:T(4,128)S(1)} %bitcast.16, s32[8]{0:T(128)S(1)} %copy-done.13, bf16[8,512,128]{2,1,0:T(8,128)(2,1)S(1)} %bitcast.8), custom_call_target="tpu_custom_call" | custom-call | flops 1000 | bytes 100000 | tf_op jit(solution)/shard_map/pallas_call | solution.py:350
  12.4 1.7 %shard_map.152 = (bf16[272,128]{1,0:T(8,128)(2,1)S(1)}, bf16[272,128]{1,0:T(8,128)(2,1)S(1)}, bf16[272,128]{1,0:T(8,128)(2,1)S(1)}, bf16[272,128]{1,0:T(8,128)(2...) custom-call(s32[16]{0:T(128)S(1)} %get-tuple-element.31.table, ...), custom_call_target="tpu_custom_call" | custom-call | flops 1000 | bytes 100000 | tf_op jit(solution)/shard_map/pallas_call | solution.py:350
  14.1 0.1 collective-permute-start.6
  14.2 1.5 %collective-permute-start.7 = (bf16[272,128]{1,0:T(8,128)(2,1)S(1)}, bf16[272,128]{1,0:T(8,128)(2,1)S(1)}, u32[]{:S(2)}, u32[]{:S(2)}) collective-permute-start(bf16[272,128]{1,0:T(8,128)(2,1)S(1)} %get-tuple-element.46), channel_id=1, source_target_pairs={{0,8},{4,12},{8,0},{12,4},{16,24},{20,28},{24,16},{28,20},{1,9},{5... | collective-permute-start | bytes 208904 | tf_op jit(solution)/shard_map/ppermute | solution.py:490
  15.7 3.3 %collective-permute-start.3 = (bf16[272,128]{1,0:T(8,128)(2,1)S(1)}, bf16[272,128]{1,0:T(8,128)(2,1)S(1)}, u32[]{:S(2)}, u32[]{:S(2)}) collective-permute-start(bf16[272,128]{1,0:T(8,128)(2,1)S(1)} %get-tuple-element.41), channel_id=1, source_target_pairs={{0,20},{4,16},{8,28},{12,24},{16,4},{20,0},{24,12},{28,8},{1,21},{... | collective-permute-start | bytes 208904 | tf_op jit(solution)/shard_map/ppermute | solution.py:490
  19.0 0.1 collective-permute-start.8
  19.2 3.3 %collective-permute-start.4 = (bf16[272,128]{1,0:T(8,128)(2,1)S(1)}, bf16[272,128]{1,0:T(8,128)(2,1)S(1)}, u32[]{:S(2)}, u32[]{:S(2)}) collective-permute-start(bf16[272,128]{1,0:T(8,128)(2,1)S(1)} %get-tuple-element.42), channel_id=1, source_target_pairs={{0,24},{4,28},{8,16},{12,20},{16,8},{20,12},{24,0},{28,4},{1,25},{... | collective-permute-start | bytes 208904 | tf_op jit(solution)/shard_map/ppermute | solution.py:490
  22.5 1.0 %collective-permute-start.5 = (bf16[272,128]{1,0:T(8,128)(2,1)S(1)}, bf16[272,128]{1,0:T(8,128)(2,1)S(1)}, u32[]{:S(2)}, u32[]{:S(2)}) collective-permute-start(bf16[272,128]{1,0:T(8,128)(2,1)S(1)} %get-tuple-element.43), channel_id=1, source_target_pairs={{0,28},{4,24},{8,20},{12,16},{16,12},{20,8},{24,4},{28,0},{1,29},{... | collective-permute-start | bytes 208904 | tf_op jit(solution)/shard_map/ppermute | solution.py:490
  23.5 2.8 %shard_map.154 = (f32[1024,128]{1,0:T(8,128)S(1)}, f32[8,1024]{1,0:T(8,128)S(1)}, bf16[8,1024,128]{2,1,0:T(8,128)(2,1)S(1)}, s32[8,128]{1,0:T(8,128)S(1)}, s32[2,8,128]{2,1,0:T(8,128)S(1)}) custom-call(s32[8,1024]{1,0:T(8,128)S(1)} %copy-done.2, f32[3,1024]{1,0:T(4,128)S(1)} %copy-done.5, f32[1,1024]{1,0:T(1,128)S(1)} %bitcast.9, f32[6,128]{1,0:T(8,128)S(1)} %bitcast.13, ...), custom_call_target="tpu_custom_call" | custom-call | flops 1000 | bytes 100000 | tf_op jit(solution)/shard_map/pallas_call | solution.py:350
  26.3 0.7 %collective-permute-done.9.refs_4_ = bf16[272,128]{1,0:T(8,128)(2,1)S(1)} collective-permute-done((bf16[272,128]{1,0:T(8,128)(2,1)S(1)}, bf16[272,128]{1,0:T(8,128)(2,1)S(1)}, u32[]{:S(2)}, u32[]{:S(2)}) %collective-permute-start.9) | collective-permute-done | bytes 69664 | tf_op jit(solution)/shard_map/ppermute | solution.py:490
  27.0 0.9 %shard_map.153.refs_3_ = f32[1024,128]{1,0:T(8,128)S(1)} custom-call(bf16[272,128]{1,0:T(8,128)(2,1)S(1)} %get-tuple-element.44.refs_0_, bf16[272,128]{1,0:T(8,128)(2,1)S(1)} %collective-permute-done.6.refs_1_, bf16[272,128]{1,0:T(8,128)(2,1)S(1)} %collective-permute-done.7.refs_2_, bf16[272,128]{1,0:T(8,128)(2,1)S(1)} %collective-permute-done.8.refs_3_, ...), custom_call_target="tpu_custom_call" | custom-call | flops 1000 | bytes 100000 | tf_op jit(solution)/shard_map/pallas_call | solution.py:350
  27.9 0.4 collective-permute-done.5.refs_2_
  28.4 1.5 %shard_map.155 = (bf16[1024,128]{1,0:T(8,128)(2,1)S(1)}, f32[3,8,128]{2,1,0:T(8,128)S(1)}, f32[3,128]{1,0:T(4,128)S(1)}, f32[3,128]{1,0:T(4,128)S(1)}, f32[3,128]{1,0:T(4,128)S(1)}, /*index=5*/f32[3,128]{1,0:T(4,128)S(1)}) custom-call(bf16[272,128]{1,0:T(8,128)(2,1)S(1)} %collective-permute-done.3.refs_0_, ...), custom_call_target="tpu_custom_call" | custom-call | flops 1000 | bytes 100000 | tf_op jit(solution)/shard_map/pallas_call | solution.py:350
  29.9 1.4 %collective-permute-start.10 = (f32[3,128]{1,0:T(4,128)S(1)}, f32[3,128]{1,0:T(4,128)S(1)}, u32[]{:S(2)}, u32[]{:S(2)}) collective-permute-start(f32[3,128]{1,0:T(4,128)S(1)} %get-tuple-element.56), channel_id=1, source_target_pairs={{0,4},{4,0},{8,12},{12,8},{16,20},{20,16},{24,28},{28,24},{1,5},{5... | collective-permute-start | bytes 4616 | tf_op jit(solution)/shard_map/ppermute | solution.py:520
  31.3 5.0 %collective-permute-start.11 = (f32[3,128]{1,0:T(4,128)S(1)}, f32[3,128]{1,0:T(4,128)S(1)}, u32[]{:S(2)}, u32[]{:S(2)}) collective-permute-start(f32[3,128]{1,0:T(4,128)S(1)} %get-tuple-element.57), channel_id=1, source_target_pairs={{4,8},{8,4},{12,16},{16,12},{20,24},{24,20},{5,9},{9,5},{13,17},{1... | collective-permute-start | bytes 4616 | tf_op jit(solution)/shard_map/ppermute | solution.py:520
  36.3 2.3 %collective-permute-start.12 = (f32[3,128]{1,0:T(4,128)S(1)}, f32[3,128]{1,0:T(4,128)S(1)}, u32[]{:S(2)}, u32[]{:S(2)}) collective-permute-start(f32[3,128]{1,0:T(4,128)S(1)} %get-tuple-element.58), channel_id=1, source_target_pairs={{0,1},{1,0},{2,3},{3,2},{4,5},{5,4},{6,7},{7,6},{8,9},{9,8},{10,11... | collective-permute-start | bytes 4616 | tf_op jit(solution)/shard_map/ppermute | solution.py:520
  38.7 3.0 %collective-permute-start.13 = (f32[3,128]{1,0:T(4,128)S(1)}, f32[3,128]{1,0:T(4,128)S(1)}, u32[]{:S(2)}, u32[]{:S(2)}) collective-permute-start(f32[3,128]{1,0:T(4,128)S(1)} %get-tuple-element.59), channel_id=1, source_target_pairs={{1,2},{2,1},{5,6},{6,5},{9,10},{10,9},{13,14},{14,13},{17,18},{18,... | collective-permute-start | bytes 4616 | tf_op jit(solution)/shard_map/ppermute | solution.py:520
  41.7 0.8 %shard_map.156 = bf16[1024,128]{1,0:T(8,128)(2,1)} custom-call(bf16[1024,128]{1,0:T(8,128)(2,1)S(1)} %get-tuple-element.52.arrived, f32[1024,128]{1,0:T(8,128)S(1)} %get-tuple-element.53.drive, f32[1,128]{1,0:T(1,128)S(1)} %bitcast.18), custom_call_target="tpu_custom_call" | custom-call | flops 1000 | bytes 100000 | tf_op jit(solution)/shard_map/pallas_call | solution.py:350
  42.5 1.1 %collective-permute-done.13.rest_3_ = f32[3,128]{1,0:T(4,128)S(1)} collective-permute-done((f32[3,128]{1,0:T(4,128)S(1)}, f32[3,128]{1,0:T(4,128)S(1)}, u32[]{:S(2)}, u32[]{:S(2)}) %collective-permute-start.13) | collective-permute-done | bytes 1568 | tf_op jit(solution)/shard_map/ppermute | solution.py:520
  43.6 0.7 %shard_map.157 = f32[3,1024]{1,0:T(4,128)} custom-call(f32[3,8,128]{2,1,0:T(8,128)S(1)} %get-tuple-element.54.local, s32[2,8,128]{2,1,0:T(8,128)S(1)} %get-tuple-element.55.inverse, f32[3,128]{1,0:T(4,128)S(1)} %collective-permute-done.10.rest_0_, f32[3,128]{1,0:T(4,128)S(1)} %collective-permute-done.11.rest_1_, ...), custom_call_target="tpu_custom_call" | custom-call | flops 1000 | bytes 100000 | tf_op jit(solution)/shard_map/pallas_call | solution.py:350
  (33 shorter events, 0.1 us)
Async XLA Ops:
  0.6 1.0 %copy-start.1 = (bf16[8,128,128]{2,1,0:T(8,128)(2,1)S(1)}, bf16[8,128,128]{2,1,0:T(8,128)(2,1)}, u32[]{:S(2)}) copy-start(bf16[8,128,128]{2,1,0:T(8,128)(2,1)} %old.1) | copy-start | bytes 786436
  1.6 0.7 %copy-start.12 = (s32[8]{0:T(128)S(1)}, s32[8]{0:T(128)}, u32[]{:S(2)}) copy-start(s32[8]{0:T(128)} %route.1) | copy-start | bytes 100
  2.9 9.5 %collective-permute-start = (bf16[4,128,128]{2,1,0:T(8,128)(2,1)S(1)}, bf16[4,128,128]{2,1,0:T(8,128)(2,1)S(1)}, u32[]{:S(2)}, u32[]{:S(2)}) collective-permute-start(bf16[4,128,128]{2,1,0:T(8,128)(2,1)S(1)} %get-tuple-element.38), channel_id=1, source_target_pairs={{0,1},{1,0},{2,3},{3,2},{4,5},{5,4},{6,7},{7,6},{8,9},{9,8},{10,11... | collective-permute-start | bytes 393224 | tf_op jit(solution)/shard_map/ppermute | solution.py:427
  3.6 8.8 %collective-permute-start.1 = (bf16[4,128,128]{2,1,0:T(8,128)(2,1)S(1)}, bf16[4,128,128]{2,1,0:T(8,128)(2,1)S(1)}, u32[]{:S(2)}, u32[]{:S(2)}) collective-permute-start(bf16[4,128,128]{2,1,0:T(8,128)(2,1)S(1)} %get-tuple-element.39), channel_id=1, source_target_pairs={{0,2},{1,3},{2,0},{3,1},{4,6},{5,7},{6,4},{7,5},{8,10},{9,11},{10,... | collective-permute-start | bytes 393224 | tf_op jit(solution)/shard_map/ppermute | solution.py:427
  4.8 7.6 %collective-permute-start.2 = (bf16[4,128,128]{2,1,0:T(8,128)(2,1)S(1)}, bf16[4,128,128]{2,1,0:T(8,128)(2,1)S(1)}, u32[]{:S(2)}, u32[]{:S(2)}) collective-permute-start(bf16[4,128,128]{2,1,0:T(8,128)(2,1)S(1)} %get-tuple-element.40), channel_id=1, source_target_pairs={{0,3},{1,2},{2,1},{3,0},{4,7},{5,6},{6,5},{7,4},{8,11},{9,10},{10,... | collective-permute-start | bytes 393224 | tf_op jit(solution)/shard_map/ppermute | solution.py:427
  5.3 0.7 %copy-start.7 = (s32[1024]{0:T(1024)S(1)}, s32[1024]{0:T(1024)}, u32[]{:S(2)}) copy-start(s32[1024]{0:T(1024)} %param.19) | copy-start | bytes 12292
  6.0 0.7 %copy-start.8 = (s32[1024]{0:T(1024)S(1)}, s32[1024]{0:T(1024)}, u32[]{:S(2)}) copy-start(s32[1024]{0:T(1024)} %param.20) | copy-start | bytes 12292
  8.3 1.2 %copy-start = (bf16[8,4,128,128]{3,2,1,0:T(8,128)(2,1)S(1)}, bf16[8,4,128,128]{3,2,1,0:T(8,128)(2,1)}, u32[]{:S(2)}) copy-start(bf16[8,4,128,128]{3,2,1,0:T(8,128)(2,1)} %param.18) | copy-start | bytes 3145732
  9.6 0.7 %copy-start.9 = (s32[8,4]{0,1:T(4,128)S(1)}, s32[8,4]{0,1:T(4,128)}, u32[]{:S(2)}) copy-start(s32[8,4]{0,1:T(4,128)} %param.16) | copy-start | bytes 388
  10.2 0.7 %copy-start.13 = (s32[8]{0:T(128)S(1)}, s32[8]{0:T(128)}, u32[]{:S(2)}) copy-start(s32[8]{0:T(128)} %count.1) | copy-start | bytes 100
  12.3 11.2 %copy-start.2 = (s32[8,1024]{1,0:T(8,128)S(1)}, s32[8,1024]{1,0:T(8,128)}, u32[]{:S(2)}) copy-start(s32[8,1024]{1,0:T(8,128)} %refs_6_.1) | copy-start | bytes 98308
  12.3 11.2 %copy-start.3 = (f32[1024]{0:T(1024)S(1)}, f32[1024]{0:T(1024)}, u32[]{:S(2)}) copy-start(f32[1024]{0:T(1024)} %param.24) | copy-start | bytes 12292
  12.3 11.2 %copy-start.4 = (f32[128,6]{0,1:T(8,128)S(1)}, f32[128,6]{0,1:T(8,128)}, u32[]{:S(2)}) copy-start(f32[128,6]{0,1:T(8,128)} %param.27) | copy-start | bytes 9220
  12.4 11.2 %copy-start.5 = (f32[3,1024]{1,0:T(4,128)S(1)}, f32[3,1024]{1,0:T(4,128)}, u32[]{:S(2)}) copy-start(f32[3,1024]{1,0:T(4,128)} %motion.1) | copy-start | bytes 36868
  12.4 11.2 %copy-start.6 = (f32[128,6]{0,1:T(8,128)S(1)}, f32[128,6]{0,1:T(8,128)}, u32[]{:S(2)}) copy-start(f32[128,6]{0,1:T(8,128)} %param.26) | copy-start | bytes 9220
  12.4 11.2 %copy-start.11 = (s32[4,128]{1,0:T(4,128)S(1)}, s32[4,128]{1,0:T(4,128)}, u32[]{:S(2)}) copy-start(s32[4,128]{1,0:T(4,128)} %shared.1) | copy-start | bytes 6148
  12.4 15.9 %copy-start.10 = (f32[128]{0:T(128)S(1)}, f32[128]{0:T(128)}, u32[]{:S(2)}) copy-start(f32[128]{0:T(128)} %param.25) | copy-start | bytes 1540
  14.1 5.0 %collective-permute-start.6 = (bf16[272,128]{1,0:T(8,128)(2,1)S(1)}, bf16[272,128]{1,0:T(8,128)(2,1)S(1)}, u32[]{:S(2)}, u32[]{:S(2)}) collective-permute-start(bf16[272,128]{1,0:T(8,128)(2,1)S(1)} %get-tuple-element.45), channel_id=1, source_target_pairs={{0,4},{4,0},{8,12},{12,8},{16,20},{20,16},{24,28},{28,24},{1,5},{5... | collective-permute-start | bytes 208904 | tf_op jit(solution)/shard_map/ppermute | solution.py:490
  14.2 8.3 %collective-permute-start.7 = (bf16[272,128]{1,0:T(8,128)(2,1)S(1)}, bf16[272,128]{1,0:T(8,128)(2,1)S(1)}, u32[]{:S(2)}, u32[]{:S(2)}) collective-permute-start(bf16[272,128]{1,0:T(8,128)(2,1)S(1)} %get-tuple-element.46), channel_id=1, source_target_pairs={{0,8},{4,12},{8,0},{12,4},{16,24},{20,28},{24,16},{28,20},{1,9},{5... | collective-permute-start | bytes 208904 | tf_op jit(solution)/shard_map/ppermute | solution.py:490
  15.7 12.2 %collective-permute-start.3 = (bf16[272,128]{1,0:T(8,128)(2,1)S(1)}, bf16[272,128]{1,0:T(8,128)(2,1)S(1)}, u32[]{:S(2)}, u32[]{:S(2)}) collective-permute-start(bf16[272,128]{1,0:T(8,128)(2,1)S(1)} %get-tuple-element.41), channel_id=1, source_target_pairs={{0,20},{4,16},{8,28},{12,24},{16,4},{20,0},{24,12},{28,8},{1,21},{... | collective-permute-start | bytes 208904 | tf_op jit(solution)/shard_map/ppermute | solution.py:490
  19.0 7.3 %collective-permute-start.8 = (bf16[272,128]{1,0:T(8,128)(2,1)S(1)}, bf16[272,128]{1,0:T(8,128)(2,1)S(1)}, u32[]{:S(2)}, u32[]{:S(2)}) collective-permute-start(bf16[272,128]{1,0:T(8,128)(2,1)S(1)} %get-tuple-element.47), channel_id=1, source_target_pairs={{0,12},{4,8},{8,4},{12,0},{16,28},{20,24},{24,20},{28,16},{1,13},{... | collective-permute-start | bytes 208904 | tf_op jit(solution)/shard_map/ppermute | solution.py:490
  19.1 7.9 %collective-permute-start.9 = (bf16[272,128]{1,0:T(8,128)(2,1)S(1)}, bf16[272,128]{1,0:T(8,128)(2,1)S(1)}, u32[]{:S(2)}, u32[]{:S(2)}) collective-permute-start(bf16[272,128]{1,0:T(8,128)(2,1)S(1)} %get-tuple-element.48), channel_id=1, source_target_pairs={{0,16},{4,20},{8,24},{12,28},{16,0},{20,4},{24,8},{28,12},{1,17},{... | collective-permute-start | bytes 208904 | tf_op jit(solution)/shard_map/ppermute | solution.py:490
  19.2 8.8 %collective-permute-start.4 = (bf16[272,128]{1,0:T(8,128)(2,1)S(1)}, bf16[272,128]{1,0:T(8,128)(2,1)S(1)}, u32[]{:S(2)}, u32[]{:S(2)}) collective-permute-start(bf16[272,128]{1,0:T(8,128)(2,1)S(1)} %get-tuple-element.42), channel_id=1, source_target_pairs={{0,24},{4,28},{8,16},{12,20},{16,8},{20,12},{24,0},{28,4},{1,25},{... | collective-permute-start | bytes 208904 | tf_op jit(solution)/shard_map/ppermute | solution.py:490
  22.5 5.9 %collective-permute-start.5 = (bf16[272,128]{1,0:T(8,128)(2,1)S(1)}, bf16[272,128]{1,0:T(8,128)(2,1)S(1)}, u32[]{:S(2)}, u32[]{:S(2)}) collective-permute-start(bf16[272,128]{1,0:T(8,128)(2,1)S(1)} %get-tuple-element.43), channel_id=1, source_target_pairs={{0,28},{4,24},{8,20},{12,16},{16,12},{20,8},{24,4},{28,0},{1,29},{... | collective-permute-start | bytes 208904 | tf_op jit(solution)/shard_map/ppermute | solution.py:490
  29.9 12.6 %collective-permute-start.10 = (f32[3,128]{1,0:T(4,128)S(1)}, f32[3,128]{1,0:T(4,128)S(1)}, u32[]{:S(2)}, u32[]{:S(2)}) collective-permute-start(f32[3,128]{1,0:T(4,128)S(1)} %get-tuple-element.56), channel_id=1, source_target_pairs={{0,4},{4,0},{8,12},{12,8},{16,20},{20,16},{24,28},{28,24},{1,5},{5... | collective-permute-start | bytes 4616 | tf_op jit(solution)/shard_map/ppermute | solution.py:520
  31.3 11.2 %collective-permute-start.11 = (f32[3,128]{1,0:T(4,128)S(1)}, f32[3,128]{1,0:T(4,128)S(1)}, u32[]{:S(2)}, u32[]{:S(2)}) collective-permute-start(f32[3,128]{1,0:T(4,128)S(1)} %get-tuple-element.57), channel_id=1, source_target_pairs={{4,8},{8,4},{12,16},{16,12},{20,24},{24,20},{5,9},{9,5},{13,17},{1... | collective-permute-start | bytes 4616 | tf_op jit(solution)/shard_map/ppermute | solution.py:520
  36.3 6.2 %collective-permute-start.12 = (f32[3,128]{1,0:T(4,128)S(1)}, f32[3,128]{1,0:T(4,128)S(1)}, u32[]{:S(2)}, u32[]{:S(2)}) collective-permute-start(f32[3,128]{1,0:T(4,128)S(1)} %get-tuple-element.58), channel_id=1, source_target_pairs={{0,1},{1,0},{2,3},{3,2},{4,5},{5,4},{6,7},{7,6},{8,9},{9,8},{10,11... | collective-permute-start | bytes 4616 | tf_op jit(solution)/shard_map/ppermute | solution.py:520
  38.7 4.9 %collective-permute-start.13 = (f32[3,128]{1,0:T(4,128)S(1)}, f32[3,128]{1,0:T(4,128)S(1)}, u32[]{:S(2)}, u32[]{:S(2)}) collective-permute-start(f32[3,128]{1,0:T(4,128)S(1)} %get-tuple-element.59), channel_id=1, source_target_pairs={{1,2},{2,1},{5,6},{6,5},{9,10},{10,9},{13,14},{14,13},{17,18},{18,... | collective-permute-start | bytes 4616 | tf_op jit(solution)/shard_map/ppermute | solution.py:520

commit v4 on v3

--- a/solution.py
+++ b/solution.py
@@ -203,7 +203,11 @@
     lane = iota((groups, LANES), 1)
     total = jnp.zeros((2 * groups, LANES), F32)
     for m in range(4):
-        nodes = chosen[m : m + 1]
+        axis = "dom" if m < 2 else "box"
+        here = lax.axis_index(axis)
+        partner = here + (1 - 2 * (here & 1)) * (1 if m % 2 == 0 else -1)
+        paired = (partner >= 0) & (partner < lax.axis_size(axis))
+        nodes = jnp.where(paired, chosen[m : m + 1], groups * LANES)
         here = group == (nodes >> 7)
         marks = jnp.concatenate(
             [jnp.where(here, m + 1, 0), jnp.where(here, lane, 0)], axis=0
@@ -345,7 +349,7 @@
 SMEM = pl.BlockSpec(memory_space=pltpu.SMEM)
 
 
-def call(kernel, ins, outs, scratch, args, cost=100_000, out_specs=None):
+def call(kernel, ins, outs, scratch, args, cost=2_000_000_000, out_specs=None):
     single = not isinstance(outs, (list, tuple))
     return pl.pallas_call(
         kernel,
@@ -353,17 +357,17 @@
         in_specs=ins,
         out_specs=out_specs or (VMEM if single else [VMEM] * len(outs)),
         scratch_shapes=scratch,
-        cost_estimate=pl.CostEstimate(flops=1000, bytes_accessed=cost, transcendentals=0),
+        cost_estimate=pl.CostEstimate(flops=cost, bytes_accessed=100_000, transcendentals=0),
         compiler_params=pltpu.CompilerParams(vmem_limit_bytes=24 * 1024 * 1024),
     )(*args)
 
 
 def swaps(axis, first):
     total = lax.axis_size(axis)
-    pairs = []
-    for i in range(first, total - 1, 2):
-        pairs += [(i, i + 1), (i + 1, i)]
-    return pairs
+    pairs = [(i, i + 1) for i in range(first, total - 1, 2)]
+    left = sorted(set(range(total)) - {i for pair in pairs for i in pair})
+    pairs += [(left[0], left[-1])] if left else []
+    return [(a, b) for a, b in pairs] + [(b, a) for a, b in pairs if a != b]
 
 
 def arrays(shape, dtype):
@@ -488,8 +492,8 @@
         payloads = {0: outgoing[0]}
         for k in range(1, dom_total):
             payloads[k] = lax.ppermute(outgoing[k], "dom", [(i, i ^ k) for i in range(dom_total)])
-        soon = [0, *range(1, far + 1)]
-        late = [payloads[k] for k in range(far + 1, dom_total)]
+        soon = [0, *range(dom_total - 1, far - 1, -1)]
+        late = [payloads[k] for k in range(far - 1, 0, -1)]
 
         def placing(count):
             return [

time: 44.6 us -> 43.6 us (0.978)
  the two profiles are of different devices: /device:TPU:5 before, /device:TPU:1 now
where the time goes in v4:
time: 43.6 us; the launch traced here: 43.4 us
  starting transfers between devices  19.5 us (45%)
  Pallas kernels  12 us (28%)
  waiting for transfers between devices  9.54 us (22%)
  local copies, waits for them, and re-layouts  1.65 us (4%)
  between operations  0.8 us (2%)
    pallas_call x9, Pallas kernels, call(): pl.pallas_call(kernel, out_shape=outs, in_specs=ins, out_specs=out_specs...  12 us
    ppermute x7, starting transfers between devices, body(): lax.ppermute(outgoing[k], 'dom', [(i, i ^ k) for i in range(dom_total)])  9.68 us
    ppermute x4, starting transfers between devices, body(): halo[m] = lax.ppermute(exports[m], axis, swaps(axis, first))  6.97 us
    ppermute x7, waiting for transfers between devices, body(): lax.ppermute(outgoing[k], 'dom', [(i, i ^ k) for i in range(dom_total)])  4.98 us
    ppermute x3, waiting for transfers between devices, body(): lax.ppermute(packed[k], 'box', [(i, i ^ k) for i in range(box_total)])  3.43 us
    ppermute x3, starting transfers between devices, body(): lax.ppermute(packed[k], 'box', [(i, i ^ k) for i in range(box_total)])  2.81 us
    unnamed x28, local copies, waits for them, and re-layouts  1.65 us
    ppermute x4, waiting for transfers between devices, body(): halo[m] = lax.ppermute(exports[m], axis, swaps(axis, first))  1.13 us
  transfers between devices with their start and end apart: 14, of which 6 were waited for; matrix products, arithmetic and copies ran while one was open for 0% of the time, Pallas kernels for 17%

profile of v4, /device:TPU:1, one launch (start us, length us, event | category | flops | bytes accessed | tf_op | source)
XLA Modules:
  0.0 43.4 jit_solution(1130793989045818847)
XLA Ops:
  0.6 0.9 %copy-done.1 = bf16[8,128,128]{2,1,0:T(8,128)(2,1)S(1)} copy-done((bf16[8,128,128]{2,1,0:T(8,128)(2,1)S(1)}, bf16[8,128,128]{2,1,0:T(8,128)(2,1)}, u32[]{:S(2)}) %copy-start.1) | copy-done | bytes 262168
  1.6 0.7 %copy-done.11 = s32[8]{0:T(128)S(1)} copy-done((s32[8]{0:T(128)S(1)}, s32[8]{0:T(128)}, u32[]{:S(2)}) %copy-start.11) | copy-done | bytes 56
  2.2 0.6 %shard_map.151 = (bf16[4,128,128]{2,1,0:T(8,128)(2,1)S(1)}, bf16[4,128,128]{2,1,0:T(8,128)(2,1)S(1)}, bf16[4,128,128]{2,1,0:T(8,128)(2,1)S(1)}, bf16[4,128,128]{2,1,0:T(8,128)(2,1)S(1)}) custom-call(s32[8]{0:T(128)S(1)} %copy-done.11, bf16[8,128,128]{2,1,0:T(8,128)(2,1)S(1)} %copy-done.1), custom_call_target="tpu_custom_call" | custom-call | flops 2000000000 | bytes 100000 | tf_op jit(solution)/shard_map/pallas_call | solution.py:354
  2.9 0.1 collective-permute-start
  3.0 2.7 %collective-permute-start.1 = (bf16[4,128,128]{2,1,0:T(8,128)(2,1)S(1)}, bf16[4,128,128]{2,1,0:T(8,128)(2,1)S(1)}, u32[]{:S(2)}, u32[]{:S(2)}) collective-permute-start(bf16[4,128,128]{2,1,0:T(8,128)(2,1)S(1)} %get-tuple-element.39), channel_id=1, source_target_pairs={{0,2},{1,3},{2,0},{3,1},{4,6},{5,7},{6,4},{7,5},{8,10},{9,11},{10,... | collective-permute-start | bytes 393224 | tf_op jit(solution)/shard_map/ppermute | solution.py:431
  5.6 0.0 collective-permute-start.2
  5.7 0.0 copy-start.12
  5.7 1.6 %shard_map.149 = (bf16[1024,1024]{1,0:T(8,128)(2,1)S(1)}, bf16[8,16,128]{2,1,0:T(8,128)(2,1)S(1)}, s32[16]{0:T(128)S(1)}) custom-call(s32[8,128]{1,0:T(8,128)S(1)} %bitcast.9, s32[1,1024]{1,0:T(1,128)S(1)} %bitcast.10), custom_call_target="tpu_custom_call" | custom-call | flops 2000000000 | bytes 100000 | tf_op jit(solution)/shard_map/pallas_call | solution.py:354
  7.4 1.4 %shard_map.150 = (bf16[8,512,128]{2,1,0:T(8,128)(2,1)S(1)}, f32[8,128]{1,0:T(8,128)S(1)}, s32[32]{0:T(128)S(1)}) custom-call(s32[4,8]{1,0:T(4,128)S(1)} %bitcast.16, s32[8]{0:T(128)S(1)} %copy-done.12, bf16[8,512,128]{2,1,0:T(8,128)(2,1)S(1)} %bitcast.8), custom_call_target="tpu_custom_call" | custom-call | flops 2000000000 | bytes 100000 | tf_op jit(solution)/shard_map/pallas_call | solution.py:354
  8.8 0.6 %collective-permute-done.1.rest_2_ = bf16[4,128,128]{2,1,0:T(8,128)(2,1)S(1)} collective-permute-done((bf16[4,128,128]{2,1,0:T(8,128)(2,1)S(1)}, bf16[4,128,128]{2,1,0:T(8,128)(2,1)S(1)}, u32[]{:S(2)}, u32[]{:S(2)}) %collective-permute-start.1) | collective-permute-done | bytes 131104 | tf_op jit(solution)/shard_map/ppermute | solution.py:431
  9.4 2.8 %collective-permute-done.2.rest_3_ = bf16[4,128,128]{2,1,0:T(8,128)(2,1)S(1)} collective-permute-done((bf16[4,128,128]{2,1,0:T(8,128)(2,1)S(1)}, bf16[4,128,128]{2,1,0:T(8,128)(2,1)S(1)}, u32[]{:S(2)}, u32[]{:S(2)}) %collective-permute-start.2) | collective-permute-done | bytes 131104 | tf_op jit(solution)/shard_map/ppermute | solution.py:431
  12.3 0.0 copy-start.10
  12.3 1.7 %shard_map.152 = (bf16[272,128]{1,0:T(8,128)(2,1)S(1)}, bf16[272,128]{1,0:T(8,128)(2,1)S(1)}, bf16[272,128]{1,0:T(8,128)(2,1)S(1)}, bf16[272,128]{1,0:T(8,128)(2...) custom-call(s32[16]{0:T(128)S(1)} %get-tuple-element.31.table, ...), custom_call_target="tpu_custom_call" | custom-call | flops 2000000000 | bytes 100000 | tf_op jit(solution)/shard_map/pallas_call | solution.py:354
  14.0 4.6 %collective-permute-start.6 = (bf16[272,128]{1,0:T(8,128)(2,1)S(1)}, bf16[272,128]{1,0:T(8,128)(2,1)S(1)}, u32[]{:S(2)}, u32[]{:S(2)}) collective-permute-start(bf16[272,128]{1,0:T(8,128)(2,1)S(1)} %get-tuple-element.45), channel_id=1, source_target_pairs={{0,28},{4,24},{8,20},{12,16},{16,12},{20,8},{24,4},{28,0},{1,29},{... | collective-permute-start | bytes 208904 | tf_op jit(solution)/shard_map/ppermute | solution.py:494
  18.5 0.4 collective-permute-start.8
  18.9 2.1 %collective-permute-start.9 = (bf16[272,128]{1,0:T(8,128)(2,1)S(1)}, bf16[272,128]{1,0:T(8,128)(2,1)S(1)}, u32[]{:S(2)}, u32[]{:S(2)}) collective-permute-start(bf16[272,128]{1,0:T(8,128)(2,1)S(1)} %get-tuple-element.48), channel_id=1, source_target_pairs={{0,16},{4,20},{8,24},{12,28},{16,0},{20,4},{24,8},{28,12},{1,17},{... | collective-permute-start | bytes 208904 | tf_op jit(solution)/shard_map/ppermute | solution.py:494
  21.0 2.8 %shard_map.154 = (f32[1024,128]{1,0:T(8,128)S(1)}, f32[8,1024]{1,0:T(8,128)S(1)}, bf16[8,1024,128]{2,1,0:T(8,128)(2,1)S(1)}, s32[8,128]{1,0:T(8,128)S(1)}, s32[2,8,128]{2,1,0:T(8,128)S(1)}) custom-call(s32[8,1024]{1,0:T(8,128)S(1)} %copy-done.2, f32[3,1024]{1,0:T(4,128)S(1)} %copy-done.3, f32[1,1024]{1,0:T(1,128)S(1)} %bitcast.12, f32[6,128]{1,0:T(8,128)S(1)} %bitcast.11, ...), custom_call_target="tpu_custom_call" | custom-call | flops 2000000000 | bytes 100000 | tf_op jit(solution)/shard_map/pallas_call | solution.py:354
  23.8 2.0 %collective-permute-start.3 = (bf16[272,128]{1,0:T(8,128)(2,1)S(1)}, bf16[272,128]{1,0:T(8,128)(2,1)S(1)}, u32[]{:S(2)}, u32[]{:S(2)}) collective-permute-start(bf16[272,128]{1,0:T(8,128)(2,1)S(1)} %get-tuple-element.41), channel_id=1, source_target_pairs={{0,12},{4,8},{8,4},{12,0},{16,28},{20,24},{24,20},{28,16},{1,13},{... | collective-permute-start | bytes 208904 | tf_op jit(solution)/shard_map/ppermute | solution.py:494
  25.8 0.3 collective-permute-start.4
  26.1 0.4 collective-permute-start.5
  26.5 2.5 %collective-permute-done.8.refs_3_ = bf16[272,128]{1,0:T(8,128)(2,1)S(1)} collective-permute-done((bf16[272,128]{1,0:T(8,128)(2,1)S(1)}, bf16[272,128]{1,0:T(8,128)(2,1)S(1)}, u32[]{:S(2)}, u32[]{:S(2)}) %collective-permute-start.8) | collective-permute-done | bytes 69664 | tf_op jit(solution)/shard_map/ppermute | solution.py:494
  29.0 1.3 %collective-permute-done.9.refs_4_ = bf16[272,128]{1,0:T(8,128)(2,1)S(1)} collective-permute-done((bf16[272,128]{1,0:T(8,128)(2,1)S(1)}, bf16[272,128]{1,0:T(8,128)(2,1)S(1)}, u32[]{:S(2)}, u32[]{:S(2)}) %collective-permute-start.9) | collective-permute-done | bytes 69664 | tf_op jit(solution)/shard_map/ppermute | solution.py:494
  30.3 0.9 %shard_map.153.refs_3_ = f32[1024,128]{1,0:T(8,128)S(1)} custom-call(bf16[272,128]{1,0:T(8,128)(2,1)S(1)} %get-tuple-element.44.refs_0_, bf16[272,128]{1,0:T(8,128)(2,1)S(1)} %collective-permute-done.6.refs_1_, bf16[272,128]{1,0:T(8,128)(2,1)S(1)} %collective-permute-done.7.refs_2_, bf16[272,128]{1,0:T(8,128)(2,1)S(1)} %collective-permute-done.8.refs_3_, ...), custom_call_target="tpu_custom_call" | custom-call | flops 2000000000 | bytes 100000 | tf_op jit(solution)/shard_map/pallas_call | solution.py:354
  31.2 1.1 %collective-permute-done.4.refs_1_ = bf16[272,128]{1,0:T(8,128)(2,1)S(1)} collective-permute-done((bf16[272,128]{1,0:T(8,128)(2,1)S(1)}, bf16[272,128]{1,0:T(8,128)(2,1)S(1)}, u32[]{:S(2)}, u32[]{:S(2)}) %collective-permute-start.4) | collective-permute-done | bytes 69664 | tf_op jit(solution)/shard_map/ppermute | solution.py:494
  32.3 1.5 %shard_map.155 = (bf16[1024,128]{1,0:T(8,128)(2,1)S(1)}, f32[3,8,128]{2,1,0:T(8,128)S(1)}, f32[3,128]{1,0:T(4,128)S(1)}, f32[3,128]{1,0:T(4,128)S(1)}, f32[3,128]{1,0:T(4,128)S(1)}, /*index=5*/f32[3,128]{1,0:T(4,128)S(1)}) custom-call(bf16[272,128]{1,0:T(8,128)(2,1)S(1)} %collective-permute-done.3.refs_0_, ...), custom_call_target="tpu_custom_call" | custom-call | flops 2000000000 | bytes 100000 | tf_op jit(solution)/shard_map/pallas_call | solution.py:354
  33.9 0.2 collective-permute-start.10
  34.1 4.5 %collective-permute-start.11 = (f32[3,128]{1,0:T(4,128)S(1)}, f32[3,128]{1,0:T(4,128)S(1)}, u32[]{:S(2)}, u32[]{:S(2)}) collective-permute-start(f32[3,128]{1,0:T(4,128)S(1)} %get-tuple-element.57), channel_id=1, source_target_pairs={{4,8},{12,16},{20,24},{0,28},{8,4},{16,12},{24,20},{28,0},{5,9},{1... | collective-permute-start | bytes 4616 | tf_op jit(solution)/shard_map/ppermute | solution.py:524
  38.6 1.1 %collective-permute-start.12 = (f32[3,128]{1,0:T(4,128)S(1)}, f32[3,128]{1,0:T(4,128)S(1)}, u32[]{:S(2)}, u32[]{:S(2)}) collective-permute-start(f32[3,128]{1,0:T(4,128)S(1)} %get-tuple-element.58), channel_id=1, source_target_pairs={{0,1},{2,3},{1,0},{3,2},{4,5},{6,7},{5,4},{7,6},{8,9},{10,11},{9,8... | collective-permute-start | bytes 4616 | tf_op jit(solution)/shard_map/ppermute | solution.py:524
  39.7 1.1 %collective-permute-start.13 = (f32[3,128]{1,0:T(4,128)S(1)}, f32[3,128]{1,0:T(4,128)S(1)}, u32[]{:S(2)}, u32[]{:S(2)}) collective-permute-start(f32[3,128]{1,0:T(4,128)S(1)} %get-tuple-element.59), channel_id=1, source_target_pairs={{1,2},{0,3},{2,1},{3,0},{5,6},{4,7},{6,5},{7,4},{9,10},{8,11},{10,... | collective-permute-start | bytes 4616 | tf_op jit(solution)/shard_map/ppermute | solution.py:524
  40.8 0.8 %shard_map.156 = bf16[1024,128]{1,0:T(8,128)(2,1)} custom-call(bf16[1024,128]{1,0:T(8,128)(2,1)S(1)} %get-tuple-element.52.arrived, f32[1024,128]{1,0:T(8,128)S(1)} %get-tuple-element.53.drive, f32[1,128]{1,0:T(1,128)S(1)} %bitcast.18), custom_call_target="tpu_custom_call" | custom-call | flops 2000000000 | bytes 100000 | tf_op jit(solution)/shard_map/pallas_call | solution.py:354
  41.6 1.1 %collective-permute-done.13.rest_3_ = f32[3,128]{1,0:T(4,128)S(1)} collective-permute-done((f32[3,128]{1,0:T(4,128)S(1)}, f32[3,128]{1,0:T(4,128)S(1)}, u32[]{:S(2)}, u32[]{:S(2)}) %collective-permute-start.13) | collective-permute-done | bytes 1568 | tf_op jit(solution)/shard_map/ppermute | solution.py:524
  42.8 0.7 %shard_map.157 = f32[3,1024]{1,0:T(4,128)} custom-call(f32[3,8,128]{2,1,0:T(8,128)S(1)} %get-tuple-element.54.local, s32[2,8,128]{2,1,0:T(8,128)S(1)} %get-tuple-element.55.inverse, f32[3,128]{1,0:T(4,128)S(1)} %collective-permute-done.10.rest_0_, f32[3,128]{1,0:T(4,128)S(1)} %collective-permute-done.11.rest_1_, ...), custom_call_target="tpu_custom_call" | custom-call | flops 2000000000 | bytes 100000 | tf_op jit(solution)/shard_map/pallas_call | solution.py:354
  (33 shorter events, 0.1 us)
Async XLA Ops:
  0.6 1.0 %copy-start.1 = (bf16[8,128,128]{2,1,0:T(8,128)(2,1)S(1)}, bf16[8,128,128]{2,1,0:T(8,128)(2,1)}, u32[]{:S(2)}) copy-start(bf16[8,128,128]{2,1,0:T(8,128)(2,1)} %old.1) | copy-start | bytes 786436
  1.6 0.7 %copy-start.11 = (s32[8]{0:T(128)S(1)}, s32[8]{0:T(128)}, u32[]{:S(2)}) copy-start(s32[8]{0:T(128)} %route.1) | copy-start | bytes 100
  2.2 3.5 %copy-start.4 = (s32[1024]{0:T(1024)S(1)}, s32[1024]{0:T(1024)}, u32[]{:S(2)}) copy-start(s32[1024]{0:T(1024)} %param.19) | copy-start | bytes 12292
  2.2 3.5 %copy-start.5 = (s32[1024]{0:T(1024)S(1)}, s32[1024]{0:T(1024)}, u32[]{:S(2)}) copy-start(s32[1024]{0:T(1024)} %param.20) | copy-start | bytes 12292
  2.9 5.9 %collective-permute-start = (bf16[4,128,128]{2,1,0:T(8,128)(2,1)S(1)}, bf16[4,128,128]{2,1,0:T(8,128)(2,1)S(1)}, u32[]{:S(2)}, u32[]{:S(2)}) collective-permute-start(bf16[4,128,128]{2,1,0:T(8,128)(2,1)S(1)} %get-tuple-element.38), channel_id=1, source_target_pairs={{0,1},{1,0},{2,3},{3,2},{4,5},{5,4},{6,7},{7,6},{8,9},{9,8},{10,11... | collective-permute-start | bytes 393224 | tf_op jit(solution)/shard_map/ppermute | solution.py:431
  3.0 6.5 %collective-permute-start.1 = (bf16[4,128,128]{2,1,0:T(8,128)(2,1)S(1)}, bf16[4,128,128]{2,1,0:T(8,128)(2,1)S(1)}, u32[]{:S(2)}, u32[]{:S(2)}) collective-permute-start(bf16[4,128,128]{2,1,0:T(8,128)(2,1)S(1)} %get-tuple-element.39), channel_id=1, source_target_pairs={{0,2},{1,3},{2,0},{3,1},{4,6},{5,7},{6,4},{7,5},{8,10},{9,11},{10,... | collective-permute-start | bytes 393224 | tf_op jit(solution)/shard_map/ppermute | solution.py:431
  5.6 6.6 %collective-permute-start.2 = (bf16[4,128,128]{2,1,0:T(8,128)(2,1)S(1)}, bf16[4,128,128]{2,1,0:T(8,128)(2,1)S(1)}, u32[]{:S(2)}, u32[]{:S(2)}) collective-permute-start(bf16[4,128,128]{2,1,0:T(8,128)(2,1)S(1)} %get-tuple-element.40), channel_id=1, source_target_pairs={{0,3},{1,2},{2,1},{3,0},{4,7},{5,6},{6,5},{7,4},{8,11},{9,10},{10,... | collective-permute-start | bytes 393224 | tf_op jit(solution)/shard_map/ppermute | solution.py:431
  5.7 1.7 %copy-start = (bf16[8,4,128,128]{3,2,1,0:T(8,128)(2,1)S(1)}, bf16[8,4,128,128]{3,2,1,0:T(8,128)(2,1)}, u32[]{:S(2)}) copy-start(bf16[8,4,128,128]{3,2,1,0:T(8,128)(2,1)} %param.18) | copy-start | bytes 3145732
  5.7 1.7 %copy-start.9 = (s32[8,4]{0,1:T(4,128)S(1)}, s32[8,4]{0,1:T(4,128)}, u32[]{:S(2)}) copy-start(s32[8,4]{0,1:T(4,128)} %param.16) | copy-start | bytes 388
  5.7 1.7 %copy-start.12 = (s32[8]{0:T(128)S(1)}, s32[8]{0:T(128)}, u32[]{:S(2)}) copy-start(s32[8]{0:T(128)} %count.1) | copy-start | bytes 100
  12.2 8.7 %copy-start.2 = (s32[8,1024]{1,0:T(8,128)S(1)}, s32[8,1024]{1,0:T(8,128)}, u32[]{:S(2)}) copy-start(s32[8,1024]{1,0:T(8,128)} %refs_6_.1) | copy-start | bytes 98308
  12.2 8.7 %copy-start.3 = (f32[3,1024]{1,0:T(4,128)S(1)}, f32[3,1024]{1,0:T(4,128)}, u32[]{:S(2)}) copy-start(f32[3,1024]{1,0:T(4,128)} %motion.1) | copy-start | bytes 36868
  12.3 8.7 %copy-start.6 = (f32[128,6]{0,1:T(8,128)S(1)}, f32[128,6]{0,1:T(8,128)}, u32[]{:S(2)}) copy-start(f32[128,6]{0,1:T(8,128)} %param.26) | copy-start | bytes 9220
  12.3 8.7 %copy-start.7 = (f32[1024]{0:T(1024)S(1)}, f32[1024]{0:T(1024)}, u32[]{:S(2)}) copy-start(f32[1024]{0:T(1024)} %param.24) | copy-start | bytes 12292
  12.3 8.7 %copy-start.8 = (f32[128,6]{0,1:T(8,128)S(1)}, f32[128,6]{0,1:T(8,128)}, u32[]{:S(2)}) copy-start(f32[128,6]{0,1:T(8,128)} %param.27) | copy-start | bytes 9220
  12.3 8.7 %copy-start.10 = (s32[4,128]{1,0:T(4,128)S(1)}, s32[4,128]{1,0:T(4,128)}, u32[]{:S(2)}) copy-start(s32[4,128]{1,0:T(4,128)} %shared.1) | copy-start | bytes 6148
  14.0 11.9 %collective-permute-start.6 = (bf16[272,128]{1,0:T(8,128)(2,1)S(1)}, bf16[272,128]{1,0:T(8,128)(2,1)S(1)}, u32[]{:S(2)}, u32[]{:S(2)}) collective-permute-start(bf16[272,128]{1,0:T(8,128)(2,1)S(1)} %get-tuple-element.45), channel_id=1, source_target_pairs={{0,28},{4,24},{8,20},{12,16},{16,12},{20,8},{24,4},{28,0},{1,29},{... | collective-permute-start | bytes 208904 | tf_op jit(solution)/shard_map/ppermute | solution.py:494
  18.5 7.6 %collective-permute-start.7 = (bf16[272,128]{1,0:T(8,128)(2,1)S(1)}, bf16[272,128]{1,0:T(8,128)(2,1)S(1)}, u32[]{:S(2)}, u32[]{:S(2)}) collective-permute-start(bf16[272,128]{1,0:T(8,128)(2,1)S(1)} %get-tuple-element.46), channel_id=1, source_target_pairs={{0,24},{4,28},{8,16},{12,20},{16,8},{20,12},{24,0},{28,4},{1,25},{... | collective-permute-start | bytes 208904 | tf_op jit(solution)/shard_map/ppermute | solution.py:494
  18.5 10.5 %collective-permute-start.8 = (bf16[272,128]{1,0:T(8,128)(2,1)S(1)}, bf16[272,128]{1,0:T(8,128)(2,1)S(1)}, u32[]{:S(2)}, u32[]{:S(2)}) collective-permute-start(bf16[272,128]{1,0:T(8,128)(2,1)S(1)} %get-tuple-element.47), channel_id=1, source_target_pairs={{0,20},{4,16},{8,28},{12,24},{16,4},{20,0},{24,12},{28,8},{1,21},{... | collective-permute-start | bytes 208904 | tf_op jit(solution)/shard_map/ppermute | solution.py:494
  18.9 11.4 %collective-permute-start.9 = (bf16[272,128]{1,0:T(8,128)(2,1)S(1)}, bf16[272,128]{1,0:T(8,128)(2,1)S(1)}, u32[]{:S(2)}, u32[]{:S(2)}) collective-permute-start(bf16[272,128]{1,0:T(8,128)(2,1)S(1)} %get-tuple-element.48), channel_id=1, source_target_pairs={{0,16},{4,20},{8,24},{12,28},{16,0},{20,4},{24,8},{28,12},{1,17},{... | collective-permute-start | bytes 208904 | tf_op jit(solution)/shard_map/ppermute | solution.py:494
  23.8 7.4 %collective-permute-start.3 = (bf16[272,128]{1,0:T(8,128)(2,1)S(1)}, bf16[272,128]{1,0:T(8,128)(2,1)S(1)}, u32[]{:S(2)}, u32[]{:S(2)}) collective-permute-start(bf16[272,128]{1,0:T(8,128)(2,1)S(1)} %get-tuple-element.41), channel_id=1, source_target_pairs={{0,12},{4,8},{8,4},{12,0},{16,28},{20,24},{24,20},{28,16},{1,13},{... | collective-permute-start | bytes 208904 | tf_op jit(solution)/shard_map/ppermute | solution.py:494
  25.8 6.5 %collective-permute-start.4 = (bf16[272,128]{1,0:T(8,128)(2,1)S(1)}, bf16[272,128]{1,0:T(8,128)(2,1)S(1)}, u32[]{:S(2)}, u32[]{:S(2)}) collective-permute-start(bf16[272,128]{1,0:T(8,128)(2,1)S(1)} %get-tuple-element.42), channel_id=1, source_target_pairs={{0,8},{4,12},{8,0},{12,4},{16,24},{20,28},{24,16},{28,20},{1,9},{5... | collective-permute-start | bytes 208904 | tf_op jit(solution)/shard_map/ppermute | solution.py:494
  26.1 6.2 %collective-permute-start.5 = (bf16[272,128]{1,0:T(8,128)(2,1)S(1)}, bf16[272,128]{1,0:T(8,128)(2,1)S(1)}, u32[]{:S(2)}, u32[]{:S(2)}) collective-permute-start(bf16[272,128]{1,0:T(8,128)(2,1)S(1)} %get-tuple-element.43), channel_id=1, source_target_pairs={{0,4},{4,0},{8,12},{12,8},{16,20},{20,16},{24,28},{28,24},{1,5},{5... | collective-permute-start | bytes 208904 | tf_op jit(solution)/shard_map/ppermute | solution.py:494
  30.3 2.0 %copy-start.13 = (f32[128]{0:T(128)S(1)}, f32[128]{0:T(128)}, u32[]{:S(2)}) copy-start(f32[128]{0:T(128)} %param.25) | copy-start | bytes 1540
  33.9 7.7 %collective-permute-start.10 = (f32[3,128]{1,0:T(4,128)S(1)}, f32[3,128]{1,0:T(4,128)S(1)}, u32[]{:S(2)}, u32[]{:S(2)}) collective-permute-start(f32[3,128]{1,0:T(4,128)S(1)} %get-tuple-element.56), channel_id=1, source_target_pairs={{0,4},{8,12},{16,20},{24,28},{4,0},{12,8},{20,16},{28,24},{1,5},{9... | collective-permute-start | bytes 4616 | tf_op jit(solution)/shard_map/ppermute | solution.py:524
  34.1 7.5 %collective-permute-start.11 = (f32[3,128]{1,0:T(4,128)S(1)}, f32[3,128]{1,0:T(4,128)S(1)}, u32[]{:S(2)}, u32[]{:S(2)}) collective-permute-start(f32[3,128]{1,0:T(4,128)S(1)} %get-tuple-element.57), channel_id=1, source_target_pairs={{4,8},{12,16},{20,24},{0,28},{8,4},{16,12},{24,20},{28,0},{5,9},{1... | collective-permute-start | bytes 4616 | tf_op jit(solution)/shard_map/ppermute | solution.py:524
  38.6 3.0 %collective-permute-start.12 = (f32[3,128]{1,0:T(4,128)S(1)}, f32[3,128]{1,0:T(4,128)S(1)}, u32[]{:S(2)}, u32[]{:S(2)}) collective-permute-start(f32[3,128]{1,0:T(4,128)S(1)} %get-tuple-element.58), channel_id=1, source_target_pairs={{0,1},{2,3},{1,0},{3,2},{4,5},{6,7},{5,4},{7,6},{8,9},{10,11},{9,8... | collective-permute-start | bytes 4616 | tf_op jit(solution)/shard_map/ppermute | solution.py:524
  39.7 3.0 %collective-permute-start.13 = (f32[3,128]{1,0:T(4,128)S(1)}, f32[3,128]{1,0:T(4,128)S(1)}, u32[]{:S(2)}, u32[]{:S(2)}) collective-permute-start(f32[3,128]{1,0:T(4,128)S(1)} %get-tuple-element.59), channel_id=1, source_target_pairs={{1,2},{0,3},{2,1},{3,0},{5,6},{4,7},{6,5},{7,4},{9,10},{8,11},{10,... | collective-permute-start | bytes 4616 | tf_op jit(solution)/shard_map/ppermute | solution.py:524

commit v5 on v4

--- a/solution.py
+++ b/solution.py
@@ -447,6 +447,7 @@
             pltpu.VMEM((2, SUBS, width), F32),
         ],
         (connectivity, node_motion, edge, couple.T, readout.T, shared_nodes),
+        cost=1000,
     )
     usual = rows // dom_total
     relaxing = decay.reshape(1, width)
@@ -492,8 +493,8 @@
         payloads = {0: outgoing[0]}
         for k in range(1, dom_total):
             payloads[k] = lax.ppermute(outgoing[k], "dom", [(i, i ^ k) for i in range(dom_total)])
-        soon = [0, *range(dom_total - 1, far - 1, -1)]
-        late = [payloads[k] for k in range(far - 1, 0, -1)]
+        soon = [0, *range(dom_total - 1, far - 1, -1), 1]
+        late = [payloads[k] for k in range(far - 1, 1, -1)]
 
         def placing(count):
             return [

time: 43.6 us -> 43.3 us (level)
  starting transfers between devices: 19.5 us -> 19 us
  waiting for transfers between devices: 9.54 us -> 9.98 us
    ppermute x4, starting transfers between devices: 6.97 us -> 6.4 us  [body(): halo[m] = lax.ppermute(exports[m], axis, swaps(axis, first))]
    ppermute x7, waiting for transfers between devices: 4.98 us -> 5.42 us  [body(): lax.ppermute(outgoing[k], 'dom', [(i, i ^ k) for i in range(dom_total)])]
  transfers between devices with their start and end apart: 14 -> 14, of which waited for: 6 -> 7; matrix products, arithmetic and copies ran while one was open for 0% -> 0% of each run, Pallas kernels for 17% -> 18%
where the time goes in v5:
time: 43.3 us; the launch traced here: 43.2 us
  starting transfers between devices  19 us (44%)
  Pallas kernels  11.8 us (27%)
  waiting for transfers between devices  9.98 us (23%)
  local copies, waits for them, and re-layouts  1.65 us (4%)
  between operations  0.79 us (2%)
    pallas_call x9, Pallas kernels, call(): pl.pallas_call(kernel, out_shape=outs, in_specs=ins, out_specs=out_specs...  11.8 us
    ppermute x7, starting transfers between devices, body(): lax.ppermute(outgoing[k], 'dom', [(i, i ^ k) for i in range(dom_total)])  9.75 us
    ppermute x4, starting transfers between devices, body(): halo[m] = lax.ppermute(exports[m], axis, swaps(axis, first))  6.4 us
    ppermute x7, waiting for transfers between devices, body(): lax.ppermute(outgoing[k], 'dom', [(i, i ^ k) for i in range(dom_total)])  5.42 us
    ppermute x3, waiting for transfers between devices, body(): lax.ppermute(packed[k], 'box', [(i, i ^ k) for i in range(box_total)])  3.43 us
    ppermute x3, starting transfers between devices, body(): lax.ppermute(packed[k], 'box', [(i, i ^ k) for i in range(box_total)])  2.81 us
    unnamed x28, local copies, waits for them, and re-layouts  1.65 us
    ppermute x4, waiting for transfers between devices, body(): halo[m] = lax.ppermute(exports[m], axis, swaps(axis, first))  1.13 us
  transfers between devices with their start and end apart: 14, of which 7 were waited for; matrix products, arithmetic and copies ran while one was open for 0% of the time, Pallas kernels for 18%

profile of v5, /device:TPU:1, one launch (start us, length us, event | category | flops | bytes accessed | tf_op | source)
XLA Modules:
  0.0 43.2 jit_solution(13316023782147481665)
XLA Ops:
  0.6 0.9 %copy-done.7 = bf16[8,128,128]{2,1,0:T(8,128)(2,1)S(1)} copy-done((bf16[8,128,128]{2,1,0:T(8,128)(2,1)S(1)}, bf16[8,128,128]{2,1,0:T(8,128)(2,1)}, u32[]{:S(2)}) %copy-start.7) | copy-done | bytes 262168
  1.6 0.7 %copy-done.11 = s32[8]{0:T(128)S(1)} copy-done((s32[8]{0:T(128)S(1)}, s32[8]{0:T(128)}, u32[]{:S(2)}) %copy-start.11) | copy-done | bytes 56
  2.2 0.6 %shard_map.151 = (bf16[4,128,128]{2,1,0:T(8,128)(2,1)S(1)}, bf16[4,128,128]{2,1,0:T(8,128)(2,1)S(1)}, bf16[4,128,128]{2,1,0:T(8,128)(2,1)S(1)}, bf16[4,128,128]{2,1,0:T(8,128)(2,1)S(1)}) custom-call(s32[8]{0:T(128)S(1)} %copy-done.11, bf16[8,128,128]{2,1,0:T(8,128)(2,1)S(1)} %copy-done.7), custom_call_target="tpu_custom_call" | custom-call | flops 2000000000 | bytes 100000 | tf_op jit(solution)/shard_map/pallas_call | solution.py:354
  2.9 0.1 collective-permute-start
  3.0 2.7 %collective-permute-start.1 = (bf16[4,128,128]{2,1,0:T(8,128)(2,1)S(1)}, bf16[4,128,128]{2,1,0:T(8,128)(2,1)S(1)}, u32[]{:S(2)}, u32[]{:S(2)}) collective-permute-start(bf16[4,128,128]{2,1,0:T(8,128)(2,1)S(1)} %get-tuple-element.39), channel_id=1, source_target_pairs={{0,2},{1,3},{2,0},{3,1},{4,6},{5,7},{6,4},{7,5},{8,10},{9,11},{10,... | collective-permute-start | bytes 393224 | tf_op jit(solution)/shard_map/ppermute | solution.py:431
  5.6 0.0 collective-permute-start.2
  5.7 1.6 %shard_map.149 = (bf16[1024,1024]{1,0:T(8,128)(2,1)S(1)}, bf16[8,16,128]{2,1,0:T(8,128)(2,1)S(1)}, s32[16]{0:T(128)S(1)}) custom-call(s32[8,128]{1,0:T(8,128)S(1)} %bitcast.14, s32[1,1024]{1,0:T(1,128)S(1)} %bitcast.15), custom_call_target="tpu_custom_call" | custom-call | flops 2000000000 | bytes 100000 | tf_op jit(solution)/shard_map/pallas_call | solution.py:354
  7.4 1.4 %shard_map.150 = (bf16[8,512,128]{2,1,0:T(8,128)(2,1)S(1)}, f32[8,128]{1,0:T(8,128)S(1)}, s32[32]{0:T(128)S(1)}) custom-call(s32[4,8]{1,0:T(4,128)S(1)} %bitcast.16, s32[8]{0:T(128)S(1)} %copy-done.12, bf16[8,512,128]{2,1,0:T(8,128)(2,1)S(1)} %bitcast.13), custom_call_target="tpu_custom_call" | custom-call | flops 2000000000 | bytes 100000 | tf_op jit(solution)/shard_map/pallas_call | solution.py:354
  8.8 0.6 %collective-permute-done.1.rest_2_ = bf16[4,128,128]{2,1,0:T(8,128)(2,1)S(1)} collective-permute-done((bf16[4,128,128]{2,1,0:T(8,128)(2,1)S(1)}, bf16[4,128,128]{2,1,0:T(8,128)(2,1)S(1)}, u32[]{:S(2)}, u32[]{:S(2)}) %collective-permute-start.1) | collective-permute-done | bytes 131104 | tf_op jit(solution)/shard_map/ppermute | solution.py:431
  9.4 2.8 %collective-permute-done.2.rest_3_ = bf16[4,128,128]{2,1,0:T(8,128)(2,1)S(1)} collective-permute-done((bf16[4,128,128]{2,1,0:T(8,128)(2,1)S(1)}, bf16[4,128,128]{2,1,0:T(8,128)(2,1)S(1)}, u32[]{:S(2)}, u32[]{:S(2)}) %collective-permute-start.2) | collective-permute-done | bytes 131104 | tf_op jit(solution)/shard_map/ppermute | solution.py:431
  12.3 0.0 copy-start.5
  12.3 1.7 %shard_map.152 = (bf16[272,128]{1,0:T(8,128)(2,1)S(1)}, bf16[272,128]{1,0:T(8,128)(2,1)S(1)}, bf16[272,128]{1,0:T(8,128)(2,1)S(1)}, bf16[272,128]{1,0:T(8,128)(2...) custom-call(s32[16]{0:T(128)S(1)} %get-tuple-element.31.table, ...), custom_call_target="tpu_custom_call" | custom-call | flops 2000000000 | bytes 100000 | tf_op jit(solution)/shard_map/pallas_call | solution.py:354
  14.0 4.6 %collective-permute-start.5 = (bf16[272,128]{1,0:T(8,128)(2,1)S(1)}, bf16[272,128]{1,0:T(8,128)(2,1)S(1)}, u32[]{:S(2)}, u32[]{:S(2)}) collective-permute-start(bf16[272,128]{1,0:T(8,128)(2,1)S(1)} %get-tuple-element.44), channel_id=1, source_target_pairs={{0,28},{4,24},{8,20},{12,16},{16,12},{20,8},{24,4},{28,0},{1,29},{... | collective-permute-start | bytes 208904 | tf_op jit(solution)/shard_map/ppermute | solution.py:495
  18.5 0.4 collective-permute-start.7
  18.9 2.1 %collective-permute-start.8 = (bf16[272,128]{1,0:T(8,128)(2,1)S(1)}, bf16[272,128]{1,0:T(8,128)(2,1)S(1)}, u32[]{:S(2)}, u32[]{:S(2)}) collective-permute-start(bf16[272,128]{1,0:T(8,128)(2,1)S(1)} %get-tuple-element.47), channel_id=1, source_target_pairs={{0,16},{4,20},{8,24},{12,28},{16,0},{20,4},{24,8},{28,12},{1,17},{... | collective-permute-start | bytes 208904 | tf_op jit(solution)/shard_map/ppermute | solution.py:495
  21.0 1.1 %collective-permute-start.9 = (bf16[272,128]{1,0:T(8,128)(2,1)S(1)}, bf16[272,128]{1,0:T(8,128)(2,1)S(1)}, u32[]{:S(2)}, u32[]{:S(2)}) collective-permute-start(bf16[272,128]{1,0:T(8,128)(2,1)S(1)} %get-tuple-element.48), channel_id=1, source_target_pairs={{0,4},{4,0},{8,12},{12,8},{16,20},{20,16},{24,28},{28,24},{1,5},{5... | collective-permute-start | bytes 208904 | tf_op jit(solution)/shard_map/ppermute | solution.py:495
  22.1 2.8 %shard_map.154 = (f32[1024,128]{1,0:T(8,128)S(1)}, f32[8,1024]{1,0:T(8,128)S(1)}, bf16[8,1024,128]{2,1,0:T(8,128)(2,1)S(1)}, s32[8,128]{1,0:T(8,128)S(1)}, s32[2,8,128]{2,1,0:T(8,128)S(1)}) custom-call(s32[8,1024]{1,0:T(8,128)S(1)} %copy-done, f32[3,1024]{1,0:T(4,128)S(1)} %copy-done.1, f32[1,1024]{1,0:T(1,128)S(1)} %bitcast.9, f32[6,128]{1,0:T(8,128)S(1)} %bitcast.8, ...), custom_call_target="tpu_custom_call" | custom-call | flops 1000 | bytes 100000 | tf_op jit(solution)/shard_map/pallas_call | solution.py:354
  24.9 1.2 %collective-permute-start.3 = (bf16[272,128]{1,0:T(8,128)(2,1)S(1)}, bf16[272,128]{1,0:T(8,128)(2,1)S(1)}, u32[]{:S(2)}, u32[]{:S(2)}) collective-permute-start(bf16[272,128]{1,0:T(8,128)(2,1)S(1)} %get-tuple-element.41), channel_id=1, source_target_pairs={{0,12},{4,8},{8,4},{12,0},{16,28},{20,24},{24,20},{28,16},{1,13},{... | collective-permute-start | bytes 208904 | tf_op jit(solution)/shard_map/ppermute | solution.py:495
  26.1 0.4 collective-permute-start.4
  26.5 2.5 %collective-permute-done.7.refs_3_ = bf16[272,128]{1,0:T(8,128)(2,1)S(1)} collective-permute-done((bf16[272,128]{1,0:T(8,128)(2,1)S(1)}, bf16[272,128]{1,0:T(8,128)(2,1)S(1)}, u32[]{:S(2)}, u32[]{:S(2)}) %collective-permute-start.7) | collective-permute-done | bytes 69664 | tf_op jit(solution)/shard_map/ppermute | solution.py:495
  29.0 1.3 %collective-permute-done.8.refs_4_ = bf16[272,128]{1,0:T(8,128)(2,1)S(1)} collective-permute-done((bf16[272,128]{1,0:T(8,128)(2,1)S(1)}, bf16[272,128]{1,0:T(8,128)(2,1)S(1)}, u32[]{:S(2)}, u32[]{:S(2)}) %collective-permute-start.8) | collective-permute-done | bytes 69664 | tf_op jit(solution)/shard_map/ppermute | solution.py:495
  30.3 1.0 %shard_map.153.refs_2_ = f32[1024,128]{1,0:T(8,128)S(1)} custom-call(bf16[272,128]{1,0:T(8,128)(2,1)S(1)} %get-tuple-element.43.refs_0_, bf16[272,128]{1,0:T(8,128)(2,1)S(1)} %collective-permute-done.5.refs_1_, bf16[272,128]{1,0:T(8,128)(2,1)S(1)} %collective-permute-done.6.refs_2_, bf16[272,128]{1,0:T(8,128)(2,1)S(1)} %collective-permute-done.7.refs_3_, ...), custom_call_target="tpu_custom_call" | custom-call | flops 2000000000 | bytes 100000 | tf_op jit(solution)/shard_map/pallas_call | solution.py:354
  31.3 0.7 %collective-permute-done.3.refs_0_ = bf16[272,128]{1,0:T(8,128)(2,1)S(1)} collective-permute-done((bf16[272,128]{1,0:T(8,128)(2,1)S(1)}, bf16[272,128]{1,0:T(8,128)(2,1)S(1)}, u32[]{:S(2)}, u32[]{:S(2)}) %collective-permute-start.3) | collective-permute-done | bytes 69664 | tf_op jit(solution)/shard_map/ppermute | solution.py:495
  32.0 0.9 %collective-permute-done.4.refs_1_ = bf16[272,128]{1,0:T(8,128)(2,1)S(1)} collective-permute-done((bf16[272,128]{1,0:T(8,128)(2,1)S(1)}, bf16[272,128]{1,0:T(8,128)(2,1)S(1)}, u32[]{:S(2)}, u32[]{:S(2)}) %collective-permute-start.4) | collective-permute-done | bytes 69664 | tf_op jit(solution)/shard_map/ppermute | solution.py:495
  33.0 1.2 %shard_map.155 = (bf16[1024,128]{1,0:T(8,128)(2,1)S(1)}, f32[3,8,128]{2,1,0:T(8,128)S(1)}, f32[3,128]{1,0:T(4,128)S(1)}, f32[3,128]{1,0:T(4,128)S(1)}, f32[3,128]{1,0:T(4,128)S(1)}, /*index=5*/f32[3,128]{1,0:T(4,128)S(1)}) custom-call(bf16[272,128]{1,0:T(8,128)(2,1)S(1)} %collective-permute-done.3.refs_0_, ...), custom_call_target="tpu_custom_call" | custom-call | flops 2000000000 | bytes 100000 | tf_op jit(solution)/shard_map/pallas_call | solution.py:354
  34.2 0.9 %collective-permute-start.10 = (f32[3,128]{1,0:T(4,128)S(1)}, f32[3,128]{1,0:T(4,128)S(1)}, u32[]{:S(2)}, u32[]{:S(2)}) collective-permute-start(f32[3,128]{1,0:T(4,128)S(1)} %get-tuple-element.56), channel_id=1, source_target_pairs={{0,4},{8,12},{16,20},{24,28},{4,0},{12,8},{20,16},{28,24},{1,5},{9... | collective-permute-start | bytes 4616 | tf_op jit(solution)/shard_map/ppermute | solution.py:525
  35.1 3.3 %collective-permute-start.11 = (f32[3,128]{1,0:T(4,128)S(1)}, f32[3,128]{1,0:T(4,128)S(1)}, u32[]{:S(2)}, u32[]{:S(2)}) collective-permute-start(f32[3,128]{1,0:T(4,128)S(1)} %get-tuple-element.57), channel_id=1, source_target_pairs={{4,8},{12,16},{20,24},{0,28},{8,4},{16,12},{24,20},{28,0},{5,9},{1... | collective-permute-start | bytes 4616 | tf_op jit(solution)/shard_map/ppermute | solution.py:525
  38.4 1.1 %collective-permute-start.12 = (f32[3,128]{1,0:T(4,128)S(1)}, f32[3,128]{1,0:T(4,128)S(1)}, u32[]{:S(2)}, u32[]{:S(2)}) collective-permute-start(f32[3,128]{1,0:T(4,128)S(1)} %get-tuple-element.58), channel_id=1, source_target_pairs={{0,1},{2,3},{1,0},{3,2},{4,5},{6,7},{5,4},{7,6},{8,9},{10,11},{9,8... | collective-permute-start | bytes 4616 | tf_op jit(solution)/shard_map/ppermute | solution.py:525
  39.5 1.1 %collective-permute-start.13 = (f32[3,128]{1,0:T(4,128)S(1)}, f32[3,128]{1,0:T(4,128)S(1)}, u32[]{:S(2)}, u32[]{:S(2)}) collective-permute-start(f32[3,128]{1,0:T(4,128)S(1)} %get-tuple-element.59), channel_id=1, source_target_pairs={{1,2},{0,3},{2,1},{3,0},{5,6},{4,7},{6,5},{7,4},{9,10},{8,11},{10,... | collective-permute-start | bytes 4616 | tf_op jit(solution)/shard_map/ppermute | solution.py:525
  40.6 0.8 %shard_map.156 = bf16[1024,128]{1,0:T(8,128)(2,1)} custom-call(bf16[1024,128]{1,0:T(8,128)(2,1)S(1)} %get-tuple-element.52.arrived, f32[1024,128]{1,0:T(8,128)S(1)} %get-tuple-element.53.drive, f32[1,128]{1,0:T(1,128)S(1)} %bitcast.18), custom_call_target="tpu_custom_call" | custom-call | flops 2000000000 | bytes 100000 | tf_op jit(solution)/shard_map/pallas_call | solution.py:354
  41.3 1.1 %collective-permute-done.13.rest_3_ = f32[3,128]{1,0:T(4,128)S(1)} collective-permute-done((f32[3,128]{1,0:T(4,128)S(1)}, f32[3,128]{1,0:T(4,128)S(1)}, u32[]{:S(2)}, u32[]{:S(2)}) %collective-permute-start.13) | collective-permute-done | bytes 1568 | tf_op jit(solution)/shard_map/ppermute | solution.py:525
  42.5 0.7 %shard_map.157 = f32[3,1024]{1,0:T(4,128)} custom-call(f32[3,8,128]{2,1,0:T(8,128)S(1)} %get-tuple-element.54.local, s32[2,8,128]{2,1,0:T(8,128)S(1)} %get-tuple-element.55.inverse, f32[3,128]{1,0:T(4,128)S(1)} %collective-permute-done.10.rest_0_, f32[3,128]{1,0:T(4,128)S(1)} %collective-permute-done.11.rest_1_, ...), custom_call_target="tpu_custom_call" | custom-call | flops 2000000000 | bytes 100000 | tf_op jit(solution)/shard_map/pallas_call | solution.py:354
  (33 shorter events, 0.1 us)
Async XLA Ops:
  0.6 1.0 %copy-start.7 = (bf16[8,128,128]{2,1,0:T(8,128)(2,1)S(1)}, bf16[8,128,128]{2,1,0:T(8,128)(2,1)}, u32[]{:S(2)}) copy-start(bf16[8,128,128]{2,1,0:T(8,128)(2,1)} %old.1) | copy-start | bytes 786436
  1.6 0.7 %copy-start.11 = (s32[8]{0:T(128)S(1)}, s32[8]{0:T(128)}, u32[]{:S(2)}) copy-start(s32[8]{0:T(128)} %route.1) | copy-start | bytes 100
  2.2 3.5 %copy-start.8 = (s32[1024]{0:T(1024)S(1)}, s32[1024]{0:T(1024)}, u32[]{:S(2)}) copy-start(s32[1024]{0:T(1024)} %param.19) | copy-start | bytes 12292
  2.2 3.5 %copy-start.9 = (s32[1024]{0:T(1024)S(1)}, s32[1024]{0:T(1024)}, u32[]{:S(2)}) copy-start(s32[1024]{0:T(1024)} %param.20) | copy-start | bytes 12292
  2.9 5.9 %collective-permute-start = (bf16[4,128,128]{2,1,0:T(8,128)(2,1)S(1)}, bf16[4,128,128]{2,1,0:T(8,128)(2,1)S(1)}, u32[]{:S(2)}, u32[]{:S(2)}) collective-permute-start(bf16[4,128,128]{2,1,0:T(8,128)(2,1)S(1)} %get-tuple-element.38), channel_id=1, source_target_pairs={{0,1},{1,0},{2,3},{3,2},{4,5},{5,4},{6,7},{7,6},{8,9},{9,8},{10,11... | collective-permute-start | bytes 393224 | tf_op jit(solution)/shard_map/ppermute | solution.py:431
  3.0 6.5 %collective-permute-start.1 = (bf16[4,128,128]{2,1,0:T(8,128)(2,1)S(1)}, bf16[4,128,128]{2,1,0:T(8,128)(2,1)S(1)}, u32[]{:S(2)}, u32[]{:S(2)}) collective-permute-start(bf16[4,128,128]{2,1,0:T(8,128)(2,1)S(1)} %get-tuple-element.39), channel_id=1, source_target_pairs={{0,2},{1,3},{2,0},{3,1},{4,6},{5,7},{6,4},{7,5},{8,10},{9,11},{10,... | collective-permute-start | bytes 393224 | tf_op jit(solution)/shard_map/ppermute | solution.py:431
  5.6 6.6 %collective-permute-start.2 = (bf16[4,128,128]{2,1,0:T(8,128)(2,1)S(1)}, bf16[4,128,128]{2,1,0:T(8,128)(2,1)S(1)}, u32[]{:S(2)}, u32[]{:S(2)}) collective-permute-start(bf16[4,128,128]{2,1,0:T(8,128)(2,1)S(1)} %get-tuple-element.40), channel_id=1, source_target_pairs={{0,3},{1,2},{2,1},{3,0},{4,7},{5,6},{6,5},{7,4},{8,11},{9,10},{10,... | collective-permute-start | bytes 393224 | tf_op jit(solution)/shard_map/ppermute | solution.py:431
  5.7 1.7 %copy-start.6 = (bf16[8,4,128,128]{3,2,1,0:T(8,128)(2,1)S(1)}, bf16[8,4,128,128]{3,2,1,0:T(8,128)(2,1)}, u32[]{:S(2)}) copy-start(bf16[8,4,128,128]{3,2,1,0:T(8,128)(2,1)} %param.18) | copy-start | bytes 3145732
  5.7 1.7 %copy-start.10 = (s32[8,4]{0,1:T(4,128)S(1)}, s32[8,4]{0,1:T(4,128)}, u32[]{:S(2)}) copy-start(s32[8,4]{0,1:T(4,128)} %param.16) | copy-start | bytes 388
  5.7 1.7 %copy-start.12 = (s32[8]{0:T(128)S(1)}, s32[8]{0:T(128)}, u32[]{:S(2)}) copy-start(s32[8]{0:T(128)} %count.1) | copy-start | bytes 100
  12.2 9.8 %copy-start = (s32[8,1024]{1,0:T(8,128)S(1)}, s32[8,1024]{1,0:T(8,128)}, u32[]{:S(2)}) copy-start(s32[8,1024]{1,0:T(8,128)} %refs_5_.1) | copy-start | bytes 98308
  12.2 9.8 %copy-start.1 = (f32[3,1024]{1,0:T(4,128)S(1)}, f32[3,1024]{1,0:T(4,128)}, u32[]{:S(2)}) copy-start(f32[3,1024]{1,0:T(4,128)} %motion.1) | copy-start | bytes 36868
  12.3 9.8 %copy-start.2 = (f32[128,6]{0,1:T(8,128)S(1)}, f32[128,6]{0,1:T(8,128)}, u32[]{:S(2)}) copy-start(f32[128,6]{0,1:T(8,128)} %param.26) | copy-start | bytes 9220
  12.3 9.8 %copy-start.3 = (f32[1024]{0:T(1024)S(1)}, f32[1024]{0:T(1024)}, u32[]{:S(2)}) copy-start(f32[1024]{0:T(1024)} %param.24) | copy-start | bytes 12292
  12.3 9.8 %copy-start.4 = (f32[128,6]{0,1:T(8,128)S(1)}, f32[128,6]{0,1:T(8,128)}, u32[]{:S(2)}) copy-start(f32[128,6]{0,1:T(8,128)} %param.27) | copy-start | bytes 9220
  12.3 9.8 %copy-start.5 = (s32[4,128]{1,0:T(4,128)S(1)}, s32[4,128]{1,0:T(4,128)}, u32[]{:S(2)}) copy-start(s32[4,128]{1,0:T(4,128)} %shared.1) | copy-start | bytes 6148
  14.0 10.9 %collective-permute-start.5 = (bf16[272,128]{1,0:T(8,128)(2,1)S(1)}, bf16[272,128]{1,0:T(8,128)(2,1)S(1)}, u32[]{:S(2)}, u32[]{:S(2)}) collective-permute-start(bf16[272,128]{1,0:T(8,128)(2,1)S(1)} %get-tuple-element.44), channel_id=1, source_target_pairs={{0,28},{4,24},{8,20},{12,16},{16,12},{20,8},{24,4},{28,0},{1,29},{... | collective-permute-start | bytes 208904 | tf_op jit(solution)/shard_map/ppermute | solution.py:495
  18.5 7.6 %collective-permute-start.6 = (bf16[272,128]{1,0:T(8,128)(2,1)S(1)}, bf16[272,128]{1,0:T(8,128)(2,1)S(1)}, u32[]{:S(2)}, u32[]{:S(2)}) collective-permute-start(bf16[272,128]{1,0:T(8,128)(2,1)S(1)} %get-tuple-element.45), channel_id=1, source_target_pairs={{0,24},{4,28},{8,16},{12,20},{16,8},{20,12},{24,0},{28,4},{1,25},{... | collective-permute-start | bytes 208904 | tf_op jit(solution)/shard_map/ppermute | solution.py:495
  18.5 10.5 %collective-permute-start.7 = (bf16[272,128]{1,0:T(8,128)(2,1)S(1)}, bf16[272,128]{1,0:T(8,128)(2,1)S(1)}, u32[]{:S(2)}, u32[]{:S(2)}) collective-permute-start(bf16[272,128]{1,0:T(8,128)(2,1)S(1)} %get-tuple-element.46), channel_id=1, source_target_pairs={{0,20},{4,16},{8,28},{12,24},{16,4},{20,0},{24,12},{28,8},{1,21},{... | collective-permute-start | bytes 208904 | tf_op jit(solution)/shard_map/ppermute | solution.py:495
  18.9 11.4 %collective-permute-start.8 = (bf16[272,128]{1,0:T(8,128)(2,1)S(1)}, bf16[272,128]{1,0:T(8,128)(2,1)S(1)}, u32[]{:S(2)}, u32[]{:S(2)}) collective-permute-start(bf16[272,128]{1,0:T(8,128)(2,1)S(1)} %get-tuple-element.47), channel_id=1, source_target_pairs={{0,16},{4,20},{8,24},{12,28},{16,0},{20,4},{24,8},{28,12},{1,17},{... | collective-permute-start | bytes 208904 | tf_op jit(solution)/shard_map/ppermute | solution.py:495
  21.0 9.3 %collective-permute-start.9 = (bf16[272,128]{1,0:T(8,128)(2,1)S(1)}, bf16[272,128]{1,0:T(8,128)(2,1)S(1)}, u32[]{:S(2)}, u32[]{:S(2)}) collective-permute-start(bf16[272,128]{1,0:T(8,128)(2,1)S(1)} %get-tuple-element.48), channel_id=1, source_target_pairs={{0,4},{4,0},{8,12},{12,8},{16,20},{20,16},{24,28},{28,24},{1,5},{5... | collective-permute-start | bytes 208904 | tf_op jit(solution)/shard_map/ppermute | solution.py:495
  24.9 7.1 %collective-permute-start.3 = (bf16[272,128]{1,0:T(8,128)(2,1)S(1)}, bf16[272,128]{1,0:T(8,128)(2,1)S(1)}, u32[]{:S(2)}, u32[]{:S(2)}) collective-permute-start(bf16[272,128]{1,0:T(8,128)(2,1)S(1)} %get-tuple-element.41), channel_id=1, source_target_pairs={{0,12},{4,8},{8,4},{12,0},{16,28},{20,24},{24,20},{28,16},{1,13},{... | collective-permute-start | bytes 208904 | tf_op jit(solution)/shard_map/ppermute | solution.py:495
  26.1 6.9 %collective-permute-start.4 = (bf16[272,128]{1,0:T(8,128)(2,1)S(1)}, bf16[272,128]{1,0:T(8,128)(2,1)S(1)}, u32[]{:S(2)}, u32[]{:S(2)}) collective-permute-start(bf16[272,128]{1,0:T(8,128)(2,1)S(1)} %get-tuple-element.42), channel_id=1, source_target_pairs={{0,8},{4,12},{8,0},{12,4},{16,24},{20,28},{24,16},{28,20},{1,9},{5... | collective-permute-start | bytes 208904 | tf_op jit(solution)/shard_map/ppermute | solution.py:495
  30.3 2.6 %copy-start.13 = (f32[128]{0:T(128)S(1)}, f32[128]{0:T(128)}, u32[]{:S(2)}) copy-start(f32[128]{0:T(128)} %param.25) | copy-start | bytes 1540
  34.2 7.2 %collective-permute-start.10 = (f32[3,128]{1,0:T(4,128)S(1)}, f32[3,128]{1,0:T(4,128)S(1)}, u32[]{:S(2)}, u32[]{:S(2)}) collective-permute-start(f32[3,128]{1,0:T(4,128)S(1)} %get-tuple-element.56), channel_id=1, source_target_pairs={{0,4},{8,12},{16,20},{24,28},{4,0},{12,8},{20,16},{28,24},{1,5},{9... | collective-permute-start | bytes 4616 | tf_op jit(solution)/shard_map/ppermute | solution.py:525
  35.1 6.3 %collective-permute-start.11 = (f32[3,128]{1,0:T(4,128)S(1)}, f32[3,128]{1,0:T(4,128)S(1)}, u32[]{:S(2)}, u32[]{:S(2)}) collective-permute-start(f32[3,128]{1,0:T(4,128)S(1)} %get-tuple-element.57), channel_id=1, source_target_pairs={{4,8},{12,16},{20,24},{0,28},{8,4},{16,12},{24,20},{28,0},{5,9},{1... | collective-permute-start | bytes 4616 | tf_op jit(solution)/shard_map/ppermute | solution.py:525
  38.4 2.9 %collective-permute-start.12 = (f32[3,128]{1,0:T(4,128)S(1)}, f32[3,128]{1,0:T(4,128)S(1)}, u32[]{:S(2)}, u32[]{:S(2)}) collective-permute-start(f32[3,128]{1,0:T(4,128)S(1)} %get-tuple-element.58), channel_id=1, source_target_pairs={{0,1},{2,3},{1,0},{3,2},{4,5},{6,7},{5,4},{7,6},{8,9},{10,11},{9,8... | collective-permute-start | bytes 4616 | tf_op jit(solution)/shard_map/ppermute | solution.py:525
  39.5 3.0 %collective-permute-start.13 = (f32[3,128]{1,0:T(4,128)S(1)}, f32[3,128]{1,0:T(4,128)S(1)}, u32[]{:S(2)}, u32[]{:S(2)}) collective-permute-start(f32[3,128]{1,0:T(4,128)S(1)} %get-tuple-element.59), channel_id=1, source_target_pairs={{1,2},{0,3},{2,1},{3,0},{5,6},{4,7},{6,5},{7,4},{9,10},{8,11},{10,... | collective-permute-start | bytes 4616 | tf_op jit(solution)/shard_map/ppermute | solution.py:525

commit v6 on v5

--- a/solution.py
+++ b/solution.py
@@ -13,7 +13,8 @@
 I32 = jnp.int32
 LANES = 128
 SUBS = 8
-POS_ROWS = 16
+META = 8
+PARTS = 16
 NOWHERE = 16.0
 TENSOR = ((0, 3, 5), (3, 1, 4), (5, 4, 2))
 NT_DIMS = (((1,), (1,)), ((), ()))
@@ -103,7 +104,7 @@
     for g in range(row_groups):
         mark_places(sorter, g, high[g : g + 1], low[g : g + 1])
     spot = owner_slot[...]
-    which = iota((POS_ROWS, rows), 0)
+    which = iota((PARTS, rows), 0)
     parts = jnp.where(which == 0, spot >> 7, jnp.where(which == 1, spot & (LANES - 1), 0))
     ordered = lax.dot_general(
         parts.astype(F32).astype(BF), sorter[...], NT_DIMS, preferred_element_type=F32
@@ -111,18 +112,29 @@
     for g in range(row_groups):
         high_rows[g : g + 1] = ordered[0:1, g * LANES : (g + 1) * LANES]
         low_rows[g : g + 1] = ordered[1:2, g * LANES : (g + 1) * LANES]
-    which = iota((POS_ROWS, LANES), 0)
-    for k in range(dom_total):
+    which = iota((META, LANES), 0)
+    far = dom_total // 2
+    extra, tag = jnp.int32(0), jnp.float32(NOWHERE)
+    for k in reversed(range(dom_total)):
         owner = me ^ k
         start = starts[owner]
         held = starts[owner + 1] - start
-        block = jnp.zeros((POS_ROWS, LANES), F32)
-        for j in range(2):
+        block = jnp.full((META, LANES), NOWHERE, F32)
+        for j in range(2 if k < far else 1):
             chunk = jnp.minimum(start // LANES + j, row_groups - 1)
             table[2 * k + j] = chunk
             high = jnp.where(held > j * LANES, high_rows[pl.ds(chunk, 1)], NOWHERE)
-            block = jnp.where(which == j, high, block)
-            block = jnp.where(which == 2 + j, low_rows[pl.ds(chunk, 1)], block)
+            block = jnp.where(which == 2 * j, high, block)
+            block = jnp.where(which == 2 * j + 1, low_rows[pl.ds(chunk, 1)], block)
+        if k >= far:
+            more = held > LANES
+            extra = jnp.where(more, jnp.minimum(start // LANES + 1, row_groups - 1), extra)
+            tag = jnp.where(more, jnp.float32(k ^ far), tag)
+        if k == far:
+            table[2 * k + 1] = extra
+            block = jnp.where(which == 2, high_rows[pl.ds(extra, 1)], block)
+            block = jnp.where(which == 3, low_rows[pl.ds(extra, 1)], block)
+            block = jnp.where(which == 4, tag, block)
         positions[k] = block.astype(BF)
 
 
@@ -245,26 +257,45 @@
     for g in range(ordered.shape[0]):
         ordered[g] = sort[g * LANES : (g + 1) * LANES].astype(BF)
     for k, out in enumerate(outs):
-        for j in range(2):
+        for j in range(2 if k <= dom_total // 2 else 1):
             out[j * LANES : (j + 1) * LANES] = ordered[table[2 * k + j]]
-        out[2 * LANES :] = positions[k]
-
-
-def place(payloads, placing, rows):
-    for k, payload in enumerate(payloads):
-        rows[k * 2 * LANES : (k + 1) * 2 * LANES] = payload[: 2 * LANES]
-        where = payload[2 * LANES :].astype(F32)
-        for j in range(2):
-            mark_places(placing, 2 * k + j, where[j : j + 1], where[2 + j : 3 + j])
+        out[out.shape[0] - META :] = positions[k]
+
+
+def pass_on(relayed, *refs):
+    count = len(refs) // 2
+    meta = relayed[2 * LANES :].astype(F32)
+    which = iota((META, LANES), 0)
+    for k, (held, out) in enumerate(zip(refs[:count], refs[count:]), 1):
+        out[2 * LANES : 3 * LANES] = relayed[LANES : 2 * LANES]
+        block = held[3 * LANES :].astype(F32)
+        block = jnp.where(which == 4, jnp.where(meta[4:5] == k, meta[2:3], NOWHERE), block)
+        block = jnp.where(which == 5, meta[3:4], block)
+        out[3 * LANES :] = block.astype(BF)
+
+
+def place(payloads, chunks, placing, rows):
+    column = 0
+    for payload, parts in zip(payloads, chunks):
+        meta = payload[payload.shape[0] - META :].astype(F32)
+        for j, tagged in parts:
+            high, low = meta[2 * j : 2 * j + 1], meta[2 * j + 1 : 2 * j + 2]
+            if tagged:
+                high = jnp.where(meta[4:5] == 0, high, NOWHERE)
+            rows[column * LANES : (column + 1) * LANES] = payload[j * LANES : (j + 1) * LANES]
+            mark_places(placing, column, high, low)
+            column += 1
     return jnp.dot(placing[...], rows[...], preferred_element_type=F32)
 
 
-def place_early(count, *refs):
+def place_early(chunks, *refs):
+    count = len(chunks)
     out, placing, rows = refs[count:]
-    out[...] = place(refs[:count], placing, rows)
-
-
-def finish(placed, count, *refs):
+    out[...] = place(refs[:count], chunks, placing, rows)
+
+
+def finish(placed, chunks, *refs):
+    count = len(chunks)
     payloads = refs[:count]
     early, base, size, connectivity, onehot, decay, readout, chosen = refs[count : count + 8]
     settled, local = refs[count + 8 : count + 10]
@@ -274,7 +305,7 @@
     if placed:
         arrived = early[...]
     else:
-        arrived = (early[...] + place(payloads, *scratch)).astype(BF)
+        arrived = (early[...] + place(payloads, chunks, *scratch)).astype(BF)
     settled[...] = arrived
     taken = readout[...] * decay[...]
     taken = jnp.concatenate([taken, jnp.zeros((SUBS - 6, LANES), F32)], axis=0)
@@ -349,7 +380,7 @@
 SMEM = pl.BlockSpec(memory_space=pltpu.SMEM)
 
 
-def call(kernel, ins, outs, scratch, args, cost=2_000_000_000, out_specs=None):
+def call(kernel, ins, outs, scratch, args, cost=2_000_000_000, out_specs=None, aliases=None):
     single = not isinstance(outs, (list, tuple))
     return pl.pallas_call(
         kernel,
@@ -357,6 +388,7 @@
         in_specs=ins,
         out_specs=out_specs or (VMEM if single else [VMEM] * len(outs)),
         scratch_shapes=scratch,
+        input_output_aliases=aliases or {},
         cost_estimate=pl.CostEstimate(flops=cost, bytes_accessed=100_000, transcendentals=0),
         compiler_params=pltpu.CompilerParams(vmem_limit_bytes=24 * 1024 * 1024),
     )(*args)
@@ -456,7 +488,7 @@
             sort_rows, [VMEM, VMEM],
             [
                 arrays((rows, rows), BF),
-                arrays((dom_total, POS_ROWS, LANES), BF),
+                arrays((dom_total, META, LANES), BF),
                 arrays((2 * dom_total,), I32),
             ],
             [
@@ -478,42 +510,58 @@
             (entry_slot.T, entry_count, flat_weights),
             out_specs=[VMEM, VMEM, SMEM],
         )
-        payload = arrays((2 * usual + POS_ROWS, width), BF)
-        outgoing = call(
-            project_rows, [SMEM, SMEM] + [VMEM] * (4 + box_total),
-            [payload] * dom_total,
-            [
-                pltpu.VMEM((box_total * capacity, width, block_size), BF),
-                pltpu.VMEM((width, rows), BF),
-                pltpu.VMEM((row_groups, LANES, width), BF),
-            ],
-            (table, block_of, masked, mass_inv, sorter, positions, *received),
-        )
         far = dom_total // 2
+        lengths = [2] + [3] * (far - 1) + [2] + [1] * (far - 1)
+        outgoing = list(
+            call(
+                project_rows, [SMEM, SMEM] + [VMEM] * (4 + box_total),
+                [arrays((n * LANES + META, width), BF) for n in lengths],
+                [
+                    pltpu.VMEM((box_total * capacity, width, block_size), BF),
+                    pltpu.VMEM((width, rows), BF),
+                    pltpu.VMEM((row_groups, LANES, width), BF),
+                ],
+                (table, block_of, masked, mass_inv, sorter, positions, *received),
+            )
+        )
         payloads = {0: outgoing[0]}
-        for k in range(1, dom_total):
+
+        def swap(k):
             payloads[k] = lax.ppermute(outgoing[k], "dom", [(i, i ^ k) for i in range(dom_total)])
-        soon = [0, *range(dom_total - 1, far - 1, -1), 1]
-        late = [payloads[k] for k in range(far - 1, 1, -1)]
-
-        def placing(count):
-            return [
-                pltpu.VMEM((elements, count * 2 * usual), BF),
-                pltpu.VMEM((count * 2 * usual, width), BF),
-            ]
-
+
+        for k in range(far, dom_total):
+            swap(k)
+        near = list(range(1, far))
+        outgoing[1:far] = call(
+            pass_on, [VMEM] * far, [arrays(outgoing[k].shape, BF) for k in near], [],
+            (payloads[far], *outgoing[1:far]), cost=1000, aliases={k: k - 1 for k in near},
+        )
+        for k in near:
+            swap(k)
+        parts = [[(0, False), (1, False)]] + [[(0, False), (1, False), (2, False)]] * (far - 1)
+        parts += [[(0, False), (1, True)]] + [[(0, False)]] * (far - 1)
+        soon = [0, *range(far, dom_total), 1]
+        last = list(range(far - 1, 1, -1))
+        late = [payloads[k] for k in last]
+        chunks = [parts[k] for k in last]
+
+        def placing(chosen):
+            total = LANES * sum(len(part) for part in chosen)
+            return [pltpu.VMEM((elements, total), BF), pltpu.VMEM((total, width), BF)]
+
+        first = [parts[k] for k in soon]
         early = call(
-            functools.partial(place_early, len(soon)), [VMEM] * len(soon),
-            arrays((elements, width), F32), placing(len(soon)), [payloads[k] for k in soon],
-        )
-        placed, scratch = False, placing(len(late))
+            functools.partial(place_early, first), [VMEM] * len(soon),
+            arrays((elements, width), F32), placing(first), [payloads[k] for k in soon],
+        )
+        placed, scratch = False, placing(chunks)
     else:
         early = spread_rows(received, entry_slot, entry_count, weights, owner_route, owner_slot)
-        late = []
+        late, chunks = [], []
         placed, scratch = True, []
     export = arrays((3, shared_nodes.shape[1]), F32)
     arrived, local, *exports = call(
-        functools.partial(finish, placed, len(late)),
+        functools.partial(finish, placed, chunks),
         [VMEM] * (len(late) + 8),
         [arrays((elements, width), BF), arrays((3, nodes // LANES, LANES), F32)] + [export] * 4,
         scratch,

time: 43.3 us -> 47.4 us (1.095)
  the two profiles are of different devices: /device:TPU:1 before, /device:TPU:0 now
where the time goes in v6:
time: 47.4 us; the launch traced here: 47.3 us
  starting transfers between devices  21.2 us (45%)
  Pallas kernels  12 us (25%)
  waiting for transfers between devices  11.6 us (24%)
  local copies, waits for them, and re-layouts  1.65 us (3%)
  between operations  0.8 us (2%)
    ppermute x7, starting transfers between devices, swap(): lax.ppermute(outgoing[k], 'dom', [(i, i ^ k) for i in range(dom_total)])  12.2 us
    pallas_call x10, Pallas kernels, call(): pl.pallas_call(kernel, out_shape=outs, in_specs=ins, out_specs=out_specs...  12 us
    ppermute x7, waiting for transfers between devices, swap(): lax.ppermute(outgoing[k], 'dom', [(i, i ^ k) for i in range(dom_total)])  6.87 us
    ppermute x4, starting transfers between devices, body(): halo[m] = lax.ppermute(exports[m], axis, swaps(axis, first))  5.84 us
    ppermute x3, waiting for transfers between devices, body(): lax.ppermute(packed[k], 'box', [(i, i ^ k) for i in range(box_total)])  3.47 us
    ppermute x3, starting transfers between devices, body(): lax.ppermute(packed[k], 'box', [(i, i ^ k) for i in range(box_total)])  3.15 us
    unnamed x28, local copies, waits for them, and re-layouts  1.65 us
    ppermute x4, waiting for transfers between devices, body(): halo[m] = lax.ppermute(exports[m], axis, swaps(axis, first))  1.25 us
  transfers between devices with their start and end apart: 14, of which 6 were waited for; matrix products, arithmetic and copies ran while one was open for 0% of the time, Pallas kernels for 16%

profile of v6, /device:TPU:0, one launch (start us, length us, event | category | flops | bytes accessed | tf_op | source)
XLA Modules:
  0.0 47.3 jit_solution(5512393872568673160)
XLA Ops:
  0.6 0.9 %copy-done.7 = bf16[8,128,128]{2,1,0:T(8,128)(2,1)S(1)} copy-done((bf16[8,128,128]{2,1,0:T(8,128)(2,1)S(1)}, bf16[8,128,128]{2,1,0:T(8,128)(2,1)}, u32[]{:S(2)}) %copy-start.7) | copy-done | bytes 262168
  1.6 0.7 %copy-done.11 = s32[8]{0:T(128)S(1)} copy-done((s32[8]{0:T(128)S(1)}, s32[8]{0:T(128)}, u32[]{:S(2)}) %copy-start.11) | copy-done | bytes 56
  2.2 0.6 %shard_map.151 = (bf16[4,128,128]{2,1,0:T(8,128)(2,1)S(1)}, bf16[4,128,128]{2,1,0:T(8,128)(2,1)S(1)}, bf16[4,128,128]{2,1,0:T(8,128)(2,1)S(1)}, bf16[4,128,128]{2,1,0:T(8,128)(2,1)S(1)}) custom-call(s32[8]{0:T(128)S(1)} %copy-done.11, bf16[8,128,128]{2,1,0:T(8,128)(2,1)S(1)} %copy-done.7), custom_call_target="tpu_custom_call" | custom-call | flops 2000000000 | bytes 100000 | tf_op jit(solution)/shard_map/pallas_call | solution.py:385
  2.9 0.6 %collective-permute-start = (bf16[4,128,128]{2,1,0:T(8,128)(2,1)S(1)}, bf16[4,128,128]{2,1,0:T(8,128)(2,1)S(1)}, u32[]{:S(2)}, u32[]{:S(2)}) collective-permute-start(bf16[4,128,128]{2,1,0:T(8,128)(2,1)S(1)} %get-tuple-element.41), channel_id=1, source_target_pairs={{0,1},{1,0},{2,3},{3,2},{4,5},{5,4},{6,7},{7,6},{8,9},{9,8},{10,11... | collective-permute-start | bytes 393224 | tf_op jit(solution)/shard_map/ppermute | solution.py:463
  3.4 2.6 %collective-permute-start.1 = (bf16[4,128,128]{2,1,0:T(8,128)(2,1)S(1)}, bf16[4,128,128]{2,1,0:T(8,128)(2,1)S(1)}, u32[]{:S(2)}, u32[]{:S(2)}) collective-permute-start(bf16[4,128,128]{2,1,0:T(8,128)(2,1)S(1)} %get-tuple-element.42), channel_id=1, source_target_pairs={{0,2},{1,3},{2,0},{3,1},{4,6},{5,7},{6,4},{7,5},{8,10},{9,11},{10,... | collective-permute-start | bytes 393224 | tf_op jit(solution)/shard_map/ppermute | solution.py:463
  6.0 0.0 collective-permute-start.2
  6.0 0.0 copy-start.12
  6.1 1.6 %shard_map.149 = (bf16[1024,1024]{1,0:T(8,128)(2,1)S(1)}, bf16[8,8,128]{2,1,0:T(8,128)(2,1)S(1)}, s32[16]{0:T(128)S(1)}) custom-call(s32[8,128]{1,0:T(8,128)S(1)} %bitcast.14, s32[1,1024]{1,0:T(1,128)S(1)} %bitcast.15), custom_call_target="tpu_custom_call" | custom-call | flops 2000000000 | bytes 100000 | tf_op jit(solution)/shard_map/pallas_call | solution.py:385
  7.7 1.4 %shard_map.150 = (bf16[8,512,128]{2,1,0:T(8,128)(2,1)S(1)}, f32[8,128]{1,0:T(8,128)S(1)}, s32[32]{0:T(128)S(1)}) custom-call(s32[4,8]{1,0:T(4,128)S(1)} %bitcast.16, s32[8]{0:T(128)S(1)} %copy-done.12, bf16[8,512,128]{2,1,0:T(8,128)(2,1)S(1)} %bitcast.13), custom_call_target="tpu_custom_call" | custom-call | flops 2000000000 | bytes 100000 | tf_op jit(solution)/shard_map/pallas_call | solution.py:385
  9.2 1.2 %collective-permute-done.1.rest_2_ = bf16[4,128,128]{2,1,0:T(8,128)(2,1)S(1)} collective-permute-done((bf16[4,128,128]{2,1,0:T(8,128)(2,1)S(1)}, bf16[4,128,128]{2,1,0:T(8,128)(2,1)S(1)}, u32[]{:S(2)}, u32[]{:S(2)}) %collective-permute-start.1) | collective-permute-done | bytes 131104 | tf_op jit(solution)/shard_map/ppermute | solution.py:463
  10.3 2.3 %collective-permute-done.2.rest_3_ = bf16[4,128,128]{2,1,0:T(8,128)(2,1)S(1)} collective-permute-done((bf16[4,128,128]{2,1,0:T(8,128)(2,1)S(1)}, bf16[4,128,128]{2,1,0:T(8,128)(2,1)S(1)}, u32[]{:S(2)}, u32[]{:S(2)}) %collective-permute-start.2) | collective-permute-done | bytes 131104 | tf_op jit(solution)/shard_map/ppermute | solution.py:463
  12.6 0.0 copy-start.5
  12.7 1.7 %shard_map.152 = (bf16[264,128]{1,0:T(8,128)(2,1)S(1)}, bf16[392,128]{1,0:T(8,128)(2,1)S(1)}, bf16[392,128]{1,0:T(8,128)(2,1)S(1)}, bf16[392,128]{1,0:T(8,128)(2...) custom-call(s32[16]{0:T(128)S(1)} %get-tuple-element.34.table, ...), custom_call_target="tpu_custom_call" | custom-call | flops 2000000000 | bytes 100000 | tf_op jit(solution)/shard_map/pallas_call | solution.py:385
  14.3 2.6 %collective-permute-start.3 = (bf16[264,128]{1,0:T(8,128)(2,1)S(1)}, bf16[264,128]{1,0:T(8,128)(2,1)S(1)}, u32[]{:S(2)}, u32[]{:S(2)}) collective-permute-start(bf16[264,128]{1,0:T(8,128)(2,1)S(1)} %get-tuple-element.44), channel_id=1, source_target_pairs={{0,16},{4,20},{8,24},{12,28},{16,0},{20,4},{24,8},{28,12},{1,17},{... | collective-permute-start | bytes 202760 | tf_op jit(solution)/shard_map/ppermute | solution.py:530
  17.0 4.1 %collective-permute-done.3.relayed.refs_1_ = bf16[264,128]{1,0:T(8,128)(2,1)S(1)} collective-permute-done((bf16[264,128]{1,0:T(8,128)(2,1)S(1)}, bf16[264,128]{1,0:T(8,128)(2,1)S(1)}, u32[]{:S(2)}, u32[]{:S(2)}) %collective-permute-start.3) | collective-permute-done | bytes 67616 | tf_op jit(solution)/shard_map/ppermute | solution.py:530
  21.1 1.6 %collective-permute-start.9 = (bf16[392,128]{1,0:T(8,128)(2,1)S(1)}, bf16[392,128]{1,0:T(8,128)(2,1)S(1)}, u32[]{:S(2)}, u32[]{:S(2)}) collective-permute-start(bf16[392,128]{1,0:T(8,128)(2,1)S(1)} %get-tuple-element.54), channel_id=1, source_target_pairs={{0,4},{4,0},{8,12},{12,8},{16,20},{20,16},{24,28},{28,24},{1,5},{5... | collective-permute-start | bytes 301064 | tf_op jit(solution)/shard_map/ppermute | solution.py:530
  22.7 1.2 %collective-permute-start.6 = (bf16[136,128]{1,0:T(8,128)(2,1)S(1)}, bf16[136,128]{1,0:T(8,128)(2,1)S(1)}, u32[]{:S(2)}, u32[]{:S(2)}) collective-permute-start(bf16[136,128]{1,0:T(8,128)(2,1)S(1)} %get-tuple-element.51), channel_id=1, source_target_pairs={{0,20},{4,16},{8,28},{12,24},{16,4},{20,0},{24,12},{28,8},{1,21},{... | collective-permute-start | bytes 104456 | tf_op jit(solution)/shard_map/ppermute | solution.py:530
  23.9 2.3 %collective-permute-start.7 = (bf16[136,128]{1,0:T(8,128)(2,1)S(1)}, bf16[136,128]{1,0:T(8,128)(2,1)S(1)}, u32[]{:S(2)}, u32[]{:S(2)}) collective-permute-start(bf16[136,128]{1,0:T(8,128)(2,1)S(1)} %get-tuple-element.52), channel_id=1, source_target_pairs={{0,24},{4,28},{8,16},{12,20},{16,8},{20,12},{24,0},{28,4},{1,25},{... | collective-permute-start | bytes 104456 | tf_op jit(solution)/shard_map/ppermute | solution.py:530
  26.2 2.5 %collective-permute-start.8 = (bf16[136,128]{1,0:T(8,128)(2,1)S(1)}, bf16[136,128]{1,0:T(8,128)(2,1)S(1)}, u32[]{:S(2)}, u32[]{:S(2)}) collective-permute-start(bf16[136,128]{1,0:T(8,128)(2,1)S(1)} %get-tuple-element.53), channel_id=1, source_target_pairs={{0,28},{4,24},{8,20},{12,16},{16,12},{20,8},{24,4},{28,0},{1,29},{... | collective-permute-start | bytes 104456 | tf_op jit(solution)/shard_map/ppermute | solution.py:530
  28.7 2.8 %shard_map.155 = (f32[1024,128]{1,0:T(8,128)S(1)}, f32[8,1024]{1,0:T(8,128)S(1)}, bf16[8,1024,128]{2,1,0:T(8,128)(2,1)S(1)}, s32[8,128]{1,0:T(8,128)S(1)}, s32[2,8,128]{2,1,0:T(8,128)S(1)}) custom-call(s32[8,1024]{1,0:T(8,128)S(1)} %copy-done, f32[3,1024]{1,0:T(4,128)S(1)} %copy-done.1, f32[1,1024]{1,0:T(1,128)S(1)} %bitcast.9, f32[6,128]{1,0:T(8,128)S(1)} %bitcast.8, ...), custom_call_target="tpu_custom_call" | custom-call | flops 1000 | bytes 100000 | tf_op jit(solution)/shard_map/pallas_call | solution.py:385
  31.5 1.0 %collective-permute-start.4 = (bf16[392,128]{1,0:T(8,128)(2,1)S(1)}, bf16[392,128]{1,0:T(8,128)(2,1)S(1)}, u32[]{:S(2)}, u32[]{:S(2)}) collective-permute-start(bf16[392,128]{1,0:T(8,128)(2,1)S(1)} %get-tuple-element.48), channel_id=1, source_target_pairs={{0,12},{4,8},{8,4},{12,0},{16,28},{20,24},{24,20},{28,16},{1,13},{... | collective-permute-start | bytes 301064 | tf_op jit(solution)/shard_map/ppermute | solution.py:530
  32.5 1.0 %collective-permute-start.5 = (bf16[392,128]{1,0:T(8,128)(2,1)S(1)}, bf16[392,128]{1,0:T(8,128)(2,1)S(1)}, u32[]{:S(2)}, u32[]{:S(2)}) collective-permute-start(bf16[392,128]{1,0:T(8,128)(2,1)S(1)} %get-tuple-element.49), channel_id=1, source_target_pairs={{0,8},{4,12},{8,0},{12,4},{16,24},{20,28},{24,16},{28,20},{1,9},{5... | collective-permute-start | bytes 301064 | tf_op jit(solution)/shard_map/ppermute | solution.py:530
  33.5 0.9 %shard_map.154.refs_2_ = f32[1024,128]{1,0:T(8,128)S(1)} custom-call(bf16[264,128]{1,0:T(8,128)(2,1)S(1)} %get-tuple-element.50.refs_0_, bf16[264,128]{1,0:T(8,128)(2,1)S(1)} %collective-permute-done.3.relayed.refs_1_, bf16[136,128]{1,0:T(8,128)(2,1)S(1)} %collective-permute-done.6.refs_2_, bf16[136,128]{1,0:T(8,128)(2,1)S(1)} %collective-permute-done.7.refs_3_, ...), custom_call_target="tpu_custom_call" | custom-call | flops 2000000000 | bytes 100000 | tf_op jit(solution)/shard_map/pallas_call | solution.py:385
  34.4 2.6 %collective-permute-done.4.refs_0_ = bf16[392,128]{1,0:T(8,128)(2,1)S(1)} collective-permute-done((bf16[392,128]{1,0:T(8,128)(2,1)S(1)}, bf16[392,128]{1,0:T(8,128)(2,1)S(1)}, u32[]{:S(2)}, u32[]{:S(2)}) %collective-permute-start.4) | collective-permute-done | bytes 100384 | tf_op jit(solution)/shard_map/ppermute | solution.py:530
  37.1 0.1 collective-permute-done.5.refs_1_
  37.2 1.5 %shard_map.156 = (bf16[1024,128]{1,0:T(8,128)(2,1)S(1)}, f32[3,8,128]{2,1,0:T(8,128)S(1)}, f32[3,128]{1,0:T(4,128)S(1)}, f32[3,128]{1,0:T(4,128)S(1)}, f32[3,128]{1,0:T(4,128)S(1)}, /*index=5*/f32[3,128]{1,0:T(4,128)S(1)}) custom-call(bf16[392,128]{1,0:T(8,128)(2,1)S(1)} %collective-permute-done.4.refs_0_, ...), custom_call_target="tpu_custom_call" | custom-call | flops 2000000000 | bytes 100000 | tf_op jit(solution)/shard_map/pallas_call | solution.py:385
  38.7 1.6 %collective-permute-start.10 = (f32[3,128]{1,0:T(4,128)S(1)}, f32[3,128]{1,0:T(4,128)S(1)}, u32[]{:S(2)}, u32[]{:S(2)}) collective-permute-start(f32[3,128]{1,0:T(4,128)S(1)} %get-tuple-element.62), channel_id=1, source_target_pairs={{0,4},{8,12},{16,20},{24,28},{4,0},{12,8},{20,16},{28,24},{1,5},{9... | collective-permute-start | bytes 4616 | tf_op jit(solution)/shard_map/ppermute | solution.py:573
  40.3 2.6 %collective-permute-start.11 = (f32[3,128]{1,0:T(4,128)S(1)}, f32[3,128]{1,0:T(4,128)S(1)}, u32[]{:S(2)}, u32[]{:S(2)}) collective-permute-start(f32[3,128]{1,0:T(4,128)S(1)} %get-tuple-element.63), channel_id=1, source_target_pairs={{4,8},{12,16},{20,24},{0,28},{8,4},{16,12},{24,20},{28,0},{5,9},{1... | collective-permute-start | bytes 4616 | tf_op jit(solution)/shard_map/ppermute | solution.py:573
  42.9 1.6 %collective-permute-start.13 = (f32[3,128]{1,0:T(4,128)S(1)}, f32[3,128]{1,0:T(4,128)S(1)}, u32[]{:S(2)}, u32[]{:S(2)}) collective-permute-start(f32[3,128]{1,0:T(4,128)S(1)} %get-tuple-element.65), channel_id=1, source_target_pairs={{1,2},{0,3},{2,1},{3,0},{5,6},{4,7},{6,5},{7,4},{9,10},{8,11},{10,... | collective-permute-start | bytes 4616 | tf_op jit(solution)/shard_map/ppermute | solution.py:573
  44.5 0.8 %shard_map.157 = bf16[1024,128]{1,0:T(8,128)(2,1)} custom-call(bf16[1024,128]{1,0:T(8,128)(2,1)S(1)} %get-tuple-element.58.arrived, f32[1024,128]{1,0:T(8,128)S(1)} %get-tuple-element.59.drive, f32[1,128]{1,0:T(1,128)S(1)} %bitcast.18), custom_call_target="tpu_custom_call" | custom-call | flops 2000000000 | bytes 100000 | tf_op jit(solution)/shard_map/pallas_call | solution.py:385
  45.3 1.2 %collective-permute-done.11.rest_1_ = f32[3,128]{1,0:T(4,128)S(1)} collective-permute-done((f32[3,128]{1,0:T(4,128)S(1)}, f32[3,128]{1,0:T(4,128)S(1)}, u32[]{:S(2)}, u32[]{:S(2)}) %collective-permute-start.11) | collective-permute-done | bytes 1568 | tf_op jit(solution)/shard_map/ppermute | solution.py:573
  46.6 0.7 %shard_map.158 = f32[3,1024]{1,0:T(4,128)} custom-call(f32[3,8,128]{2,1,0:T(8,128)S(1)} %get-tuple-element.60.local, s32[2,8,128]{2,1,0:T(8,128)S(1)} %get-tuple-element.61.inverse, f32[3,128]{1,0:T(4,128)S(1)} %collective-permute-done.10.rest_0_, f32[3,128]{1,0:T(4,128)S(1)} %collective-permute-done.11.rest_1_, ...), custom_call_target="tpu_custom_call" | custom-call | flops 2000000000 | bytes 100000 | tf_op jit(solution)/shard_map/pallas_call | solution.py:385
  (34 shorter events, 0.1 us)
Async XLA Ops:
  0.6 1.0 %copy-start.7 = (bf16[8,128,128]{2,1,0:T(8,128)(2,1)S(1)}, bf16[8,128,128]{2,1,0:T(8,128)(2,1)}, u32[]{:S(2)}) copy-start(bf16[8,128,128]{2,1,0:T(8,128)(2,1)} %old.1) | copy-start | bytes 786436
  1.6 0.7 %copy-start.11 = (s32[8]{0:T(128)S(1)}, s32[8]{0:T(128)}, u32[]{:S(2)}) copy-start(s32[8]{0:T(128)} %route.1) | copy-start | bytes 100
  2.2 3.8 %copy-start.8 = (s32[1024]{0:T(1024)S(1)}, s32[1024]{0:T(1024)}, u32[]{:S(2)}) copy-start(s32[1024]{0:T(1024)} %param.19) | copy-start | bytes 12292
  2.2 3.8 %copy-start.9 = (s32[1024]{0:T(1024)S(1)}, s32[1024]{0:T(1024)}, u32[]{:S(2)}) copy-start(s32[1024]{0:T(1024)} %param.20) | copy-start | bytes 12292
  2.9 6.3 %collective-permute-start = (bf16[4,128,128]{2,1,0:T(8,128)(2,1)S(1)}, bf16[4,128,128]{2,1,0:T(8,128)(2,1)S(1)}, u32[]{:S(2)}, u32[]{:S(2)}) collective-permute-start(bf16[4,128,128]{2,1,0:T(8,128)(2,1)S(1)} %get-tuple-element.41), channel_id=1, source_target_pairs={{0,1},{1,0},{2,3},{3,2},{4,5},{5,4},{6,7},{7,6},{8,9},{9,8},{10,11... | collective-permute-start | bytes 393224 | tf_op jit(solution)/shard_map/ppermute | solution.py:463
  3.4 6.9 %collective-permute-start.1 = (bf16[4,128,128]{2,1,0:T(8,128)(2,1)S(1)}, bf16[4,128,128]{2,1,0:T(8,128)(2,1)S(1)}, u32[]{:S(2)}, u32[]{:S(2)}) collective-permute-start(bf16[4,128,128]{2,1,0:T(8,128)(2,1)S(1)} %get-tuple-element.42), channel_id=1, source_target_pairs={{0,2},{1,3},{2,0},{3,1},{4,6},{5,7},{6,4},{7,5},{8,10},{9,11},{10,... | collective-permute-start | bytes 393224 | tf_op jit(solution)/shard_map/ppermute | solution.py:463
  6.0 6.6 %collective-permute-start.2 = (bf16[4,128,128]{2,1,0:T(8,128)(2,1)S(1)}, bf16[4,128,128]{2,1,0:T(8,128)(2,1)S(1)}, u32[]{:S(2)}, u32[]{:S(2)}) collective-permute-start(bf16[4,128,128]{2,1,0:T(8,128)(2,1)S(1)} %get-tuple-element.43), channel_id=1, source_target_pairs={{0,3},{1,2},{2,1},{3,0},{4,7},{5,6},{6,5},{7,4},{8,11},{9,10},{10,... | collective-permute-start | bytes 393224 | tf_op jit(solution)/shard_map/ppermute | solution.py:463
  6.0 1.7 %copy-start.6 = (bf16[8,4,128,128]{3,2,1,0:T(8,128)(2,1)S(1)}, bf16[8,4,128,128]{3,2,1,0:T(8,128)(2,1)}, u32[]{:S(2)}) copy-start(bf16[8,4,128,128]{3,2,1,0:T(8,128)(2,1)} %param.18) | copy-start | bytes 3145732
  6.0 1.7 %copy-start.10 = (s32[8,4]{0,1:T(4,128)S(1)}, s32[8,4]{0,1:T(4,128)}, u32[]{:S(2)}) copy-start(s32[8,4]{0,1:T(4,128)} %param.16) | copy-start | bytes 388
  6.0 1.7 %copy-start.12 = (s32[8]{0:T(128)S(1)}, s32[8]{0:T(128)}, u32[]{:S(2)}) copy-start(s32[8]{0:T(128)} %count.1) | copy-start | bytes 100
  12.6 16.1 %copy-start = (s32[8,1024]{1,0:T(8,128)S(1)}, s32[8,1024]{1,0:T(8,128)}, u32[]{:S(2)}) copy-start(s32[8,1024]{1,0:T(8,128)} %refs_5_.1) | copy-start | bytes 98308
  12.6 16.1 %copy-start.1 = (f32[3,1024]{1,0:T(4,128)S(1)}, f32[3,1024]{1,0:T(4,128)}, u32[]{:S(2)}) copy-start(f32[3,1024]{1,0:T(4,128)} %motion.1) | copy-start | bytes 36868
  12.6 16.1 %copy-start.2 = (f32[128,6]{0,1:T(8,128)S(1)}, f32[128,6]{0,1:T(8,128)}, u32[]{:S(2)}) copy-start(f32[128,6]{0,1:T(8,128)} %param.26) | copy-start | bytes 9220
  12.6 16.1 %copy-start.3 = (f32[1024]{0:T(1024)S(1)}, f32[1024]{0:T(1024)}, u32[]{:S(2)}) copy-start(f32[1024]{0:T(1024)} %param.24) | copy-start | bytes 12292
  12.6 16.1 %copy-start.4 = (f32[128,6]{0,1:T(8,128)S(1)}, f32[128,6]{0,1:T(8,128)}, u32[]{:S(2)}) copy-start(f32[128,6]{0,1:T(8,128)} %param.27) | copy-start | bytes 9220
  12.6 16.1 %copy-start.5 = (s32[4,128]{1,0:T(4,128)S(1)}, s32[4,128]{1,0:T(4,128)}, u32[]{:S(2)}) copy-start(s32[4,128]{1,0:T(4,128)} %shared.1) | copy-start | bytes 6148
  14.3 6.7 %collective-permute-start.3 = (bf16[264,128]{1,0:T(8,128)(2,1)S(1)}, bf16[264,128]{1,0:T(8,128)(2,1)S(1)}, u32[]{:S(2)}, u32[]{:S(2)}) collective-permute-start(bf16[264,128]{1,0:T(8,128)(2,1)S(1)} %get-tuple-element.44), channel_id=1, source_target_pairs={{0,16},{4,20},{8,24},{12,28},{16,0},{20,4},{24,8},{28,12},{1,17},{... | collective-permute-start | bytes 202760 | tf_op jit(solution)/shard_map/ppermute | solution.py:530
  21.1 12.4 %collective-permute-start.9 = (bf16[392,128]{1,0:T(8,128)(2,1)S(1)}, bf16[392,128]{1,0:T(8,128)(2,1)S(1)}, u32[]{:S(2)}, u32[]{:S(2)}) collective-permute-start(bf16[392,128]{1,0:T(8,128)(2,1)S(1)} %get-tuple-element.54), channel_id=1, source_target_pairs={{0,4},{4,0},{8,12},{12,8},{16,20},{20,16},{24,28},{28,24},{1,5},{5... | collective-permute-start | bytes 301064 | tf_op jit(solution)/shard_map/ppermute | solution.py:530
  22.7 9.7 %collective-permute-start.6 = (bf16[136,128]{1,0:T(8,128)(2,1)S(1)}, bf16[136,128]{1,0:T(8,128)(2,1)S(1)}, u32[]{:S(2)}, u32[]{:S(2)}) collective-permute-start(bf16[136,128]{1,0:T(8,128)(2,1)S(1)} %get-tuple-element.51), channel_id=1, source_target_pairs={{0,20},{4,16},{8,28},{12,24},{16,4},{20,0},{24,12},{28,8},{1,21},{... | collective-permute-start | bytes 104456 | tf_op jit(solution)/shard_map/ppermute | solution.py:530
  23.9 9.6 %collective-permute-start.7 = (bf16[136,128]{1,0:T(8,128)(2,1)S(1)}, bf16[136,128]{1,0:T(8,128)(2,1)S(1)}, u32[]{:S(2)}, u32[]{:S(2)}) collective-permute-start(bf16[136,128]{1,0:T(8,128)(2,1)S(1)} %get-tuple-element.52), channel_id=1, source_target_pairs={{0,24},{4,28},{8,16},{12,20},{16,8},{20,12},{24,0},{28,4},{1,25},{... | collective-permute-start | bytes 104456 | tf_op jit(solution)/shard_map/ppermute | solution.py:530
  26.2 7.3 %collective-permute-start.8 = (bf16[136,128]{1,0:T(8,128)(2,1)S(1)}, bf16[136,128]{1,0:T(8,128)(2,1)S(1)}, u32[]{:S(2)}, u32[]{:S(2)}) collective-permute-start(bf16[136,128]{1,0:T(8,128)(2,1)S(1)} %get-tuple-element.53), channel_id=1, source_target_pairs={{0,28},{4,24},{8,20},{12,16},{16,12},{20,8},{24,4},{28,0},{1,29},{... | collective-permute-start | bytes 104456 | tf_op jit(solution)/shard_map/ppermute | solution.py:530
  31.5 5.6 %collective-permute-start.4 = (bf16[392,128]{1,0:T(8,128)(2,1)S(1)}, bf16[392,128]{1,0:T(8,128)(2,1)S(1)}, u32[]{:S(2)}, u32[]{:S(2)}) collective-permute-start(bf16[392,128]{1,0:T(8,128)(2,1)S(1)} %get-tuple-element.48), channel_id=1, source_target_pairs={{0,12},{4,8},{8,4},{12,0},{16,28},{20,24},{24,20},{28,16},{1,13},{... | collective-permute-start | bytes 301064 | tf_op jit(solution)/shard_map/ppermute | solution.py:530
  32.5 4.7 %collective-permute-start.5 = (bf16[392,128]{1,0:T(8,128)(2,1)S(1)}, bf16[392,128]{1,0:T(8,128)(2,1)S(1)}, u32[]{:S(2)}, u32[]{:S(2)}) collective-permute-start(bf16[392,128]{1,0:T(8,128)(2,1)S(1)} %get-tuple-element.49), channel_id=1, source_target_pairs={{0,8},{4,12},{8,0},{12,4},{16,24},{20,28},{24,16},{28,20},{1,9},{5... | collective-permute-start | bytes 301064 | tf_op jit(solution)/shard_map/ppermute | solution.py:530
  33.5 3.7 %copy-start.13 = (f32[128]{0:T(128)S(1)}, f32[128]{0:T(128)}, u32[]{:S(2)}) copy-start(f32[128]{0:T(128)} %param.25) | copy-start | bytes 1540
  38.7 6.6 %collective-permute-start.10 = (f32[3,128]{1,0:T(4,128)S(1)}, f32[3,128]{1,0:T(4,128)S(1)}, u32[]{:S(2)}, u32[]{:S(2)}) collective-permute-start(f32[3,128]{1,0:T(4,128)S(1)} %get-tuple-element.62), channel_id=1, source_target_pairs={{0,4},{8,12},{16,20},{24,28},{4,0},{12,8},{20,16},{28,24},{1,5},{9... | collective-permute-start | bytes 4616 | tf_op jit(solution)/shard_map/ppermute | solution.py:573
  40.3 6.3 %collective-permute-start.11 = (f32[3,128]{1,0:T(4,128)S(1)}, f32[3,128]{1,0:T(4,128)S(1)}, u32[]{:S(2)}, u32[]{:S(2)}) collective-permute-start(f32[3,128]{1,0:T(4,128)S(1)} %get-tuple-element.63), channel_id=1, source_target_pairs={{4,8},{12,16},{20,24},{0,28},{8,4},{16,12},{24,20},{28,0},{5,9},{1... | collective-permute-start | bytes 4616 | tf_op jit(solution)/shard_map/ppermute | solution.py:573
  42.9 3.6 %collective-permute-start.12 = (f32[3,128]{1,0:T(4,128)S(1)}, f32[3,128]{1,0:T(4,128)S(1)}, u32[]{:S(2)}, u32[]{:S(2)}) collective-permute-start(f32[3,128]{1,0:T(4,128)S(1)} %get-tuple-element.64), channel_id=1, source_target_pairs={{0,1},{2,3},{1,0},{3,2},{4,5},{6,7},{5,4},{7,6},{8,9},{10,11},{9,8... | collective-permute-start | bytes 4616 | tf_op jit(solution)/shard_map/ppermute | solution.py:573
  42.9 3.6 %collective-permute-start.13 = (f32[3,128]{1,0:T(4,128)S(1)}, f32[3,128]{1,0:T(4,128)S(1)}, u32[]{:S(2)}, u32[]{:S(2)}) collective-permute-start(f32[3,128]{1,0:T(4,128)S(1)} %get-tuple-element.65), channel_id=1, source_target_pairs={{1,2},{0,3},{2,1},{3,0},{5,6},{4,7},{6,5},{7,4},{9,10},{8,11},{10,... | collective-permute-start | bytes 4616 | tf_op jit(solution)/shard_map/ppermute | solution.py:573

commit v7 on v5

--- a/solution.py
+++ b/solution.py
@@ -13,7 +13,8 @@
 I32 = jnp.int32
 LANES = 128
 SUBS = 8
-POS_ROWS = 16
+META = 8
+PARTS = 16
 NOWHERE = 16.0
 TENSOR = ((0, 3, 5), (3, 1, 4), (5, 4, 2))
 NT_DIMS = (((1,), (1,)), ((), ()))
@@ -51,8 +52,14 @@
     return out
 
 
-def pack_blocks(route, old, *rest):
-    outs, table = rest[:-1], rest[-1]
+def pack_blocks(route_hbm, old_hbm, *rest):
+    outs = rest[:-4]
+    table, route, old, sems = rest[-4:]
+    find = pltpu.make_async_copy(route_hbm, route, sems.at[0])
+    take = pltpu.make_async_copy(old_hbm, old, sems.at[1])
+    find.start()
+    take.start()
+    find.wait()
     me = lax.axis_index("box")
     capacity = outs[0].shape[0]
     for m in range(len(outs) * capacity):
@@ -63,6 +70,7 @@
         for earlier in routes[:i]:
             order = order + (earlier == target).astype(I32)
         table[(target ^ me) * capacity + order] = i
+    take.wait()
     for k, out in enumerate(outs):
         for s in range(capacity):
             out[s] = old[table[k * capacity + s]]
@@ -103,7 +111,7 @@
     for g in range(row_groups):
         mark_places(sorter, g, high[g : g + 1], low[g : g + 1])
     spot = owner_slot[...]
-    which = iota((POS_ROWS, rows), 0)
+    which = iota((PARTS, rows), 0)
     parts = jnp.where(which == 0, spot >> 7, jnp.where(which == 1, spot & (LANES - 1), 0))
     ordered = lax.dot_general(
         parts.astype(F32).astype(BF), sorter[...], NT_DIMS, preferred_element_type=F32
@@ -111,12 +119,12 @@
     for g in range(row_groups):
         high_rows[g : g + 1] = ordered[0:1, g * LANES : (g + 1) * LANES]
         low_rows[g : g + 1] = ordered[1:2, g * LANES : (g + 1) * LANES]
-    which = iota((POS_ROWS, LANES), 0)
+    which = iota((META, LANES), 0)
     for k in range(dom_total):
         owner = me ^ k
         start = starts[owner]
         held = starts[owner + 1] - start
-        block = jnp.zeros((POS_ROWS, LANES), F32)
+        block = jnp.zeros((META, LANES), F32)
         for j in range(2):
             chunk = jnp.minimum(start // LANES + j, row_groups - 1)
             table[2 * k + j] = chunk
@@ -259,9 +267,12 @@
     return jnp.dot(placing[...], rows[...], preferred_element_type=F32)
 
 
-def place_early(count, *refs):
-    out, placing, rows = refs[count:]
-    out[...] = place(refs[:count], placing, rows)
+def place_more(count, *refs):
+    before, (out, placing, rows) = refs[count:-3], refs[-3:]
+    placed = place(refs[:count], placing, rows)
+    for held in before:
+        placed = placed + held[...]
+    out[...] = placed
 
 
 def finish(placed, count, *refs):
@@ -347,6 +358,7 @@
 
 VMEM = pl.BlockSpec(memory_space=pltpu.VMEM)
 SMEM = pl.BlockSpec(memory_space=pltpu.SMEM)
+HBM = pl.BlockSpec(memory_space=pltpu.HBM)
 
 
 def call(kernel, ins, outs, scratch, args, cost=2_000_000_000, out_specs=None):
@@ -421,10 +433,18 @@
     nodes = node_motion.shape[1]
 
     packed = call(
-        pack_blocks, [SMEM, VMEM],
+        pack_blocks, [HBM, HBM],
         [arrays((capacity, width, block_size), BF)] * box_total,
-        [pltpu.SMEM((box_total * capacity,), I32)],
-        (box_route, old_history),
+        [
+            pltpu.SMEM((box_total * capacity,), I32),
+            pltpu.SMEM((blocks,), I32),
+            pltpu.VMEM(old_history.shape, BF),
+            pltpu.SemaphoreType.DMA((2,)),
+        ],
+        (
+            pltpu.with_memory_space_constraint(box_route, pltpu.HBM),
+            pltpu.with_memory_space_constraint(old_history, pltpu.HBM),
+        ),
     )
     received = {0: packed[0]}
     for k in [k for k in range(2, box_total)] + [1]:
@@ -456,7 +476,7 @@
             sort_rows, [VMEM, VMEM],
             [
                 arrays((rows, rows), BF),
-                arrays((dom_total, POS_ROWS, LANES), BF),
+                arrays((dom_total, META, LANES), BF),
                 arrays((2 * dom_total,), I32),
             ],
             [
@@ -478,7 +498,7 @@
             (entry_slot.T, entry_count, flat_weights),
             out_specs=[VMEM, VMEM, SMEM],
         )
-        payload = arrays((2 * usual + POS_ROWS, width), BF)
+        payload = arrays((2 * usual + META, width), BF)
         outgoing = call(
             project_rows, [SMEM, SMEM] + [VMEM] * (4 + box_total),
             [payload] * dom_total,
@@ -489,12 +509,11 @@
             ],
             (table, block_of, masked, mass_inv, sorter, positions, *received),
         )
-        far = dom_total // 2
         payloads = {0: outgoing[0]}
         for k in range(1, dom_total):
             payloads[k] = lax.ppermute(outgoing[k], "dom", [(i, i ^ k) for i in range(dom_total)])
-        soon = [0, *range(dom_total - 1, far - 1, -1), 1]
-        late = [payloads[k] for k in range(far - 1, 1, -1)]
+        order = arrival(dom_total)
+        stages = [[0, *order[0]], *order[1:]]
 
         def placing(count):
             return [
@@ -502,10 +521,18 @@
                 pltpu.VMEM((count * 2 * usual, width), BF),
             ]
 
-        early = call(
-            functools.partial(place_early, len(soon)), [VMEM] * len(soon),
-            arrays((elements, width), F32), placing(len(soon)), [payloads[k] for k in soon],
-        )
+        early = []
+        for stage in stages[:-1]:
+            count = len(stage)
+            early = [
+                call(
+                    functools.partial(place_more, count),
+                    [VMEM] * (count + len(early)), arrays((elements, width), F32),
+                    placing(count), [*[payloads[k] for k in stage], *early], cost=1000,
+                )
+            ]
+        early = early[0]
+        late = [payloads[k] for k in stages[-1]]
         placed, scratch = False, placing(len(late))
     else:
         early = spread_rows(received, entry_slot, entry_count, weights, owner_route, owner_slot)
@@ -528,6 +555,15 @@
         (local, inverse, *halo),
     )
     return history, force
+
+
+def arrival(dom_total):
+    far = dom_total // 2
+    return [
+        [dom_total - 1, *range(far + 1, dom_total - 2), 1],
+        [dom_total - 2, far - 1],
+        [far, *range(far - 2, 1, -1)],
+    ]
 
 
 def solution(mesh):

time: 43.3 us -> 40.9 us (0.945)
  the two profiles are of different devices: /device:TPU:1 before, /device:TPU:0 now
where the time goes in v7:
time: 40.9 us; the launch traced here: 40.7 us
  starting transfers between devices  23.1 us (56%)
  Pallas kernels  12.4 us (30%)
  waiting for transfers between devices  4.42 us (11%)
  between operations  0.83 us (2%)
    ppermute x7, starting transfers between devices, body(): lax.ppermute(outgoing[k], 'dom', [(i, i ^ k) for i in range(dom_total)])  13.5 us
    pallas_call x10, Pallas kernels, call(): pl.pallas_call(kernel, out_shape=outs, in_specs=ins, out_specs=out_specs...  12.4 us
    ppermute x4, starting transfers between devices, body(): halo[m] = lax.ppermute(exports[m], axis, swaps(axis, first))  6.36 us
    ppermute x3, waiting for transfers between devices, body(): lax.ppermute(packed[k], 'box', [(i, i ^ k) for i in range(box_total)])  3.47 us
    ppermute x3, starting transfers between devices, body(): lax.ppermute(packed[k], 'box', [(i, i ^ k) for i in range(box_total)])  3.15 us
  transfers between devices with their start and end apart: 14, of which 4 were waited for; matrix products, arithmetic and copies ran while one was open for 0% of the time, Pallas kernels for 19%

profile of v7, /device:TPU:0, one launch (start us, length us, event | category | flops | bytes accessed | tf_op | source)
XLA Modules:
  0.0 40.7 jit_solution(8414300802798155107)
XLA Ops:
  0.7 1.0 %shard_map.151 = (bf16[4,128,128]{2,1,0:T(8,128)(2,1)S(1)}, bf16[4,128,128]{2,1,0:T(8,128)(2,1)S(1)}, bf16[4,128,128]{2,1,0:T(8,128)(2,1)S(1)}, bf16[4,128,128]{2,1,0:T(8,128)(2,1)S(1)}) custom-call(s32[8]{0:T(128)} %route_hbm.1, bf16[8,128,128]{2,1,0:T(8,128)(2,1)} %old_hbm.1), custom_call_target="tpu_custom_call" | custom-call | flops 2000000000 | bytes 100000 | tf_op jit(solution)/shard_map/pallas_call | solution.py:366
  1.7 0.6 %collective-permute-start = (bf16[4,128,128]{2,1,0:T(8,128)(2,1)S(1)}, bf16[4,128,128]{2,1,0:T(8,128)(2,1)S(1)}, u32[]{:S(2)}, u32[]{:S(2)}) collective-permute-start(bf16[4,128,128]{2,1,0:T(8,128)(2,1)S(1)} %get-tuple-element.38), channel_id=1, source_target_pairs={{0,1},{1,0},{2,3},{3,2},{4,5},{5,4},{6,7},{7,6},{8,9},{9,8},{10,11... | collective-permute-start | bytes 393224 | tf_op jit(solution)/shard_map/ppermute | solution.py:451
  2.2 2.6 %collective-permute-start.1 = (bf16[4,128,128]{2,1,0:T(8,128)(2,1)S(1)}, bf16[4,128,128]{2,1,0:T(8,128)(2,1)S(1)}, u32[]{:S(2)}, u32[]{:S(2)}) collective-permute-start(bf16[4,128,128]{2,1,0:T(8,128)(2,1)S(1)} %get-tuple-element.39), channel_id=1, source_target_pairs={{0,2},{1,3},{2,0},{3,1},{4,6},{5,7},{6,4},{7,5},{8,10},{9,11},{10,... | collective-permute-start | bytes 393224 | tf_op jit(solution)/shard_map/ppermute | solution.py:451
  4.8 0.0 collective-permute-start.2
  4.8 0.0 copy-start.10
  4.8 1.6 %shard_map.149 = (bf16[1024,1024]{1,0:T(8,128)(2,1)S(1)}, bf16[8,8,128]{2,1,0:T(8,128)(2,1)S(1)}, s32[16]{0:T(128)S(1)}) custom-call(s32[8,128]{1,0:T(8,128)S(1)} %bitcast.14, s32[1,1024]{1,0:T(1,128)S(1)} %bitcast.15), custom_call_target="tpu_custom_call" | custom-call | flops 2000000000 | bytes 100000 | tf_op jit(solution)/shard_map/pallas_call | solution.py:366
  6.5 1.4 %shard_map.150 = (bf16[8,512,128]{2,1,0:T(8,128)(2,1)S(1)}, f32[8,128]{1,0:T(8,128)S(1)}, s32[32]{0:T(128)S(1)}) custom-call(s32[4,8]{1,0:T(4,128)S(1)} %bitcast.16, s32[8]{0:T(128)S(1)} %copy-done.10, bf16[8,512,128]{2,1,0:T(8,128)(2,1)S(1)} %bitcast.13), custom_call_target="tpu_custom_call" | custom-call | flops 2000000000 | bytes 100000 | tf_op jit(solution)/shard_map/pallas_call | solution.py:366
  7.9 0.0 collective-permute-done.rest_1_
  8.0 1.2 %collective-permute-done.1.rest_2_ = bf16[4,128,128]{2,1,0:T(8,128)(2,1)S(1)} collective-permute-done((bf16[4,128,128]{2,1,0:T(8,128)(2,1)S(1)}, bf16[4,128,128]{2,1,0:T(8,128)(2,1)S(1)}, u32[]{:S(2)}, u32[]{:S(2)}) %collective-permute-start.1) | collective-permute-done | bytes 131104 | tf_op jit(solution)/shard_map/ppermute | solution.py:451
  9.1 2.3 %collective-permute-done.2.rest_3_ = bf16[4,128,128]{2,1,0:T(8,128)(2,1)S(1)} collective-permute-done((bf16[4,128,128]{2,1,0:T(8,128)(2,1)S(1)}, bf16[4,128,128]{2,1,0:T(8,128)(2,1)S(1)}, u32[]{:S(2)}, u32[]{:S(2)}) %collective-permute-start.2) | collective-permute-done | bytes 131104 | tf_op jit(solution)/shard_map/ppermute | solution.py:451
  11.4 0.0 copy-start.4
  11.4 0.0 copy-start.5
  11.5 0.0 copy-start.11
  11.5 1.7 %shard_map.152 = (bf16[264,128]{1,0:T(8,128)(2,1)S(1)}, bf16[264,128]{1,0:T(8,128)(2,1)S(1)}, bf16[264,128]{1,0:T(8,128)(2,1)S(1)}, bf16[264,128]{1,0:T(8,128)(2...) custom-call(s32[16]{0:T(128)S(1)} %get-tuple-element.31.table, ...), custom_call_target="tpu_custom_call" | custom-call | flops 2000000000 | bytes 100000 | tf_op jit(solution)/shard_map/pallas_call | solution.py:366
  13.1 4.6 %collective-permute-start.7 = (bf16[264,128]{1,0:T(8,128)(2,1)S(1)}, bf16[264,128]{1,0:T(8,128)(2,1)S(1)}, u32[]{:S(2)}, u32[]{:S(2)}) collective-permute-start(bf16[264,128]{1,0:T(8,128)(2,1)S(1)} %get-tuple-element.46), channel_id=1, source_target_pairs={{0,28},{4,24},{8,20},{12,16},{16,12},{20,8},{24,4},{28,0},{1,29},{... | collective-permute-start | bytes 202760 | tf_op jit(solution)/shard_map/ppermute | solution.py:514
  17.7 2.9 %collective-permute-start.3 = (bf16[264,128]{1,0:T(8,128)(2,1)S(1)}, bf16[264,128]{1,0:T(8,128)(2,1)S(1)}, u32[]{:S(2)}, u32[]{:S(2)}) collective-permute-start(bf16[264,128]{1,0:T(8,128)(2,1)S(1)} %get-tuple-element.41), channel_id=1, source_target_pairs={{0,16},{4,20},{8,24},{12,28},{16,0},{20,4},{24,8},{28,12},{1,17},{... | collective-permute-start | bytes 202760 | tf_op jit(solution)/shard_map/ppermute | solution.py:514
  20.6 1.5 %collective-permute-start.9 = (bf16[264,128]{1,0:T(8,128)(2,1)S(1)}, bf16[264,128]{1,0:T(8,128)(2,1)S(1)}, u32[]{:S(2)}, u32[]{:S(2)}) collective-permute-start(bf16[264,128]{1,0:T(8,128)(2,1)S(1)} %get-tuple-element.48), channel_id=1, source_target_pairs={{0,4},{4,0},{8,12},{12,8},{16,20},{20,16},{24,28},{28,24},{1,5},{5... | collective-permute-start | bytes 202760 | tf_op jit(solution)/shard_map/ppermute | solution.py:514
  22.1 0.2 collective-permute-start.5
  22.4 3.6 %collective-permute-start.6 = (bf16[264,128]{1,0:T(8,128)(2,1)S(1)}, bf16[264,128]{1,0:T(8,128)(2,1)S(1)}, u32[]{:S(2)}, u32[]{:S(2)}) collective-permute-start(bf16[264,128]{1,0:T(8,128)(2,1)S(1)} %get-tuple-element.44), channel_id=1, source_target_pairs={{0,12},{4,8},{8,4},{12,0},{16,28},{20,24},{24,20},{28,16},{1,13},{... | collective-permute-start | bytes 202760 | tf_op jit(solution)/shard_map/ppermute | solution.py:514
  25.9 0.0 collective-permute-done.8.refs_2_
  25.9 0.8 %collective-permute-start.4 = (bf16[264,128]{1,0:T(8,128)(2,1)S(1)}, bf16[264,128]{1,0:T(8,128)(2,1)S(1)}, u32[]{:S(2)}, u32[]{:S(2)}) collective-permute-start(bf16[264,128]{1,0:T(8,128)(2,1)S(1)} %get-tuple-element.42), channel_id=1, source_target_pairs={{0,8},{4,12},{8,0},{12,4},{16,24},{20,28},{24,16},{28,20},{1,9},{5... | collective-permute-start | bytes 202760 | tf_op jit(solution)/shard_map/ppermute | solution.py:514
  26.8 2.8 %shard_map.155 = (f32[1024,128]{1,0:T(8,128)S(1)}, f32[8,1024]{1,0:T(8,128)S(1)}, bf16[8,1024,128]{2,1,0:T(8,128)(2,1)S(1)}, s32[8,128]{1,0:T(8,128)S(1)}, s32[2,8,128]{2,1,0:T(8,128)S(1)}) custom-call(s32[8,1024]{1,0:T(8,128)S(1)} %copy-done, f32[3,1024]{1,0:T(4,128)S(1)} %copy-done.1, f32[1,1024]{1,0:T(1,128)S(1)} %bitcast.9, f32[6,128]{1,0:T(8,128)S(1)} %bitcast.8, ...), custom_call_target="tpu_custom_call" | custom-call | flops 1000 | bytes 100000 | tf_op jit(solution)/shard_map/pallas_call | solution.py:366
  29.5 0.8 %shard_map.153.refs_2_ = f32[1024,128]{1,0:T(8,128)S(1)} custom-call(bf16[264,128]{1,0:T(8,128)(2,1)S(1)} %get-tuple-element.45.refs_0_, bf16[264,128]{1,0:T(8,128)(2,1)S(1)} %collective-permute-done.7.refs_1_, bf16[264,128]{1,0:T(8,128)(2,1)S(1)} %collective-permute-done.8.refs_2_, bf16[264,128]{1,0:T(8,128)(2,1)S(1)} %collective-permute-done.9.refs_3_), custom_call_target="tpu_custom_call" | custom-call | flops 1000 | bytes 100000 | tf_op jit(solution)/shard_map/pallas_call | solution.py:366
  30.3 0.5 %shard_map.154.refs_2_ = f32[1024,128]{1,0:T(8,128)S(1)} custom-call(bf16[264,128]{1,0:T(8,128)(2,1)S(1)} %collective-permute-done.5.refs_0_, bf16[264,128]{1,0:T(8,128)(2,1)S(1)} %collective-permute-done.6.refs_1_, f32[1024,128]{1,0:T(8,128)S(1)} %shard_map.153.refs_2_), custom_call_target="tpu_custom_call" | custom-call | flops 1000 | bytes 100000 | tf_op jit(solution)/shard_map/pallas_call | solution.py:366
  30.8 0.2 collective-permute-done.4.refs_1_
  30.9 1.2 %shard_map.156 = (bf16[1024,128]{1,0:T(8,128)(2,1)S(1)}, f32[3,8,128]{2,1,0:T(8,128)S(1)}, f32[3,128]{1,0:T(4,128)S(1)}, f32[3,128]{1,0:T(4,128)S(1)}, f32[3,128]{1,0:T(4,128)S(1)}, /*index=5*/f32[3,128]{1,0:T(4,128)S(1)}) custom-call(bf16[264,128]{1,0:T(8,128)(2,1)S(1)} %collective-permute-done.3.refs_0_, ...), custom_call_target="tpu_custom_call" | custom-call | flops 2000000000 | bytes 100000 | tf_op jit(solution)/shard_map/pallas_call | solution.py:366
  32.1 1.6 %collective-permute-start.10 = (f32[3,128]{1,0:T(4,128)S(1)}, f32[3,128]{1,0:T(4,128)S(1)}, u32[]{:S(2)}, u32[]{:S(2)}) collective-permute-start(f32[3,128]{1,0:T(4,128)S(1)} %get-tuple-element.56), channel_id=1, source_target_pairs={{0,4},{8,12},{16,20},{24,28},{4,0},{12,8},{20,16},{28,24},{1,5},{9... | collective-permute-start | bytes 4616 | tf_op jit(solution)/shard_map/ppermute | solution.py:552
  33.7 3.1 %collective-permute-start.11 = (f32[3,128]{1,0:T(4,128)S(1)}, f32[3,128]{1,0:T(4,128)S(1)}, u32[]{:S(2)}, u32[]{:S(2)}) collective-permute-start(f32[3,128]{1,0:T(4,128)S(1)} %get-tuple-element.57), channel_id=1, source_target_pairs={{4,8},{12,16},{20,24},{0,28},{8,4},{16,12},{24,20},{28,0},{5,9},{1... | collective-permute-start | bytes 4616 | tf_op jit(solution)/shard_map/ppermute | solution.py:552
  36.9 1.6 %collective-permute-start.13 = (f32[3,128]{1,0:T(4,128)S(1)}, f32[3,128]{1,0:T(4,128)S(1)}, u32[]{:S(2)}, u32[]{:S(2)}) collective-permute-start(f32[3,128]{1,0:T(4,128)S(1)} %get-tuple-element.59), channel_id=1, source_target_pairs={{1,2},{0,3},{2,1},{3,0},{5,6},{4,7},{6,5},{7,4},{9,10},{8,11},{10,... | collective-permute-start | bytes 4616 | tf_op jit(solution)/shard_map/ppermute | solution.py:552
  38.5 0.8 %shard_map.157 = bf16[1024,128]{1,0:T(8,128)(2,1)} custom-call(bf16[1024,128]{1,0:T(8,128)(2,1)S(1)} %get-tuple-element.52.arrived, f32[1024,128]{1,0:T(8,128)S(1)} %get-tuple-element.53.drive, f32[1,128]{1,0:T(1,128)S(1)} %bitcast.18), custom_call_target="tpu_custom_call" | custom-call | flops 2000000000 | bytes 100000 | tf_op jit(solution)/shard_map/pallas_call | solution.py:366
  39.3 0.8 %collective-permute-done.11.rest_1_ = f32[3,128]{1,0:T(4,128)S(1)} collective-permute-done((f32[3,128]{1,0:T(4,128)S(1)}, f32[3,128]{1,0:T(4,128)S(1)}, u32[]{:S(2)}, u32[]{:S(2)}) %collective-permute-start.11) | collective-permute-done | bytes 1568 | tf_op jit(solution)/shard_map/ppermute | solution.py:552
  40.0 0.7 %shard_map.158 = f32[3,1024]{1,0:T(4,128)} custom-call(f32[3,8,128]{2,1,0:T(8,128)S(1)} %get-tuple-element.54.local, s32[2,8,128]{2,1,0:T(8,128)S(1)} %get-tuple-element.55.inverse, f32[3,128]{1,0:T(4,128)S(1)} %collective-permute-done.10.rest_0_, f32[3,128]{1,0:T(4,128)S(1)} %collective-permute-done.11.rest_1_, ...), custom_call_target="tpu_custom_call" | custom-call | flops 2000000000 | bytes 100000 | tf_op jit(solution)/shard_map/pallas_call | solution.py:366
  (30 shorter events, 0.1 us)
Async XLA Ops:
  0.6 4.2 %copy-start.8 = (s32[1024]{0:T(1024)S(1)}, s32[1024]{0:T(1024)}, u32[]{:S(2)}) copy-start(s32[1024]{0:T(1024)} %param.20) | copy-start | bytes 12292
  0.6 4.2 %copy-start.7 = (s32[1024]{0:T(1024)S(1)}, s32[1024]{0:T(1024)}, u32[]{:S(2)}) copy-start(s32[1024]{0:T(1024)} %param.19) | copy-start | bytes 12292
  1.7 6.3 %collective-permute-start = (bf16[4,128,128]{2,1,0:T(8,128)(2,1)S(1)}, bf16[4,128,128]{2,1,0:T(8,128)(2,1)S(1)}, u32[]{:S(2)}, u32[]{:S(2)}) collective-permute-start(bf16[4,128,128]{2,1,0:T(8,128)(2,1)S(1)} %get-tuple-element.38), channel_id=1, source_target_pairs={{0,1},{1,0},{2,3},{3,2},{4,5},{5,4},{6,7},{7,6},{8,9},{9,8},{10,11... | collective-permute-start | bytes 393224 | tf_op jit(solution)/shard_map/ppermute | solution.py:451
  2.2 6.9 %collective-permute-start.1 = (bf16[4,128,128]{2,1,0:T(8,128)(2,1)S(1)}, bf16[4,128,128]{2,1,0:T(8,128)(2,1)S(1)}, u32[]{:S(2)}, u32[]{:S(2)}) collective-permute-start(bf16[4,128,128]{2,1,0:T(8,128)(2,1)S(1)} %get-tuple-element.39), channel_id=1, source_target_pairs={{0,2},{1,3},{2,0},{3,1},{4,6},{5,7},{6,4},{7,5},{8,10},{9,11},{10,... | collective-permute-start | bytes 393224 | tf_op jit(solution)/shard_map/ppermute | solution.py:451
  4.8 6.6 %collective-permute-start.2 = (bf16[4,128,128]{2,1,0:T(8,128)(2,1)S(1)}, bf16[4,128,128]{2,1,0:T(8,128)(2,1)S(1)}, u32[]{:S(2)}, u32[]{:S(2)}) collective-permute-start(bf16[4,128,128]{2,1,0:T(8,128)(2,1)S(1)} %get-tuple-element.40), channel_id=1, source_target_pairs={{0,3},{1,2},{2,1},{3,0},{4,7},{5,6},{6,5},{7,4},{8,11},{9,10},{10,... | collective-permute-start | bytes 393224 | tf_op jit(solution)/shard_map/ppermute | solution.py:451
  4.8 1.7 %copy-start.6 = (bf16[8,4,128,128]{3,2,1,0:T(8,128)(2,1)S(1)}, bf16[8,4,128,128]{3,2,1,0:T(8,128)(2,1)}, u32[]{:S(2)}) copy-start(bf16[8,4,128,128]{3,2,1,0:T(8,128)(2,1)} %param.18) | copy-start | bytes 3145732
  4.8 1.7 %copy-start.9 = (s32[8,4]{0,1:T(4,128)S(1)}, s32[8,4]{0,1:T(4,128)}, u32[]{:S(2)}) copy-start(s32[8,4]{0,1:T(4,128)} %param.16) | copy-start | bytes 388
  4.8 1.7 %copy-start.10 = (s32[8]{0:T(128)S(1)}, s32[8]{0:T(128)}, u32[]{:S(2)}) copy-start(s32[8]{0:T(128)} %count.1) | copy-start | bytes 100
  11.4 15.3 %copy-start = (s32[8,1024]{1,0:T(8,128)S(1)}, s32[8,1024]{1,0:T(8,128)}, u32[]{:S(2)}) copy-start(s32[8,1024]{1,0:T(8,128)} %refs_5_.1) | copy-start | bytes 98308
  11.4 15.3 %copy-start.1 = (f32[3,1024]{1,0:T(4,128)S(1)}, f32[3,1024]{1,0:T(4,128)}, u32[]{:S(2)}) copy-start(f32[3,1024]{1,0:T(4,128)} %motion.1) | copy-start | bytes 36868
  11.4 15.3 %copy-start.2 = (f32[128,6]{0,1:T(8,128)S(1)}, f32[128,6]{0,1:T(8,128)}, u32[]{:S(2)}) copy-start(f32[128,6]{0,1:T(8,128)} %param.26) | copy-start | bytes 9220
  11.4 15.3 %copy-start.3 = (f32[1024]{0:T(1024)S(1)}, f32[1024]{0:T(1024)}, u32[]{:S(2)}) copy-start(f32[1024]{0:T(1024)} %param.24) | copy-start | bytes 12292
  11.4 15.3 %copy-start.4 = (f32[128,6]{0,1:T(8,128)S(1)}, f32[128,6]{0,1:T(8,128)}, u32[]{:S(2)}) copy-start(f32[128,6]{0,1:T(8,128)} %param.27) | copy-start | bytes 9220
  11.4 15.3 %copy-start.5 = (s32[4,128]{1,0:T(4,128)S(1)}, s32[4,128]{1,0:T(4,128)}, u32[]{:S(2)}) copy-start(s32[4,128]{1,0:T(4,128)} %shared.1) | copy-start | bytes 6148
  11.5 19.5 %copy-start.11 = (f32[128]{0:T(128)S(1)}, f32[128]{0:T(128)}, u32[]{:S(2)}) copy-start(f32[128]{0:T(128)} %param.25) | copy-start | bytes 1540
  13.1 9.2 %collective-permute-start.7 = (bf16[264,128]{1,0:T(8,128)(2,1)S(1)}, bf16[264,128]{1,0:T(8,128)(2,1)S(1)}, u32[]{:S(2)}, u32[]{:S(2)}) collective-permute-start(bf16[264,128]{1,0:T(8,128)(2,1)S(1)} %get-tuple-element.46), channel_id=1, source_target_pairs={{0,28},{4,24},{8,20},{12,16},{16,12},{20,8},{24,4},{28,0},{1,29},{... | collective-permute-start | bytes 202760 | tf_op jit(solution)/shard_map/ppermute | solution.py:514
  17.7 8.2 %collective-permute-start.8 = (bf16[264,128]{1,0:T(8,128)(2,1)S(1)}, bf16[264,128]{1,0:T(8,128)(2,1)S(1)}, u32[]{:S(2)}, u32[]{:S(2)}) collective-permute-start(bf16[264,128]{1,0:T(8,128)(2,1)S(1)} %get-tuple-element.47), channel_id=1, source_target_pairs={{0,20},{4,16},{8,28},{12,24},{16,4},{20,0},{24,12},{28,8},{1,21},{... | collective-permute-start | bytes 202760 | tf_op jit(solution)/shard_map/ppermute | solution.py:514
  17.7 13.0 %collective-permute-start.3 = (bf16[264,128]{1,0:T(8,128)(2,1)S(1)}, bf16[264,128]{1,0:T(8,128)(2,1)S(1)}, u32[]{:S(2)}, u32[]{:S(2)}) collective-permute-start(bf16[264,128]{1,0:T(8,128)(2,1)S(1)} %get-tuple-element.41), channel_id=1, source_target_pairs={{0,16},{4,20},{8,24},{12,28},{16,0},{20,4},{24,8},{28,12},{1,17},{... | collective-permute-start | bytes 202760 | tf_op jit(solution)/shard_map/ppermute | solution.py:514
  20.6 8.9 %collective-permute-start.9 = (bf16[264,128]{1,0:T(8,128)(2,1)S(1)}, bf16[264,128]{1,0:T(8,128)(2,1)S(1)}, u32[]{:S(2)}, u32[]{:S(2)}) collective-permute-start(bf16[264,128]{1,0:T(8,128)(2,1)S(1)} %get-tuple-element.48), channel_id=1, source_target_pairs={{0,4},{4,0},{8,12},{12,8},{16,20},{20,16},{24,28},{28,24},{1,5},{5... | collective-permute-start | bytes 202760 | tf_op jit(solution)/shard_map/ppermute | solution.py:514
  22.1 8.2 %collective-permute-start.5 = (bf16[264,128]{1,0:T(8,128)(2,1)S(1)}, bf16[264,128]{1,0:T(8,128)(2,1)S(1)}, u32[]{:S(2)}, u32[]{:S(2)}) collective-permute-start(bf16[264,128]{1,0:T(8,128)(2,1)S(1)} %get-tuple-element.43), channel_id=1, source_target_pairs={{0,24},{4,28},{8,16},{12,20},{16,8},{20,12},{24,0},{28,4},{1,25},{... | collective-permute-start | bytes 202760 | tf_op jit(solution)/shard_map/ppermute | solution.py:514
  22.4 7.9 %collective-permute-start.6 = (bf16[264,128]{1,0:T(8,128)(2,1)S(1)}, bf16[264,128]{1,0:T(8,128)(2,1)S(1)}, u32[]{:S(2)}, u32[]{:S(2)}) collective-permute-start(bf16[264,128]{1,0:T(8,128)(2,1)S(1)} %get-tuple-element.44), channel_id=1, source_target_pairs={{0,12},{4,8},{8,4},{12,0},{16,28},{20,24},{24,20},{28,16},{1,13},{... | collective-permute-start | bytes 202760 | tf_op jit(solution)/shard_map/ppermute | solution.py:514
  25.9 5.0 %collective-permute-start.4 = (bf16[264,128]{1,0:T(8,128)(2,1)S(1)}, bf16[264,128]{1,0:T(8,128)(2,1)S(1)}, u32[]{:S(2)}, u32[]{:S(2)}) collective-permute-start(bf16[264,128]{1,0:T(8,128)(2,1)S(1)} %get-tuple-element.42), channel_id=1, source_target_pairs={{0,8},{4,12},{8,0},{12,4},{16,24},{20,28},{24,16},{28,20},{1,9},{5... | collective-permute-start | bytes 202760 | tf_op jit(solution)/shard_map/ppermute | solution.py:514
  32.1 7.1 %collective-permute-start.10 = (f32[3,128]{1,0:T(4,128)S(1)}, f32[3,128]{1,0:T(4,128)S(1)}, u32[]{:S(2)}, u32[]{:S(2)}) collective-permute-start(f32[3,128]{1,0:T(4,128)S(1)} %get-tuple-element.56), channel_id=1, source_target_pairs={{0,4},{8,12},{16,20},{24,28},{4,0},{12,8},{20,16},{28,24},{1,5},{9... | collective-permute-start | bytes 4616 | tf_op jit(solution)/shard_map/ppermute | solution.py:552
  33.7 6.3 %collective-permute-start.11 = (f32[3,128]{1,0:T(4,128)S(1)}, f32[3,128]{1,0:T(4,128)S(1)}, u32[]{:S(2)}, u32[]{:S(2)}) collective-permute-start(f32[3,128]{1,0:T(4,128)S(1)} %get-tuple-element.57), channel_id=1, source_target_pairs={{4,8},{12,16},{20,24},{0,28},{8,4},{16,12},{24,20},{28,0},{5,9},{1... | collective-permute-start | bytes 4616 | tf_op jit(solution)/shard_map/ppermute | solution.py:552
  36.9 3.1 %collective-permute-start.12 = (f32[3,128]{1,0:T(4,128)S(1)}, f32[3,128]{1,0:T(4,128)S(1)}, u32[]{:S(2)}, u32[]{:S(2)}) collective-permute-start(f32[3,128]{1,0:T(4,128)S(1)} %get-tuple-element.58), channel_id=1, source_target_pairs={{0,1},{2,3},{1,0},{3,2},{4,5},{6,7},{5,4},{7,6},{8,9},{10,11},{9,8... | collective-permute-start | bytes 4616 | tf_op jit(solution)/shard_map/ppermute | solution.py:552
  36.9 3.1 %collective-permute-start.13 = (f32[3,128]{1,0:T(4,128)S(1)}, f32[3,128]{1,0:T(4,128)S(1)}, u32[]{:S(2)}, u32[]{:S(2)}) collective-permute-start(f32[3,128]{1,0:T(4,128)S(1)} %get-tuple-element.59), channel_id=1, source_target_pairs={{1,2},{0,3},{2,1},{3,0},{5,6},{4,7},{6,5},{7,4},{9,10},{8,11},{10,... | collective-permute-start | bytes 4616 | tf_op jit(solution)/shard_map/ppermute | solution.py:552

commit v8 on v7

--- a/solution.py
+++ b/solution.py
@@ -76,17 +76,25 @@
             out[s] = old[table[k * capacity + s]]
 
 
-def mark_places(target, column, high, low):
-    low_iota = iota((LANES, LANES), 0).astype(F32).astype(BF)
-    low = jnp.broadcast_to(low, (LANES, LANES)).astype(BF)
+def marks(high, low, rows):
+    shape = (LANES, high.shape[1])
+    low = jnp.broadcast_to(low, shape).astype(BF)
+    low_iota = iota(shape, 0).astype(F32).astype(BF)
     match = jnp.where(low_iota == low, jnp.ones_like(low), jnp.zeros_like(low))
-    lanes = slice(column * LANES, (column + 1) * LANES)
-    for g in range(target.shape[0] // LANES):
-        here = jnp.broadcast_to(jnp.where(high == g, 1.0, 0.0), (LANES, LANES)).astype(BF)
-        target[g * LANES : (g + 1) * LANES, lanes] = match * here
-
-
-def sort_rows(owner_route, owner_slot, sorter, positions, table, high_rows, low_rows, starts):
+    return jnp.concatenate(
+        [
+            match * jnp.broadcast_to(jnp.where(high == g, 1.0, 0.0), shape).astype(BF)
+            for g in range(rows // LANES)
+        ],
+        axis=0,
+    )
+
+
+def side_by_side(x, first, count):
+    return jnp.concatenate([x[first + i : first + i + 1] for i in range(count)], axis=1)
+
+
+def sort_rows(owner_route, owner_slot, spots, positions, table, high_rows, low_rows, starts):
     dom_total = positions.shape[0]
     row_groups = owner_route.shape[0]
     rows = row_groups * LANES
@@ -108,14 +116,20 @@
     place = place.astype(I32)
     high = (place >> 7).astype(F32)
     low = (place & (LANES - 1)).astype(F32)
-    for g in range(row_groups):
-        mark_places(sorter, g, high[g : g + 1], low[g : g + 1])
+    spots[0] = high
+    spots[1] = low
     spot = owner_slot[...]
     which = iota((PARTS, rows), 0)
     parts = jnp.where(which == 0, spot >> 7, jnp.where(which == 1, spot & (LANES - 1), 0))
-    ordered = lax.dot_general(
-        parts.astype(F32).astype(BF), sorter[...], NT_DIMS, preferred_element_type=F32
-    )
+    parts = parts.astype(F32).astype(BF)
+    ordered = jnp.zeros((PARTS, rows), F32)
+    for g in range(0, row_groups, 2):
+        ordered = ordered + lax.dot_general(
+            parts[:, g * LANES : (g + 2) * LANES],
+            marks(side_by_side(high, g, 2), side_by_side(low, g, 2), rows),
+            NT_DIMS,
+            preferred_element_type=F32,
+        )
     for g in range(row_groups):
         high_rows[g : g + 1] = ordered[0:1, g * LANES : (g + 1) * LANES]
         low_rows[g : g + 1] = ordered[1:2, g * LANES : (g + 1) * LANES]
@@ -154,7 +168,7 @@
 
 
 def element_parts(connectivity, motion, size, couple, readout, shared, drive, base, onehot,
-                  chosen, inverse, strain, elastic, wide):
+                  grouped, quarter, chosen, inverse, strain, elastic, wide):
     elements = connectivity.shape[1]
     corners = connectivity.shape[0]
     groups = motion.shape[1] // LANES
@@ -162,12 +176,15 @@
     signs = [(2 * ((corner >> c) & 1) - 1).astype(F32) for c in range(3)]
     low_iota = iota((LANES, LANES), 0)
     lane_iota = iota((LANES, LANES), 1).astype(F32)
+    eighth = iota((groups, LANES), 0)
     strain[...] = jnp.zeros_like(strain)
     elastic[...] = jnp.zeros_like(elastic)
     for j in range(elements // LANES):
         lanes = slice(j * LANES, (j + 1) * LANES)
         nodes = connectivity[:, lanes]
-        scale = 1.0 / (4.0 * size[:, lanes])
+        edge = size[:, lanes]
+        scale = 1.0 / (4.0 * edge)
+        quarter[:, lanes] = edge * edge * 0.25
         grad = []
         for i in range(3):
             moved = lookup(
@@ -190,6 +207,8 @@
             elastic[c : c + 1, lanes] = volume + 1.6 * rows[c] if c < 3 else 0.8 * rows[c]
         turned = (nodes & (LANES - 1)).astype(F32).T
         for a in range(corners):
+            here = as_onehot(eighth == (nodes[a : a + 1] >> 7))
+            grouped[a, :, lanes] = jnp.concatenate([here, here], axis=0)
             onehot[a, lanes, :] = as_onehot(lane_iota == turned[:, a : a + 1])
     wide[...] = jnp.zeros_like(wide)
     wide[0, 0:6] = couple[...]
@@ -231,7 +250,7 @@
     inverse[1] = total[groups:]
 
 
-def project_rows(table, blocks, masked, mass_inv, sorter, positions, *rest):
+def project_rows(table, blocks, masked, mass_inv, spots, positions, *rest):
     dom_total = positions.shape[0]
     box_total = lax.axis_size("box")
     received = rest[:box_total]
@@ -249,7 +268,16 @@
             jnp.concatenate(picked, axis=1), masked[t], preferred_element_type=F32
         )
         turned[:, t * LANES : (t + 1) * LANES] = (numerator * mass_inv[t : t + 1]).astype(BF)
-    sort = lax.dot_general(sorter[...], turned[...], NT_DIMS, preferred_element_type=F32)
+    high, low = spots[0], spots[1]
+    rows = turned.shape[1]
+    sort = jnp.zeros((rows, LANES), F32)
+    for g in range(0, rows // LANES, 2):
+        sort = sort + lax.dot_general(
+            marks(side_by_side(high, g, 2), side_by_side(low, g, 2), rows),
+            turned[:, g * LANES : (g + 2) * LANES],
+            NT_DIMS,
+            preferred_element_type=F32,
+        )
     for g in range(ordered.shape[0]):
         ordered[g] = sort[g * LANES : (g + 1) * LANES].astype(BF)
     for k, out in enumerate(outs):
@@ -258,18 +286,22 @@
         out[2 * LANES :] = positions[k]
 
 
-def place(payloads, placing, rows):
-    for k, payload in enumerate(payloads):
-        rows[k * 2 * LANES : (k + 1) * 2 * LANES] = payload[: 2 * LANES]
+def place(payloads, elements):
+    total = None
+    for payload in payloads:
         where = payload[2 * LANES :].astype(F32)
-        for j in range(2):
-            mark_places(placing, 2 * k + j, where[j : j + 1], where[2 + j : 3 + j])
-    return jnp.dot(placing[...], rows[...], preferred_element_type=F32)
+        part = jnp.dot(
+            marks(side_by_side(where, 0, 2), side_by_side(where, 2, 2), elements),
+            payload[: 2 * LANES],
+            preferred_element_type=F32,
+        )
+        total = part if total is None else total + part
+    return total
 
 
 def place_more(count, *refs):
-    before, (out, placing, rows) = refs[count:-3], refs[-3:]
-    placed = place(refs[:count], placing, rows)
+    before, out = refs[count:-1], refs[-1]
+    placed = place(refs[:count], out.shape[0])
     for held in before:
         placed = placed + held[...]
     out[...] = placed
@@ -277,15 +309,15 @@
 
 def finish(placed, count, *refs):
     payloads = refs[:count]
-    early, base, size, connectivity, onehot, decay, readout, chosen = refs[count : count + 8]
+    early, base, quarter, grouped, onehot, decay, readout, chosen = refs[count : count + 8]
     settled, local = refs[count + 8 : count + 10]
     exports = refs[count + 10 : count + 14]
-    scratch = refs[count + 14 :]
+    (spread_forces,) = refs[count + 14 :]
     elements = base.shape[1]
     if placed:
         arrived = early[...]
     else:
-        arrived = (early[...] + place(payloads, *scratch)).astype(BF)
+        arrived = (early[...] + place(payloads, elements)).astype(BF)
     settled[...] = arrived
     taken = readout[...] * decay[...]
     taken = jnp.concatenate([taken, jnp.zeros((SUBS - 6, LANES), F32)], axis=0)
@@ -308,26 +340,29 @@
         jnp.concatenate(pieces(stress, 2), axis=0),
         preferred_element_type=F32,
     )
-    edge = size[...]
-    forces = forces * (edge * edge * 0.25)
-    group = iota((SUBS, elements), 0)
+    forces = forces * quarter[...]
+    high = forces.astype(BF).astype(F32)
+    spread_forces[: 3 * SUBS] = high
+    spread_forces[3 * SUBS :] = forces - high
     halves = [jnp.zeros((6 * SUBS, LANES), F32) for _ in range(2)]
     for a in range(SUBS):
-        here = group == (connectivity[a : a + 1] >> 7)
-        highs, lows = [], []
+        mask = grouped[a]
+        values = []
         for i in range(3):
-            value = jnp.where(here, forces[i * SUBS + a : i * SUBS + a + 1], 0.0)
-            high, low = pieces(value, 2)
-            highs.append(high)
-            lows.append(low)
+            both = [
+                spread_forces[pl.ds(n * 3 * SUBS + i * SUBS + a, SUBS, stride=0), :]
+                for n in range(2)
+            ]
+            values.append(jnp.concatenate(both, axis=0).astype(BF) * mask)
         halves[a % 2] = halves[a % 2] + jnp.dot(
-            jnp.concatenate(highs + lows, axis=0), onehot[a], preferred_element_type=F32
+            jnp.concatenate(values, axis=0), onehot[a], preferred_element_type=F32
         )
     total = halves[0] + halves[1]
     nodes = chosen[...]
     for i in range(3):
         summed = (
-            total[i * SUBS : (i + 1) * SUBS] + total[(3 + i) * SUBS : (4 + i) * SUBS]
+            total[2 * i * SUBS : (2 * i + 1) * SUBS]
+            + total[(2 * i + 1) * SUBS : (2 * i + 2) * SUBS]
         )
         local[i] = summed
         got = lookup([summed[r : r + 1] for r in range(SUBS)], nodes)
@@ -452,12 +487,14 @@
     received = [received[k] for k in range(box_total)]
     flat_weights = weights.reshape(targets, entries * block_size, block_size)
     edge = elem_size.reshape(1, elements)
-    drive, base, onehot, chosen, inverse = call(
+    drive, base, onehot, grouped, quarter, chosen, inverse = call(
         element_parts, [VMEM] * 6,
         [
             arrays((elements, width), F32),
             arrays((SUBS, elements), F32),
             arrays((connectivity.shape[0], elements, LANES), BF),
+            arrays((connectivity.shape[0], 2 * nodes // LANES, elements), BF),
+            arrays((1, elements), F32),
             arrays((SUBS, shared_nodes.shape[1]), I32),
             arrays((2, nodes // LANES, LANES), I32),
         ],
@@ -472,10 +509,10 @@
     usual = rows // dom_total
     relaxing = decay.reshape(1, width)
     if usual == LANES:
-        sorter, positions, table = call(
+        spots, positions, table = call(
             sort_rows, [VMEM, VMEM],
             [
-                arrays((rows, rows), BF),
+                arrays((2, row_groups, LANES), F32),
                 arrays((dom_total, META, LANES), BF),
                 arrays((2 * dom_total,), I32),
             ],
@@ -507,19 +544,13 @@
                 pltpu.VMEM((width, rows), BF),
                 pltpu.VMEM((row_groups, LANES, width), BF),
             ],
-            (table, block_of, masked, mass_inv, sorter, positions, *received),
+            (table, block_of, masked, mass_inv, spots, positions, *received),
         )
         payloads = {0: outgoing[0]}
         for k in range(1, dom_total):
             payloads[k] = lax.ppermute(outgoing[k], "dom", [(i, i ^ k) for i in range(dom_total)])
         order = arrival(dom_total)
         stages = [[0, *order[0]], *order[1:]]
-
-        def placing(count):
-            return [
-                pltpu.VMEM((elements, count * 2 * usual), BF),
-                pltpu.VMEM((count * 2 * usual, width), BF),
-            ]
 
         early = []
         for stage in stages[:-1]:
@@ -528,23 +559,23 @@
                 call(
                     functools.partial(place_more, count),
                     [VMEM] * (count + len(early)), arrays((elements, width), F32),
-                    placing(count), [*[payloads[k] for k in stage], *early], cost=1000,
+                    [], [*[payloads[k] for k in stage], *early], cost=1000,
                 )
             ]
         early = early[0]
         late = [payloads[k] for k in stages[-1]]
-        placed, scratch = False, placing(len(late))
+        placed = False
     else:
         early = spread_rows(received, entry_slot, entry_count, weights, owner_route, owner_slot)
         late = []
-        placed, scratch = True, []
+        placed = True
     export = arrays((3, shared_nodes.shape[1]), F32)
     arrived, local, *exports = call(
         functools.partial(finish, placed, len(late)),
         [VMEM] * (len(late) + 8),
         [arrays((elements, width), BF), arrays((3, nodes // LANES, LANES), F32)] + [export] * 4,
-        scratch,
-        (*late, early, base, edge, connectivity, onehot, relaxing, readout.T, chosen),
+        [pltpu.VMEM((6 * SUBS, elements), F32)],
+        (*late, early, base, quarter, grouped, onehot, relaxing, readout.T, chosen),
     )
     history = call(relax, [VMEM] * 3, arrays((elements, width), BF), [], (arrived, drive, relaxing))
     halo = [None] * 4

time: 40.9 us -> 40.9 us (level)
  no operation moved by 1% of the time
where the time goes in v8:
time: 40.9 us; the launch traced here: 40.7 us
  starting transfers between devices  23.1 us (56%)
  Pallas kernels  12.3 us (30%)
  waiting for transfers between devices  4.5 us (11%)
  between operations  0.83 us (2%)
    ppermute x7, starting transfers between devices, body(): lax.ppermute(outgoing[k], 'dom', [(i, i ^ k) for i in range(dom_total)])  13.6 us
    pallas_call x10, Pallas kernels, call(): pl.pallas_call(kernel, out_shape=outs, in_specs=ins, out_specs=out_specs...  12.3 us
    ppermute x4, starting transfers between devices, body(): halo[m] = lax.ppermute(exports[m], axis, swaps(axis, first))  6.37 us
    ppermute x3, waiting for transfers between devices, body(): lax.ppermute(packed[k], 'box', [(i, i ^ k) for i in range(box_total)])  3.53 us
    ppermute x3, starting transfers between devices, body(): lax.ppermute(packed[k], 'box', [(i, i ^ k) for i in range(box_total)])  3.15 us
  transfers between devices with their start and end apart: 14, of which 4 were waited for; matrix products, arithmetic and copies ran while one was open for 0% of the time, Pallas kernels for 19%

profile of v8, /device:TPU:0, one launch (start us, length us, event | category | flops | bytes accessed | tf_op | source)
XLA Modules:
  0.0 40.7 jit_solution(11497174866320034821)
XLA Ops:
  0.7 1.0 %shard_map.151 = (bf16[4,128,128]{2,1,0:T(8,128)(2,1)S(1)}, bf16[4,128,128]{2,1,0:T(8,128)(2,1)S(1)}, bf16[4,128,128]{2,1,0:T(8,128)(2,1)S(1)}, bf16[4,128,128]{2,1,0:T(8,128)(2,1)S(1)}) custom-call(s32[8]{0:T(128)} %route_hbm.1, bf16[8,128,128]{2,1,0:T(8,128)(2,1)} %old_hbm.1), custom_call_target="tpu_custom_call" | custom-call | flops 2000000000 | bytes 100000 | tf_op jit(solution)/shard_map/pallas_call | solution.py:401
  1.7 0.6 %collective-permute-start = (bf16[4,128,128]{2,1,0:T(8,128)(2,1)S(1)}, bf16[4,128,128]{2,1,0:T(8,128)(2,1)S(1)}, u32[]{:S(2)}, u32[]{:S(2)}) collective-permute-start(bf16[4,128,128]{2,1,0:T(8,128)(2,1)S(1)} %get-tuple-element.40), channel_id=1, source_target_pairs={{0,1},{1,0},{2,3},{3,2},{4,5},{5,4},{6,7},{7,6},{8,9},{9,8},{10,11... | collective-permute-start | bytes 393224 | tf_op jit(solution)/shard_map/ppermute | solution.py:486
  2.2 2.6 %collective-permute-start.1 = (bf16[4,128,128]{2,1,0:T(8,128)(2,1)S(1)}, bf16[4,128,128]{2,1,0:T(8,128)(2,1)S(1)}, u32[]{:S(2)}, u32[]{:S(2)}) collective-permute-start(bf16[4,128,128]{2,1,0:T(8,128)(2,1)S(1)} %get-tuple-element.41), channel_id=1, source_target_pairs={{0,2},{1,3},{2,0},{3,1},{4,6},{5,7},{6,4},{7,5},{8,10},{9,11},{10,... | collective-permute-start | bytes 393224 | tf_op jit(solution)/shard_map/ppermute | solution.py:486
  4.8 0.0 collective-permute-start.2
  4.8 0.0 copy-start.10
  4.8 1.6 %shard_map.149 = (f32[2,8,128]{2,1,0:T(8,128)S(1)}, bf16[8,8,128]{2,1,0:T(8,128)(2,1)S(1)}, s32[16]{0:T(128)S(1)}) custom-call(s32[8,128]{1,0:T(8,128)S(1)} %bitcast.13, s32[1,1024]{1,0:T(1,128)S(1)} %bitcast.14), custom_call_target="tpu_custom_call" | custom-call | flops 2000000000 | bytes 100000 | tf_op jit(solution)/shard_map/pallas_call | solution.py:401
  6.5 1.4 %shard_map.150 = (bf16[8,512,128]{2,1,0:T(8,128)(2,1)S(1)}, f32[8,128]{1,0:T(8,128)S(1)}, s32[32]{0:T(128)S(1)}) custom-call(s32[4,8]{1,0:T(4,128)S(1)} %bitcast.15, s32[8]{0:T(128)S(1)} %copy-done.10, bf16[8,512,128]{2,1,0:T(8,128)(2,1)S(1)} %bitcast.12), custom_call_target="tpu_custom_call" | custom-call | flops 2000000000 | bytes 100000 | tf_op jit(solution)/shard_map/pallas_call | solution.py:401
  7.9 1.2 %collective-permute-done.1.rest_2_ = bf16[4,128,128]{2,1,0:T(8,128)(2,1)S(1)} collective-permute-done((bf16[4,128,128]{2,1,0:T(8,128)(2,1)S(1)}, bf16[4,128,128]{2,1,0:T(8,128)(2,1)S(1)}, u32[]{:S(2)}, u32[]{:S(2)}) %collective-permute-start.1) | collective-permute-done | bytes 131104 | tf_op jit(solution)/shard_map/ppermute | solution.py:486
  9.1 2.3 %collective-permute-done.2.rest_3_ = bf16[4,128,128]{2,1,0:T(8,128)(2,1)S(1)} collective-permute-done((bf16[4,128,128]{2,1,0:T(8,128)(2,1)S(1)}, bf16[4,128,128]{2,1,0:T(8,128)(2,1)S(1)}, u32[]{:S(2)}, u32[]{:S(2)}) %collective-permute-start.2) | collective-permute-done | bytes 131104 | tf_op jit(solution)/shard_map/ppermute | solution.py:486
  11.4 0.0 copy-start.4
  11.4 0.0 copy-start.5
  11.5 0.0 copy-start.11
  11.5 1.7 %shard_map.152 = (bf16[264,128]{1,0:T(8,128)(2,1)S(1)}, bf16[264,128]{1,0:T(8,128)(2,1)S(1)}, bf16[264,128]{1,0:T(8,128)(2,1)S(1)}, bf16[264,128]{1,0:T(8,128)(2...) custom-call(s32[16]{0:T(128)S(1)} %get-tuple-element.33.table, ...), custom_call_target="tpu_custom_call" | custom-call | flops 2000000000 | bytes 100000 | tf_op jit(solution)/shard_map/pallas_call | solution.py:401
  13.2 4.6 %collective-permute-start.7 = (bf16[264,128]{1,0:T(8,128)(2,1)S(1)}, bf16[264,128]{1,0:T(8,128)(2,1)S(1)}, u32[]{:S(2)}, u32[]{:S(2)}) collective-permute-start(bf16[264,128]{1,0:T(8,128)(2,1)S(1)} %get-tuple-element.48), channel_id=1, source_target_pairs={{0,28},{4,24},{8,20},{12,16},{16,12},{20,8},{24,4},{28,0},{1,29},{... | collective-permute-start | bytes 202760 | tf_op jit(solution)/shard_map/ppermute | solution.py:551
  17.8 2.9 %collective-permute-start.3 = (bf16[264,128]{1,0:T(8,128)(2,1)S(1)}, bf16[264,128]{1,0:T(8,128)(2,1)S(1)}, u32[]{:S(2)}, u32[]{:S(2)}) collective-permute-start(bf16[264,128]{1,0:T(8,128)(2,1)S(1)} %get-tuple-element.43), channel_id=1, source_target_pairs={{0,16},{4,20},{8,24},{12,28},{16,0},{20,4},{24,8},{28,12},{1,17},{... | collective-permute-start | bytes 202760 | tf_op jit(solution)/shard_map/ppermute | solution.py:551
  20.6 1.5 %collective-permute-start.9 = (bf16[264,128]{1,0:T(8,128)(2,1)S(1)}, bf16[264,128]{1,0:T(8,128)(2,1)S(1)}, u32[]{:S(2)}, u32[]{:S(2)}) collective-permute-start(bf16[264,128]{1,0:T(8,128)(2,1)S(1)} %get-tuple-element.50), channel_id=1, source_target_pairs={{0,4},{4,0},{8,12},{12,8},{16,20},{20,16},{24,28},{28,24},{1,5},{5... | collective-permute-start | bytes 202760 | tf_op jit(solution)/shard_map/ppermute | solution.py:551
  22.1 0.2 collective-permute-start.5
  22.4 0.0 collective-permute-done.7.refs_1_
  22.4 3.6 %collective-permute-start.6 = (bf16[264,128]{1,0:T(8,128)(2,1)S(1)}, bf16[264,128]{1,0:T(8,128)(2,1)S(1)}, u32[]{:S(2)}, u32[]{:S(2)}) collective-permute-start(bf16[264,128]{1,0:T(8,128)(2,1)S(1)} %get-tuple-element.46), channel_id=1, source_target_pairs={{0,12},{4,8},{8,4},{12,0},{16,28},{20,24},{24,20},{28,16},{1,13},{... | collective-permute-start | bytes 202760 | tf_op jit(solution)/shard_map/ppermute | solution.py:551
  25.9 0.0 collective-permute-done.8.refs_2_
  26.0 0.8 %collective-permute-start.4 = (bf16[264,128]{1,0:T(8,128)(2,1)S(1)}, bf16[264,128]{1,0:T(8,128)(2,1)S(1)}, u32[]{:S(2)}, u32[]{:S(2)}) collective-permute-start(bf16[264,128]{1,0:T(8,128)(2,1)S(1)} %get-tuple-element.44), channel_id=1, source_target_pairs={{0,8},{4,12},{8,0},{12,4},{16,24},{20,28},{24,16},{28,20},{1,9},{5... | collective-permute-start | bytes 202760 | tf_op jit(solution)/shard_map/ppermute | solution.py:551
  26.8 2.8 %shard_map.155 = (f32[1024,128]{1,0:T(8,128)S(1)}, f32[8,1024]{1,0:T(8,128)S(1)}, bf16[8,1024,128]{2,1,0:T(8,128)(2,1)S(1)}, bf16[8,16,1024]{2,1,0:T(8,128)(2,1)...) custom-call(s32[8,1024]{1,0:T(8,128)S(1)} %copy-done, f32[3,1024]{1,0:T(4,128)S(1)} %copy-done.1, ...), custom_call_target="tpu_custom_call" | custom-call | flops 1000 | bytes 100000 | tf_op jit(solution)/shard_map/pallas_call | solution.py:401
  29.5 0.7 %shard_map.153.refs_2_ = f32[1024,128]{1,0:T(8,128)S(1)} custom-call(bf16[264,128]{1,0:T(8,128)(2,1)S(1)} %get-tuple-element.47.refs_0_, bf16[264,128]{1,0:T(8,128)(2,1)S(1)} %collective-permute-done.7.refs_1_, bf16[264,128]{1,0:T(8,128)(2,1)S(1)} %collective-permute-done.8.refs_2_, bf16[264,128]{1,0:T(8,128)(2,1)S(1)} %collective-permute-done.9.refs_3_), custom_call_target="tpu_custom_call" | custom-call | flops 1000 | bytes 100000 | tf_op jit(solution)/shard_map/pallas_call | solution.py:401
  30.3 0.4 %shard_map.154.refs_2_ = f32[1024,128]{1,0:T(8,128)S(1)} custom-call(bf16[264,128]{1,0:T(8,128)(2,1)S(1)} %collective-permute-done.5.refs_0_, bf16[264,128]{1,0:T(8,128)(2,1)S(1)} %collective-permute-done.6.refs_1_, f32[1024,128]{1,0:T(8,128)S(1)} %shard_map.153.refs_2_), custom_call_target="tpu_custom_call" | custom-call | flops 1000 | bytes 100000 | tf_op jit(solution)/shard_map/pallas_call | solution.py:401
  30.8 0.2 collective-permute-done.4.refs_1_
  30.9 1.2 %shard_map.156 = (bf16[1024,128]{1,0:T(8,128)(2,1)S(1)}, f32[3,8,128]{2,1,0:T(8,128)S(1)}, f32[3,128]{1,0:T(4,128)S(1)}, f32[3,128]{1,0:T(4,128)S(1)}, f32[3,128]{1,0:T(4,128)S(1)}, /*index=5*/f32[3,128]{1,0:T(4,128)S(1)}) custom-call(bf16[264,128]{1,0:T(8,128)(2,1)S(1)} %collective-permute-done.3.refs_0_, ...), custom_call_target="tpu_custom_call" | custom-call | flops 2000000000 | bytes 100000 | tf_op jit(solution)/shard_map/pallas_call | solution.py:401
  32.1 1.6 %collective-permute-start.10 = (f32[3,128]{1,0:T(4,128)S(1)}, f32[3,128]{1,0:T(4,128)S(1)}, u32[]{:S(2)}, u32[]{:S(2)}) collective-permute-start(f32[3,128]{1,0:T(4,128)S(1)} %get-tuple-element.60), channel_id=1, source_target_pairs={{0,4},{8,12},{16,20},{24,28},{4,0},{12,8},{20,16},{28,24},{1,5},{9... | collective-permute-start | bytes 4616 | tf_op jit(solution)/shard_map/ppermute | solution.py:583
  33.8 3.1 %collective-permute-start.11 = (f32[3,128]{1,0:T(4,128)S(1)}, f32[3,128]{1,0:T(4,128)S(1)}, u32[]{:S(2)}, u32[]{:S(2)}) collective-permute-start(f32[3,128]{1,0:T(4,128)S(1)} %get-tuple-element.61), channel_id=1, source_target_pairs={{4,8},{12,16},{20,24},{0,28},{8,4},{16,12},{24,20},{28,0},{5,9},{1... | collective-permute-start | bytes 4616 | tf_op jit(solution)/shard_map/ppermute | solution.py:583
  36.9 1.6 %collective-permute-start.13 = (f32[3,128]{1,0:T(4,128)S(1)}, f32[3,128]{1,0:T(4,128)S(1)}, u32[]{:S(2)}, u32[]{:S(2)}) collective-permute-start(f32[3,128]{1,0:T(4,128)S(1)} %get-tuple-element.63), channel_id=1, source_target_pairs={{1,2},{0,3},{2,1},{3,0},{5,6},{4,7},{6,5},{7,4},{9,10},{8,11},{10,... | collective-permute-start | bytes 4616 | tf_op jit(solution)/shard_map/ppermute | solution.py:583
  38.5 0.8 %shard_map.157 = bf16[1024,128]{1,0:T(8,128)(2,1)} custom-call(bf16[1024,128]{1,0:T(8,128)(2,1)S(1)} %get-tuple-element.56.arrived, f32[1024,128]{1,0:T(8,128)S(1)} %get-tuple-element.57.drive, f32[1,128]{1,0:T(1,128)S(1)} %bitcast.17), custom_call_target="tpu_custom_call" | custom-call | flops 2000000000 | bytes 100000 | tf_op jit(solution)/shard_map/pallas_call | solution.py:401
  39.3 0.8 %collective-permute-done.11.rest_1_ = f32[3,128]{1,0:T(4,128)S(1)} collective-permute-done((f32[3,128]{1,0:T(4,128)S(1)}, f32[3,128]{1,0:T(4,128)S(1)}, u32[]{:S(2)}, u32[]{:S(2)}) %collective-permute-start.11) | collective-permute-done | bytes 1568 | tf_op jit(solution)/shard_map/ppermute | solution.py:583
  40.0 0.7 %shard_map.158 = f32[3,1024]{1,0:T(4,128)} custom-call(f32[3,8,128]{2,1,0:T(8,128)S(1)} %get-tuple-element.58.local, s32[2,8,128]{2,1,0:T(8,128)S(1)} %get-tuple-element.59.inverse, f32[3,128]{1,0:T(4,128)S(1)} %collective-permute-done.10.rest_0_, f32[3,128]{1,0:T(4,128)S(1)} %collective-permute-done.11.rest_1_, ...), custom_call_target="tpu_custom_call" | custom-call | flops 2000000000 | bytes 100000 | tf_op jit(solution)/shard_map/pallas_call | solution.py:401
  (30 shorter events, 0.1 us)
Async XLA Ops:
  0.6 4.2 %copy-start.8 = (s32[1024]{0:T(1024)S(1)}, s32[1024]{0:T(1024)}, u32[]{:S(2)}) copy-start(s32[1024]{0:T(1024)} %param.20) | copy-start | bytes 12292
  0.6 4.2 %copy-start.7 = (s32[1024]{0:T(1024)S(1)}, s32[1024]{0:T(1024)}, u32[]{:S(2)}) copy-start(s32[1024]{0:T(1024)} %param.19) | copy-start | bytes 12292
  1.7 6.2 %collective-permute-start = (bf16[4,128,128]{2,1,0:T(8,128)(2,1)S(1)}, bf16[4,128,128]{2,1,0:T(8,128)(2,1)S(1)}, u32[]{:S(2)}, u32[]{:S(2)}) collective-permute-start(bf16[4,128,128]{2,1,0:T(8,128)(2,1)S(1)} %get-tuple-element.40), channel_id=1, source_target_pairs={{0,1},{1,0},{2,3},{3,2},{4,5},{5,4},{6,7},{7,6},{8,9},{9,8},{10,11... | collective-permute-start | bytes 393224 | tf_op jit(solution)/shard_map/ppermute | solution.py:486
  2.2 6.9 %collective-permute-start.1 = (bf16[4,128,128]{2,1,0:T(8,128)(2,1)S(1)}, bf16[4,128,128]{2,1,0:T(8,128)(2,1)S(1)}, u32[]{:S(2)}, u32[]{:S(2)}) collective-permute-start(bf16[4,128,128]{2,1,0:T(8,128)(2,1)S(1)} %get-tuple-element.41), channel_id=1, source_target_pairs={{0,2},{1,3},{2,0},{3,1},{4,6},{5,7},{6,4},{7,5},{8,10},{9,11},{10,... | collective-permute-start | bytes 393224 | tf_op jit(solution)/shard_map/ppermute | solution.py:486
  4.8 6.6 %collective-permute-start.2 = (bf16[4,128,128]{2,1,0:T(8,128)(2,1)S(1)}, bf16[4,128,128]{2,1,0:T(8,128)(2,1)S(1)}, u32[]{:S(2)}, u32[]{:S(2)}) collective-permute-start(bf16[4,128,128]{2,1,0:T(8,128)(2,1)S(1)} %get-tuple-element.42), channel_id=1, source_target_pairs={{0,3},{1,2},{2,1},{3,0},{4,7},{5,6},{6,5},{7,4},{8,11},{9,10},{10,... | collective-permute-start | bytes 393224 | tf_op jit(solution)/shard_map/ppermute | solution.py:486
  4.8 1.6 %copy-start.6 = (bf16[8,4,128,128]{3,2,1,0:T(8,128)(2,1)S(1)}, bf16[8,4,128,128]{3,2,1,0:T(8,128)(2,1)}, u32[]{:S(2)}) copy-start(bf16[8,4,128,128]{3,2,1,0:T(8,128)(2,1)} %param.18) | copy-start | bytes 3145732
  4.8 1.6 %copy-start.9 = (s32[8,4]{0,1:T(4,128)S(1)}, s32[8,4]{0,1:T(4,128)}, u32[]{:S(2)}) copy-start(s32[8,4]{0,1:T(4,128)} %param.16) | copy-start | bytes 388
  4.8 1.6 %copy-start.10 = (s32[8]{0:T(128)S(1)}, s32[8]{0:T(128)}, u32[]{:S(2)}) copy-start(s32[8]{0:T(128)} %count.1) | copy-start | bytes 100
  11.4 15.3 %copy-start = (s32[8,1024]{1,0:T(8,128)S(1)}, s32[8,1024]{1,0:T(8,128)}, u32[]{:S(2)}) copy-start(s32[8,1024]{1,0:T(8,128)} %connectivity.1) | copy-start | bytes 98308
  11.4 15.3 %copy-start.1 = (f32[3,1024]{1,0:T(4,128)S(1)}, f32[3,1024]{1,0:T(4,128)}, u32[]{:S(2)}) copy-start(f32[3,1024]{1,0:T(4,128)} %motion.1) | copy-start | bytes 36868
  11.4 15.3 %copy-start.2 = (f32[1024]{0:T(1024)S(1)}, f32[1024]{0:T(1024)}, u32[]{:S(2)}) copy-start(f32[1024]{0:T(1024)} %param.24) | copy-start | bytes 12292
  11.4 15.3 %copy-start.3 = (f32[128,6]{0,1:T(8,128)S(1)}, f32[128,6]{0,1:T(8,128)}, u32[]{:S(2)}) copy-start(f32[128,6]{0,1:T(8,128)} %param.26) | copy-start | bytes 9220
  11.4 15.3 %copy-start.4 = (f32[128,6]{0,1:T(8,128)S(1)}, f32[128,6]{0,1:T(8,128)}, u32[]{:S(2)}) copy-start(f32[128,6]{0,1:T(8,128)} %param.27) | copy-start | bytes 9220
  11.4 15.3 %copy-start.5 = (s32[4,128]{1,0:T(4,128)S(1)}, s32[4,128]{1,0:T(4,128)}, u32[]{:S(2)}) copy-start(s32[4,128]{1,0:T(4,128)} %shared.1) | copy-start | bytes 6148
  11.5 19.5 %copy-start.11 = (f32[128]{0:T(128)S(1)}, f32[128]{0:T(128)}, u32[]{:S(2)}) copy-start(f32[128]{0:T(128)} %param.25) | copy-start | bytes 1540
  13.2 9.2 %collective-permute-start.7 = (bf16[264,128]{1,0:T(8,128)(2,1)S(1)}, bf16[264,128]{1,0:T(8,128)(2,1)S(1)}, u32[]{:S(2)}, u32[]{:S(2)}) collective-permute-start(bf16[264,128]{1,0:T(8,128)(2,1)S(1)} %get-tuple-element.48), channel_id=1, source_target_pairs={{0,28},{4,24},{8,20},{12,16},{16,12},{20,8},{24,4},{28,0},{1,29},{... | collective-permute-start | bytes 202760 | tf_op jit(solution)/shard_map/ppermute | solution.py:551
  17.8 8.2 %collective-permute-start.8 = (bf16[264,128]{1,0:T(8,128)(2,1)S(1)}, bf16[264,128]{1,0:T(8,128)(2,1)S(1)}, u32[]{:S(2)}, u32[]{:S(2)}) collective-permute-start(bf16[264,128]{1,0:T(8,128)(2,1)S(1)} %get-tuple-element.49), channel_id=1, source_target_pairs={{0,20},{4,16},{8,28},{12,24},{16,4},{20,0},{24,12},{28,8},{1,21},{... | collective-permute-start | bytes 202760 | tf_op jit(solution)/shard_map/ppermute | solution.py:551
  17.8 13.0 %collective-permute-start.3 = (bf16[264,128]{1,0:T(8,128)(2,1)S(1)}, bf16[264,128]{1,0:T(8,128)(2,1)S(1)}, u32[]{:S(2)}, u32[]{:S(2)}) collective-permute-start(bf16[264,128]{1,0:T(8,128)(2,1)S(1)} %get-tuple-element.43), channel_id=1, source_target_pairs={{0,16},{4,20},{8,24},{12,28},{16,0},{20,4},{24,8},{28,12},{1,17},{... | collective-permute-start | bytes 202760 | tf_op jit(solution)/shard_map/ppermute | solution.py:551
  20.6 8.9 %collective-permute-start.9 = (bf16[264,128]{1,0:T(8,128)(2,1)S(1)}, bf16[264,128]{1,0:T(8,128)(2,1)S(1)}, u32[]{:S(2)}, u32[]{:S(2)}) collective-permute-start(bf16[264,128]{1,0:T(8,128)(2,1)S(1)} %get-tuple-element.50), channel_id=1, source_target_pairs={{0,4},{4,0},{8,12},{12,8},{16,20},{20,16},{24,28},{28,24},{1,5},{5... | collective-permute-start | bytes 202760 | tf_op jit(solution)/shard_map/ppermute | solution.py:551
  22.1 8.1 %collective-permute-start.5 = (bf16[264,128]{1,0:T(8,128)(2,1)S(1)}, bf16[264,128]{1,0:T(8,128)(2,1)S(1)}, u32[]{:S(2)}, u32[]{:S(2)}) collective-permute-start(bf16[264,128]{1,0:T(8,128)(2,1)S(1)} %get-tuple-element.45), channel_id=1, source_target_pairs={{0,24},{4,28},{8,16},{12,20},{16,8},{20,12},{24,0},{28,4},{1,25},{... | collective-permute-start | bytes 202760 | tf_op jit(solution)/shard_map/ppermute | solution.py:551
  22.4 7.9 %collective-permute-start.6 = (bf16[264,128]{1,0:T(8,128)(2,1)S(1)}, bf16[264,128]{1,0:T(8,128)(2,1)S(1)}, u32[]{:S(2)}, u32[]{:S(2)}) collective-permute-start(bf16[264,128]{1,0:T(8,128)(2,1)S(1)} %get-tuple-element.46), channel_id=1, source_target_pairs={{0,12},{4,8},{8,4},{12,0},{16,28},{20,24},{24,20},{28,16},{1,13},{... | collective-permute-start | bytes 202760 | tf_op jit(solution)/shard_map/ppermute | solution.py:551
  26.0 5.0 %collective-permute-start.4 = (bf16[264,128]{1,0:T(8,128)(2,1)S(1)}, bf16[264,128]{1,0:T(8,128)(2,1)S(1)}, u32[]{:S(2)}, u32[]{:S(2)}) collective-permute-start(bf16[264,128]{1,0:T(8,128)(2,1)S(1)} %get-tuple-element.44), channel_id=1, source_target_pairs={{0,8},{4,12},{8,0},{12,4},{16,24},{20,28},{24,16},{28,20},{1,9},{5... | collective-permute-start | bytes 202760 | tf_op jit(solution)/shard_map/ppermute | solution.py:551
  32.1 7.1 %collective-permute-start.10 = (f32[3,128]{1,0:T(4,128)S(1)}, f32[3,128]{1,0:T(4,128)S(1)}, u32[]{:S(2)}, u32[]{:S(2)}) collective-permute-start(f32[3,128]{1,0:T(4,128)S(1)} %get-tuple-element.60), channel_id=1, source_target_pairs={{0,4},{8,12},{16,20},{24,28},{4,0},{12,8},{20,16},{28,24},{1,5},{9... | collective-permute-start | bytes 4616 | tf_op jit(solution)/shard_map/ppermute | solution.py:583
  33.8 6.3 %collective-permute-start.11 = (f32[3,128]{1,0:T(4,128)S(1)}, f32[3,128]{1,0:T(4,128)S(1)}, u32[]{:S(2)}, u32[]{:S(2)}) collective-permute-start(f32[3,128]{1,0:T(4,128)S(1)} %get-tuple-element.61), channel_id=1, source_target_pairs={{4,8},{12,16},{20,24},{0,28},{8,4},{16,12},{24,20},{28,0},{5,9},{1... | collective-permute-start | bytes 4616 | tf_op jit(solution)/shard_map/ppermute | solution.py:583
  36.9 3.1 %collective-permute-start.12 = (f32[3,128]{1,0:T(4,128)S(1)}, f32[3,128]{1,0:T(4,128)S(1)}, u32[]{:S(2)}, u32[]{:S(2)}) collective-permute-start(f32[3,128]{1,0:T(4,128)S(1)} %get-tuple-element.62), channel_id=1, source_target_pairs={{0,1},{2,3},{1,0},{3,2},{4,5},{6,7},{5,4},{7,6},{8,9},{10,11},{9,8... | collective-permute-start | bytes 4616 | tf_op jit(solution)/shard_map/ppermute | solution.py:583
  36.9 3.1 %collective-permute-start.13 = (f32[3,128]{1,0:T(4,128)S(1)}, f32[3,128]{1,0:T(4,128)S(1)}, u32[]{:S(2)}, u32[]{:S(2)}) collective-permute-start(f32[3,128]{1,0:T(4,128)S(1)} %get-tuple-element.63), channel_id=1, source_target_pairs={{1,2},{0,3},{2,1},{3,0},{5,6},{4,7},{6,5},{7,4},{9,10},{8,11},{10,... | collective-permute-start | bytes 4616 | tf_op jit(solution)/shard_map/ppermute | solution.py:583

commit v9 on v8

--- a/solution.py
+++ b/solution.py
@@ -250,16 +250,24 @@
     inverse[1] = total[groups:]
 
 
-def project_rows(table, blocks, masked, mass_inv, spots, positions, *rest):
+def project_rows(table_in, blocks_in, masked, mass_inv, spots, positions, *rest):
     dom_total = positions.shape[0]
     box_total = lax.axis_size("box")
     received = rest[:box_total]
     outs = rest[box_total : box_total + dom_total]
-    held, turned, ordered = rest[box_total + dom_total :]
+    held, turned, ordered, table, blocks, sems = rest[box_total + dom_total :]
     capacity = received[0].shape[0]
+    copies = [
+        pltpu.make_async_copy(source, target, sems.at[i])
+        for i, (source, target) in enumerate([(table_in, table), (blocks_in, blocks)])
+    ]
+    for copy in copies:
+        copy.start()
     for k, block in enumerate(received):
         for s in range(capacity):
             held[k * capacity + s] = block[s]
+    for copy in copies:
+        copy.wait()
     targets = masked.shape[0]
     entries = masked.shape[1] // LANES
     for t in range(targets):
@@ -409,12 +417,19 @@
     )(*args)
 
 
-def swaps(axis, first):
-    total = lax.axis_size(axis)
-    pairs = [(i, i + 1) for i in range(first, total - 1, 2)]
-    left = sorted(set(range(total)) - {i for pair in pairs for i in pair})
-    pairs += [(left[0], left[-1])] if left else []
-    return [(a, b) for a, b in pairs] + [(b, a) for a, b in pairs if a != b]
+def swaps(which):
+    dom_total, box_total = lax.axis_size("dom"), lax.axis_size("box")
+    pairs = []
+    for d in range(dom_total):
+        for b in range(box_total):
+            here, total = (d, dom_total) if which < 2 else (b, box_total)
+            other = here + (1 - 2 * (here & 1)) * (1 if which % 2 == 0 else -1)
+            if not 0 <= other < total:
+                partner = (d, b ^ 1 if which < 2 else box_total - 1 - b)
+            else:
+                partner = (other, b) if which < 2 else (d, other)
+            pairs.append((d * box_total + b, partner[0] * box_total + partner[1]))
+    return pairs
 
 
 def arrays(shape, dtype):
@@ -537,12 +552,15 @@
         )
         payload = arrays((2 * usual + META, width), BF)
         outgoing = call(
-            project_rows, [SMEM, SMEM] + [VMEM] * (4 + box_total),
+            project_rows, [VMEM] * (6 + box_total),
             [payload] * dom_total,
             [
                 pltpu.VMEM((box_total * capacity, width, block_size), BF),
                 pltpu.VMEM((width, rows), BF),
                 pltpu.VMEM((row_groups, LANES, width), BF),
+                pltpu.SMEM(table.shape, I32),
+                pltpu.SMEM(block_of.shape, I32),
+                pltpu.SemaphoreType.DMA((2,)),
             ],
             (table, block_of, masked, mass_inv, spots, positions, *received),
         )
@@ -579,8 +597,8 @@
     )
     history = call(relax, [VMEM] * 3, arrays((elements, width), BF), [], (arrived, drive, relaxing))
     halo = [None] * 4
-    for m, axis, first in ((3, "box", 1), (1, "dom", 1), (0, "dom", 0), (2, "box", 0)):
-        halo[m] = lax.ppermute(exports[m], axis, swaps(axis, first))
+    for m in (1, 0, 3, 2):
+        halo[m] = lax.ppermute(exports[m], ("dom", "box"), swaps(m))
     force = call(
         add_shared, [VMEM] * (2 + len(halo)), arrays((3, nodes), F32), [],
         (local, inverse, *halo),
@@ -592,8 +610,8 @@
     far = dom_total // 2
     return [
         [dom_total - 1, *range(far + 1, dom_total - 2), 1],
-        [dom_total - 2, far - 1],
-        [far, *range(far - 2, 1, -1)],
+        list(range(far - 1, 1, -1)),
+        [dom_total - 2, far],
     ]
 
 

time: 40.9 us -> 38.6 us (0.944)
  the two profiles are of different devices: /device:TPU:0 before, /device:TPU:5 now
where the time goes in v9:
time: 38.6 us; the launch traced here: 38.4 us
  starting transfers between devices  17 us (44%)
  Pallas kernels  12.3 us (32%)
  waiting for transfers between devices  8.2 us (21%)
  between operations  0.85 us (2%)
    pallas_call x10, Pallas kernels, call(): pl.pallas_call(kernel, out_shape=outs, in_specs=ins, out_specs=out_specs...  12.3 us
    ppermute x7, starting transfers between devices, body(): lax.ppermute(outgoing[k], 'dom', [(i, i ^ k) for i in range(dom_total)])  8.29 us
    ppermute x4, starting transfers between devices, body(): halo[m] = lax.ppermute(exports[m], ('dom', 'box'), swaps(m))  6.3 us
    ppermute x7, waiting for transfers between devices, body(): lax.ppermute(outgoing[k], 'dom', [(i, i ^ k) for i in range(dom_total)])  3.81 us
    ppermute x3, waiting for transfers between devices, body(): lax.ppermute(packed[k], 'box', [(i, i ^ k) for i in range(box_total)])  3.25 us
    ppermute x3, starting transfers between devices, body(): lax.ppermute(packed[k], 'box', [(i, i ^ k) for i in range(box_total)])  2.45 us
    ppermute x4, waiting for transfers between devices, body(): halo[m] = lax.ppermute(exports[m], ('dom', 'box'), swaps(m))  1.14 us
  transfers between devices with their start and end apart: 14, of which 5 were waited for; matrix products, arithmetic and copies ran while one was open for 0% of the time, Pallas kernels for 20%

profile of v9, /device:TPU:5, one launch (start us, length us, event | category | flops | bytes accessed | tf_op | source)
XLA Modules:
  0.0 38.4 jit_solution(2589719051760064496)
XLA Ops:
  0.7 1.0 %shard_map.151 = (bf16[4,128,128]{2,1,0:T(8,128)(2,1)S(1)}, bf16[4,128,128]{2,1,0:T(8,128)(2,1)S(1)}, bf16[4,128,128]{2,1,0:T(8,128)(2,1)S(1)}, bf16[4,128,128]{2,1,0:T(8,128)(2,1)S(1)}) custom-call(s32[8]{0:T(128)} %route_hbm.1, bf16[8,128,128]{2,1,0:T(8,128)(2,1)} %old_hbm.1), custom_call_target="tpu_custom_call" | custom-call | flops 2000000000 | bytes 100000 | tf_op jit(solution)/shard_map/pallas_call | solution.py:409
  1.7 0.7 %collective-permute-start = (bf16[4,128,128]{2,1,0:T(8,128)(2,1)S(1)}, bf16[4,128,128]{2,1,0:T(8,128)(2,1)S(1)}, u32[]{:S(2)}, u32[]{:S(2)}) collective-permute-start(bf16[4,128,128]{2,1,0:T(8,128)(2,1)S(1)} %get-tuple-element.40), channel_id=1, source_target_pairs={{0,1},{1,0},{2,3},{3,2},{4,5},{5,4},{6,7},{7,6},{8,9},{9,8},{10,11... | collective-permute-start | bytes 393224 | tf_op jit(solution)/shard_map/ppermute | solution.py:501
  2.4 1.2 %collective-permute-start.1 = (bf16[4,128,128]{2,1,0:T(8,128)(2,1)S(1)}, bf16[4,128,128]{2,1,0:T(8,128)(2,1)S(1)}, u32[]{:S(2)}, u32[]{:S(2)}) collective-permute-start(bf16[4,128,128]{2,1,0:T(8,128)(2,1)S(1)} %get-tuple-element.41), channel_id=1, source_target_pairs={{0,2},{1,3},{2,0},{3,1},{4,6},{5,7},{6,4},{7,5},{8,10},{9,11},{10,... | collective-permute-start | bytes 393224 | tf_op jit(solution)/shard_map/ppermute | solution.py:501
  3.6 0.5 %collective-permute-start.2 = (bf16[4,128,128]{2,1,0:T(8,128)(2,1)S(1)}, bf16[4,128,128]{2,1,0:T(8,128)(2,1)S(1)}, u32[]{:S(2)}, u32[]{:S(2)}) collective-permute-start(bf16[4,128,128]{2,1,0:T(8,128)(2,1)S(1)} %get-tuple-element.42), channel_id=1, source_target_pairs={{0,3},{1,2},{2,1},{3,0},{4,7},{5,6},{6,5},{7,4},{8,11},{9,10},{10,... | collective-permute-start | bytes 393224 | tf_op jit(solution)/shard_map/ppermute | solution.py:501
  4.1 0.0 copy-start.10
  4.2 1.6 %shard_map.149 = (f32[2,8,128]{2,1,0:T(8,128)S(1)}, bf16[8,8,128]{2,1,0:T(8,128)(2,1)S(1)}, s32[16]{0:T(128)S(1)}) custom-call(s32[8,128]{1,0:T(8,128)S(1)} %bitcast.13, s32[1,1024]{1,0:T(1,128)S(1)} %bitcast.14), custom_call_target="tpu_custom_call" | custom-call | flops 2000000000 | bytes 100000 | tf_op jit(solution)/shard_map/pallas_call | solution.py:409
  5.8 1.4 %shard_map.150 = (bf16[8,512,128]{2,1,0:T(8,128)(2,1)S(1)}, f32[8,128]{1,0:T(8,128)S(1)}, s32[32]{0:T(128)S(1)}) custom-call(s32[4,8]{1,0:T(4,128)S(1)} %bitcast.15, s32[8]{0:T(128)S(1)} %copy-done.10, bf16[8,512,128]{2,1,0:T(8,128)(2,1)S(1)} %bitcast.12), custom_call_target="tpu_custom_call" | custom-call | flops 2000000000 | bytes 100000 | tf_op jit(solution)/shard_map/pallas_call | solution.py:409
  7.2 0.2 collective-permute-done.1.rest_2_
  7.4 3.1 %collective-permute-done.2.rest_3_ = bf16[4,128,128]{2,1,0:T(8,128)(2,1)S(1)} collective-permute-done((bf16[4,128,128]{2,1,0:T(8,128)(2,1)S(1)}, bf16[4,128,128]{2,1,0:T(8,128)(2,1)S(1)}, u32[]{:S(2)}, u32[]{:S(2)}) %collective-permute-start.2) | collective-permute-done | bytes 131104 | tf_op jit(solution)/shard_map/ppermute | solution.py:501
  10.5 0.0 copy-start.4
  10.5 0.0 copy-start.5
  10.5 0.0 copy-start.11
  10.5 1.7 %shard_map.152 = (bf16[264,128]{1,0:T(8,128)(2,1)S(1)}, bf16[264,128]{1,0:T(8,128)(2,1)S(1)}, bf16[264,128]{1,0:T(8,128)(2,1)S(1)}, bf16[264,128]{1,0:T(8,128)(2...) custom-call(s32[16]{0:T(128)S(1)} %get-tuple-element.33.table_in, ...), custom_call_target="tpu_custom_call" | custom-call | flops 2000000000 | bytes 100000 | tf_op jit(solution)/shard_map/pallas_call | solution.py:409
  12.2 3.3 %collective-permute-start.7 = (bf16[264,128]{1,0:T(8,128)(2,1)S(1)}, bf16[264,128]{1,0:T(8,128)(2,1)S(1)}, u32[]{:S(2)}, u32[]{:S(2)}) collective-permute-start(bf16[264,128]{1,0:T(8,128)(2,1)S(1)} %get-tuple-element.48), channel_id=1, source_target_pairs={{0,28},{4,24},{8,20},{12,16},{16,12},{20,8},{24,4},{28,0},{1,29},{... | collective-permute-start | bytes 202760 | tf_op jit(solution)/shard_map/ppermute | solution.py:569
  15.5 0.1 collective-permute-start.8
  15.6 2.2 %collective-permute-start.3 = (bf16[264,128]{1,0:T(8,128)(2,1)S(1)}, bf16[264,128]{1,0:T(8,128)(2,1)S(1)}, u32[]{:S(2)}, u32[]{:S(2)}) collective-permute-start(bf16[264,128]{1,0:T(8,128)(2,1)S(1)} %get-tuple-element.43), channel_id=1, source_target_pairs={{0,24},{4,28},{8,16},{12,20},{16,8},{20,12},{24,0},{28,4},{1,25},{... | collective-permute-start | bytes 202760 | tf_op jit(solution)/shard_map/ppermute | solution.py:569
  17.8 0.2 collective-permute-start.9
  18.1 2.3 %collective-permute-start.5 = (bf16[264,128]{1,0:T(8,128)(2,1)S(1)}, bf16[264,128]{1,0:T(8,128)(2,1)S(1)}, u32[]{:S(2)}, u32[]{:S(2)}) collective-permute-start(bf16[264,128]{1,0:T(8,128)(2,1)S(1)} %get-tuple-element.45), channel_id=1, source_target_pairs={{0,12},{4,8},{8,4},{12,0},{16,28},{20,24},{24,20},{28,16},{1,13},{... | collective-permute-start | bytes 202760 | tf_op jit(solution)/shard_map/ppermute | solution.py:569
  20.3 0.2 collective-permute-start.6
  20.5 3.1 %collective-permute-done.8.refs_2_ = bf16[264,128]{1,0:T(8,128)(2,1)S(1)} collective-permute-done((bf16[264,128]{1,0:T(8,128)(2,1)S(1)}, bf16[264,128]{1,0:T(8,128)(2,1)S(1)}, u32[]{:S(2)}, u32[]{:S(2)}) %collective-permute-start.8) | collective-permute-done | bytes 67616 | tf_op jit(solution)/shard_map/ppermute | solution.py:569
  23.6 2.8 %shard_map.155 = (f32[1024,128]{1,0:T(8,128)S(1)}, f32[8,1024]{1,0:T(8,128)S(1)}, bf16[8,1024,128]{2,1,0:T(8,128)(2,1)S(1)}, bf16[8,16,1024]{2,1,0:T(8,128)(2,1)...) custom-call(s32[8,1024]{1,0:T(8,128)S(1)} %copy-done, f32[3,1024]{1,0:T(4,128)S(1)} %copy-done.1, ...), custom_call_target="tpu_custom_call" | custom-call | flops 1000 | bytes 100000 | tf_op jit(solution)/shard_map/pallas_call | solution.py:409
  26.4 0.7 %shard_map.153.refs_2_ = f32[1024,128]{1,0:T(8,128)S(1)} custom-call(bf16[264,128]{1,0:T(8,128)(2,1)S(1)} %get-tuple-element.47.refs_0_, bf16[264,128]{1,0:T(8,128)(2,1)S(1)} %collective-permute-done.7.refs_1_, bf16[264,128]{1,0:T(8,128)(2,1)S(1)} %collective-permute-done.8.refs_2_, bf16[264,128]{1,0:T(8,128)(2,1)S(1)} %collective-permute-done.9.refs_3_), custom_call_target="tpu_custom_call" | custom-call | flops 1000 | bytes 100000 | tf_op jit(solution)/shard_map/pallas_call | solution.py:409
  27.1 0.4 %shard_map.154.refs_2_ = f32[1024,128]{1,0:T(8,128)S(1)} custom-call(bf16[264,128]{1,0:T(8,128)(2,1)S(1)} %collective-permute-done.5.refs_0_, bf16[264,128]{1,0:T(8,128)(2,1)S(1)} %collective-permute-done.6.refs_1_, f32[1024,128]{1,0:T(8,128)S(1)} %shard_map.153.refs_2_), custom_call_target="tpu_custom_call" | custom-call | flops 1000 | bytes 100000 | tf_op jit(solution)/shard_map/pallas_call | solution.py:409
  27.6 0.7 %collective-permute-done.4.refs_1_ = bf16[264,128]{1,0:T(8,128)(2,1)S(1)} collective-permute-done((bf16[264,128]{1,0:T(8,128)(2,1)S(1)}, bf16[264,128]{1,0:T(8,128)(2,1)S(1)}, u32[]{:S(2)}, u32[]{:S(2)}) %collective-permute-start.4) | collective-permute-done | bytes 67616 | tf_op jit(solution)/shard_map/ppermute | solution.py:569
  28.3 1.2 %shard_map.156 = (bf16[1024,128]{1,0:T(8,128)(2,1)S(1)}, f32[3,8,128]{2,1,0:T(8,128)S(1)}, f32[3,128]{1,0:T(4,128)S(1)}, f32[3,128]{1,0:T(4,128)S(1)}, f32[3,128]{1,0:T(4,128)S(1)}, /*index=5*/f32[3,128]{1,0:T(4,128)S(1)}) custom-call(bf16[264,128]{1,0:T(8,128)(2,1)S(1)} %collective-permute-done.3.refs_0_, ...), custom_call_target="tpu_custom_call" | custom-call | flops 2000000000 | bytes 100000 | tf_op jit(solution)/shard_map/pallas_call | solution.py:409
  29.5 2.7 %collective-permute-start.10 = (f32[3,128]{1,0:T(4,128)S(1)}, f32[3,128]{1,0:T(4,128)S(1)}, u32[]{:S(2)}, u32[]{:S(2)}) collective-permute-start(f32[3,128]{1,0:T(4,128)S(1)} %get-tuple-element.60), channel_id=1, source_target_pairs={{0,4},{1,5},{2,6},{3,7},{4,0},{5,1},{6,2},{7,3},{8,12},{9,13},{10,... | collective-permute-start | bytes 4616 | tf_op jit(solution)/shard_map/ppermute | solution.py:601
  32.2 0.5 %collective-permute-start.11 = (f32[3,128]{1,0:T(4,128)S(1)}, f32[3,128]{1,0:T(4,128)S(1)}, u32[]{:S(2)}, u32[]{:S(2)}) collective-permute-start(f32[3,128]{1,0:T(4,128)S(1)} %get-tuple-element.61), channel_id=1, source_target_pairs={{0,1},{1,0},{2,3},{3,2},{4,8},{5,9},{6,10},{7,11},{8,4},{9,5},{10,... | collective-permute-start | bytes 4616 | tf_op jit(solution)/shard_map/ppermute | solution.py:601
  32.8 2.0 %collective-permute-start.12 = (f32[3,128]{1,0:T(4,128)S(1)}, f32[3,128]{1,0:T(4,128)S(1)}, u32[]{:S(2)}, u32[]{:S(2)}) collective-permute-start(f32[3,128]{1,0:T(4,128)S(1)} %get-tuple-element.62), channel_id=1, source_target_pairs={{0,1},{1,0},{2,3},{3,2},{4,5},{5,4},{6,7},{7,6},{8,9},{9,8},{10,11... | collective-permute-start | bytes 4616 | tf_op jit(solution)/shard_map/ppermute | solution.py:601
  34.7 1.1 %collective-permute-start.13 = (f32[3,128]{1,0:T(4,128)S(1)}, f32[3,128]{1,0:T(4,128)S(1)}, u32[]{:S(2)}, u32[]{:S(2)}) collective-permute-start(f32[3,128]{1,0:T(4,128)S(1)} %get-tuple-element.63), channel_id=1, source_target_pairs={{0,3},{1,2},{2,1},{3,0},{4,7},{5,6},{6,5},{7,4},{8,11},{9,10},{10,... | collective-permute-start | bytes 4616 | tf_op jit(solution)/shard_map/ppermute | solution.py:601
  35.8 0.8 %shard_map.157 = bf16[1024,128]{1,0:T(8,128)(2,1)} custom-call(bf16[1024,128]{1,0:T(8,128)(2,1)S(1)} %get-tuple-element.56.arrived, f32[1024,128]{1,0:T(8,128)S(1)} %get-tuple-element.57.drive, f32[1,128]{1,0:T(1,128)S(1)} %bitcast.17), custom_call_target="tpu_custom_call" | custom-call | flops 2000000000 | bytes 100000 | tf_op jit(solution)/shard_map/pallas_call | solution.py:409
  36.6 1.1 %collective-permute-done.13.rest_3_ = f32[3,128]{1,0:T(4,128)S(1)} collective-permute-done((f32[3,128]{1,0:T(4,128)S(1)}, f32[3,128]{1,0:T(4,128)S(1)}, u32[]{:S(2)}, u32[]{:S(2)}) %collective-permute-start.13) | collective-permute-done | bytes 1568 | tf_op jit(solution)/shard_map/ppermute | solution.py:601
  37.7 0.7 %shard_map.158 = f32[3,1024]{1,0:T(4,128)} custom-call(f32[3,8,128]{2,1,0:T(8,128)S(1)} %get-tuple-element.58.local, s32[2,8,128]{2,1,0:T(8,128)S(1)} %get-tuple-element.59.inverse, f32[3,128]{1,0:T(4,128)S(1)} %collective-permute-done.10.rest_0_, f32[3,128]{1,0:T(4,128)S(1)} %collective-permute-done.11.rest_1_, ...), custom_call_target="tpu_custom_call" | custom-call | flops 2000000000 | bytes 100000 | tf_op jit(solution)/shard_map/pallas_call | solution.py:409
  (30 shorter events, 0.1 us)
Async XLA Ops:
  0.6 3.5 %copy-start.8 = (s32[1024]{0:T(1024)S(1)}, s32[1024]{0:T(1024)}, u32[]{:S(2)}) copy-start(s32[1024]{0:T(1024)} %param.20) | copy-start | bytes 12292
  0.6 3.5 %copy-start.7 = (s32[1024]{0:T(1024)S(1)}, s32[1024]{0:T(1024)}, u32[]{:S(2)}) copy-start(s32[1024]{0:T(1024)} %param.19) | copy-start | bytes 12292
  1.7 5.5 %collective-permute-start = (bf16[4,128,128]{2,1,0:T(8,128)(2,1)S(1)}, bf16[4,128,128]{2,1,0:T(8,128)(2,1)S(1)}, u32[]{:S(2)}, u32[]{:S(2)}) collective-permute-start(bf16[4,128,128]{2,1,0:T(8,128)(2,1)S(1)} %get-tuple-element.40), channel_id=1, source_target_pairs={{0,1},{1,0},{2,3},{3,2},{4,5},{5,4},{6,7},{7,6},{8,9},{9,8},{10,11... | collective-permute-start | bytes 393224 | tf_op jit(solution)/shard_map/ppermute | solution.py:501
  2.4 5.0 %collective-permute-start.1 = (bf16[4,128,128]{2,1,0:T(8,128)(2,1)S(1)}, bf16[4,128,128]{2,1,0:T(8,128)(2,1)S(1)}, u32[]{:S(2)}, u32[]{:S(2)}) collective-permute-start(bf16[4,128,128]{2,1,0:T(8,128)(2,1)S(1)} %get-tuple-element.41), channel_id=1, source_target_pairs={{0,2},{1,3},{2,0},{3,1},{4,6},{5,7},{6,4},{7,5},{8,10},{9,11},{10,... | collective-permute-start | bytes 393224 | tf_op jit(solution)/shard_map/ppermute | solution.py:501
  3.6 6.8 %collective-permute-start.2 = (bf16[4,128,128]{2,1,0:T(8,128)(2,1)S(1)}, bf16[4,128,128]{2,1,0:T(8,128)(2,1)S(1)}, u32[]{:S(2)}, u32[]{:S(2)}) collective-permute-start(bf16[4,128,128]{2,1,0:T(8,128)(2,1)S(1)} %get-tuple-element.42), channel_id=1, source_target_pairs={{0,3},{1,2},{2,1},{3,0},{4,7},{5,6},{6,5},{7,4},{8,11},{9,10},{10,... | collective-permute-start | bytes 393224 | tf_op jit(solution)/shard_map/ppermute | solution.py:501
  4.1 1.6 %copy-start.6 = (bf16[8,4,128,128]{3,2,1,0:T(8,128)(2,1)S(1)}, bf16[8,4,128,128]{3,2,1,0:T(8,128)(2,1)}, u32[]{:S(2)}) copy-start(bf16[8,4,128,128]{3,2,1,0:T(8,128)(2,1)} %param.18) | copy-start | bytes 3145732
  4.1 1.6 %copy-start.9 = (s32[8,4]{0,1:T(4,128)S(1)}, s32[8,4]{0,1:T(4,128)}, u32[]{:S(2)}) copy-start(s32[8,4]{0,1:T(4,128)} %param.16) | copy-start | bytes 388
  4.1 1.6 %copy-start.10 = (s32[8]{0:T(128)S(1)}, s32[8]{0:T(128)}, u32[]{:S(2)}) copy-start(s32[8]{0:T(128)} %count.1) | copy-start | bytes 100
  10.4 13.1 %copy-start = (s32[8,1024]{1,0:T(8,128)S(1)}, s32[8,1024]{1,0:T(8,128)}, u32[]{:S(2)}) copy-start(s32[8,1024]{1,0:T(8,128)} %connectivity.1) | copy-start | bytes 98308
  10.4 13.1 %copy-start.1 = (f32[3,1024]{1,0:T(4,128)S(1)}, f32[3,1024]{1,0:T(4,128)}, u32[]{:S(2)}) copy-start(f32[3,1024]{1,0:T(4,128)} %motion.1) | copy-start | bytes 36868
  10.4 13.1 %copy-start.2 = (f32[1024]{0:T(1024)S(1)}, f32[1024]{0:T(1024)}, u32[]{:S(2)}) copy-start(f32[1024]{0:T(1024)} %param.24) | copy-start | bytes 12292
  10.5 13.1 %copy-start.3 = (f32[128,6]{0,1:T(8,128)S(1)}, f32[128,6]{0,1:T(8,128)}, u32[]{:S(2)}) copy-start(f32[128,6]{0,1:T(8,128)} %param.26) | copy-start | bytes 9220
  10.5 13.1 %copy-start.4 = (f32[128,6]{0,1:T(8,128)S(1)}, f32[128,6]{0,1:T(8,128)}, u32[]{:S(2)}) copy-start(f32[128,6]{0,1:T(8,128)} %param.27) | copy-start | bytes 9220
  10.5 13.1 %copy-start.5 = (s32[4,128]{1,0:T(4,128)S(1)}, s32[4,128]{1,0:T(4,128)}, u32[]{:S(2)}) copy-start(s32[4,128]{1,0:T(4,128)} %shared.1) | copy-start | bytes 6148
  10.5 17.8 %copy-start.11 = (f32[128]{0:T(128)S(1)}, f32[128]{0:T(128)}, u32[]{:S(2)}) copy-start(f32[128]{0:T(128)} %param.25) | copy-start | bytes 1540
  12.2 8.1 %collective-permute-start.7 = (bf16[264,128]{1,0:T(8,128)(2,1)S(1)}, bf16[264,128]{1,0:T(8,128)(2,1)S(1)}, u32[]{:S(2)}, u32[]{:S(2)}) collective-permute-start(bf16[264,128]{1,0:T(8,128)(2,1)S(1)} %get-tuple-element.48), channel_id=1, source_target_pairs={{0,28},{4,24},{8,20},{12,16},{16,12},{20,8},{24,4},{28,0},{1,29},{... | collective-permute-start | bytes 202760 | tf_op jit(solution)/shard_map/ppermute | solution.py:569
  15.5 8.0 %collective-permute-start.8 = (bf16[264,128]{1,0:T(8,128)(2,1)S(1)}, bf16[264,128]{1,0:T(8,128)(2,1)S(1)}, u32[]{:S(2)}, u32[]{:S(2)}) collective-permute-start(bf16[264,128]{1,0:T(8,128)(2,1)S(1)} %get-tuple-element.49), channel_id=1, source_target_pairs={{0,20},{4,16},{8,28},{12,24},{16,4},{20,0},{24,12},{28,8},{1,21},{... | collective-permute-start | bytes 202760 | tf_op jit(solution)/shard_map/ppermute | solution.py:569
  15.6 12.0 %collective-permute-start.3 = (bf16[264,128]{1,0:T(8,128)(2,1)S(1)}, bf16[264,128]{1,0:T(8,128)(2,1)S(1)}, u32[]{:S(2)}, u32[]{:S(2)}) collective-permute-start(bf16[264,128]{1,0:T(8,128)(2,1)S(1)} %get-tuple-element.43), channel_id=1, source_target_pairs={{0,24},{4,28},{8,16},{12,20},{16,8},{20,12},{24,0},{28,4},{1,25},{... | collective-permute-start | bytes 202760 | tf_op jit(solution)/shard_map/ppermute | solution.py:569
  17.8 8.6 %collective-permute-start.9 = (bf16[264,128]{1,0:T(8,128)(2,1)S(1)}, bf16[264,128]{1,0:T(8,128)(2,1)S(1)}, u32[]{:S(2)}, u32[]{:S(2)}) collective-permute-start(bf16[264,128]{1,0:T(8,128)(2,1)S(1)} %get-tuple-element.50), channel_id=1, source_target_pairs={{0,4},{4,0},{8,12},{12,8},{16,20},{20,16},{24,28},{28,24},{1,5},{5... | collective-permute-start | bytes 202760 | tf_op jit(solution)/shard_map/ppermute | solution.py:569
  18.1 9.1 %collective-permute-start.5 = (bf16[264,128]{1,0:T(8,128)(2,1)S(1)}, bf16[264,128]{1,0:T(8,128)(2,1)S(1)}, u32[]{:S(2)}, u32[]{:S(2)}) collective-permute-start(bf16[264,128]{1,0:T(8,128)(2,1)S(1)} %get-tuple-element.45), channel_id=1, source_target_pairs={{0,12},{4,8},{8,4},{12,0},{16,28},{20,24},{24,20},{28,16},{1,13},{... | collective-permute-start | bytes 202760 | tf_op jit(solution)/shard_map/ppermute | solution.py:569
  20.3 6.8 %collective-permute-start.6 = (bf16[264,128]{1,0:T(8,128)(2,1)S(1)}, bf16[264,128]{1,0:T(8,128)(2,1)S(1)}, u32[]{:S(2)}, u32[]{:S(2)}) collective-permute-start(bf16[264,128]{1,0:T(8,128)(2,1)S(1)} %get-tuple-element.46), channel_id=1, source_target_pairs={{0,8},{4,12},{8,0},{12,4},{16,24},{20,28},{24,16},{28,20},{1,9},{5... | collective-permute-start | bytes 202760 | tf_op jit(solution)/shard_map/ppermute | solution.py:569
  23.5 4.8 %collective-permute-start.4 = (bf16[264,128]{1,0:T(8,128)(2,1)S(1)}, bf16[264,128]{1,0:T(8,128)(2,1)S(1)}, u32[]{:S(2)}, u32[]{:S(2)}) collective-permute-start(bf16[264,128]{1,0:T(8,128)(2,1)S(1)} %get-tuple-element.44), channel_id=1, source_target_pairs={{0,16},{4,20},{8,24},{12,28},{16,0},{20,4},{24,8},{28,12},{1,17},{... | collective-permute-start | bytes 202760 | tf_op jit(solution)/shard_map/ppermute | solution.py:569
  29.5 7.1 %collective-permute-start.10 = (f32[3,128]{1,0:T(4,128)S(1)}, f32[3,128]{1,0:T(4,128)S(1)}, u32[]{:S(2)}, u32[]{:S(2)}) collective-permute-start(f32[3,128]{1,0:T(4,128)S(1)} %get-tuple-element.60), channel_id=1, source_target_pairs={{0,4},{1,5},{2,6},{3,7},{4,0},{5,1},{6,2},{7,3},{8,12},{9,13},{10,... | collective-permute-start | bytes 4616 | tf_op jit(solution)/shard_map/ppermute | solution.py:601
  32.2 4.4 %collective-permute-start.11 = (f32[3,128]{1,0:T(4,128)S(1)}, f32[3,128]{1,0:T(4,128)S(1)}, u32[]{:S(2)}, u32[]{:S(2)}) collective-permute-start(f32[3,128]{1,0:T(4,128)S(1)} %get-tuple-element.61), channel_id=1, source_target_pairs={{0,1},{1,0},{2,3},{3,2},{4,8},{5,9},{6,10},{7,11},{8,4},{9,5},{10,... | collective-permute-start | bytes 4616 | tf_op jit(solution)/shard_map/ppermute | solution.py:601
  32.8 3.8 %collective-permute-start.12 = (f32[3,128]{1,0:T(4,128)S(1)}, f32[3,128]{1,0:T(4,128)S(1)}, u32[]{:S(2)}, u32[]{:S(2)}) collective-permute-start(f32[3,128]{1,0:T(4,128)S(1)} %get-tuple-element.62), channel_id=1, source_target_pairs={{0,1},{1,0},{2,3},{3,2},{4,5},{5,4},{6,7},{7,6},{8,9},{9,8},{10,11... | collective-permute-start | bytes 4616 | tf_op jit(solution)/shard_map/ppermute | solution.py:601
  34.7 3.0 %collective-permute-start.13 = (f32[3,128]{1,0:T(4,128)S(1)}, f32[3,128]{1,0:T(4,128)S(1)}, u32[]{:S(2)}, u32[]{:S(2)}) collective-permute-start(f32[3,128]{1,0:T(4,128)S(1)} %get-tuple-element.63), channel_id=1, source_target_pairs={{0,3},{1,2},{2,1},{3,0},{4,7},{5,6},{6,5},{7,4},{8,11},{9,10},{10,... | collective-permute-start | bytes 4616 | tf_op jit(solution)/shard_map/ppermute | solution.py:601

commit v10 on v9

--- a/solution.py
+++ b/solution.py
@@ -279,10 +279,10 @@
     high, low = spots[0], spots[1]
     rows = turned.shape[1]
     sort = jnp.zeros((rows, LANES), F32)
-    for g in range(0, rows // LANES, 2):
+    for g in range(rows // LANES):
         sort = sort + lax.dot_general(
-            marks(side_by_side(high, g, 2), side_by_side(low, g, 2), rows),
-            turned[:, g * LANES : (g + 2) * LANES],
+            marks(high[g : g + 1], low[g : g + 1], rows),
+            turned[:, g * LANES : (g + 1) * LANES],
             NT_DIMS,
             preferred_element_type=F32,
         )
@@ -607,11 +607,11 @@
 
 
 def arrival(dom_total):
-    far = dom_total // 2
+    far, last = dom_total // 2, dom_total - 1
     return [
-        [dom_total - 1, *range(far + 1, dom_total - 2), 1],
-        list(range(far - 1, 1, -1)),
-        [dom_total - 2, far],
+        [far, last, 1],
+        [last - 1, far - 1],
+        [*range(far + 1, last - 1), *range(2, far - 1)],
     ]
 
 

time: 38.6 us -> 37.9 us (0.982)
  the two profiles are of different devices: /device:TPU:5 before, /device:TPU:0 now
where the time goes in v10:
time: 37.9 us; the launch traced here: 37.8 us
  starting transfers between devices  20 us (53%)
  Pallas kernels  12.2 us (32%)
  waiting for transfers between devices  4.68 us (12%)
  between operations  0.85 us (2%)
    ppermute x7, starting transfers between devices, body(): lax.ppermute(outgoing[k], 'dom', [(i, i ^ k) for i in range(dom_total)])  13.8 us
    pallas_call x10, Pallas kernels, call(): pl.pallas_call(kernel, out_shape=outs, in_specs=ins, out_specs=out_specs...  12.2 us
    ppermute x3, waiting for transfers between devices, body(): lax.ppermute(packed[k], 'box', [(i, i ^ k) for i in range(box_total)])  3.53 us
    ppermute x3, starting transfers between devices, body(): lax.ppermute(packed[k], 'box', [(i, i ^ k) for i in range(box_total)])  3.15 us
    ppermute x4, starting transfers between devices, body(): halo[m] = lax.ppermute(exports[m], ('dom', 'box'), swaps(m))  3.05 us
    ppermute x4, waiting for transfers between devices, body(): halo[m] = lax.ppermute(exports[m], ('dom', 'box'), swaps(m))  1.13 us
  transfers between devices with their start and end apart: 14, of which 3 were waited for; matrix products, arithmetic and copies ran while one was open for 0% of the time, Pallas kernels for 20%

profile of v10, /device:TPU:0, one launch (start us, length us, event | category | flops | bytes accessed | tf_op | source)
XLA Modules:
  0.0 37.8 jit_solution(1061716011518860486)
XLA Ops:
  0.7 1.0 %shard_map.151 = (bf16[4,128,128]{2,1,0:T(8,128)(2,1)S(1)}, bf16[4,128,128]{2,1,0:T(8,128)(2,1)S(1)}, bf16[4,128,128]{2,1,0:T(8,128)(2,1)S(1)}, bf16[4,128,128]{2,1,0:T(8,128)(2,1)S(1)}) custom-call(s32[8]{0:T(128)} %route_hbm.1, bf16[8,128,128]{2,1,0:T(8,128)(2,1)} %old_hbm.1), custom_call_target="tpu_custom_call" | custom-call | flops 2000000000 | bytes 100000 | tf_op jit(solution)/shard_map/pallas_call | solution.py:409
  1.7 0.6 %collective-permute-start = (bf16[4,128,128]{2,1,0:T(8,128)(2,1)S(1)}, bf16[4,128,128]{2,1,0:T(8,128)(2,1)S(1)}, u32[]{:S(2)}, u32[]{:S(2)}) collective-permute-start(bf16[4,128,128]{2,1,0:T(8,128)(2,1)S(1)} %get-tuple-element.40), channel_id=1, source_target_pairs={{0,1},{1,0},{2,3},{3,2},{4,5},{5,4},{6,7},{7,6},{8,9},{9,8},{10,11... | collective-permute-start | bytes 393224 | tf_op jit(solution)/shard_map/ppermute | solution.py:501
  2.2 2.6 %collective-permute-start.1 = (bf16[4,128,128]{2,1,0:T(8,128)(2,1)S(1)}, bf16[4,128,128]{2,1,0:T(8,128)(2,1)S(1)}, u32[]{:S(2)}, u32[]{:S(2)}) collective-permute-start(bf16[4,128,128]{2,1,0:T(8,128)(2,1)S(1)} %get-tuple-element.41), channel_id=1, source_target_pairs={{0,2},{1,3},{2,0},{3,1},{4,6},{5,7},{6,4},{7,5},{8,10},{9,11},{10,... | collective-permute-start | bytes 393224 | tf_op jit(solution)/shard_map/ppermute | solution.py:501
  4.8 0.0 collective-permute-start.2
  4.8 0.0 copy-start.10
  4.8 1.6 %shard_map.149 = (f32[2,8,128]{2,1,0:T(8,128)S(1)}, bf16[8,8,128]{2,1,0:T(8,128)(2,1)S(1)}, s32[16]{0:T(128)S(1)}) custom-call(s32[8,128]{1,0:T(8,128)S(1)} %bitcast.13, s32[1,1024]{1,0:T(1,128)S(1)} %bitcast.14), custom_call_target="tpu_custom_call" | custom-call | flops 2000000000 | bytes 100000 | tf_op jit(solution)/shard_map/pallas_call | solution.py:409
  6.5 1.4 %shard_map.150 = (bf16[8,512,128]{2,1,0:T(8,128)(2,1)S(1)}, f32[8,128]{1,0:T(8,128)S(1)}, s32[32]{0:T(128)S(1)}) custom-call(s32[4,8]{1,0:T(4,128)S(1)} %bitcast.15, s32[8]{0:T(128)S(1)} %copy-done.10, bf16[8,512,128]{2,1,0:T(8,128)(2,1)S(1)} %bitcast.12), custom_call_target="tpu_custom_call" | custom-call | flops 2000000000 | bytes 100000 | tf_op jit(solution)/shard_map/pallas_call | solution.py:409
  7.9 1.2 %collective-permute-done.1.rest_2_ = bf16[4,128,128]{2,1,0:T(8,128)(2,1)S(1)} collective-permute-done((bf16[4,128,128]{2,1,0:T(8,128)(2,1)S(1)}, bf16[4,128,128]{2,1,0:T(8,128)(2,1)S(1)}, u32[]{:S(2)}, u32[]{:S(2)}) %collective-permute-start.1) | collective-permute-done | bytes 131104 | tf_op jit(solution)/shard_map/ppermute | solution.py:501
  9.1 2.3 %collective-permute-done.2.rest_3_ = bf16[4,128,128]{2,1,0:T(8,128)(2,1)S(1)} collective-permute-done((bf16[4,128,128]{2,1,0:T(8,128)(2,1)S(1)}, bf16[4,128,128]{2,1,0:T(8,128)(2,1)S(1)}, u32[]{:S(2)}, u32[]{:S(2)}) %collective-permute-start.2) | collective-permute-done | bytes 131104 | tf_op jit(solution)/shard_map/ppermute | solution.py:501
  11.4 0.0 copy-start.4
  11.4 0.0 copy-start.5
  11.5 0.0 copy-start.11
  11.5 1.6 %shard_map.152 = (bf16[264,128]{1,0:T(8,128)(2,1)S(1)}, bf16[264,128]{1,0:T(8,128)(2,1)S(1)}, bf16[264,128]{1,0:T(8,128)(2,1)S(1)}, bf16[264,128]{1,0:T(8,128)(2...) custom-call(s32[16]{0:T(128)S(1)} %get-tuple-element.33.table_in, ...), custom_call_target="tpu_custom_call" | custom-call | flops 2000000000 | bytes 100000 | tf_op jit(solution)/shard_map/pallas_call | solution.py:409
  13.1 2.6 %collective-permute-start.7 = (bf16[264,128]{1,0:T(8,128)(2,1)S(1)}, bf16[264,128]{1,0:T(8,128)(2,1)S(1)}, u32[]{:S(2)}, u32[]{:S(2)}) collective-permute-start(bf16[264,128]{1,0:T(8,128)(2,1)S(1)} %get-tuple-element.48), channel_id=1, source_target_pairs={{0,16},{4,20},{8,24},{12,28},{16,0},{20,4},{24,8},{28,12},{1,17},{... | collective-permute-start | bytes 202760 | tf_op jit(solution)/shard_map/ppermute | solution.py:569
  15.7 2.3 %collective-permute-start.8 = (bf16[264,128]{1,0:T(8,128)(2,1)S(1)}, bf16[264,128]{1,0:T(8,128)(2,1)S(1)}, u32[]{:S(2)}, u32[]{:S(2)}) collective-permute-start(bf16[264,128]{1,0:T(8,128)(2,1)S(1)} %get-tuple-element.49), channel_id=1, source_target_pairs={{0,28},{4,24},{8,20},{12,16},{16,12},{20,8},{24,4},{28,0},{1,29},{... | collective-permute-start | bytes 202760 | tf_op jit(solution)/shard_map/ppermute | solution.py:569
  18.0 1.6 %collective-permute-start.3 = (bf16[264,128]{1,0:T(8,128)(2,1)S(1)}, bf16[264,128]{1,0:T(8,128)(2,1)S(1)}, u32[]{:S(2)}, u32[]{:S(2)}) collective-permute-start(bf16[264,128]{1,0:T(8,128)(2,1)S(1)} %get-tuple-element.43), channel_id=1, source_target_pairs={{0,20},{4,16},{8,28},{12,24},{16,4},{20,0},{24,12},{28,8},{1,21},{... | collective-permute-start | bytes 202760 | tf_op jit(solution)/shard_map/ppermute | solution.py:569
  19.7 1.5 %collective-permute-start.9 = (bf16[264,128]{1,0:T(8,128)(2,1)S(1)}, bf16[264,128]{1,0:T(8,128)(2,1)S(1)}, u32[]{:S(2)}, u32[]{:S(2)}) collective-permute-start(bf16[264,128]{1,0:T(8,128)(2,1)S(1)} %get-tuple-element.50), channel_id=1, source_target_pairs={{0,4},{4,0},{8,12},{12,8},{16,20},{20,16},{24,28},{28,24},{1,5},{5... | collective-permute-start | bytes 202760 | tf_op jit(solution)/shard_map/ppermute | solution.py:569
  21.2 0.2 collective-permute-start.5
  21.4 4.5 %collective-permute-start.6 = (bf16[264,128]{1,0:T(8,128)(2,1)S(1)}, bf16[264,128]{1,0:T(8,128)(2,1)S(1)}, u32[]{:S(2)}, u32[]{:S(2)}) collective-permute-start(bf16[264,128]{1,0:T(8,128)(2,1)S(1)} %get-tuple-element.46), channel_id=1, source_target_pairs={{0,12},{4,8},{8,4},{12,0},{16,28},{20,24},{24,20},{28,16},{1,13},{... | collective-permute-start | bytes 202760 | tf_op jit(solution)/shard_map/ppermute | solution.py:569
  25.9 1.0 %collective-permute-start.4 = (bf16[264,128]{1,0:T(8,128)(2,1)S(1)}, bf16[264,128]{1,0:T(8,128)(2,1)S(1)}, u32[]{:S(2)}, u32[]{:S(2)}) collective-permute-start(bf16[264,128]{1,0:T(8,128)(2,1)S(1)} %get-tuple-element.44), channel_id=1, source_target_pairs={{0,8},{4,12},{8,0},{12,4},{16,24},{20,28},{24,16},{28,20},{1,9},{5... | collective-permute-start | bytes 202760 | tf_op jit(solution)/shard_map/ppermute | solution.py:569
  26.9 2.8 %shard_map.155 = (f32[1024,128]{1,0:T(8,128)S(1)}, f32[8,1024]{1,0:T(8,128)S(1)}, bf16[8,1024,128]{2,1,0:T(8,128)(2,1)S(1)}, bf16[8,16,1024]{2,1,0:T(8,128)(2,1)...) custom-call(s32[8,1024]{1,0:T(8,128)S(1)} %copy-done, f32[3,1024]{1,0:T(4,128)S(1)} %copy-done.1, ...), custom_call_target="tpu_custom_call" | custom-call | flops 1000 | bytes 100000 | tf_op jit(solution)/shard_map/pallas_call | solution.py:409
  29.7 0.7 %shard_map.153.refs_2_ = f32[1024,128]{1,0:T(8,128)S(1)} custom-call(bf16[264,128]{1,0:T(8,128)(2,1)S(1)} %get-tuple-element.47.refs_0_, bf16[264,128]{1,0:T(8,128)(2,1)S(1)} %collective-permute-done.7.refs_1_, bf16[264,128]{1,0:T(8,128)(2,1)S(1)} %collective-permute-done.8.refs_2_, bf16[264,128]{1,0:T(8,128)(2,1)S(1)} %collective-permute-done.9.refs_3_), custom_call_target="tpu_custom_call" | custom-call | flops 1000 | bytes 100000 | tf_op jit(solution)/shard_map/pallas_call | solution.py:409
  30.5 0.0 collective-permute-done.6.refs_1_
  30.5 0.4 %shard_map.154.refs_2_ = f32[1024,128]{1,0:T(8,128)S(1)} custom-call(bf16[264,128]{1,0:T(8,128)(2,1)S(1)} %collective-permute-done.5.refs_0_, bf16[264,128]{1,0:T(8,128)(2,1)S(1)} %collective-permute-done.6.refs_1_, f32[1024,128]{1,0:T(8,128)S(1)} %shard_map.153.refs_2_), custom_call_target="tpu_custom_call" | custom-call | flops 1000 | bytes 100000 | tf_op jit(solution)/shard_map/pallas_call | solution.py:409
  30.9 0.0 collective-permute-done.3.refs_0_
  30.9 1.2 %shard_map.156 = (bf16[1024,128]{1,0:T(8,128)(2,1)S(1)}, f32[3,8,128]{2,1,0:T(8,128)S(1)}, f32[3,128]{1,0:T(4,128)S(1)}, f32[3,128]{1,0:T(4,128)S(1)}, f32[3,128]{1,0:T(4,128)S(1)}, /*index=5*/f32[3,128]{1,0:T(4,128)S(1)}) custom-call(bf16[264,128]{1,0:T(8,128)(2,1)S(1)} %collective-permute-done.3.refs_0_, ...), custom_call_target="tpu_custom_call" | custom-call | flops 2000000000 | bytes 100000 | tf_op jit(solution)/shard_map/pallas_call | solution.py:409
  32.1 1.4 %collective-permute-start.10 = (f32[3,128]{1,0:T(4,128)S(1)}, f32[3,128]{1,0:T(4,128)S(1)}, u32[]{:S(2)}, u32[]{:S(2)}) collective-permute-start(f32[3,128]{1,0:T(4,128)S(1)} %get-tuple-element.60), channel_id=1, source_target_pairs={{0,4},{1,5},{2,6},{3,7},{4,0},{5,1},{6,2},{7,3},{8,12},{9,13},{10,... | collective-permute-start | bytes 4616 | tf_op jit(solution)/shard_map/ppermute | solution.py:601
  33.6 0.5 %collective-permute-start.12 = (f32[3,128]{1,0:T(4,128)S(1)}, f32[3,128]{1,0:T(4,128)S(1)}, u32[]{:S(2)}, u32[]{:S(2)}) collective-permute-start(f32[3,128]{1,0:T(4,128)S(1)} %get-tuple-element.62), channel_id=1, source_target_pairs={{0,1},{1,0},{2,3},{3,2},{4,5},{5,4},{6,7},{7,6},{8,9},{9,8},{10,11... | collective-permute-start | bytes 4616 | tf_op jit(solution)/shard_map/ppermute | solution.py:601
  34.1 1.1 %collective-permute-start.13 = (f32[3,128]{1,0:T(4,128)S(1)}, f32[3,128]{1,0:T(4,128)S(1)}, u32[]{:S(2)}, u32[]{:S(2)}) collective-permute-start(f32[3,128]{1,0:T(4,128)S(1)} %get-tuple-element.63), channel_id=1, source_target_pairs={{0,3},{1,2},{2,1},{3,0},{4,7},{5,6},{6,5},{7,4},{8,11},{9,10},{10,... | collective-permute-start | bytes 4616 | tf_op jit(solution)/shard_map/ppermute | solution.py:601
  35.2 0.8 %shard_map.157 = bf16[1024,128]{1,0:T(8,128)(2,1)} custom-call(bf16[1024,128]{1,0:T(8,128)(2,1)S(1)} %get-tuple-element.56.arrived, f32[1024,128]{1,0:T(8,128)S(1)} %get-tuple-element.57.drive, f32[1,128]{1,0:T(1,128)S(1)} %bitcast.17), custom_call_target="tpu_custom_call" | custom-call | flops 2000000000 | bytes 100000 | tf_op jit(solution)/shard_map/pallas_call | solution.py:409
  36.0 1.1 %collective-permute-done.13.rest_3_ = f32[3,128]{1,0:T(4,128)S(1)} collective-permute-done((f32[3,128]{1,0:T(4,128)S(1)}, f32[3,128]{1,0:T(4,128)S(1)}, u32[]{:S(2)}, u32[]{:S(2)}) %collective-permute-start.13) | collective-permute-done | bytes 1568 | tf_op jit(solution)/shard_map/ppermute | solution.py:601
  37.1 0.7 %shard_map.158 = f32[3,1024]{1,0:T(4,128)} custom-call(f32[3,8,128]{2,1,0:T(8,128)S(1)} %get-tuple-element.58.local, s32[2,8,128]{2,1,0:T(8,128)S(1)} %get-tuple-element.59.inverse, f32[3,128]{1,0:T(4,128)S(1)} %collective-permute-done.10.rest_0_, f32[3,128]{1,0:T(4,128)S(1)} %collective-permute-done.11.rest_1_, ...), custom_call_target="tpu_custom_call" | custom-call | flops 2000000000 | bytes 100000 | tf_op jit(solution)/shard_map/pallas_call | solution.py:409
  (30 shorter events, 0.1 us)
Async XLA Ops:
  0.6 4.2 %copy-start.8 = (s32[1024]{0:T(1024)S(1)}, s32[1024]{0:T(1024)}, u32[]{:S(2)}) copy-start(s32[1024]{0:T(1024)} %param.20) | copy-start | bytes 12292
  0.6 4.2 %copy-start.7 = (s32[1024]{0:T(1024)S(1)}, s32[1024]{0:T(1024)}, u32[]{:S(2)}) copy-start(s32[1024]{0:T(1024)} %param.19) | copy-start | bytes 12292
  1.7 6.2 %collective-permute-start = (bf16[4,128,128]{2,1,0:T(8,128)(2,1)S(1)}, bf16[4,128,128]{2,1,0:T(8,128)(2,1)S(1)}, u32[]{:S(2)}, u32[]{:S(2)}) collective-permute-start(bf16[4,128,128]{2,1,0:T(8,128)(2,1)S(1)} %get-tuple-element.40), channel_id=1, source_target_pairs={{0,1},{1,0},{2,3},{3,2},{4,5},{5,4},{6,7},{7,6},{8,9},{9,8},{10,11... | collective-permute-start | bytes 393224 | tf_op jit(solution)/shard_map/ppermute | solution.py:501
  2.2 6.9 %collective-permute-start.1 = (bf16[4,128,128]{2,1,0:T(8,128)(2,1)S(1)}, bf16[4,128,128]{2,1,0:T(8,128)(2,1)S(1)}, u32[]{:S(2)}, u32[]{:S(2)}) collective-permute-start(bf16[4,128,128]{2,1,0:T(8,128)(2,1)S(1)} %get-tuple-element.41), channel_id=1, source_target_pairs={{0,2},{1,3},{2,0},{3,1},{4,6},{5,7},{6,4},{7,5},{8,10},{9,11},{10,... | collective-permute-start | bytes 393224 | tf_op jit(solution)/shard_map/ppermute | solution.py:501
  4.8 6.6 %collective-permute-start.2 = (bf16[4,128,128]{2,1,0:T(8,128)(2,1)S(1)}, bf16[4,128,128]{2,1,0:T(8,128)(2,1)S(1)}, u32[]{:S(2)}, u32[]{:S(2)}) collective-permute-start(bf16[4,128,128]{2,1,0:T(8,128)(2,1)S(1)} %get-tuple-element.42), channel_id=1, source_target_pairs={{0,3},{1,2},{2,1},{3,0},{4,7},{5,6},{6,5},{7,4},{8,11},{9,10},{10,... | collective-permute-start | bytes 393224 | tf_op jit(solution)/shard_map/ppermute | solution.py:501
  4.8 1.6 %copy-start.6 = (bf16[8,4,128,128]{3,2,1,0:T(8,128)(2,1)S(1)}, bf16[8,4,128,128]{3,2,1,0:T(8,128)(2,1)}, u32[]{:S(2)}) copy-start(bf16[8,4,128,128]{3,2,1,0:T(8,128)(2,1)} %param.18) | copy-start | bytes 3145732
  4.8 1.6 %copy-start.9 = (s32[8,4]{0,1:T(4,128)S(1)}, s32[8,4]{0,1:T(4,128)}, u32[]{:S(2)}) copy-start(s32[8,4]{0,1:T(4,128)} %param.16) | copy-start | bytes 388
  4.8 1.6 %copy-start.10 = (s32[8]{0:T(128)S(1)}, s32[8]{0:T(128)}, u32[]{:S(2)}) copy-start(s32[8]{0:T(128)} %count.1) | copy-start | bytes 100
  11.4 15.5 %copy-start = (s32[8,1024]{1,0:T(8,128)S(1)}, s32[8,1024]{1,0:T(8,128)}, u32[]{:S(2)}) copy-start(s32[8,1024]{1,0:T(8,128)} %connectivity.1) | copy-start | bytes 98308
  11.4 15.5 %copy-start.1 = (f32[3,1024]{1,0:T(4,128)S(1)}, f32[3,1024]{1,0:T(4,128)}, u32[]{:S(2)}) copy-start(f32[3,1024]{1,0:T(4,128)} %motion.1) | copy-start | bytes 36868
  11.4 15.5 %copy-start.2 = (f32[1024]{0:T(1024)S(1)}, f32[1024]{0:T(1024)}, u32[]{:S(2)}) copy-start(f32[1024]{0:T(1024)} %param.24) | copy-start | bytes 12292
  11.4 15.5 %copy-start.3 = (f32[128,6]{0,1:T(8,128)S(1)}, f32[128,6]{0,1:T(8,128)}, u32[]{:S(2)}) copy-start(f32[128,6]{0,1:T(8,128)} %param.26) | copy-start | bytes 9220
  11.4 15.5 %copy-start.4 = (f32[128,6]{0,1:T(8,128)S(1)}, f32[128,6]{0,1:T(8,128)}, u32[]{:S(2)}) copy-start(f32[128,6]{0,1:T(8,128)} %param.27) | copy-start | bytes 9220
  11.4 15.5 %copy-start.5 = (s32[4,128]{1,0:T(4,128)S(1)}, s32[4,128]{1,0:T(4,128)}, u32[]{:S(2)}) copy-start(s32[4,128]{1,0:T(4,128)} %shared.1) | copy-start | bytes 6148
  11.5 19.5 %copy-start.11 = (f32[128]{0:T(128)S(1)}, f32[128]{0:T(128)}, u32[]{:S(2)}) copy-start(f32[128]{0:T(128)} %param.25) | copy-start | bytes 1540
  13.1 8.3 %collective-permute-start.7 = (bf16[264,128]{1,0:T(8,128)(2,1)S(1)}, bf16[264,128]{1,0:T(8,128)(2,1)S(1)}, u32[]{:S(2)}, u32[]{:S(2)}) collective-permute-start(bf16[264,128]{1,0:T(8,128)(2,1)S(1)} %get-tuple-element.48), channel_id=1, source_target_pairs={{0,16},{4,20},{8,24},{12,28},{16,0},{20,4},{24,8},{28,12},{1,17},{... | collective-permute-start | bytes 202760 | tf_op jit(solution)/shard_map/ppermute | solution.py:569
  15.7 10.2 %collective-permute-start.8 = (bf16[264,128]{1,0:T(8,128)(2,1)S(1)}, bf16[264,128]{1,0:T(8,128)(2,1)S(1)}, u32[]{:S(2)}, u32[]{:S(2)}) collective-permute-start(bf16[264,128]{1,0:T(8,128)(2,1)S(1)} %get-tuple-element.49), channel_id=1, source_target_pairs={{0,28},{4,24},{8,20},{12,16},{16,12},{20,8},{24,4},{28,0},{1,29},{... | collective-permute-start | bytes 202760 | tf_op jit(solution)/shard_map/ppermute | solution.py:569
  18.0 12.9 %collective-permute-start.3 = (bf16[264,128]{1,0:T(8,128)(2,1)S(1)}, bf16[264,128]{1,0:T(8,128)(2,1)S(1)}, u32[]{:S(2)}, u32[]{:S(2)}) collective-permute-start(bf16[264,128]{1,0:T(8,128)(2,1)S(1)} %get-tuple-element.43), channel_id=1, source_target_pairs={{0,20},{4,16},{8,28},{12,24},{16,4},{20,0},{24,12},{28,8},{1,21},{... | collective-permute-start | bytes 202760 | tf_op jit(solution)/shard_map/ppermute | solution.py:569
  19.7 10.0 %collective-permute-start.9 = (bf16[264,128]{1,0:T(8,128)(2,1)S(1)}, bf16[264,128]{1,0:T(8,128)(2,1)S(1)}, u32[]{:S(2)}, u32[]{:S(2)}) collective-permute-start(bf16[264,128]{1,0:T(8,128)(2,1)S(1)} %get-tuple-element.50), channel_id=1, source_target_pairs={{0,4},{4,0},{8,12},{12,8},{16,20},{20,16},{24,28},{28,24},{1,5},{5... | collective-permute-start | bytes 202760 | tf_op jit(solution)/shard_map/ppermute | solution.py:569
  21.2 9.2 %collective-permute-start.5 = (bf16[264,128]{1,0:T(8,128)(2,1)S(1)}, bf16[264,128]{1,0:T(8,128)(2,1)S(1)}, u32[]{:S(2)}, u32[]{:S(2)}) collective-permute-start(bf16[264,128]{1,0:T(8,128)(2,1)S(1)} %get-tuple-element.45), channel_id=1, source_target_pairs={{0,24},{4,28},{8,16},{12,20},{16,8},{20,12},{24,0},{28,4},{1,25},{... | collective-permute-start | bytes 202760 | tf_op jit(solution)/shard_map/ppermute | solution.py:569
  21.4 9.0 %collective-permute-start.6 = (bf16[264,128]{1,0:T(8,128)(2,1)S(1)}, bf16[264,128]{1,0:T(8,128)(2,1)S(1)}, u32[]{:S(2)}, u32[]{:S(2)}) collective-permute-start(bf16[264,128]{1,0:T(8,128)(2,1)S(1)} %get-tuple-element.46), channel_id=1, source_target_pairs={{0,12},{4,8},{8,4},{12,0},{16,28},{20,24},{24,20},{28,16},{1,13},{... | collective-permute-start | bytes 202760 | tf_op jit(solution)/shard_map/ppermute | solution.py:569
  25.9 5.0 %collective-permute-start.4 = (bf16[264,128]{1,0:T(8,128)(2,1)S(1)}, bf16[264,128]{1,0:T(8,128)(2,1)S(1)}, u32[]{:S(2)}, u32[]{:S(2)}) collective-permute-start(bf16[264,128]{1,0:T(8,128)(2,1)S(1)} %get-tuple-element.44), channel_id=1, source_target_pairs={{0,8},{4,12},{8,0},{12,4},{16,24},{20,28},{24,16},{28,20},{1,9},{5... | collective-permute-start | bytes 202760 | tf_op jit(solution)/shard_map/ppermute | solution.py:569
  32.1 3.8 %collective-permute-start.10 = (f32[3,128]{1,0:T(4,128)S(1)}, f32[3,128]{1,0:T(4,128)S(1)}, u32[]{:S(2)}, u32[]{:S(2)}) collective-permute-start(f32[3,128]{1,0:T(4,128)S(1)} %get-tuple-element.60), channel_id=1, source_target_pairs={{0,4},{1,5},{2,6},{3,7},{4,0},{5,1},{6,2},{7,3},{8,12},{9,13},{10,... | collective-permute-start | bytes 4616 | tf_op jit(solution)/shard_map/ppermute | solution.py:601
  33.6 2.4 %collective-permute-start.11 = (f32[3,128]{1,0:T(4,128)S(1)}, f32[3,128]{1,0:T(4,128)S(1)}, u32[]{:S(2)}, u32[]{:S(2)}) collective-permute-start(f32[3,128]{1,0:T(4,128)S(1)} %get-tuple-element.61), channel_id=1, source_target_pairs={{0,1},{1,0},{2,3},{3,2},{4,8},{5,9},{6,10},{7,11},{8,4},{9,5},{10,... | collective-permute-start | bytes 4616 | tf_op jit(solution)/shard_map/ppermute | solution.py:601
  33.6 2.4 %collective-permute-start.12 = (f32[3,128]{1,0:T(4,128)S(1)}, f32[3,128]{1,0:T(4,128)S(1)}, u32[]{:S(2)}, u32[]{:S(2)}) collective-permute-start(f32[3,128]{1,0:T(4,128)S(1)} %get-tuple-element.62), channel_id=1, source_target_pairs={{0,1},{1,0},{2,3},{3,2},{4,5},{5,4},{6,7},{7,6},{8,9},{9,8},{10,11... | collective-permute-start | bytes 4616 | tf_op jit(solution)/shard_map/ppermute | solution.py:601
  34.1 3.0 %collective-permute-start.13 = (f32[3,128]{1,0:T(4,128)S(1)}, f32[3,128]{1,0:T(4,128)S(1)}, u32[]{:S(2)}, u32[]{:S(2)}) collective-permute-start(f32[3,128]{1,0:T(4,128)S(1)} %get-tuple-element.63), channel_id=1, source_target_pairs={{0,3},{1,2},{2,1},{3,0},{4,7},{5,6},{6,5},{7,4},{8,11},{9,10},{10,... | collective-permute-start | bytes 4616 | tf_op jit(solution)/shard_map/ppermute | solution.py:601

commit v11 on v10

--- a/solution.py
+++ b/solution.py
@@ -135,7 +135,11 @@
         low_rows[g : g + 1] = ordered[1:2, g * LANES : (g + 1) * LANES]
     which = iota((META, LANES), 0)
     for k in range(dom_total):
-        owner = me ^ k
+        hop = jnp.int32(0)
+        for b in range(lax.axis_size("box") if k else 0):
+            here = lax.axis_index("box") == b
+            hop = jnp.where(here, hops(dom_total, b)[k - 1], hop)
+        owner = me ^ hop
         start = starts[owner]
         held = starts[owner + 1] - start
         block = jnp.zeros((META, LANES), F32)
@@ -566,7 +570,12 @@
         )
         payloads = {0: outgoing[0]}
         for k in range(1, dom_total):
-            payloads[k] = lax.ppermute(outgoing[k], "dom", [(i, i ^ k) for i in range(dom_total)])
+            pairs = [
+                (d * box_total + b, (d ^ hops(dom_total, b)[k - 1]) * box_total + b)
+                for d in range(dom_total)
+                for b in range(box_total)
+            ]
+            payloads[k] = lax.ppermute(outgoing[k], ("dom", "box"), pairs)
         order = arrival(dom_total)
         stages = [[0, *order[0]], *order[1:]]
 
@@ -606,12 +615,20 @@
     return history, force
 
 
+def hops(dom_total, box):
+    far = dom_total // 2
+    first = [dom_total - 1, *range(far + 1, dom_total - 1), far]
+    near = list(range(1, far))
+    turn = (1 - box) % len(near)
+    return [k ^ (box % far) for k in first] + near[turn:] + near[:turn]
+
+
 def arrival(dom_total):
-    far, last = dom_total // 2, dom_total - 1
+    far = dom_total // 2
     return [
-        [far, last, 1],
-        [last - 1, far - 1],
-        [*range(far + 1, last - 1), *range(2, far - 1)],
+        [*range(1, far - 1), far + 1],
+        [far - 1, far + 2],
+        [far, *range(far + 3, dom_total)],
     ]
 
 

time: 37.9 us -> 37.9 us (level)
  starting transfers between devices: 20 us -> 15.6 us
  waiting for transfers between devices: 4.68 us -> 9.06 us
    ppermute x7, waiting for transfers between devices: 0.02 us -> 3.38 us  [body(): payloads[k] = lax.ppermute(outgoing[k], ('dom', 'box'), pairs)]
    ppermute x7, starting transfers between devices: 13.8 us -> 10.9 us  [body(): payloads[k] = lax.ppermute(outgoing[k], ('dom', 'box'), pairs)]
    ppermute x4, starting transfers between devices: 3.05 us -> 1.53 us  [body(): halo[m] = lax.ppermute(exports[m], ('dom', 'box'), swaps(m))]
    ppermute x4, waiting for transfers between devices: 1.13 us -> 2.15 us  [body(): halo[m] = lax.ppermute(exports[m], ('dom', 'box'), swaps(m))]
  transfers between devices with their start and end apart: 14 -> 14, of which waited for: 3 -> 6; matrix products, arithmetic and copies ran while one was open for 0% -> 0% of each run, Pallas kernels for 20% -> 20%
where the time goes in v11:
time: 37.9 us; the launch traced here: 37.8 us
  starting transfers between devices  15.6 us (41%)
  Pallas kernels  12.2 us (32%)
  waiting for transfers between devices  9.06 us (24%)
  between operations  0.84 us (2%)
    pallas_call x10, Pallas kernels, call(): pl.pallas_call(kernel, out_shape=outs, in_specs=ins, out_specs=out_specs...  12.2 us
    ppermute x7, starting transfers between devices, body(): payloads[k] = lax.ppermute(outgoing[k], ('dom', 'box'), pairs)  10.9 us
    ppermute x3, waiting for transfers between devices, body(): lax.ppermute(packed[k], 'box', [(i, i ^ k) for i in range(box_total)])  3.52 us
    ppermute x7, waiting for transfers between devices, body(): payloads[k] = lax.ppermute(outgoing[k], ('dom', 'box'), pairs)  3.38 us
    ppermute x3, starting transfers between devices, body(): lax.ppermute(packed[k], 'box', [(i, i ^ k) for i in range(box_total)])  3.15 us
    ppermute x4, waiting for transfers between devices, body(): halo[m] = lax.ppermute(exports[m], ('dom', 'box'), swaps(m))  2.15 us
    ppermute x4, starting transfers between devices, body(): halo[m] = lax.ppermute(exports[m], ('dom', 'box'), swaps(m))  1.53 us
  transfers between devices with their start and end apart: 14, of which 6 were waited for; matrix products, arithmetic and copies ran while one was open for 0% of the time, Pallas kernels for 20%

profile of v11, /device:TPU:0, one launch (start us, length us, event | category | flops | bytes accessed | tf_op | source)
XLA Modules:
  0.0 37.8 jit_solution(10069359506130558852)
XLA Ops:
  0.7 1.0 %shard_map.151 = (bf16[4,128,128]{2,1,0:T(8,128)(2,1)S(1)}, bf16[4,128,128]{2,1,0:T(8,128)(2,1)S(1)}, bf16[4,128,128]{2,1,0:T(8,128)(2,1)S(1)}, bf16[4,128,128]{2,1,0:T(8,128)(2,1)S(1)}) custom-call(s32[8]{0:T(128)} %route_hbm.1, bf16[8,128,128]{2,1,0:T(8,128)(2,1)} %old_hbm.1), custom_call_target="tpu_custom_call" | custom-call | flops 2000000000 | bytes 100000 | tf_op jit(solution)/shard_map/pallas_call | solution.py:413
  1.7 0.6 %collective-permute-start = (bf16[4,128,128]{2,1,0:T(8,128)(2,1)S(1)}, bf16[4,128,128]{2,1,0:T(8,128)(2,1)S(1)}, u32[]{:S(2)}, u32[]{:S(2)}) collective-permute-start(bf16[4,128,128]{2,1,0:T(8,128)(2,1)S(1)} %get-tuple-element.40), channel_id=1, source_target_pairs={{0,1},{1,0},{2,3},{3,2},{4,5},{5,4},{6,7},{7,6},{8,9},{9,8},{10,11... | collective-permute-start | bytes 393224 | tf_op jit(solution)/shard_map/ppermute | solution.py:505
  2.2 2.6 %collective-permute-start.1 = (bf16[4,128,128]{2,1,0:T(8,128)(2,1)S(1)}, bf16[4,128,128]{2,1,0:T(8,128)(2,1)S(1)}, u32[]{:S(2)}, u32[]{:S(2)}) collective-permute-start(bf16[4,128,128]{2,1,0:T(8,128)(2,1)S(1)} %get-tuple-element.41), channel_id=1, source_target_pairs={{0,2},{1,3},{2,0},{3,1},{4,6},{5,7},{6,4},{7,5},{8,10},{9,11},{10,... | collective-permute-start | bytes 393224 | tf_op jit(solution)/shard_map/ppermute | solution.py:505
  4.8 0.0 collective-permute-start.2
  4.8 0.0 copy-start.10
  4.8 1.6 %shard_map.149 = (f32[2,8,128]{2,1,0:T(8,128)S(1)}, bf16[8,8,128]{2,1,0:T(8,128)(2,1)S(1)}, s32[16]{0:T(128)S(1)}) custom-call(s32[8,128]{1,0:T(8,128)S(1)} %bitcast.13, s32[1,1024]{1,0:T(1,128)S(1)} %bitcast.14), custom_call_target="tpu_custom_call" | custom-call | flops 2000000000 | bytes 100000 | tf_op jit(solution)/shard_map/pallas_call | solution.py:413
  6.5 1.4 %shard_map.150 = (bf16[8,512,128]{2,1,0:T(8,128)(2,1)S(1)}, f32[8,128]{1,0:T(8,128)S(1)}, s32[32]{0:T(128)S(1)}) custom-call(s32[4,8]{1,0:T(4,128)S(1)} %bitcast.15, s32[8]{0:T(128)S(1)} %copy-done.10, bf16[8,512,128]{2,1,0:T(8,128)(2,1)S(1)} %bitcast.12), custom_call_target="tpu_custom_call" | custom-call | flops 2000000000 | bytes 100000 | tf_op jit(solution)/shard_map/pallas_call | solution.py:413
  7.9 1.2 %collective-permute-done.1.rest_2_ = bf16[4,128,128]{2,1,0:T(8,128)(2,1)S(1)} collective-permute-done((bf16[4,128,128]{2,1,0:T(8,128)(2,1)S(1)}, bf16[4,128,128]{2,1,0:T(8,128)(2,1)S(1)}, u32[]{:S(2)}, u32[]{:S(2)}) %collective-permute-start.1) | collective-permute-done | bytes 131104 | tf_op jit(solution)/shard_map/ppermute | solution.py:505
  9.1 2.3 %collective-permute-done.2.rest_3_ = bf16[4,128,128]{2,1,0:T(8,128)(2,1)S(1)} collective-permute-done((bf16[4,128,128]{2,1,0:T(8,128)(2,1)S(1)}, bf16[4,128,128]{2,1,0:T(8,128)(2,1)S(1)}, u32[]{:S(2)}, u32[]{:S(2)}) %collective-permute-start.2) | collective-permute-done | bytes 131104 | tf_op jit(solution)/shard_map/ppermute | solution.py:505
  11.4 0.0 copy-start.4
  11.4 0.0 copy-start.5
  11.5 0.0 copy-start.11
  11.5 1.6 %shard_map.152 = (bf16[264,128]{1,0:T(8,128)(2,1)S(1)}, bf16[264,128]{1,0:T(8,128)(2,1)S(1)}, bf16[264,128]{1,0:T(8,128)(2,1)S(1)}, bf16[264,128]{1,0:T(8,128)(2...) custom-call(s32[16]{0:T(128)S(1)} %get-tuple-element.33.table_in, ...), custom_call_target="tpu_custom_call" | custom-call | flops 2000000000 | bytes 100000 | tf_op jit(solution)/shard_map/pallas_call | solution.py:413
  13.1 4.6 %collective-permute-start.7 = (bf16[264,128]{1,0:T(8,128)(2,1)S(1)}, bf16[264,128]{1,0:T(8,128)(2,1)S(1)}, u32[]{:S(2)}, u32[]{:S(2)}) collective-permute-start(bf16[264,128]{1,0:T(8,128)(2,1)S(1)} %get-tuple-element.48), channel_id=1, source_target_pairs={{0,28},{1,25},{2,22},{3,19},{4,24},{5,29},{6,18},{7,23},{8,20},{9,... | collective-permute-start | bytes 202760 | tf_op jit(solution)/shard_map/ppermute | solution.py:578
  17.7 2.9 %collective-permute-start.3 = (bf16[264,128]{1,0:T(8,128)(2,1)S(1)}, bf16[264,128]{1,0:T(8,128)(2,1)S(1)}, u32[]{:S(2)}, u32[]{:S(2)}) collective-permute-start(bf16[264,128]{1,0:T(8,128)(2,1)S(1)} %get-tuple-element.43), channel_id=1, source_target_pairs={{0,16},{1,21},{2,26},{3,31},{4,20},{5,17},{6,30},{7,27},{8,24},{9,... | collective-permute-start | bytes 202760 | tf_op jit(solution)/shard_map/ppermute | solution.py:578
  20.6 1.5 %collective-permute-start.5 = (bf16[264,128]{1,0:T(8,128)(2,1)S(1)}, bf16[264,128]{1,0:T(8,128)(2,1)S(1)}, u32[]{:S(2)}, u32[]{:S(2)}) collective-permute-start(bf16[264,128]{1,0:T(8,128)(2,1)S(1)} %get-tuple-element.45), channel_id=1, source_target_pairs={{0,24},{1,29},{2,18},{3,23},{4,28},{5,25},{6,22},{7,19},{8,16},{9,... | collective-permute-start | bytes 202760 | tf_op jit(solution)/shard_map/ppermute | solution.py:578
  22.1 1.5 %collective-permute-start.6 = (bf16[264,128]{1,0:T(8,128)(2,1)S(1)}, bf16[264,128]{1,0:T(8,128)(2,1)S(1)}, u32[]{:S(2)}, u32[]{:S(2)}) collective-permute-start(bf16[264,128]{1,0:T(8,128)(2,1)S(1)} %get-tuple-element.46), channel_id=1, source_target_pairs={{0,12},{1,9},{2,6},{3,15},{4,8},{5,13},{6,2},{7,11},{8,4},{9,1},{1... | collective-permute-start | bytes 202760 | tf_op jit(solution)/shard_map/ppermute | solution.py:578
  23.6 2.3 %collective-permute-done.8.refs_2_ = bf16[264,128]{1,0:T(8,128)(2,1)S(1)} collective-permute-done((bf16[264,128]{1,0:T(8,128)(2,1)S(1)}, bf16[264,128]{1,0:T(8,128)(2,1)S(1)}, u32[]{:S(2)}, u32[]{:S(2)}) %collective-permute-start.8) | collective-permute-done | bytes 67616 | tf_op jit(solution)/shard_map/ppermute | solution.py:578
  25.8 0.5 %collective-permute-start.4 = (bf16[264,128]{1,0:T(8,128)(2,1)S(1)}, bf16[264,128]{1,0:T(8,128)(2,1)S(1)}, u32[]{:S(2)}, u32[]{:S(2)}) collective-permute-start(bf16[264,128]{1,0:T(8,128)(2,1)S(1)} %get-tuple-element.44), channel_id=1, source_target_pairs={{0,4},{1,13},{2,10},{3,7},{4,0},{5,9},{6,14},{7,3},{8,12},{9,5},{1... | collective-permute-start | bytes 202760 | tf_op jit(solution)/shard_map/ppermute | solution.py:578
  26.3 2.8 %shard_map.155 = (f32[1024,128]{1,0:T(8,128)S(1)}, f32[8,1024]{1,0:T(8,128)S(1)}, bf16[8,1024,128]{2,1,0:T(8,128)(2,1)S(1)}, bf16[8,16,1024]{2,1,0:T(8,128)(2,1)...) custom-call(s32[8,1024]{1,0:T(8,128)S(1)} %copy-done, f32[3,1024]{1,0:T(4,128)S(1)} %copy-done.1, ...), custom_call_target="tpu_custom_call" | custom-call | flops 1000 | bytes 100000 | tf_op jit(solution)/shard_map/pallas_call | solution.py:413
  29.1 0.7 %shard_map.153.refs_2_ = f32[1024,128]{1,0:T(8,128)S(1)} custom-call(bf16[264,128]{1,0:T(8,128)(2,1)S(1)} %get-tuple-element.47.refs_0_, bf16[264,128]{1,0:T(8,128)(2,1)S(1)} %collective-permute-done.7.refs_1_, bf16[264,128]{1,0:T(8,128)(2,1)S(1)} %collective-permute-done.8.refs_2_, bf16[264,128]{1,0:T(8,128)(2,1)S(1)} %collective-permute-done.9.refs_3_), custom_call_target="tpu_custom_call" | custom-call | flops 1000 | bytes 100000 | tf_op jit(solution)/shard_map/pallas_call | solution.py:413
  29.9 0.0 collective-permute-done.5.refs_0_
  29.9 1.1 %collective-permute-done.6.refs_1_ = bf16[264,128]{1,0:T(8,128)(2,1)S(1)} collective-permute-done((bf16[264,128]{1,0:T(8,128)(2,1)S(1)}, bf16[264,128]{1,0:T(8,128)(2,1)S(1)}, u32[]{:S(2)}, u32[]{:S(2)}) %collective-permute-start.6) | collective-permute-done | bytes 67616 | tf_op jit(solution)/shard_map/ppermute | solution.py:578
  31.0 0.4 %shard_map.154.refs_2_ = f32[1024,128]{1,0:T(8,128)S(1)} custom-call(bf16[264,128]{1,0:T(8,128)(2,1)S(1)} %collective-permute-done.5.refs_0_, bf16[264,128]{1,0:T(8,128)(2,1)S(1)} %collective-permute-done.6.refs_1_, f32[1024,128]{1,0:T(8,128)S(1)} %shard_map.153.refs_2_), custom_call_target="tpu_custom_call" | custom-call | flops 1000 | bytes 100000 | tf_op jit(solution)/shard_map/pallas_call | solution.py:413
  31.4 1.2 %shard_map.156 = (bf16[1024,128]{1,0:T(8,128)(2,1)S(1)}, f32[3,8,128]{2,1,0:T(8,128)S(1)}, f32[3,128]{1,0:T(4,128)S(1)}, f32[3,128]{1,0:T(4,128)S(1)}, f32[3,128]{1,0:T(4,128)S(1)}, /*index=5*/f32[3,128]{1,0:T(4,128)S(1)}) custom-call(bf16[264,128]{1,0:T(8,128)(2,1)S(1)} %collective-permute-done.3.refs_0_, ...), custom_call_target="tpu_custom_call" | custom-call | flops 2000000000 | bytes 100000 | tf_op jit(solution)/shard_map/pallas_call | solution.py:413
  32.6 0.9 %collective-permute-start.10 = (f32[3,128]{1,0:T(4,128)S(1)}, f32[3,128]{1,0:T(4,128)S(1)}, u32[]{:S(2)}, u32[]{:S(2)}) collective-permute-start(f32[3,128]{1,0:T(4,128)S(1)} %get-tuple-element.60), channel_id=1, source_target_pairs={{0,4},{1,5},{2,6},{3,7},{4,0},{5,1},{6,2},{7,3},{8,12},{9,13},{10,... | collective-permute-start | bytes 4616 | tf_op jit(solution)/shard_map/ppermute | solution.py:610
  33.6 0.5 %collective-permute-start.12 = (f32[3,128]{1,0:T(4,128)S(1)}, f32[3,128]{1,0:T(4,128)S(1)}, u32[]{:S(2)}, u32[]{:S(2)}) collective-permute-start(f32[3,128]{1,0:T(4,128)S(1)} %get-tuple-element.62), channel_id=1, source_target_pairs={{0,1},{1,0},{2,3},{3,2},{4,5},{5,4},{6,7},{7,6},{8,9},{9,8},{10,11... | collective-permute-start | bytes 4616 | tf_op jit(solution)/shard_map/ppermute | solution.py:610
  34.1 0.1 collective-permute-start.13
  34.2 0.8 %shard_map.157 = bf16[1024,128]{1,0:T(8,128)(2,1)} custom-call(bf16[1024,128]{1,0:T(8,128)(2,1)S(1)} %get-tuple-element.56.arrived, f32[1024,128]{1,0:T(8,128)S(1)} %get-tuple-element.57.drive, f32[1,128]{1,0:T(1,128)S(1)} %bitcast.17), custom_call_target="tpu_custom_call" | custom-call | flops 2000000000 | bytes 100000 | tf_op jit(solution)/shard_map/pallas_call | solution.py:413
  34.9 1.3 %collective-permute-done.10.rest_0_ = f32[3,128]{1,0:T(4,128)S(1)} collective-permute-done((f32[3,128]{1,0:T(4,128)S(1)}, f32[3,128]{1,0:T(4,128)S(1)}, u32[]{:S(2)}, u32[]{:S(2)}) %collective-permute-start.10) | collective-permute-done | bytes 1568 | tf_op jit(solution)/shard_map/ppermute | solution.py:610
  36.3 0.8 %collective-permute-done.13.rest_3_ = f32[3,128]{1,0:T(4,128)S(1)} collective-permute-done((f32[3,128]{1,0:T(4,128)S(1)}, f32[3,128]{1,0:T(4,128)S(1)}, u32[]{:S(2)}, u32[]{:S(2)}) %collective-permute-start.13) | collective-permute-done | bytes 1568 | tf_op jit(solution)/shard_map/ppermute | solution.py:610
  37.1 0.7 %shard_map.158 = f32[3,1024]{1,0:T(4,128)} custom-call(f32[3,8,128]{2,1,0:T(8,128)S(1)} %get-tuple-element.58.local, s32[2,8,128]{2,1,0:T(8,128)S(1)} %get-tuple-element.59.inverse, f32[3,128]{1,0:T(4,128)S(1)} %collective-permute-done.10.rest_0_, f32[3,128]{1,0:T(4,128)S(1)} %collective-permute-done.11.rest_1_, ...), custom_call_target="tpu_custom_call" | custom-call | flops 2000000000 | bytes 100000 | tf_op jit(solution)/shard_map/pallas_call | solution.py:413
  (30 shorter events, 0.1 us)
Async XLA Ops:
  0.6 4.2 %copy-start.8 = (s32[1024]{0:T(1024)S(1)}, s32[1024]{0:T(1024)}, u32[]{:S(2)}) copy-start(s32[1024]{0:T(1024)} %param.20) | copy-start | bytes 12292
  0.6 4.2 %copy-start.7 = (s32[1024]{0:T(1024)S(1)}, s32[1024]{0:T(1024)}, u32[]{:S(2)}) copy-start(s32[1024]{0:T(1024)} %param.19) | copy-start | bytes 12292
  1.7 6.2 %collective-permute-start = (bf16[4,128,128]{2,1,0:T(8,128)(2,1)S(1)}, bf16[4,128,128]{2,1,0:T(8,128)(2,1)S(1)}, u32[]{:S(2)}, u32[]{:S(2)}) collective-permute-start(bf16[4,128,128]{2,1,0:T(8,128)(2,1)S(1)} %get-tuple-element.40), channel_id=1, source_target_pairs={{0,1},{1,0},{2,3},{3,2},{4,5},{5,4},{6,7},{7,6},{8,9},{9,8},{10,11... | collective-permute-start | bytes 393224 | tf_op jit(solution)/shard_map/ppermute | solution.py:505
  2.2 6.9 %collective-permute-start.1 = (bf16[4,128,128]{2,1,0:T(8,128)(2,1)S(1)}, bf16[4,128,128]{2,1,0:T(8,128)(2,1)S(1)}, u32[]{:S(2)}, u32[]{:S(2)}) collective-permute-start(bf16[4,128,128]{2,1,0:T(8,128)(2,1)S(1)} %get-tuple-element.41), channel_id=1, source_target_pairs={{0,2},{1,3},{2,0},{3,1},{4,6},{5,7},{6,4},{7,5},{8,10},{9,11},{10,... | collective-permute-start | bytes 393224 | tf_op jit(solution)/shard_map/ppermute | solution.py:505
  4.8 6.6 %collective-permute-start.2 = (bf16[4,128,128]{2,1,0:T(8,128)(2,1)S(1)}, bf16[4,128,128]{2,1,0:T(8,128)(2,1)S(1)}, u32[]{:S(2)}, u32[]{:S(2)}) collective-permute-start(bf16[4,128,128]{2,1,0:T(8,128)(2,1)S(1)} %get-tuple-element.42), channel_id=1, source_target_pairs={{0,3},{1,2},{2,1},{3,0},{4,7},{5,6},{6,5},{7,4},{8,11},{9,10},{10,... | collective-permute-start | bytes 393224 | tf_op jit(solution)/shard_map/ppermute | solution.py:505
  4.8 1.6 %copy-start.6 = (bf16[8,4,128,128]{3,2,1,0:T(8,128)(2,1)S(1)}, bf16[8,4,128,128]{3,2,1,0:T(8,128)(2,1)}, u32[]{:S(2)}) copy-start(bf16[8,4,128,128]{3,2,1,0:T(8,128)(2,1)} %param.18) | copy-start | bytes 3145732
  4.8 1.6 %copy-start.9 = (s32[8,4]{0,1:T(4,128)S(1)}, s32[8,4]{0,1:T(4,128)}, u32[]{:S(2)}) copy-start(s32[8,4]{0,1:T(4,128)} %param.16) | copy-start | bytes 388
  4.8 1.6 %copy-start.10 = (s32[8]{0:T(128)S(1)}, s32[8]{0:T(128)}, u32[]{:S(2)}) copy-start(s32[8]{0:T(128)} %count.1) | copy-start | bytes 100
  11.4 14.9 %copy-start = (s32[8,1024]{1,0:T(8,128)S(1)}, s32[8,1024]{1,0:T(8,128)}, u32[]{:S(2)}) copy-start(s32[8,1024]{1,0:T(8,128)} %connectivity.1) | copy-start | bytes 98308
  11.4 14.9 %copy-start.1 = (f32[3,1024]{1,0:T(4,128)S(1)}, f32[3,1024]{1,0:T(4,128)}, u32[]{:S(2)}) copy-start(f32[3,1024]{1,0:T(4,128)} %motion.1) | copy-start | bytes 36868
  11.4 14.9 %copy-start.2 = (f32[1024]{0:T(1024)S(1)}, f32[1024]{0:T(1024)}, u32[]{:S(2)}) copy-start(f32[1024]{0:T(1024)} %param.24) | copy-start | bytes 12292
  11.4 14.9 %copy-start.3 = (f32[128,6]{0,1:T(8,128)S(1)}, f32[128,6]{0,1:T(8,128)}, u32[]{:S(2)}) copy-start(f32[128,6]{0,1:T(8,128)} %param.26) | copy-start | bytes 9220
  11.4 14.9 %copy-start.4 = (f32[128,6]{0,1:T(8,128)S(1)}, f32[128,6]{0,1:T(8,128)}, u32[]{:S(2)}) copy-start(f32[128,6]{0,1:T(8,128)} %param.27) | copy-start | bytes 9220
  11.4 14.9 %copy-start.5 = (s32[4,128]{1,0:T(4,128)S(1)}, s32[4,128]{1,0:T(4,128)}, u32[]{:S(2)}) copy-start(s32[4,128]{1,0:T(4,128)} %shared.1) | copy-start | bytes 6148
  11.5 20.0 %copy-start.11 = (f32[128]{0:T(128)S(1)}, f32[128]{0:T(128)}, u32[]{:S(2)}) copy-start(f32[128]{0:T(128)} %param.25) | copy-start | bytes 1540
  13.1 9.0 %collective-permute-start.7 = (bf16[264,128]{1,0:T(8,128)(2,1)S(1)}, bf16[264,128]{1,0:T(8,128)(2,1)S(1)}, u32[]{:S(2)}, u32[]{:S(2)}) collective-permute-start(bf16[264,128]{1,0:T(8,128)(2,1)S(1)} %get-tuple-element.48), channel_id=1, source_target_pairs={{0,28},{1,25},{2,22},{3,19},{4,24},{5,29},{6,18},{7,23},{8,20},{9,... | collective-permute-start | bytes 202760 | tf_op jit(solution)/shard_map/ppermute | solution.py:578
  17.7 8.1 %collective-permute-start.8 = (bf16[264,128]{1,0:T(8,128)(2,1)S(1)}, bf16[264,128]{1,0:T(8,128)(2,1)S(1)}, u32[]{:S(2)}, u32[]{:S(2)}) collective-permute-start(bf16[264,128]{1,0:T(8,128)(2,1)S(1)} %get-tuple-element.49), channel_id=1, source_target_pairs={{0,20},{1,17},{2,30},{3,27},{4,16},{5,21},{6,26},{7,31},{8,28},{9,... | collective-permute-start | bytes 202760 | tf_op jit(solution)/shard_map/ppermute | solution.py:578
  17.7 13.7 %collective-permute-start.3 = (bf16[264,128]{1,0:T(8,128)(2,1)S(1)}, bf16[264,128]{1,0:T(8,128)(2,1)S(1)}, u32[]{:S(2)}, u32[]{:S(2)}) collective-permute-start(bf16[264,128]{1,0:T(8,128)(2,1)S(1)} %get-tuple-element.43), channel_id=1, source_target_pairs={{0,16},{1,21},{2,26},{3,31},{4,20},{5,17},{6,30},{7,27},{8,24},{9,... | collective-permute-start | bytes 202760 | tf_op jit(solution)/shard_map/ppermute | solution.py:578
  20.6 8.5 %collective-permute-start.9 = (bf16[264,128]{1,0:T(8,128)(2,1)S(1)}, bf16[264,128]{1,0:T(8,128)(2,1)S(1)}, u32[]{:S(2)}, u32[]{:S(2)}) collective-permute-start(bf16[264,128]{1,0:T(8,128)(2,1)S(1)} %get-tuple-element.50), channel_id=1, source_target_pairs={{0,8},{1,5},{2,14},{3,11},{4,12},{5,1},{6,10},{7,15},{8,0},{9,13},... | collective-permute-start | bytes 202760 | tf_op jit(solution)/shard_map/ppermute | solution.py:578
  20.6 9.3 %collective-permute-start.5 = (bf16[264,128]{1,0:T(8,128)(2,1)S(1)}, bf16[264,128]{1,0:T(8,128)(2,1)S(1)}, u32[]{:S(2)}, u32[]{:S(2)}) collective-permute-start(bf16[264,128]{1,0:T(8,128)(2,1)S(1)} %get-tuple-element.45), channel_id=1, source_target_pairs={{0,24},{1,29},{2,18},{3,23},{4,28},{5,25},{6,22},{7,19},{8,16},{9,... | collective-permute-start | bytes 202760 | tf_op jit(solution)/shard_map/ppermute | solution.py:578
  22.1 8.9 %collective-permute-start.6 = (bf16[264,128]{1,0:T(8,128)(2,1)S(1)}, bf16[264,128]{1,0:T(8,128)(2,1)S(1)}, u32[]{:S(2)}, u32[]{:S(2)}) collective-permute-start(bf16[264,128]{1,0:T(8,128)(2,1)S(1)} %get-tuple-element.46), channel_id=1, source_target_pairs={{0,12},{1,9},{2,6},{3,15},{4,8},{5,13},{6,2},{7,11},{8,4},{9,1},{1... | collective-permute-start | bytes 202760 | tf_op jit(solution)/shard_map/ppermute | solution.py:578
  25.8 5.6 %collective-permute-start.4 = (bf16[264,128]{1,0:T(8,128)(2,1)S(1)}, bf16[264,128]{1,0:T(8,128)(2,1)S(1)}, u32[]{:S(2)}, u32[]{:S(2)}) collective-permute-start(bf16[264,128]{1,0:T(8,128)(2,1)S(1)} %get-tuple-element.44), channel_id=1, source_target_pairs={{0,4},{1,13},{2,10},{3,7},{4,0},{5,9},{6,14},{7,3},{8,12},{9,5},{1... | collective-permute-start | bytes 202760 | tf_op jit(solution)/shard_map/ppermute | solution.py:578
  32.6 3.7 %collective-permute-start.10 = (f32[3,128]{1,0:T(4,128)S(1)}, f32[3,128]{1,0:T(4,128)S(1)}, u32[]{:S(2)}, u32[]{:S(2)}) collective-permute-start(f32[3,128]{1,0:T(4,128)S(1)} %get-tuple-element.60), channel_id=1, source_target_pairs={{0,4},{1,5},{2,6},{3,7},{4,0},{5,1},{6,2},{7,3},{8,12},{9,13},{10,... | collective-permute-start | bytes 4616 | tf_op jit(solution)/shard_map/ppermute | solution.py:610
  33.6 2.7 %collective-permute-start.11 = (f32[3,128]{1,0:T(4,128)S(1)}, f32[3,128]{1,0:T(4,128)S(1)}, u32[]{:S(2)}, u32[]{:S(2)}) collective-permute-start(f32[3,128]{1,0:T(4,128)S(1)} %get-tuple-element.61), channel_id=1, source_target_pairs={{0,1},{1,0},{2,3},{3,2},{4,8},{5,9},{6,10},{7,11},{8,4},{9,5},{10,... | collective-permute-start | bytes 4616 | tf_op jit(solution)/shard_map/ppermute | solution.py:610
  33.6 2.7 %collective-permute-start.12 = (f32[3,128]{1,0:T(4,128)S(1)}, f32[3,128]{1,0:T(4,128)S(1)}, u32[]{:S(2)}, u32[]{:S(2)}) collective-permute-start(f32[3,128]{1,0:T(4,128)S(1)} %get-tuple-element.62), channel_id=1, source_target_pairs={{0,1},{1,0},{2,3},{3,2},{4,5},{5,4},{6,7},{7,6},{8,9},{9,8},{10,11... | collective-permute-start | bytes 4616 | tf_op jit(solution)/shard_map/ppermute | solution.py:610
  34.1 3.0 %collective-permute-start.13 = (f32[3,128]{1,0:T(4,128)S(1)}, f32[3,128]{1,0:T(4,128)S(1)}, u32[]{:S(2)}, u32[]{:S(2)}) collective-permute-start(f32[3,128]{1,0:T(4,128)S(1)} %get-tuple-element.63), channel_id=1, source_target_pairs={{0,3},{1,2},{2,1},{3,0},{4,7},{5,6},{6,5},{7,4},{8,11},{9,10},{10,... | collective-permute-start | bytes 4616 | tf_op jit(solution)/shard_map/ppermute | solution.py:610
